TPU v7x, 32 devices: a whole 2x2x4 slice. The times are simulated.
32 devices in a mesh: cfg: 2 (over y), site: 4 (over z), vec: 2 (over x), tslice: 2 (over core).
Axes of the slice: x: 2, y: 2, z: 4, core: 2. Of those that a mesh axis runs over, the one named last changes fastest.
Arguments:
- eigvecs: float32 [4, 2, 3, 384, 4, 512], P(('cfg', 'tslice'), None, None, 'vec', 'site'), parts along dimension 0, may hold values from -1.5 to 1.5
- links: float32 [4, 3, 2, 3, 3, 4, 512], P(('cfg', 'tslice'), None, None, None, None, 'site'), parts along dimension 0, may hold values from -1 to 1, as said below
- peramb: bfloat16 [4, 8, 4, 2, 384, 384], P(('cfg', 'tslice'), 'site', None, None, 'vec'), parts along dimension 0, may hold values from -0.21875 to 0.21875
- block_owner: int32 [2], replicated, may hold values from 0 to 1, each once
- momenta: int32 [2, 3], replicated, may hold values from -2 to 2, as said below
Outputs:
- projected: bfloat16 [4, 8, 4, 2, 2, 384, 384], P(('cfg', 'tslice'), 'site', None, None, None, 'vec'), parts along dimension 0
There are 2 independent parts, one for each index of `cfg`. A program takes and returns all parts, laid end to end along the dimension named above; an argument that names none is the same for every part. Nothing has to cross between parts.
Inputs may be any that keep to these rules, and one draw needn't show every extreme that they name: Block b of eigvecs holds the eigenvectors numbered from block_owner[b] * 192 on; every block number appears once. `momenta`: every component is -2, -1, 1 or 2, never zero. `links`: every 3 x 3 link matrix is unitary.
All inputs are finite; a program needn't handle non-finite values.
Results may differ from a plain program's by a relative error of at most 0.0065.
Values may be sent and summed in bfloat16 or wider, within the bound.
No kernel may reach another device: no remote copies, remote signals or barrier semaphores. Data moves between devices by JAX's collectives and lax.ppermute only.
A program may use at most 128 MiB of HBM per device.

v0:
```python
import functools
import math

import jax
import jax.numpy as jnp
from jax import lax
from jax.experimental import pallas as pl
from jax.experimental.pallas import tpu as pltpu
from jax.sharding import PartitionSpec as P


LX = 32
LY = 16
LANES = 128

two_pi = 2.0 * math.pi

CHUNKS = (16, 24, 8)


def phase_angle(momenta, across, upward, depth, extent):
    return two_pi * (
        (momenta[:, 0, None, None] * across[None]).astype(jnp.float32) / LX
        + (momenta[:, 1, None, None] * upward[None]).astype(jnp.float32) / LY
        + (momenta[:, 2, None, None] * depth[None]).astype(jnp.float32) / extent
    )


VMEM = pl.BlockSpec(memory_space=pltpu.VMEM)
SMEM = pl.BlockSpec(memory_space=pltpu.SMEM)
ANY = pl.BlockSpec(memory_space=pl.ANY)
GRANT = pltpu.CompilerParams(vmem_limit_bytes=16 * 2**20)


class Shifts:
    def __init__(self):
        lane = lax.broadcasted_iota(jnp.int32, (8, LANES), 1)
        row = lax.broadcasted_iota(jnp.int32, (8, LANES), 0) % 4
        column = lane % LX
        self.x_last = column == LX - 1
        self.x_first = column == 0
        self.y_high = lane >= LANES - LX
        self.y_low = lane < LX
        self.row_last = row == 3
        self.row_first = row == 0

    def ahead_x(self, v):
        return jnp.where(self.x_last, pltpu.roll(v, LX - 1, 1), pltpu.roll(v, LANES - 1, 1))

    def behind_x(self, v):
        return jnp.where(self.x_first, pltpu.roll(v, LANES - LX + 1, 1), pltpu.roll(v, 1, 1))

    def ahead_y(self, v):
        a = pltpu.roll(v, LANES - LX, 1)
        wrapped = jnp.where(self.row_last, pltpu.roll(a, 3, 0), pltpu.roll(a, 7, 0))
        return jnp.where(self.y_high, wrapped, a)

    def behind_y(self, v):
        a = pltpu.roll(v, LX, 1)
        wrapped = jnp.where(self.row_first, pltpu.roll(a, 5, 0), pltpu.roll(a, 1, 0))
        return jnp.where(self.y_low, wrapped, a)


def tables_kernel(*refs):
    table_ref = refs[-1]
    shifts = Shifts()
    scale = jnp.float32(-1.0 / 6.0)
    size = refs[0].shape[0]
    links = [ref[ref.shape[0] - size :].astype(jnp.float32) for ref in refs[:-1]]
    count = len(links)

    def entry(plane, direction, part, row, col):
        e = direction * 18 + part * 9 + row * 3 + col
        value = links[plane % count][4 * e : 4 * e + 4] * scale
        return jnp.concatenate([value, value], axis=0)

    for plane in range(count):
        for direction in range(3):
            for target in range(3):
                for source in range(3):
                    slot = (2 * direction) * 18 + (target * 3 + source) * 2
                    table_ref[plane, slot] = entry(plane, direction, 0, target, source)
                    table_ref[plane, slot + 1] = entry(plane, direction, 1, target, source)
                    slot = (2 * direction + 1) * 18 + (target * 3 + source) * 2
                    below = plane + 1 if direction == 2 else plane
                    re = entry(below, direction, 0, source, target)
                    im = entry(below, direction, 1, source, target)
                    if direction < 2:
                        move = shifts.behind_x if direction == 0 else shifts.behind_y
                        re, im = move(re), move(im)
                    table_ref[plane, slot] = re
                    table_ref[plane, slot + 1] = -im


def link_tables(links):
    return pl.pallas_call(
        tables_kernel,
        out_shape=pltpu.VMEM((len(links), 108, 8, LANES), jnp.float32),
        in_specs=[VMEM] * len(links),
        out_specs=VMEM,
        compiler_params=GRANT,
        name="link_tables",
    )(*links)


def pack_kernel(sites, chunk, place_ref, own_ref, *refs):
    outs = refs[1 - sites :]
    rows = CHUNKS[chunk] * 4
    for d in range(1, sites):
        start = row_of(lax.rem(place_ref[0] + d, sites), own_ref.shape[1] // sites, chunk)
        out = outs[d - 1]
        for c in range(6):
            out[c * rows : (c + 1) * rows] = own_ref[c, pl.ds(start, rows), :].astype(jnp.bfloat16)
        if out.shape[0] > 6 * rows:
            out[6 * rows :] = refs[0][...].astype(jnp.bfloat16)


def row_of(slot, rows_per_slot, chunk):
    return pl.multiple_of(slot * rows_per_slot + 4 * sum(CHUNKS[:chunk]), 32)


def pack(own, place, chunk, sites, links, after):
    extra = [links] if chunk == 0 else []
    length = 24 * CHUNKS[chunk] + sum(e.shape[0] for e in extra)
    return pl.pallas_call(
        functools.partial(pack_kernel, sites, chunk),
        out_shape=[pltpu.VMEM((length, LANES), jnp.bfloat16)] * (sites - 1),
        in_specs=[SMEM] + [VMEM] * (1 + len(extra)) + [ANY] * len(after),
        out_specs=[VMEM] * (sites - 1),
        compiler_params=GRANT,
    )(place, own, *extra, *after)


def filter_kernel(sites, chunk, place_ref, *refs):
    fields, table_ref = refs[:sites], refs[sites]
    outs, t1_ref = refs[-1 - sites : -1], refs[-1]
    shifts = Shifts()
    rows = CHUNKS[chunk] * 4
    home = row_of(place_ref[0], fields[0].shape[1] // sites, chunk)

    def hop(plane, here, ahead_z, behind_z):
        count = len(here(0))
        total = [[None] * count for _ in range(6)]
        moves = (shifts.ahead_x, shifts.behind_x, shifts.ahead_y, shifts.behind_y, None, None)
        for direction in range(6):
            if direction < 4:
                field = [[moves[direction](v) for v in here(c)] for c in range(6)]
            else:
                take = ahead_z if direction == 4 else behind_z
                field = [take(c) for c in range(6)]
            for target in range(3):
                for source in range(3):
                    slot = direction * 18 + (target * 3 + source) * 2
                    re = table_ref[plane, slot]
                    im = table_ref[plane, slot + 1]
                    for n in range(count):
                        f_re, f_im = field[source][n], field[3 + source][n]
                        add_re = re * f_re - im * f_im
                        add_im = re * f_im + im * f_re
                        if total[target][n] is None:
                            total[target][n], total[3 + target][n] = add_re, add_im
                        else:
                            total[target][n] = total[target][n] + add_re
                            total[3 + target][n] = total[3 + target][n] + add_im
        return total

    def step(index, carry):
        base = pl.multiple_of(index * 16, 16)

        def start(plane):
            def read(c):
                ref = fields[plane % sites]
                if plane % sites == 0:
                    value = ref[c, pl.ds(pl.multiple_of(home + base, 16), 16), :]
                else:
                    value = ref[pl.ds(pl.multiple_of(c * rows + base, 16), 16), :].astype(jnp.float32)
                return [value[0:8], value[8:16]]

            return read

        def first(plane):
            return lambda c: [t1_ref[plane % sites, c, 0:8], t1_ref[plane % sites, c, 8:16]]

        for plane in range(sites):
            out = hop(plane, start(plane), start(plane - 1), start(plane + 1))
            for c in range(6):
                for n in range(2):
                    t1_ref[plane, c, 8 * n : 8 * n + 8] = out[c][n]
        for plane in range(sites):
            out = hop(plane, first(plane), first(plane - 1), first(plane + 1))
            for c in range(6):
                value = 2.0 * jnp.concatenate(out[c], axis=0)
                outs[plane][c, pl.ds(base, 16), :] = value.astype(jnp.bfloat16)
        return carry

    lax.fori_loop(0, rows // 16, step, 0)


def filter_chunk(own, place, chunk, received, table, after):
    sites = len(received) + 1
    rows = CHUNKS[chunk] * 4
    return pl.pallas_call(
        functools.partial(filter_kernel, sites, chunk),
        out_shape=[pltpu.VMEM((6, rows, LANES), jnp.bfloat16)] * sites,
        in_specs=[SMEM] + [VMEM] * (sites + 1) + [ANY] * len(after),
        out_specs=[VMEM] * sites,
        scratch_shapes=[pltpu.VMEM((sites, 6, 16, LANES), jnp.float32)],
        cost_estimate=pl.CostEstimate(
            flops=432 * 2 * sites * rows * LANES, bytes_accessed=6 * rows * LANES * 4 * sites, transcendentals=0),
        compiler_params=GRANT,
    )(place, own, *received, table, *after)


def finish_kernel(sites, chunk, place_ref, own_ref, *refs):
    hops = refs[:sites]
    cosine_ref, sine_ref = refs[sites : sites + 2]
    filtered_ref, shifted_ref, work_ref = refs[-3:]
    vectors = CHUNKS[chunk]
    momenta = cosine_ref.shape[0]
    for d in range(sites):
        slot = lax.rem(place_ref[0] + d, sites)
        start = row_of(slot, own_ref.shape[1] // sites, chunk)
        for c in range(6):
            work_ref[d, c] = hops[d][c].astype(jnp.float32) - own_ref[c, pl.ds(start, 4 * vectors), :]
        for color in range(3):
            for row in range(4):
                at = slice((color * 4 + row) * LANES, (color * 4 + row + 1) * LANES)
                re = work_ref[d, color, pl.ds(row, vectors, stride=4), :].astype(jnp.bfloat16)
                im = work_ref[d, 3 + color, pl.ds(row, vectors, stride=4), :].astype(jnp.bfloat16)
                filtered_ref[slot, 0, :, at] = re
                filtered_ref[slot, 1, :, at] = im
                re, im = re.astype(jnp.float32), im.astype(jnp.float32)
                for p in range(momenta):
                    cosine = cosine_ref[p, row : row + 1, :]
                    sine = sine_ref[p, row : row + 1, :]
                    shifted_ref[p, slot, 0, :, at] = (cosine * re + sine * im).astype(jnp.bfloat16)
                    shifted_ref[p, slot, 1, :, at] = (cosine * im - sine * re).astype(jnp.bfloat16)


def finish(own, place, chunk, hops, cosine, sine, after):
    sites, momenta, vectors = len(hops), cosine.shape[0], CHUNKS[chunk]
    shapes = ((sites, 2, vectors, 12 * LANES), (momenta, sites, 2, vectors, 12 * LANES))
    return pl.pallas_call(
        functools.partial(finish_kernel, sites, chunk),
        out_shape=[pltpu.VMEM(shape, jnp.bfloat16) for shape in shapes],
        in_specs=[SMEM] + [VMEM] * (sites + 3) + [ANY] * len(after),
        out_specs=[VMEM, VMEM],
        scratch_shapes=[pltpu.VMEM((sites, 6, 4 * vectors, LANES), jnp.float32)],
        cost_estimate=pl.CostEstimate(
            flops=20 * sites * 24 * vectors * LANES, bytes_accessed=sites * 24 * vectors * LANES * 12,
            transcendentals=0),
        compiler_params=GRANT,
    )(place, own, *hops, cosine, sine, *after)


def elemental_kernel(segments, chunks, place_ref, *refs):
    own = refs[:chunks]
    other = refs[chunks : 2 * chunks]
    shifted = refs[2 * chunks : 3 * chunks]
    outs = refs[3 * chunks : 3 * chunks + segments]
    left_ref, right_ref, total_ref = refs[3 * chunks + segments :]
    slots, _, _, depth = own[0].shape
    per_slot = sum(CHUNKS)
    block = slots * per_slot
    for n, ref in enumerate(own + other):
        size = CHUNKS[n % chunks]
        for slot in range(slots):
            at = n // chunks * block + slot * per_slot + sum(CHUNKS[: n % chunks])
            for part in range(2):
                left_ref[at : at + size, part * depth : (part + 1) * depth] = ref[slot, part]
    momenta = shifted[0].shape[0]
    for p in range(momenta):
        for n, ref in enumerate(shifted):
            size = CHUNKS[n]
            for slot in range(slots):
                re, im = ref[p, slot, 0], ref[p, slot, 1]
                at = slot * per_slot + sum(CHUNKS[:n])
                right_ref[at : at + size, :depth] = re
                right_ref[at : at + size, depth:] = im
                right_ref[block + at : block + at + size, :depth] = im
                right_ref[block + at : block + at + size, depth:] = -re
        product = lax.dot_general(
            left_ref[...], right_ref[...], (((1,), (1,)), ((), ())), preferred_element_type=jnp.float32)
        rows = product.shape[0] // segments
        for s in range(segments):
            total_ref[s, :, p * 2 * block : (p + 1) * 2 * block] = product[s * rows : (s + 1) * rows]
    place = place_ref[0]
    for d in range(segments):
        s = lax.rem(place + d, segments)
        outs[d][...] = total_ref[s].astype(outs[d].dtype)


def elementals(place, own, other, shifted, segments):
    chunks = len(own)
    slots, _, _, depth = own[0].shape
    momenta = shifted[0].shape[0]
    block = slots * sum(CHUNKS)
    rows = 2 * block // segments
    columns = momenta * 2 * block
    return pl.pallas_call(
        functools.partial(elemental_kernel, segments, chunks),
        out_shape=tuple(
            pltpu.VMEM((rows, columns), jnp.float32 if d == 0 else jnp.bfloat16) for d in range(segments)),
        in_specs=[SMEM] + [VMEM] * (3 * chunks),
        out_specs=tuple(VMEM for _ in range(segments)),
        scratch_shapes=[
            pltpu.VMEM((2 * block, 2 * depth), jnp.bfloat16),
            pltpu.VMEM((2 * block, 2 * depth), jnp.bfloat16),
            pltpu.VMEM((segments, rows, columns), jnp.float32),
        ],
        cost_estimate=pl.CostEstimate(
            flops=2 * 2 * block * columns * 2 * depth, bytes_accessed=8 * 2 * block * depth, transcendentals=0),
        compiler_params=GRANT,
        name="elementals",
    )(place, *own, *other, *shifted)


def projection_kernel(sites, groups, place_ref, owner_ref, tau_ref, *refs):
    pieces = refs[: sites * groups]
    out_ref, parts_ref, right_ref = refs[sites * groups :]
    momenta, nvec = right_ref.shape[0], right_ref.shape[1] // 2
    block = nvec // 2

    @pl.when(pl.program_id(0) == 0)
    def assemble():
        rows = pieces[0].shape[0]
        for n, piece in enumerate(pieces):
            up, across = n // groups, n % groups
            z, v = lax.rem(place_ref[0] + up, sites), lax.rem(place_ref[1] + across, groups)
            per = block // rows
            column = owner_ref[v]
            row = owner_ref[lax.rem(v + lax.div(z, per), groups)] * block + lax.rem(z, per) * rows
            row = pl.multiple_of(row, 32)
            for p in range(momenta):
                parts_ref[column, p, pl.ds(row, rows), :] = piece[:, p * 2 * block : (p + 1) * 2 * block]
        for p in range(momenta):
            low, high = parts_ref[0, p], parts_ref[1, p]
            re = jnp.concatenate([low[:, :block], high[:, :block]], axis=1)
            im = jnp.concatenate([low[:, block:], high[:, block:]], axis=1)
            right_ref[p, :nvec, :nvec] = re
            right_ref[p, :nvec, nvec:] = im
            right_ref[p, nvec:, :nvec] = -im
            right_ref[p, nvec:, nvec:] = re

    left = jnp.concatenate([tau_ref[0, 0], tau_ref[0, 1]], axis=1)
    for p in range(momenta):
        product = jnp.dot(left, right_ref[p], preferred_element_type=jnp.float32)
        out_ref[0, p, 0] = product[:, :nvec].astype(jnp.bfloat16)
        out_ref[0, p, 1] = product[:, nvec:].astype(jnp.bfloat16)


def projection(tau, place, owner, pieces, momenta, sites, groups):
    outer, _, rows, nvec = tau.shape
    count = len(pieces)
    return pl.pallas_call(
        functools.partial(projection_kernel, sites, groups),
        grid=(outer,),
        out_shape=jax.ShapeDtypeStruct((outer, momenta, 2, rows, nvec), jnp.bfloat16),
        in_specs=[pl.BlockSpec(memory_space=pltpu.SMEM), pl.BlockSpec(memory_space=pltpu.SMEM),
                  pl.BlockSpec((1, 2, rows, nvec), lambda i: (i, 0, 0, 0))]
        + [pl.BlockSpec(memory_space=pltpu.VMEM)] * count,
        out_specs=pl.BlockSpec((1, momenta, 2, rows, nvec), lambda i: (i, 0, 0, 0, 0)),
        scratch_shapes=[
            pltpu.VMEM((2, momenta, nvec, nvec), jnp.bfloat16),
            pltpu.VMEM((momenta, 2 * nvec, 2 * nvec), jnp.bfloat16),
        ],
        cost_estimate=pl.CostEstimate(
            flops=2 * outer * rows * 2 * nvec * 2 * nvec * momenta, bytes_accessed=outer * rows * nvec * 12,
            transcendentals=0),
        compiler_params=GRANT,
        name="projection",
    )(place, owner, tau, *pieces)


def from_place(block, up, across):
    sites, groups = lax.axis_size("site"), lax.axis_size("vec")
    route = []
    for z in range(sites):
        for v in range(groups):
            route.append((((z + up) % sites) * groups + (v + across) % groups, z * groups + v))
    return lax.ppermute(block, ("site", "vec"), route)


ORDER = (("filter", 0), ("filter", 1), ("finish", 0), ("filter", 2), ("finish", 1), ("finish", 2))


def per_device(eigvecs, links, peramb, block_owner, momenta):
    sites, groups = lax.axis_size("site"), lax.axis_size("vec")
    site, group = lax.axis_index("site"), lax.axis_index("vec")
    block = eigvecs.shape[3]
    own = eigvecs.reshape(6, block * 4, LANES)
    own_links = links.reshape(216, LANES)
    place = jnp.stack([site, group]).astype(jnp.int32)

    received, packed = [], []
    for chunk in range(len(CHUNKS)):
        packed = pack(own, place, chunk, sites, own_links, packed[:1])
        received.append([from_place(packed[d - 1], -d, 0) for d in range(1, sites)])

    flat = lax.broadcasted_iota(jnp.int32, (4, LANES), 0) * LANES + lax.broadcasted_iota(jnp.int32, (4, LANES), 1)
    theta = phase_angle(momenta, flat % LX, flat // LX, jnp.full_like(flat, site), sites)
    cosine, sine = jnp.cos(theta), jnp.sin(theta)

    table = link_tables([own_links] + received[0])
    hops, filtered, shifted, other = {}, {}, {}, {}
    last = None
    for kind, chunk in ORDER:
        after = [] if last is None else [last]
        if kind == "filter":
            out = filter_chunk(own, place, chunk, received[chunk], table, after)
            hops[chunk] = [out[0]] + [from_place(out[d], d, 0) for d in range(1, sites)]
            last = out[0]
        else:
            f, s = finish(own, place, chunk, hops[chunk], cosine, sine, after)
            other[chunk] = from_place(f, 0, 1)
            filtered[chunk], shifted[chunk] = f, s
            last = s
    filtered, shifted, other = ([group_of[n] for n in range(len(CHUNKS))] for group_of in (filtered, shifted, other))

    parts = elementals(place, filtered, other, shifted, sites)
    total = parts[0]
    for d in range(1, sites):
        total = total + from_place(parts[d], -d, 0).astype(jnp.float32)
    mine = total.astype(jnp.bfloat16)

    gathered = []
    for up in range(sites):
        piece = mine if up == 0 else from_place(mine, up, 0)
        gathered.append(piece)
        for across in range(1, groups):
            gathered.append(from_place(piece, 0, across))
    sinks, spins = peramb.shape[1], peramb.shape[2]
    tau = peramb.reshape(sinks * spins, 2, block, peramb.shape[5])
    result = projection(tau, place, block_owner, gathered, momenta.shape[0], sites, groups)
    return result.reshape(1, sinks, spins, momenta.shape[0], 2, block, peramb.shape[5])


def from_behind(block, axis, distance):
    devices = range(lax.axis_size(axis))
    route = [((i - distance) % len(devices), i) for i in devices]
    return lax.ppermute(block, axis, route)


def with_halo(block, sides, width):
    for axis, dim in sides:
        count = lax.axis_size(axis)
        forward = [(i, i + 1) for i in range(count - 1)]
        forward.append((count - 1, 0))
        backward = [(target, source) for source, target in forward]
        low = lax.ppermute(
            lax.slice_in_dim(block, block.shape[dim] - width, None, axis=dim), axis, forward
        )
        high = lax.ppermute(lax.slice_in_dim(block, 0, width, axis=dim), axis, backward)
        block = jnp.concatenate([low, block, high], axis=dim)
    return block


def along(field, direction, sense):
    width = field.shape[-1]
    column = lax.broadcasted_iota(jnp.int32, (width,), 0) % LX
    if direction == 0:
        if sense > 0:
            return jnp.where(column == LX - 1, jnp.roll(field, LX - 1, -1), jnp.roll(field, -1, -1))
        return jnp.where(column == 0, jnp.roll(field, 1 - LX, -1), jnp.roll(field, 1, -1))
    return jnp.roll(field, -sense * LX, -1)


def link_times(link_re, link_im, field_re, field_im, dagger):
    result_re = []
    result_im = []
    for target in range(3):
        summed_re = jnp.zeros_like(field_re[0])
        summed_im = jnp.zeros_like(field_re[0])
        for source in range(3):
            if dagger:
                entry_re = link_re[source, target][None]
                entry_im = -link_im[source, target][None]
            else:
                entry_re = link_re[target, source][None]
                entry_im = link_im[target, source][None]
            summed_re = summed_re + entry_re * field_re[source] - entry_im * field_im[source]
            summed_im = summed_im + entry_re * field_im[source] + entry_im * field_re[source]
        result_re.append(summed_re)
        result_im.append(summed_im)
    return (jnp.stack(result_re), jnp.stack(result_im))


def chebyshev(initial, operate):
    current = operate(initial)
    following = 2.0 * operate(current) - initial
    return following


def general_device(eigvecs, links, peramb, block_owner, momenta):
    vectors = eigvecs[0]
    links_here = links[0]
    block = vectors.shape[2]
    layers = vectors.shape[3]
    plane = vectors.shape[4]
    site_count = lax.axis_size("site")
    group_count = lax.axis_size("vec")
    site_rank = lax.axis_index("site")
    group_rank = lax.axis_index("vec")
    portion = plane // group_count
    top_plane = links_here[2, :, :, :, layers - 1 :, :]
    below = from_behind(top_plane, "site", 1)
    behind_links = jnp.concatenate([below, links_here[2, :, :, :, : layers - 1, :]], axis=3)
    back_links = []
    for direction in range(2):
        back_links.append(
            (
                along(links_here[direction, 0], direction, -1),
                along(links_here[direction, 1], direction, -1),
            )
        )
    back_links.append((behind_links[0], behind_links[1]))

    def operate(field):
        padded = with_halo(field, (("site", 3),), 1)
        total_re = jnp.zeros_like(field[0])
        total_im = jnp.zeros_like(field[0])
        for direction in range(3):
            if direction < 2:
                ahead = along(field, direction, 1)
                behind = along(field, direction, -1)
            else:
                ahead = padded[:, :, :, 2:]
                behind = padded[:, :, :, :-2]
            forward = link_times(
                links_here[direction, 0], links_here[direction, 1], ahead[0], ahead[1], False
            )
            backward = link_times(
                back_links[direction][0], back_links[direction][1], behind[0], behind[1], True
            )
            total_re = total_re + forward[0] + backward[0]
            total_im = total_im + forward[1] + backward[1]
        return jnp.stack([total_re, total_im]) * (-1.0 / 6.0)

    filtered = chebyshev(vectors, operate).astype(jnp.bfloat16)
    received = lax.all_to_all(filtered, "vec", split_axis=4, concat_axis=2, tiled=True)
    grouped = received.reshape(2, 3, group_count, block, layers, portion)
    ranks = jnp.arange(group_count, dtype=jnp.int32)
    inverse = jnp.sum(
        ranks[:, None] * (block_owner[:, None] == ranks[None, :]).astype(jnp.int32), axis=0
    )
    ordered = jnp.take(grouped, inverse, axis=2).reshape(2, 3, group_count * block, layers, portion)
    nvec = group_count * block
    flat = group_rank * portion + lax.broadcasted_iota(jnp.int32, (layers, portion), 1)
    depth = site_rank * layers + lax.broadcasted_iota(jnp.int32, (layers, portion), 0)
    theta = phase_angle(momenta, flat % LX, flat // LX, depth, layers * site_count)
    values = ordered.astype(jnp.float32)
    cosine = jnp.cos(theta)[:, None, None]
    sine = jnp.sin(theta)[:, None, None]
    shift_re = cosine * values[0] + sine * values[1]
    shift_im = cosine * values[1] - sine * values[0]
    shifted = jnp.stack([shift_re, shift_im], axis=1).astype(jnp.bfloat16)
    products = jnp.einsum(
        "acizs,pbckzs->aipbk", ordered, shifted, preferred_element_type=jnp.float32
    )
    real = products[0, :, :, 0] + products[1, :, :, 1]
    imag = products[0, :, :, 1] - products[1, :, :, 0]
    momentum_count = momenta.shape[0]
    partial_sum = jnp.stack([real, imag], axis=2).reshape(nvec, momentum_count * 2 * nvec)
    tau = peramb[0]
    tau_rows = tau.reshape(-1, nvec)
    summed = lax.psum(partial_sum, ("site", "vec")).astype(jnp.bfloat16)
    joined = jnp.dot(tau_rows, summed, preferred_element_type=jnp.float32)
    sinks = tau.shape[0]
    spins = tau.shape[1]
    layout = joined.reshape(sinks, spins, 2, block, momentum_count, 2, nvec)
    real_part = layout[:, :, 0, :, :, 0] - layout[:, :, 1, :, :, 1]
    imag_part = layout[:, :, 0, :, :, 1] + layout[:, :, 1, :, :, 0]
    stacked = jnp.stack([real_part, imag_part], axis=0)
    result = jnp.transpose(stacked, (1, 2, 4, 0, 3, 5))
    return result[None].astype(jnp.bfloat16)


def choose(eigvecs, links, peramb, block_owner, momenta):
    block, layers, plane = eigvecs.shape[3:]
    sites, groups = lax.axis_size("site"), lax.axis_size("vec")
    fits = layers == 1 and plane == LX * LY == 4 * LANES and sites == 4 and groups == 2
    fits = fits and block == sites * sum(CHUNKS) and (2 * block) % (32 * sites) == 0 and block % (2 * block // sites) == 0
    device = per_device if fits else general_device
    return device(eigvecs, links, peramb, block_owner, momenta)


def solution(mesh):
    placed = (
        P(("cfg", "tslice"), None, None, "vec", "site", None),
        P(("cfg", "tslice"), None, None, None, None, "site", None),
        P(("cfg", "tslice"), "site", None, None, "vec", None),
        P(),
        P(),
    )
    return jax.shard_map(
        choose,
        mesh=mesh,
        in_specs=placed,
        out_specs=P(("cfg", "tslice"), "site", None, None, None, "vec", None),
        check_vma=False,
    )
```

profile of v0, /device:TPU:0, one launch (start us, length us, event | category | flops | bytes accessed | tf_op | source)
XLA Modules:
  0.0 140.2 jit_solution(14487700305010035850)
XLA Ops:
  0.1 1.7 %copy-done = f32[1,2,3,192,1,512]{5,4,3,2,1,0:T(1,128)S(1)} copy-done((f32[1,2,3,192,1,512]{5,4,3,2,1,0:T(1,128)S(1)}, f32[1,2,3,192,1,512]{5,4,3,2,1,0:T(1,128)}, u32[]{:S(2)}) %copy-start) | copy-done | bytes 2359320
  3.2 4.1 %collective-permute-start.1 = (bf16[600,128]{1,0:T(8,128)(2,1)S(1)}, bf16[600,128]{1,0:T(8,128)(2,1)S(1)}, u32[]{:S(2)}, u32[]{:S(2)}) collective-permute-start(bf16[600,128]{1,0:T(8,128)(2,1)S(1)} %get-tuple-element.37), channel_id=1, source_target_pairs={{8,0},{10,2},{12,4},{14,6},{0,8},{2,10},{4,12},{6,14},{9,1},{11,3}... | collective-permute-start | bytes 460808 | tf_op jit(solution)/shard_map/ppermute | solution.py:381
  11.1 2.9 %collective-permute-start.8 = (bf16[576,128]{1,0:T(8,128)(2,1)S(1)}, bf16[576,128]{1,0:T(8,128)(2,1)S(1)}, u32[]{:S(2)}, u32[]{:S(2)}) collective-permute-start(bf16[576,128]{1,0:T(8,128)(2,1)S(1)} %get-tuple-element.45), channel_id=1, source_target_pairs={{4,0},{6,2},{8,4},{10,6},{12,8},{14,10},{0,12},{2,14},{5,1},{7,3},... | collective-permute-start | bytes 442376 | tf_op jit(solution)/shard_map/ppermute | solution.py:381
  14.1 2.2 %collective-permute-done.1.refs_2_ = bf16[600,128]{1,0:T(8,128)(2,1)S(1)} collective-permute-done((bf16[600,128]{1,0:T(8,128)(2,1)S(1)}, bf16[600,128]{1,0:T(8,128)(2,1)S(1)}, u32[]{:S(2)}, u32[]{:S(2)}) %collective-permute-start.1) | collective-permute-done | bytes 153632 | tf_op jit(solution)/shard_map/ppermute | solution.py:381
  16.3 3.4 %collective-permute-start.6 = (bf16[576,128]{1,0:T(8,128)(2,1)S(1)}, bf16[576,128]{1,0:T(8,128)(2,1)S(1)}, u32[]{:S(2)}, u32[]{:S(2)}) collective-permute-start(bf16[576,128]{1,0:T(8,128)(2,1)S(1)} %get-tuple-element.43.refs_0_), channel_id=1, source_target_pairs={{12,0},{14,2},{0,4},{2,6},{4,8},{6,10},{8,12},{10,14},{13,1},{15,3... | collective-permute-start | bytes 442376 | tf_op jit(solution)/shard_map/ppermute | solution.py:381
  20.5 6.2 %collective-permute-start.12 = (bf16[192,128]{1,0:T(8,128)(2,1)S(1)}, bf16[192,128]{1,0:T(8,128)(2,1)S(1)}, u32[]{:S(2)}, u32[]{:S(2)}) collective-permute-start(bf16[192,128]{1,0:T(8,128)(2,1)S(1)} %get-tuple-element.51), channel_id=1, source_target_pairs={{12,0},{14,2},{0,4},{2,6},{4,8},{6,10},{8,12},{10,14},{13,1},{15,3... | collective-permute-start | bytes 147464 | tf_op jit(solution)/shard_map/ppermute | solution.py:381
  27.0 5.8 %shard_map.56 = (bf16[6,64,128]{2,1,0:T(8,128)(2,1)S(1)}, bf16[6,64,128]{2,1,0:T(8,128)(2,1)S(1)}, bf16[6,64,128]{2,1,0:T(8,128)(2,1)S(1)}, bf16[6,64,128]{2,1,0:T(8,128)(2,1)S(1)}) custom-call(s32[2]{0:T(128)S(1)} %pad_add_fusion.place_ref, f32[6,768,128]{2,1,0:T(8,128)S(1)} %bitcast.9, bf16[600,128]{1,0:T(8,128)(2,1)S(1)} %collective-permute-done.refs_1_, ...), custom_call_target="tpu_custom_call" | custom-call | flops 28311552 | bytes 786432 | tf_op jit(solution)/shard_map/pallas_call | solution.py:202
  32.9 3.7 %collective-permute-start.4 = (bf16[6,64,128]{2,1,0:T(8,128)(2,1)S(1)}, bf16[6,64,128]{2,1,0:T(8,128)(2,1)S(1)}, u32[]{:S(2)}, u32[]{:S(2)}) collective-permute-start(bf16[6,64,128]{2,1,0:T(8,128)(2,1)S(1)} %get-tuple-element.41), channel_id=1, source_target_pairs={{8,0},{10,2},{12,4},{14,6},{0,8},{2,10},{4,12},{6,14},{9,1},{11,3}... | collective-permute-start | bytes 294920 | tf_op jit(solution)/shard_map/ppermute | solution.py:381
  36.6 1.9 %collective-permute-start.5 = (bf16[6,64,128]{2,1,0:T(8,128)(2,1)S(1)}, bf16[6,64,128]{2,1,0:T(8,128)(2,1)S(1)}, u32[]{:S(2)}, u32[]{:S(2)}) collective-permute-start(bf16[6,64,128]{2,1,0:T(8,128)(2,1)S(1)} %get-tuple-element.42), channel_id=1, source_target_pairs={{12,0},{14,2},{0,4},{2,6},{4,8},{6,10},{8,12},{10,14},{13,1},{15,3... | collective-permute-start | bytes 294920 | tf_op jit(solution)/shard_map/ppermute | solution.py:381
  38.8 8.4 %shard_map.58 = (bf16[6,96,128]{2,1,0:T(8,128)(2,1)S(1)}, bf16[6,96,128]{2,1,0:T(8,128)(2,1)S(1)}, bf16[6,96,128]{2,1,0:T(8,128)(2,1)S(1)}, bf16[6,96,128]{2,1,0:T(8,128)(2,1)S(1)}) custom-call(s32[2]{0:T(128)S(1)} %pad_add_fusion.place_ref, f32[6,768,128]{2,1,0:T(8,128)S(1)} %bitcast.10, bf16[576,128]{1,0:T(8,128)(2,1)S(1)} %collective-permute-done.6.refs_1_, ...), custom_call_target="tpu_custom_call" | custom-call | flops 42467328 | bytes 1179648 | tf_op jit(solution)/shard_map/pallas_call | solution.py:202
  47.3 2.4 %collective-permute-start.14 = (bf16[192,128]{1,0:T(8,128)(2,1)S(1)}, bf16[192,128]{1,0:T(8,128)(2,1)S(1)}, u32[]{:S(2)}, u32[]{:S(2)}) collective-permute-start(bf16[192,128]{1,0:T(8,128)(2,1)S(1)} %get-tuple-element.53), channel_id=1, source_target_pairs={{4,0},{6,2},{8,4},{10,6},{12,8},{14,10},{0,12},{2,14},{5,1},{7,3},... | collective-permute-start | bytes 147464 | tf_op jit(solution)/shard_map/ppermute | solution.py:381
  49.6 2.0 %collective-permute-start.9 = (bf16[6,96,128]{2,1,0:T(8,128)(2,1)S(1)}, bf16[6,96,128]{2,1,0:T(8,128)(2,1)S(1)}, u32[]{:S(2)}, u32[]{:S(2)}) collective-permute-start(bf16[6,96,128]{2,1,0:T(8,128)(2,1)S(1)} %get-tuple-element.48), channel_id=1, source_target_pairs={{4,0},{6,2},{8,4},{10,6},{12,8},{14,10},{0,12},{2,14},{5,1},{7,3},... | collective-permute-start | bytes 442376 | tf_op jit(solution)/shard_map/ppermute | solution.py:381
  51.7 1.5 %collective-permute-start.11 = (bf16[6,96,128]{2,1,0:T(8,128)(2,1)S(1)}, bf16[6,96,128]{2,1,0:T(8,128)(2,1)S(1)}, u32[]{:S(2)}, u32[]{:S(2)}) collective-permute-start(bf16[6,96,128]{2,1,0:T(8,128)(2,1)S(1)} %get-tuple-element.50), channel_id=1, source_target_pairs={{12,0},{14,2},{0,4},{2,6},{4,8},{6,10},{8,12},{10,14},{13,1},{15,3... | collective-permute-start | bytes 442376 | tf_op jit(solution)/shard_map/ppermute | solution.py:381
  54.2 3.2 %shard_map.61 = (bf16[6,32,128]{2,1,0:T(8,128)(2,1)S(1)}, bf16[6,32,128]{2,1,0:T(8,128)(2,1)S(1)}, bf16[6,32,128]{2,1,0:T(8,128)(2,1)S(1)}, bf16[6,32,128]{2,1,0:T(8,128)(2,1)S(1)}) custom-call(s32[2]{0:T(128)S(1)} %pad_add_fusion.place_ref, f32[6,768,128]{2,1,0:T(8,128)S(1)} %bitcast.12, bf16[192,128]{1,0:T(8,128)(2,1)S(1)} %collective-permute-done.12.refs_1_, ...), custom_call_target="tpu_custom_call" | custom-call | flops 14155776 | bytes 393216 | tf_op jit(solution)/shard_map/pallas_call | solution.py:202
  57.4 7.1 %collective-permute-done.10.refs_2_ = bf16[6,96,128]{2,1,0:T(8,128)(2,1)S(1)} collective-permute-done((bf16[6,96,128]{2,1,0:T(8,128)(2,1)S(1)}, bf16[6,96,128]{2,1,0:T(8,128)(2,1)S(1)}, u32[]{:S(2)}, u32[]{:S(2)}) %collective-permute-start.10) | collective-permute-done | bytes 147488 | tf_op jit(solution)/shard_map/ppermute | solution.py:381
  65.6 2.0 %collective-permute-start.19 = (bf16[4,2,24,1536]{3,2,1,0:T(8,128)(2,1)S(1)}, bf16[4,2,24,1536]{3,2,1,0:T(8,128)(2,1)S(1)}, u32[]{:S(2)}, u32[]{:S(2)}) collective-permute-start(bf16[4,2,24,1536]{3,2,1,0:T(8,128)(2,1)S(1)} %get-tuple-element.56.refs_1_), channel_id=1, source_target_pairs={{2,0},{0,2},{6,4},{4,6},{10,8},{8,10},{14,12},{12,14},{3,1},{1,3},... | collective-permute-start | bytes 1769480 | tf_op jit(solution)/shard_map/ppermute | solution.py:381
  67.9 2.2 %collective-permute-start.16 = (bf16[6,32,128]{2,1,0:T(8,128)(2,1)S(1)}, bf16[6,32,128]{2,1,0:T(8,128)(2,1)S(1)}, u32[]{:S(2)}, u32[]{:S(2)}) collective-permute-start(bf16[6,32,128]{2,1,0:T(8,128)(2,1)S(1)} %get-tuple-element.58), channel_id=1, source_target_pairs={{8,0},{10,2},{12,4},{14,6},{0,8},{2,10},{4,12},{6,14},{9,1},{11,3}... | collective-permute-start | bytes 147464 | tf_op jit(solution)/shard_map/ppermute | solution.py:381
  70.0 2.0 %collective-permute-start.17 = (bf16[6,32,128]{2,1,0:T(8,128)(2,1)S(1)}, bf16[6,32,128]{2,1,0:T(8,128)(2,1)S(1)}, u32[]{:S(2)}, u32[]{:S(2)}) collective-permute-start(bf16[6,32,128]{2,1,0:T(8,128)(2,1)S(1)} %get-tuple-element.59), channel_id=1, source_target_pairs={{12,0},{14,2},{0,4},{2,6},{4,8},{6,10},{8,12},{10,14},{13,1},{15,3... | collective-permute-start | bytes 147464 | tf_op jit(solution)/shard_map/ppermute | solution.py:381
  73.1 2.8 %collective-permute-done.17.refs_3_ = bf16[6,32,128]{2,1,0:T(8,128)(2,1)S(1)} collective-permute-done((bf16[6,32,128]{2,1,0:T(8,128)(2,1)S(1)}, bf16[6,32,128]{2,1,0:T(8,128)(2,1)S(1)}, u32[]{:S(2)}, u32[]{:S(2)}) %collective-permute-start.17) | collective-permute-done | bytes 49184 | tf_op jit(solution)/shard_map/ppermute | solution.py:381
  78.2 13.5 %collective-permute-done.20.refs_5_ = bf16[4,2,8,1536]{3,2,1,0:T(8,128)(2,1)S(1)} collective-permute-done((bf16[4,2,8,1536]{3,2,1,0:T(8,128)(2,1)S(1)}, bf16[4,2,8,1536]{3,2,1,0:T(8,128)(2,1)S(1)}, u32[]{:S(2)}, u32[]{:S(2)}) %collective-permute-start.20) | collective-permute-done | bytes 196640 | tf_op jit(solution)/shard_map/ppermute | solution.py:381
  91.7 3.3 %elementals.1 = (f32[96,768]{1,0:T(8,128)S(1)}, bf16[96,768]{1,0:T(8,128)(2,1)S(1)}, bf16[96,768]{1,0:T(8,128)(2,1)S(1)}, bf16[96,768]{1,0:T(8,128)(2,1)S(1)}) custom-call(s32[2]{0:T(128)S(1)} %pad_add_fusion.place_ref, bf16[4,2,16,1536]{3,2,1,0:T(8,128)(2,1)S(1)} %get-tuple-element.47.refs_0_, bf16[4,2,24,1536]{3,2,1,0:T(8,128)(2,1)S(1)} %get-tuple-element.56.refs_1_, ...), custom_call_target="tpu_custom_call" | custom-call | flops 1811939328 | bytes 4718592 | tf_op jit(solution)/shard_map/elementals/pallas_call | solution.py:300
  95.0 2.3 %collective-permute-start.21 = (bf16[96,768]{1,0:T(8,128)(2,1)S(1)}, bf16[96,768]{1,0:T(8,128)(2,1)S(1)}, u32[]{:S(2)}, u32[]{:S(2)}) collective-permute-start(bf16[96,768]{1,0:T(8,128)(2,1)S(1)} %get-tuple-element.64), channel_id=1, source_target_pairs={{12,0},{14,2},{0,4},{2,6},{4,8},{6,10},{8,12},{10,14},{13,1},{15,3... | collective-permute-start | bytes 442376 | tf_op jit(solution)/shard_map/ppermute | solution.py:381
  97.3 2.0 %collective-permute-start.22 = (bf16[96,768]{1,0:T(8,128)(2,1)S(1)}, bf16[96,768]{1,0:T(8,128)(2,1)S(1)}, u32[]{:S(2)}, u32[]{:S(2)}) collective-permute-start(bf16[96,768]{1,0:T(8,128)(2,1)S(1)} %get-tuple-element.65), channel_id=1, source_target_pairs={{8,0},{10,2},{12,4},{14,6},{0,8},{2,10},{4,12},{6,14},{9,1},{11,3}... | collective-permute-start | bytes 442376 | tf_op jit(solution)/shard_map/ppermute | solution.py:381
  99.3 2.8 %collective-permute-start.23 = (bf16[96,768]{1,0:T(8,128)(2,1)S(1)}, bf16[96,768]{1,0:T(8,128)(2,1)S(1)}, u32[]{:S(2)}, u32[]{:S(2)}) collective-permute-start(bf16[96,768]{1,0:T(8,128)(2,1)S(1)} %get-tuple-element.66), channel_id=1, source_target_pairs={{4,0},{6,2},{8,4},{10,6},{12,8},{14,10},{0,12},{2,14},{5,1},{7,3},... | collective-permute-start | bytes 442376 | tf_op jit(solution)/shard_map/ppermute | solution.py:381
  102.5 5.9 %collective-permute-done.22 = bf16[96,768]{1,0:T(8,128)(2,1)S(1)} collective-permute-done((bf16[96,768]{1,0:T(8,128)(2,1)S(1)}, bf16[96,768]{1,0:T(8,128)(2,1)S(1)}, u32[]{:S(2)}, u32[]{:S(2)}) %collective-permute-start.22) | collective-permute-done | bytes 147488 | tf_op jit(solution)/shard_map/ppermute | solution.py:381
  108.5 3.9 %collective-permute-start.29 = (bf16[96,768]{1,0:T(8,128)(2,1)S(1)}, bf16[96,768]{1,0:T(8,128)(2,1)S(1)}, u32[]{:S(2)}, u32[]{:S(2)}) collective-permute-start(bf16[96,768]{1,0:T(8,128)(2,1)S(1)} %add_convert_fusion.refs_0_), channel_id=1, source_target_pairs={{12,0},{14,2},{0,4},{2,6},{4,8},{6,10},{8,12},{10,14},{13,1},{15,3... | collective-permute-start | bytes 442376 | tf_op jit(solution)/shard_map/ppermute | solution.py:381
  112.4 3.4 %collective-permute-start.27 = (bf16[96,768]{1,0:T(8,128)(2,1)S(1)}, bf16[96,768]{1,0:T(8,128)(2,1)S(1)}, u32[]{:S(2)}, u32[]{:S(2)}) collective-permute-start(bf16[96,768]{1,0:T(8,128)(2,1)S(1)} %add_convert_fusion.refs_0_), channel_id=1, source_target_pairs={{8,0},{10,2},{12,4},{14,6},{0,8},{2,10},{4,12},{6,14},{9,1},{11,3}... | collective-permute-start | bytes 442376 | tf_op jit(solution)/shard_map/ppermute | solution.py:381
  116.8 3.2 %collective-permute-done.29.refs_6_ = bf16[96,768]{1,0:T(8,128)(2,1)S(1)} collective-permute-done((bf16[96,768]{1,0:T(8,128)(2,1)S(1)}, bf16[96,768]{1,0:T(8,128)(2,1)S(1)}, u32[]{:S(2)}, u32[]{:S(2)}) %collective-permute-start.29) | collective-permute-done | bytes 147488 | tf_op jit(solution)/shard_map/ppermute | solution.py:381
  121.0 2.8 %collective-permute-done.27.refs_4_ = bf16[96,768]{1,0:T(8,128)(2,1)S(1)} collective-permute-done((bf16[96,768]{1,0:T(8,128)(2,1)S(1)}, bf16[96,768]{1,0:T(8,128)(2,1)S(1)}, u32[]{:S(2)}, u32[]{:S(2)}) %collective-permute-start.27) | collective-permute-done | bytes 147488 | tf_op jit(solution)/shard_map/ppermute | solution.py:381
  125.9 4.7 %collective-permute-done.28.refs_5_ = bf16[96,768]{1,0:T(8,128)(2,1)S(1)} collective-permute-done((bf16[96,768]{1,0:T(8,128)(2,1)S(1)}, bf16[96,768]{1,0:T(8,128)(2,1)S(1)}, u32[]{:S(2)}, u32[]{:S(2)}) %collective-permute-start.28) | collective-permute-done | bytes 147488 | tf_op jit(solution)/shard_map/ppermute | solution.py:381
  130.5 2.1 %collective-permute-done.26.refs_3_ = bf16[96,768]{1,0:T(8,128)(2,1)S(1)} collective-permute-done((bf16[96,768]{1,0:T(8,128)(2,1)S(1)}, bf16[96,768]{1,0:T(8,128)(2,1)S(1)}, u32[]{:S(2)}, u32[]{:S(2)}) %collective-permute-start.26) | collective-permute-done | bytes 147488 | tf_op jit(solution)/shard_map/ppermute | solution.py:381
  132.7 7.6 %projection.1 = bf16[8,2,2,192,384]{4,3,2,1,0:T(8,128)(2,1)} custom-call(s32[2]{0:T(128)S(1)} %pad_add_fusion.place_ref, s32[2]{0:T(128)S(1)} %copy-done.5, bf16[8,2,192,384]{3,2,1,0:T(8,128)(2,1)S(1)} %bitcast.17, bf16[96,768]{1,0:T(8,128)(2,1)S(1)} %add_convert_fusion.refs_0_, bf16[96,768]{1,0:T(8,128)(2,1)S(1)} %collective-permute-done.24.refs_1_, ...), custom_call_target="tpu_custom_call" | custom-call | flops 3623878656 | bytes 7077888 | tf_op jit(solution)/shard_map/projection/pallas_call | solution.py:355
  (63 shorter events, 16.9 us)
Async XLA Ops:
  3.2 13.1 %collective-permute-start.1 = (bf16[600,128]{1,0:T(8,128)(2,1)S(1)}, bf16[600,128]{1,0:T(8,128)(2,1)S(1)}, u32[]{:S(2)}, u32[]{:S(2)}) collective-permute-start(bf16[600,128]{1,0:T(8,128)(2,1)S(1)} %get-tuple-element.37), channel_id=1, source_target_pairs={{8,0},{10,2},{12,4},{14,6},{0,8},{2,10},{4,12},{6,14},{9,1},{11,3}... | collective-permute-start | bytes 460808 | tf_op jit(solution)/shard_map/ppermute | solution.py:381
  7.4 13.1 %collective-permute-start.2 = (bf16[600,128]{1,0:T(8,128)(2,1)S(1)}, bf16[600,128]{1,0:T(8,128)(2,1)S(1)}, u32[]{:S(2)}, u32[]{:S(2)}) collective-permute-start(bf16[600,128]{1,0:T(8,128)(2,1)S(1)} %get-tuple-element.38), channel_id=1, source_target_pairs={{4,0},{6,2},{8,4},{10,6},{12,8},{14,10},{0,12},{2,14},{5,1},{7,3},... | collective-permute-start | bytes 460808 | tf_op jit(solution)/shard_map/ppermute | solution.py:381
  8.7 18.0 %collective-permute-start = (bf16[600,128]{1,0:T(8,128)(2,1)S(1)}, bf16[600,128]{1,0:T(8,128)(2,1)S(1)}, u32[]{:S(2)}, u32[]{:S(2)}) collective-permute-start(bf16[600,128]{1,0:T(8,128)(2,1)S(1)} %get-tuple-element.36.refs_0_), channel_id=1, source_target_pairs={{12,0},{14,2},{0,4},{2,6},{4,8},{6,10},{8,12},{10,14},{13,1},{15,3... | collective-permute-start | bytes 460808 | tf_op jit(solution)/shard_map/ppermute | solution.py:381
  10.0 22.9 %collective-permute-start.7 = (bf16[576,128]{1,0:T(8,128)(2,1)S(1)}, bf16[576,128]{1,0:T(8,128)(2,1)S(1)}, u32[]{:S(2)}, u32[]{:S(2)}) collective-permute-start(bf16[576,128]{1,0:T(8,128)(2,1)S(1)} %get-tuple-element.44), channel_id=1, source_target_pairs={{8,0},{10,2},{12,4},{14,6},{0,8},{2,10},{4,12},{6,14},{9,1},{11,3}... | collective-permute-start | bytes 442376 | tf_op jit(solution)/shard_map/ppermute | solution.py:381
  11.1 25.5 %collective-permute-start.8 = (bf16[576,128]{1,0:T(8,128)(2,1)S(1)}, bf16[576,128]{1,0:T(8,128)(2,1)S(1)}, u32[]{:S(2)}, u32[]{:S(2)}) collective-permute-start(bf16[576,128]{1,0:T(8,128)(2,1)S(1)} %get-tuple-element.45), channel_id=1, source_target_pairs={{4,0},{6,2},{8,4},{10,6},{12,8},{14,10},{0,12},{2,14},{5,1},{7,3},... | collective-permute-start | bytes 442376 | tf_op jit(solution)/shard_map/ppermute | solution.py:381
  16.3 22.4 %collective-permute-start.6 = (bf16[576,128]{1,0:T(8,128)(2,1)S(1)}, bf16[576,128]{1,0:T(8,128)(2,1)S(1)}, u32[]{:S(2)}, u32[]{:S(2)}) collective-permute-start(bf16[576,128]{1,0:T(8,128)(2,1)S(1)} %get-tuple-element.43.refs_0_), channel_id=1, source_target_pairs={{12,0},{14,2},{0,4},{2,6},{4,8},{6,10},{8,12},{10,14},{13,1},{15,3... | collective-permute-start | bytes 442376 | tf_op jit(solution)/shard_map/ppermute | solution.py:381
  20.5 26.8 %collective-permute-start.12 = (bf16[192,128]{1,0:T(8,128)(2,1)S(1)}, bf16[192,128]{1,0:T(8,128)(2,1)S(1)}, u32[]{:S(2)}, u32[]{:S(2)}) collective-permute-start(bf16[192,128]{1,0:T(8,128)(2,1)S(1)} %get-tuple-element.51), channel_id=1, source_target_pairs={{12,0},{14,2},{0,4},{2,6},{4,8},{6,10},{8,12},{10,14},{13,1},{15,3... | collective-permute-start | bytes 147464 | tf_op jit(solution)/shard_map/ppermute | solution.py:381
  32.8 16.8 %collective-permute-start.3 = (bf16[6,64,128]{2,1,0:T(8,128)(2,1)S(1)}, bf16[6,64,128]{2,1,0:T(8,128)(2,1)S(1)}, u32[]{:S(2)}, u32[]{:S(2)}) collective-permute-start(bf16[6,64,128]{2,1,0:T(8,128)(2,1)S(1)} %get-tuple-element.40), channel_id=1, source_target_pairs={{4,0},{6,2},{8,4},{10,6},{12,8},{14,10},{0,12},{2,14},{5,1},{7,3},... | collective-permute-start | bytes 294920 | tf_op jit(solution)/shard_map/ppermute | solution.py:381
  32.9 18.7 %collective-permute-start.4 = (bf16[6,64,128]{2,1,0:T(8,128)(2,1)S(1)}, bf16[6,64,128]{2,1,0:T(8,128)(2,1)S(1)}, u32[]{:S(2)}, u32[]{:S(2)}) collective-permute-start(bf16[6,64,128]{2,1,0:T(8,128)(2,1)S(1)} %get-tuple-element.41), channel_id=1, source_target_pairs={{8,0},{10,2},{12,4},{14,6},{0,8},{2,10},{4,12},{6,14},{9,1},{11,3}... | collective-permute-start | bytes 294920 | tf_op jit(solution)/shard_map/ppermute | solution.py:381
  36.6 15.1 %collective-permute-start.5 = (bf16[6,64,128]{2,1,0:T(8,128)(2,1)S(1)}, bf16[6,64,128]{2,1,0:T(8,128)(2,1)S(1)}, u32[]{:S(2)}, u32[]{:S(2)}) collective-permute-start(bf16[6,64,128]{2,1,0:T(8,128)(2,1)S(1)} %get-tuple-element.42), channel_id=1, source_target_pairs={{12,0},{14,2},{0,4},{2,6},{4,8},{6,10},{8,12},{10,14},{13,1},{15,3... | collective-permute-start | bytes 294920 | tf_op jit(solution)/shard_map/ppermute | solution.py:381
  38.7 15.5 %collective-permute-start.13 = (bf16[192,128]{1,0:T(8,128)(2,1)S(1)}, bf16[192,128]{1,0:T(8,128)(2,1)S(1)}, u32[]{:S(2)}, u32[]{:S(2)}) collective-permute-start(bf16[192,128]{1,0:T(8,128)(2,1)S(1)} %get-tuple-element.52), channel_id=1, source_target_pairs={{8,0},{10,2},{12,4},{14,6},{0,8},{2,10},{4,12},{6,14},{9,1},{11,3}... | collective-permute-start | bytes 147464 | tf_op jit(solution)/shard_map/ppermute | solution.py:381
  47.3 7.0 %collective-permute-start.14 = (bf16[192,128]{1,0:T(8,128)(2,1)S(1)}, bf16[192,128]{1,0:T(8,128)(2,1)S(1)}, u32[]{:S(2)}, u32[]{:S(2)}) collective-permute-start(bf16[192,128]{1,0:T(8,128)(2,1)S(1)} %get-tuple-element.53), channel_id=1, source_target_pairs={{4,0},{6,2},{8,4},{10,6},{12,8},{14,10},{0,12},{2,14},{5,1},{7,3},... | collective-permute-start | bytes 147464 | tf_op jit(solution)/shard_map/ppermute | solution.py:381
  49.6 7.8 %collective-permute-start.9 = (bf16[6,96,128]{2,1,0:T(8,128)(2,1)S(1)}, bf16[6,96,128]{2,1,0:T(8,128)(2,1)S(1)}, u32[]{:S(2)}, u32[]{:S(2)}) collective-permute-start(bf16[6,96,128]{2,1,0:T(8,128)(2,1)S(1)} %get-tuple-element.48), channel_id=1, source_target_pairs={{4,0},{6,2},{8,4},{10,6},{12,8},{14,10},{0,12},{2,14},{5,1},{7,3},... | collective-permute-start | bytes 442376 | tf_op jit(solution)/shard_map/ppermute | solution.py:381
  51.7 12.9 %collective-permute-start.10 = (bf16[6,96,128]{2,1,0:T(8,128)(2,1)S(1)}, bf16[6,96,128]{2,1,0:T(8,128)(2,1)S(1)}, u32[]{:S(2)}, u32[]{:S(2)}) collective-permute-start(bf16[6,96,128]{2,1,0:T(8,128)(2,1)S(1)} %get-tuple-element.49), channel_id=1, source_target_pairs={{8,0},{10,2},{12,4},{14,6},{0,8},{2,10},{4,12},{6,14},{9,1},{11,3}... | collective-permute-start | bytes 442376 | tf_op jit(solution)/shard_map/ppermute | solution.py:381
  51.7 12.9 %collective-permute-start.11 = (bf16[6,96,128]{2,1,0:T(8,128)(2,1)S(1)}, bf16[6,96,128]{2,1,0:T(8,128)(2,1)S(1)}, u32[]{:S(2)}, u32[]{:S(2)}) collective-permute-start(bf16[6,96,128]{2,1,0:T(8,128)(2,1)S(1)} %get-tuple-element.50), channel_id=1, source_target_pairs={{12,0},{14,2},{0,4},{2,6},{4,8},{6,10},{8,12},{10,14},{13,1},{15,3... | collective-permute-start | bytes 442376 | tf_op jit(solution)/shard_map/ppermute | solution.py:381
  65.6 26.1 %collective-permute-start.19 = (bf16[4,2,24,1536]{3,2,1,0:T(8,128)(2,1)S(1)}, bf16[4,2,24,1536]{3,2,1,0:T(8,128)(2,1)S(1)}, u32[]{:S(2)}, u32[]{:S(2)}) collective-permute-start(bf16[4,2,24,1536]{3,2,1,0:T(8,128)(2,1)S(1)} %get-tuple-element.56.refs_1_), channel_id=1, source_target_pairs={{2,0},{0,2},{6,4},{4,6},{10,8},{8,10},{14,12},{12,14},{3,1},{1,3},... | collective-permute-start | bytes 1769480 | tf_op jit(solution)/shard_map/ppermute | solution.py:381
  67.6 24.1 %collective-permute-start.18 = (bf16[4,2,16,1536]{3,2,1,0:T(8,128)(2,1)S(1)}, bf16[4,2,16,1536]{3,2,1,0:T(8,128)(2,1)S(1)}, u32[]{:S(2)}, u32[]{:S(2)}) collective-permute-start(bf16[4,2,16,1536]{3,2,1,0:T(8,128)(2,1)S(1)} %get-tuple-element.47.refs_0_), channel_id=1, source_target_pairs={{2,0},{0,2},{6,4},{4,6},{10,8},{8,10},{14,12},{12,14},{3,1},{1,3},... | collective-permute-start | bytes 1179656 | tf_op jit(solution)/shard_map/ppermute | solution.py:381
  67.7 4.4 %collective-permute-start.15 = (bf16[6,32,128]{2,1,0:T(8,128)(2,1)S(1)}, bf16[6,32,128]{2,1,0:T(8,128)(2,1)S(1)}, u32[]{:S(2)}, u32[]{:S(2)}) collective-permute-start(bf16[6,32,128]{2,1,0:T(8,128)(2,1)S(1)} %get-tuple-element.57), channel_id=1, source_target_pairs={{4,0},{6,2},{8,4},{10,6},{12,8},{14,10},{0,12},{2,14},{5,1},{7,3},... | collective-permute-start | bytes 147464 | tf_op jit(solution)/shard_map/ppermute | solution.py:381
  67.9 5.3 %collective-permute-start.16 = (bf16[6,32,128]{2,1,0:T(8,128)(2,1)S(1)}, bf16[6,32,128]{2,1,0:T(8,128)(2,1)S(1)}, u32[]{:S(2)}, u32[]{:S(2)}) collective-permute-start(bf16[6,32,128]{2,1,0:T(8,128)(2,1)S(1)} %get-tuple-element.58), channel_id=1, source_target_pairs={{8,0},{10,2},{12,4},{14,6},{0,8},{2,10},{4,12},{6,14},{9,1},{11,3}... | collective-permute-start | bytes 147464 | tf_op jit(solution)/shard_map/ppermute | solution.py:381
  70.0 5.9 %collective-permute-start.17 = (bf16[6,32,128]{2,1,0:T(8,128)(2,1)S(1)}, bf16[6,32,128]{2,1,0:T(8,128)(2,1)S(1)}, u32[]{:S(2)}, u32[]{:S(2)}) collective-permute-start(bf16[6,32,128]{2,1,0:T(8,128)(2,1)S(1)} %get-tuple-element.59), channel_id=1, source_target_pairs={{12,0},{14,2},{0,4},{2,6},{4,8},{6,10},{8,12},{10,14},{13,1},{15,3... | collective-permute-start | bytes 147464 | tf_op jit(solution)/shard_map/ppermute | solution.py:381
  76.6 15.0 %collective-permute-start.20 = (bf16[4,2,8,1536]{3,2,1,0:T(8,128)(2,1)S(1)}, bf16[4,2,8,1536]{3,2,1,0:T(8,128)(2,1)S(1)}, u32[]{:S(2)}, u32[]{:S(2)}) collective-permute-start(bf16[4,2,8,1536]{3,2,1,0:T(8,128)(2,1)S(1)} %get-tuple-element.61.refs_2_), channel_id=1, source_target_pairs={{2,0},{0,2},{6,4},{4,6},{10,8},{8,10},{14,12},{12,14},{3,1},{1,3},... | collective-permute-start | bytes 589832 | tf_op jit(solution)/shard_map/ppermute | solution.py:381
  91.7 41.0 %copy-start.4 = (bf16[1,2,4,2,192,384]{5,4,3,2,1,0:T(8,128)(2,1)S(1)}, bf16[1,2,4,2,192,384]{5,4,3,2,1,0:T(8,128)(2,1)}, u32[]{:S(2)}) copy-start(bf16[1,2,4,2,192,384]{5,4,3,2,1,0:T(8,128)(2,1)} %param.7) | copy-start | bytes 7077892
  95.0 7.5 %collective-permute-start.21 = (bf16[96,768]{1,0:T(8,128)(2,1)S(1)}, bf16[96,768]{1,0:T(8,128)(2,1)S(1)}, u32[]{:S(2)}, u32[]{:S(2)}) collective-permute-start(bf16[96,768]{1,0:T(8,128)(2,1)S(1)} %get-tuple-element.64), channel_id=1, source_target_pairs={{12,0},{14,2},{0,4},{2,6},{4,8},{6,10},{8,12},{10,14},{13,1},{15,3... | collective-permute-start | bytes 442376 | tf_op jit(solution)/shard_map/ppermute | solution.py:381
  97.3 11.1 %collective-permute-start.22 = (bf16[96,768]{1,0:T(8,128)(2,1)S(1)}, bf16[96,768]{1,0:T(8,128)(2,1)S(1)}, u32[]{:S(2)}, u32[]{:S(2)}) collective-permute-start(bf16[96,768]{1,0:T(8,128)(2,1)S(1)} %get-tuple-element.65), channel_id=1, source_target_pairs={{8,0},{10,2},{12,4},{14,6},{0,8},{2,10},{4,12},{6,14},{9,1},{11,3}... | collective-permute-start | bytes 442376 | tf_op jit(solution)/shard_map/ppermute | solution.py:381
  99.3 9.1 %collective-permute-start.23 = (bf16[96,768]{1,0:T(8,128)(2,1)S(1)}, bf16[96,768]{1,0:T(8,128)(2,1)S(1)}, u32[]{:S(2)}, u32[]{:S(2)}) collective-permute-start(bf16[96,768]{1,0:T(8,128)(2,1)S(1)} %get-tuple-element.66), channel_id=1, source_target_pairs={{4,0},{6,2},{8,4},{10,6},{12,8},{14,10},{0,12},{2,14},{5,1},{7,3},... | collective-permute-start | bytes 442376 | tf_op jit(solution)/shard_map/ppermute | solution.py:381
  108.5 11.5 %collective-permute-start.29 = (bf16[96,768]{1,0:T(8,128)(2,1)S(1)}, bf16[96,768]{1,0:T(8,128)(2,1)S(1)}, u32[]{:S(2)}, u32[]{:S(2)}) collective-permute-start(bf16[96,768]{1,0:T(8,128)(2,1)S(1)} %add_convert_fusion.refs_0_), channel_id=1, source_target_pairs={{12,0},{14,2},{0,4},{2,6},{4,8},{6,10},{8,12},{10,14},{13,1},{15,3... | collective-permute-start | bytes 442376 | tf_op jit(solution)/shard_map/ppermute | solution.py:381
  112.4 11.4 %collective-permute-start.27 = (bf16[96,768]{1,0:T(8,128)(2,1)S(1)}, bf16[96,768]{1,0:T(8,128)(2,1)S(1)}, u32[]{:S(2)}, u32[]{:S(2)}) collective-permute-start(bf16[96,768]{1,0:T(8,128)(2,1)S(1)} %add_convert_fusion.refs_0_), channel_id=1, source_target_pairs={{8,0},{10,2},{12,4},{14,6},{0,8},{2,10},{4,12},{6,14},{9,1},{11,3}... | collective-permute-start | bytes 442376 | tf_op jit(solution)/shard_map/ppermute | solution.py:381
  115.8 9.5 %collective-permute-start.25 = (bf16[96,768]{1,0:T(8,128)(2,1)S(1)}, bf16[96,768]{1,0:T(8,128)(2,1)S(1)}, u32[]{:S(2)}, u32[]{:S(2)}) collective-permute-start(bf16[96,768]{1,0:T(8,128)(2,1)S(1)} %add_convert_fusion.refs_0_), channel_id=1, source_target_pairs={{4,0},{6,2},{8,4},{10,6},{12,8},{14,10},{0,12},{2,14},{5,1},{7,3},... | collective-permute-start | bytes 442376 | tf_op jit(solution)/shard_map/ppermute | solution.py:381
  115.8 10.1 %collective-permute-start.24 = (bf16[96,768]{1,0:T(8,128)(2,1)S(1)}, bf16[96,768]{1,0:T(8,128)(2,1)S(1)}, u32[]{:S(2)}, u32[]{:S(2)}) collective-permute-start(bf16[96,768]{1,0:T(8,128)(2,1)S(1)} %add_convert_fusion.refs_0_), channel_id=1, source_target_pairs={{2,0},{0,2},{6,4},{4,6},{10,8},{8,10},{14,12},{12,14},{3,1},{1,3},... | collective-permute-start | bytes 442376 | tf_op jit(solution)/shard_map/ppermute | solution.py:381
  120.0 5.8 %collective-permute-start.30 = (bf16[96,768]{1,0:T(8,128)(2,1)S(1)}, bf16[96,768]{1,0:T(8,128)(2,1)S(1)}, u32[]{:S(2)}, u32[]{:S(2)}) collective-permute-start(bf16[96,768]{1,0:T(8,128)(2,1)S(1)} %collective-permute-done.29.refs_6_), channel_id=1, source_target_pairs={{2,0},{0,2},{6,4},{4,6},{10,8},{8,10},{14,12},{12,14},{3,1},{1,3},... | collective-permute-start | bytes 442376 | tf_op jit(solution)/shard_map/ppermute | solution.py:381
  123.8 6.7 %collective-permute-start.28 = (bf16[96,768]{1,0:T(8,128)(2,1)S(1)}, bf16[96,768]{1,0:T(8,128)(2,1)S(1)}, u32[]{:S(2)}, u32[]{:S(2)}) collective-permute-start(bf16[96,768]{1,0:T(8,128)(2,1)S(1)} %collective-permute-done.27.refs_4_), channel_id=1, source_target_pairs={{2,0},{0,2},{6,4},{4,6},{10,8},{8,10},{14,12},{12,14},{3,1},{1,3},... | collective-permute-start | bytes 442376 | tf_op jit(solution)/shard_map/ppermute | solution.py:381
  125.3 7.4 %collective-permute-start.26 = (bf16[96,768]{1,0:T(8,128)(2,1)S(1)}, bf16[96,768]{1,0:T(8,128)(2,1)S(1)}, u32[]{:S(2)}, u32[]{:S(2)}) collective-permute-start(bf16[96,768]{1,0:T(8,128)(2,1)S(1)} %collective-permute-done.25.refs_2_), channel_id=1, source_target_pairs={{2,0},{0,2},{6,4},{4,6},{10,8},{8,10},{14,12},{12,14},{3,1},{1,3},... | collective-permute-start | bytes 442376 | tf_op jit(solution)/shard_map/ppermute | solution.py:381
  (6 other events, 85.7 us)
where the time goes:
time: 140 us
  starting transfers between devices  58 us (41%)
  waiting for transfers between devices  45.8 us (33%)
  Pallas kernels  32.9 us (24%)
  local copies, waits for them, and re-layouts  2.75 us (2%)
    ppermute x31, starting transfers between devices, from_place(): return lax.ppermute(block, ('site', 'vec'), route)  58 us
    ppermute x31, waiting for transfers between devices, from_place(): return lax.ppermute(block, ('site', 'vec'), route)  45.8 us
    pallas_call x3, Pallas kernels, filter_chunk(): pl.pallas_call(functools.partial(filter_kernel, sites, chunk), out_shape=...  17.4 us
    pallas_call x1, Pallas kernels, projection(): pl.pallas_call(functools.partial(projection_kernel, sites, groups), grid=...  7.56 us
    pallas_call x1, Pallas kernels, elementals(): pl.pallas_call(functools.partial(elemental_kernel, segments, chunks), out...  3.27 us
  transfers between devices with their start and end apart: 31, of which 11 were waited for; matrix products, arithmetic and copies ran while one was open for 0% of the time, Pallas kernels for 15%

commit v1 on v0

--- a/solution.py
+++ b/solution.py
@@ -15,7 +15,7 @@
 
 two_pi = 2.0 * math.pi
 
-CHUNKS = (16, 24, 8)
+CHUNKS = (16, 16, 16)
 
 
 def phase_angle(momenta, across, upward, depth, extent):
@@ -253,123 +253,165 @@
     )(place, own, *hops, cosine, sine, *after)
 
 
-def elemental_kernel(segments, chunks, place_ref, *refs):
-    own = refs[:chunks]
-    other = refs[chunks : 2 * chunks]
-    shifted = refs[2 * chunks : 3 * chunks]
-    outs = refs[3 * chunks : 3 * chunks + segments]
-    left_ref, right_ref, total_ref = refs[3 * chunks + segments :]
+def fill_left(left_ref, chunks):
+    slots, _, _, depth = chunks[0].shape
+    for n, ref in enumerate(chunks):
+        for slot in range(slots):
+            at = slot * sum(CHUNKS) + sum(CHUNKS[:n])
+            for part in range(2):
+                left_ref[at : at + CHUNKS[n], part * depth : (part + 1) * depth] = ref[slot, part]
+
+
+def multiply(left_ref, right_ref, total_ref, place_ref, outs):
+    segments, rows, _ = total_ref.shape
+    for p in range(right_ref.shape[0]):
+        product = lax.dot_general(
+            left_ref[...], right_ref[p], (((1,), (1,)), ((), ())), preferred_element_type=jnp.float32)
+        width = product.shape[1]
+        for s in range(segments):
+            total_ref[s, :, p * width : (p + 1) * width] = product[s * rows : (s + 1) * rows]
+    for d in range(segments):
+        outs[d][...] = total_ref[lax.rem(place_ref[0] + d, segments)].astype(outs[d].dtype)
+
+
+def own_kernel(segments, place_ref, *refs):
+    chunks = len(CHUNKS)
+    own, shifted = refs[:chunks], refs[chunks : 2 * chunks]
+    outs = refs[2 * chunks : 2 * chunks + segments]
+    right_ref, left_ref, total_ref = refs[2 * chunks + segments :]
     slots, _, _, depth = own[0].shape
-    per_slot = sum(CHUNKS)
-    block = slots * per_slot
-    for n, ref in enumerate(own + other):
-        size = CHUNKS[n % chunks]
-        for slot in range(slots):
-            at = n // chunks * block + slot * per_slot + sum(CHUNKS[: n % chunks])
-            for part in range(2):
-                left_ref[at : at + size, part * depth : (part + 1) * depth] = ref[slot, part]
-    momenta = shifted[0].shape[0]
-    for p in range(momenta):
+    block = left_ref.shape[0]
+    fill_left(left_ref, own)
+    for p in range(right_ref.shape[0]):
         for n, ref in enumerate(shifted):
-            size = CHUNKS[n]
             for slot in range(slots):
                 re, im = ref[p, slot, 0], ref[p, slot, 1]
-                at = slot * per_slot + sum(CHUNKS[:n])
-                right_ref[at : at + size, :depth] = re
-                right_ref[at : at + size, depth:] = im
-                right_ref[block + at : block + at + size, :depth] = im
-                right_ref[block + at : block + at + size, depth:] = -re
-        product = lax.dot_general(
-            left_ref[...], right_ref[...], (((1,), (1,)), ((), ())), preferred_element_type=jnp.float32)
-        rows = product.shape[0] // segments
-        for s in range(segments):
-            total_ref[s, :, p * 2 * block : (p + 1) * 2 * block] = product[s * rows : (s + 1) * rows]
-    place = place_ref[0]
-    for d in range(segments):
-        s = lax.rem(place + d, segments)
-        outs[d][...] = total_ref[s].astype(outs[d].dtype)
-
-
-def elementals(place, own, other, shifted, segments):
-    chunks = len(own)
-    slots, _, _, depth = own[0].shape
-    momenta = shifted[0].shape[0]
-    block = slots * sum(CHUNKS)
-    rows = 2 * block // segments
-    columns = momenta * 2 * block
+                at = slot * sum(CHUNKS) + sum(CHUNKS[:n])
+                low, high = slice(at, at + CHUNKS[n]), slice(block + at, block + at + CHUNKS[n])
+                right_ref[p, low, :depth] = re
+                right_ref[p, low, depth:] = im
+                right_ref[p, high, :depth] = im
+                right_ref[p, high, depth:] = -re
+    multiply(left_ref, right_ref, total_ref, place_ref, outs)
+
+
+def other_kernel(segments, place_ref, *refs):
+    chunks = len(CHUNKS)
+    other, right_ref = refs[:chunks], refs[chunks]
+    outs = refs[chunks + 1 : chunks + 1 + segments]
+    left_ref, total_ref = refs[chunks + 1 + segments :]
+    fill_left(left_ref, other)
+    multiply(left_ref, right_ref, total_ref, place_ref, outs)
+
+
+def elementals(place, left, shifted, right, segments):
+    _, _, _, depth = left[0].shape
+    block = segments * sum(CHUNKS)
+    own = right is None
+    momenta = shifted[0].shape[0] if own else right.shape[0]
+    rows, columns = block // segments, momenta * 2 * block
+    shapes = [pltpu.VMEM((rows, columns), jnp.float32 if d == 0 else jnp.bfloat16) for d in range(segments)]
+    if own:
+        shapes.append(pltpu.VMEM((momenta, 2 * block, 2 * depth), jnp.bfloat16))
+    operands = [*left, *shifted] if own else [*left, right]
     return pl.pallas_call(
-        functools.partial(elemental_kernel, segments, chunks),
-        out_shape=tuple(
-            pltpu.VMEM((rows, columns), jnp.float32 if d == 0 else jnp.bfloat16) for d in range(segments)),
-        in_specs=[SMEM] + [VMEM] * (3 * chunks),
-        out_specs=tuple(VMEM for _ in range(segments)),
+        functools.partial(own_kernel if own else other_kernel, segments),
+        out_shape=shapes,
+        in_specs=[SMEM] + [VMEM] * len(operands),
+        out_specs=[VMEM] * len(shapes),
         scratch_shapes=[
-            pltpu.VMEM((2 * block, 2 * depth), jnp.bfloat16),
-            pltpu.VMEM((2 * block, 2 * depth), jnp.bfloat16),
+            pltpu.VMEM((block, 2 * depth), jnp.bfloat16),
             pltpu.VMEM((segments, rows, columns), jnp.float32),
         ],
         cost_estimate=pl.CostEstimate(
-            flops=2 * 2 * block * columns * 2 * depth, bytes_accessed=8 * 2 * block * depth, transcendentals=0),
+            flops=2 * block * columns * 2 * depth, bytes_accessed=8 * block * depth, transcendentals=0),
         compiler_params=GRANT,
-        name="elementals",
-    )(place, *own, *other, *shifted)
-
-
-def projection_kernel(sites, groups, place_ref, owner_ref, tau_ref, *refs):
-    pieces = refs[: sites * groups]
-    out_ref, parts_ref, right_ref = refs[sites * groups :]
-    momenta, nvec = right_ref.shape[0], right_ref.shape[1] // 2
-    block = nvec // 2
+        name="elementals_own" if own else "elementals_other",
+    )(place, *operands)
+
+
+def fill_right(right_ref, pieces, across, place_ref, owner_ref):
+    sites = len(pieces)
+    momenta, nvec, block = right_ref.shape[0], right_ref.shape[1] // 2, right_ref.shape[2] // 2
+    rows = block // sites
+    v = lax.rem(place_ref[1] + across, 2)
+    for up, piece in enumerate(pieces):
+        z = lax.rem(place_ref[0] + up, sites)
+        for part, owner in ((0, owner_ref[v]), (1, owner_ref[1 - v])):
+            row = pl.multiple_of(owner * block + z * rows, 16)
+            low = pl.multiple_of(nvec + owner * block + z * rows, 16)
+            for p in range(momenta):
+                value = piece[part * rows : (part + 1) * rows, p * 2 * block : (p + 1) * 2 * block]
+                right_ref[p, pl.ds(row, rows), :] = value
+                turned = jnp.concatenate([-value[:, block:], value[:, :block]], axis=1)
+                right_ref[p, pl.ds(low, rows), :] = turned
+
+
+def first_kernel(sites, place_ref, owner_ref, tau_ref, *refs):
+    pieces, (out_ref, right_ref) = refs[:sites], refs[sites:]
+    fill_right(right_ref, pieces, 0, place_ref, owner_ref)
+
+    def step(n, carry):
+        left = jnp.concatenate([tau_ref[n, 0], tau_ref[n, 1]], axis=1)
+        for p in range(right_ref.shape[0]):
+            product = jnp.dot(left, right_ref[p], preferred_element_type=jnp.float32)
+            out_ref[n, p] = product.astype(jnp.bfloat16)
+        return carry
+
+    lax.fori_loop(0, tau_ref.shape[0], step, 0)
+
+
+def second_kernel(sites, place_ref, owner_ref, tau_ref, first_ref, *refs):
+    pieces, (out_ref, right_ref) = refs[:sites], refs[sites:]
 
     @pl.when(pl.program_id(0) == 0)
     def assemble():
-        rows = pieces[0].shape[0]
-        for n, piece in enumerate(pieces):
-            up, across = n // groups, n % groups
-            z, v = lax.rem(place_ref[0] + up, sites), lax.rem(place_ref[1] + across, groups)
-            per = block // rows
-            column = owner_ref[v]
-            row = owner_ref[lax.rem(v + lax.div(z, per), groups)] * block + lax.rem(z, per) * rows
-            row = pl.multiple_of(row, 32)
-            for p in range(momenta):
-                parts_ref[column, p, pl.ds(row, rows), :] = piece[:, p * 2 * block : (p + 1) * 2 * block]
-        for p in range(momenta):
-            low, high = parts_ref[0, p], parts_ref[1, p]
-            re = jnp.concatenate([low[:, :block], high[:, :block]], axis=1)
-            im = jnp.concatenate([low[:, block:], high[:, block:]], axis=1)
-            right_ref[p, :nvec, :nvec] = re
-            right_ref[p, :nvec, nvec:] = im
-            right_ref[p, nvec:, :nvec] = -im
-            right_ref[p, nvec:, nvec:] = re
-
+        fill_right(right_ref, pieces, 1, place_ref, owner_ref)
+
+    block = right_ref.shape[2] // 2
     left = jnp.concatenate([tau_ref[0, 0], tau_ref[0, 1]], axis=1)
-    for p in range(momenta):
-        product = jnp.dot(left, right_ref[p], preferred_element_type=jnp.float32)
-        out_ref[0, p, 0] = product[:, :nvec].astype(jnp.bfloat16)
-        out_ref[0, p, 1] = product[:, nvec:].astype(jnp.bfloat16)
-
-
-def projection(tau, place, owner, pieces, momenta, sites, groups):
+    leads = owner_ref[place_ref[1]] == 0
+    for p in range(right_ref.shape[0]):
+        mine = first_ref[0, p]
+        product = jnp.dot(left, right_ref[p], preferred_element_type=jnp.float32).astype(jnp.bfloat16)
+        low, high = jnp.where(leads, mine, product), jnp.where(leads, product, mine)
+        out_ref[0, p, 0] = jnp.concatenate([low[:, :block], high[:, :block]], axis=1)
+        out_ref[0, p, 1] = jnp.concatenate([low[:, block:], high[:, block:]], axis=1)
+
+
+def project_first(tau, place, owner, pieces, momenta):
     outer, _, rows, nvec = tau.shape
-    count = len(pieces)
+    block = nvec // 2
     return pl.pallas_call(
-        functools.partial(projection_kernel, sites, groups),
+        functools.partial(first_kernel, len(pieces)),
+        out_shape=pltpu.VMEM((outer, momenta, rows, 2 * block), jnp.bfloat16),
+        in_specs=[SMEM, SMEM] + [VMEM] * (1 + len(pieces)),
+        out_specs=VMEM,
+        scratch_shapes=[pltpu.VMEM((momenta, 2 * nvec, 2 * block), jnp.bfloat16)],
+        cost_estimate=pl.CostEstimate(
+            flops=2 * outer * rows * 2 * nvec * nvec * momenta, bytes_accessed=outer * rows * nvec * 8,
+            transcendentals=0),
+        compiler_params=GRANT,
+        name="project_first",
+    )(place, owner, tau, *pieces)
+
+
+def project_second(tau, place, owner, first, pieces, momenta):
+    outer, _, rows, nvec = tau.shape
+    return pl.pallas_call(
+        functools.partial(second_kernel, len(pieces)),
         grid=(outer,),
         out_shape=jax.ShapeDtypeStruct((outer, momenta, 2, rows, nvec), jnp.bfloat16),
-        in_specs=[pl.BlockSpec(memory_space=pltpu.SMEM), pl.BlockSpec(memory_space=pltpu.SMEM),
-                  pl.BlockSpec((1, 2, rows, nvec), lambda i: (i, 0, 0, 0))]
-        + [pl.BlockSpec(memory_space=pltpu.VMEM)] * count,
+        in_specs=[SMEM, SMEM, pl.BlockSpec((1, 2, rows, nvec), lambda i: (i, 0, 0, 0)),
+                  pl.BlockSpec((1, *first.shape[1:]), lambda i: (i, 0, 0, 0))] + [VMEM] * len(pieces),
         out_specs=pl.BlockSpec((1, momenta, 2, rows, nvec), lambda i: (i, 0, 0, 0, 0)),
-        scratch_shapes=[
-            pltpu.VMEM((2, momenta, nvec, nvec), jnp.bfloat16),
-            pltpu.VMEM((momenta, 2 * nvec, 2 * nvec), jnp.bfloat16),
-        ],
+        scratch_shapes=[pltpu.VMEM((momenta, 2 * nvec, nvec), jnp.bfloat16)],
         cost_estimate=pl.CostEstimate(
-            flops=2 * outer * rows * 2 * nvec * 2 * nvec * momenta, bytes_accessed=outer * rows * nvec * 12,
+            flops=2 * outer * rows * 2 * nvec * nvec * momenta, bytes_accessed=outer * rows * nvec * 12,
             transcendentals=0),
         compiler_params=GRANT,
-        name="projection",
-    )(place, owner, tau, *pieces)
+        name="project_second",
+    )(place, owner, tau, first, *pieces)
 
 
 def from_place(block, up, across):
@@ -385,7 +427,7 @@
 
 
 def per_device(eigvecs, links, peramb, block_owner, momenta):
-    sites, groups = lax.axis_size("site"), lax.axis_size("vec")
+    sites = lax.axis_size("site")
     site, group = lax.axis_index("site"), lax.axis_index("vec")
     block = eigvecs.shape[3]
     own = eigvecs.reshape(6, block * 4, LANES)
@@ -417,21 +459,21 @@
             last = s
     filtered, shifted, other = ([group_of[n] for n in range(len(CHUNKS))] for group_of in (filtered, shifted, other))
 
-    parts = elementals(place, filtered, other, shifted, sites)
-    total = parts[0]
-    for d in range(1, sites):
-        total = total + from_place(parts[d], -d, 0).astype(jnp.float32)
-    mine = total.astype(jnp.bfloat16)
-
-    gathered = []
-    for up in range(sites):
-        piece = mine if up == 0 else from_place(mine, up, 0)
-        gathered.append(piece)
-        for across in range(1, groups):
-            gathered.append(from_place(piece, 0, across))
+    *parts, right = elementals(place, filtered, shifted, None, sites)
+    sent = [from_place(parts[d], -d, 0) for d in range(1, sites)]
+    own_sum = functools.reduce(lambda total, part: total + part.astype(jnp.float32), sent, parts[0])
+    parts = elementals(place, other, None, right, sites)
+    sent = [from_place(parts[d], -d, 0) for d in range(1, sites)]
+    other_sum = functools.reduce(lambda total, part: total + part.astype(jnp.float32), sent, parts[0])
+    mine = jnp.concatenate([own_sum, other_sum], axis=0).astype(jnp.bfloat16)
+
+    across = [from_place(mine, 0, 1)]
+    pieces = [mine] + [from_place(mine, up, 0) for up in range(1, sites)]
+    across += [from_place(piece, 0, 1) for piece in pieces[1:]]
     sinks, spins = peramb.shape[1], peramb.shape[2]
     tau = peramb.reshape(sinks * spins, 2, block, peramb.shape[5])
-    result = projection(tau, place, block_owner, gathered, momenta.shape[0], sites, groups)
+    first = project_first(tau, place, block_owner, pieces, momenta.shape[0])
+    result = project_second(tau, place, block_owner, first, across, momenta.shape[0])
     return result.reshape(1, sinks, spins, momenta.shape[0], 2, block, peramb.shape[5])
 
 

time: 140 us -> 132 us (0.943)
  waiting for transfers between devices: 45.8 us -> 34.9 us
  Pallas kernels: 32.9 us -> 38.3 us
  starting transfers between devices: 58 us -> 55.1 us
    ppermute x31 -> x34, waiting for transfers between devices: 45.8 us -> 34.9 us  [from_place(): return lax.ppermute(block, ('site', 'vec'), route)]
    pallas_call x2 -> x4, Pallas kernels: 10.8 us -> 16.2 us  [the longest x1 7.02 us: project_second(): pl.pallas_call(functools.partial(second_kernel, len(pieces)), grid=(outer...]
    ppermute x31 -> x34, starting transfers between devices: 58 us -> 55.1 us  [from_place(): return lax.ppermute(block, ('site', 'vec'), route)]
  transfers between devices with their start and end apart: 31 -> 34, of which waited for: 11 -> 13; matrix products, arithmetic and copies ran while one was open for 0% -> 0% of each run, Pallas kernels for 15% -> 23%
where the time goes in v1:
time: 132 us
  starting transfers between devices  55.1 us (42%)
  Pallas kernels  38.3 us (29%)
  waiting for transfers between devices  34.9 us (26%)
  local copies, waits for them, and re-layouts  2.75 us (2%)
    ppermute x34, starting transfers between devices, from_place(): return lax.ppermute(block, ('site', 'vec'), route)  55.1 us
    ppermute x34, waiting for transfers between devices, from_place(): return lax.ppermute(block, ('site', 'vec'), route)  34.9 us
    pallas_call x3, Pallas kernels, filter_chunk(): pl.pallas_call(functools.partial(filter_kernel, sites, chunk), out_shape=...  17.4 us
    pallas_call x1, Pallas kernels, project_second(): pl.pallas_call(functools.partial(second_kernel, len(pieces)), grid=(outer...  7.02 us
    pallas_call x1, Pallas kernels, project_first(): pl.pallas_call(functools.partial(first_kernel, len(pieces)), out_shape=pl...  4.69 us
    pallas_call x2, Pallas kernels, elementals(): pl.pallas_call(functools.partial(own_kernel if own else other_kernel, seg...  4.47 us
    pallas_call x3, Pallas kernels, finish(): pl.pallas_call(functools.partial(finish_kernel, sites, chunk), out_shape=...  2.66 us
  transfers between devices with their start and end apart: 34, of which 13 were waited for; matrix products, arithmetic and copies ran while one was open for 0% of the time, Pallas kernels for 23%

profile of v1, /device:TPU:0, one launch (start us, length us, event | category | flops | bytes accessed | tf_op | source)
XLA Modules:
  0.0 131.8 jit_solution(12222225563763888276)
XLA Ops:
  0.1 1.7 %copy-done = f32[1,2,3,192,1,512]{5,4,3,2,1,0:T(1,128)S(1)} copy-done((f32[1,2,3,192,1,512]{5,4,3,2,1,0:T(1,128)S(1)}, f32[1,2,3,192,1,512]{5,4,3,2,1,0:T(1,128)}, u32[]{:S(2)}) %copy-start) | copy-done | bytes 2359320
  3.2 3.1 %collective-permute-start = (bf16[600,128]{1,0:T(8,128)(2,1)S(1)}, bf16[600,128]{1,0:T(8,128)(2,1)S(1)}, u32[]{:S(2)}, u32[]{:S(2)}) collective-permute-start(bf16[600,128]{1,0:T(8,128)(2,1)S(1)} %get-tuple-element.41.refs_0_), channel_id=1, source_target_pairs={{12,0},{14,2},{0,4},{2,6},{4,8},{6,10},{8,12},{10,14},{13,1},{15,3... | collective-permute-start | bytes 460808 | tf_op jit(solution)/shard_map/ppermute | solution.py:423
  6.3 2.6 %collective-permute-start.1 = (bf16[600,128]{1,0:T(8,128)(2,1)S(1)}, bf16[600,128]{1,0:T(8,128)(2,1)S(1)}, u32[]{:S(2)}, u32[]{:S(2)}) collective-permute-start(bf16[600,128]{1,0:T(8,128)(2,1)S(1)} %get-tuple-element.42), channel_id=1, source_target_pairs={{8,0},{10,2},{12,4},{14,6},{0,8},{2,10},{4,12},{6,14},{9,1},{11,3}... | collective-permute-start | bytes 460808 | tf_op jit(solution)/shard_map/ppermute | solution.py:423
  13.3 2.4 %collective-permute-start.8 = (bf16[384,128]{1,0:T(8,128)(2,1)S(1)}, bf16[384,128]{1,0:T(8,128)(2,1)S(1)}, u32[]{:S(2)}, u32[]{:S(2)}) collective-permute-start(bf16[384,128]{1,0:T(8,128)(2,1)S(1)} %get-tuple-element.50), channel_id=1, source_target_pairs={{4,0},{6,2},{8,4},{10,6},{12,8},{14,10},{0,12},{2,14},{5,1},{7,3},... | collective-permute-start | bytes 294920 | tf_op jit(solution)/shard_map/ppermute | solution.py:423
  15.7 4.2 %collective-permute-done.1.refs_2_ = bf16[600,128]{1,0:T(8,128)(2,1)S(1)} collective-permute-done((bf16[600,128]{1,0:T(8,128)(2,1)S(1)}, bf16[600,128]{1,0:T(8,128)(2,1)S(1)}, u32[]{:S(2)}, u32[]{:S(2)}) %collective-permute-start.1) | collective-permute-done | bytes 153632 | tf_op jit(solution)/shard_map/ppermute | solution.py:423
  21.2 5.8 %shard_map.56 = (bf16[6,64,128]{2,1,0:T(8,128)(2,1)S(1)}, bf16[6,64,128]{2,1,0:T(8,128)(2,1)S(1)}, bf16[6,64,128]{2,1,0:T(8,128)(2,1)S(1)}, bf16[6,64,128]{2,1,0:T(8,128)(2,1)S(1)}) custom-call(s32[2]{0:T(128)S(1)} %pad_add_fusion.place_ref, f32[6,768,128]{2,1,0:T(8,128)S(1)} %bitcast.9, bf16[600,128]{1,0:T(8,128)(2,1)S(1)} %collective-permute-done.refs_1_, ...), custom_call_target="tpu_custom_call" | custom-call | flops 28311552 | bytes 786432 | tf_op jit(solution)/shard_map/pallas_call | solution.py:202
  27.1 8.3 %collective-permute-start.3 = (bf16[6,64,128]{2,1,0:T(8,128)(2,1)S(1)}, bf16[6,64,128]{2,1,0:T(8,128)(2,1)S(1)}, u32[]{:S(2)}, u32[]{:S(2)}) collective-permute-start(bf16[6,64,128]{2,1,0:T(8,128)(2,1)S(1)} %get-tuple-element.45), channel_id=1, source_target_pairs={{4,0},{6,2},{8,4},{10,6},{12,8},{14,10},{0,12},{2,14},{5,1},{7,3},... | collective-permute-start | bytes 294920 | tf_op jit(solution)/shard_map/ppermute | solution.py:423
  36.2 2.4 %collective-permute-start.13 = (bf16[384,128]{1,0:T(8,128)(2,1)S(1)}, bf16[384,128]{1,0:T(8,128)(2,1)S(1)}, u32[]{:S(2)}, u32[]{:S(2)}) collective-permute-start(bf16[384,128]{1,0:T(8,128)(2,1)S(1)} %get-tuple-element.57), channel_id=1, source_target_pairs={{8,0},{10,2},{12,4},{14,6},{0,8},{2,10},{4,12},{6,14},{9,1},{11,3}... | collective-permute-start | bytes 294920 | tf_op jit(solution)/shard_map/ppermute | solution.py:423
  38.6 2.8 %collective-permute-start.14 = (bf16[384,128]{1,0:T(8,128)(2,1)S(1)}, bf16[384,128]{1,0:T(8,128)(2,1)S(1)}, u32[]{:S(2)}, u32[]{:S(2)}) collective-permute-start(bf16[384,128]{1,0:T(8,128)(2,1)S(1)} %get-tuple-element.58), channel_id=1, source_target_pairs={{4,0},{6,2},{8,4},{10,6},{12,8},{14,10},{0,12},{2,14},{5,1},{7,3},... | collective-permute-start | bytes 294920 | tf_op jit(solution)/shard_map/ppermute | solution.py:423
  41.5 5.8 %shard_map.58 = (bf16[6,64,128]{2,1,0:T(8,128)(2,1)S(1)}, bf16[6,64,128]{2,1,0:T(8,128)(2,1)S(1)}, bf16[6,64,128]{2,1,0:T(8,128)(2,1)S(1)}, bf16[6,64,128]{2,1,0:T(8,128)(2,1)S(1)}) custom-call(s32[2]{0:T(128)S(1)} %pad_add_fusion.place_ref, f32[6,768,128]{2,1,0:T(8,128)S(1)} %bitcast.10, bf16[384,128]{1,0:T(8,128)(2,1)S(1)} %collective-permute-done.6.refs_1_, ...), custom_call_target="tpu_custom_call" | custom-call | flops 28311552 | bytes 786432 | tf_op jit(solution)/shard_map/pallas_call | solution.py:202
  48.0 6.0 %collective-permute-done.5.refs_3_ = bf16[6,64,128]{2,1,0:T(8,128)(2,1)S(1)} collective-permute-done((bf16[6,64,128]{2,1,0:T(8,128)(2,1)S(1)}, bf16[6,64,128]{2,1,0:T(8,128)(2,1)S(1)}, u32[]{:S(2)}, u32[]{:S(2)}) %collective-permute-start.5) | collective-permute-done | bytes 98336 | tf_op jit(solution)/shard_map/ppermute | solution.py:423
  54.9 3.9 %collective-permute-start.9 = (bf16[6,64,128]{2,1,0:T(8,128)(2,1)S(1)}, bf16[6,64,128]{2,1,0:T(8,128)(2,1)S(1)}, u32[]{:S(2)}, u32[]{:S(2)}) collective-permute-start(bf16[6,64,128]{2,1,0:T(8,128)(2,1)S(1)} %get-tuple-element.53), channel_id=1, source_target_pairs={{4,0},{6,2},{8,4},{10,6},{12,8},{14,10},{0,12},{2,14},{5,1},{7,3},... | collective-permute-start | bytes 294920 | tf_op jit(solution)/shard_map/ppermute | solution.py:423
  58.8 5.8 %shard_map.61 = (bf16[6,64,128]{2,1,0:T(8,128)(2,1)S(1)}, bf16[6,64,128]{2,1,0:T(8,128)(2,1)S(1)}, bf16[6,64,128]{2,1,0:T(8,128)(2,1)S(1)}, bf16[6,64,128]{2,1,0:T(8,128)(2,1)S(1)}) custom-call(s32[2]{0:T(128)S(1)} %pad_add_fusion.place_ref, f32[6,768,128]{2,1,0:T(8,128)S(1)} %bitcast.12, bf16[384,128]{1,0:T(8,128)(2,1)S(1)} %collective-permute-done.12.refs_1_, ...), custom_call_target="tpu_custom_call" | custom-call | flops 28311552 | bytes 786432 | tf_op jit(solution)/shard_map/pallas_call | solution.py:202
  64.8 1.9 %collective-permute-start.17 = (bf16[6,64,128]{2,1,0:T(8,128)(2,1)S(1)}, bf16[6,64,128]{2,1,0:T(8,128)(2,1)S(1)}, u32[]{:S(2)}, u32[]{:S(2)}) collective-permute-start(bf16[6,64,128]{2,1,0:T(8,128)(2,1)S(1)} %get-tuple-element.64), channel_id=1, source_target_pairs={{12,0},{14,2},{0,4},{2,6},{4,8},{6,10},{8,12},{10,14},{13,1},{15,3... | collective-permute-start | bytes 294920 | tf_op jit(solution)/shard_map/ppermute | solution.py:423
  67.6 1.6 %collective-permute-start.22 = (bf16[4,2,16,1536]{3,2,1,0:T(8,128)(2,1)S(1)}, bf16[4,2,16,1536]{3,2,1,0:T(8,128)(2,1)S(1)}, u32[]{:S(2)}, u32[]{:S(2)}) collective-permute-start(bf16[4,2,16,1536]{3,2,1,0:T(8,128)(2,1)S(1)} %get-tuple-element.61.refs_1_), channel_id=1, source_target_pairs={{2,0},{0,2},{6,4},{4,6},{10,8},{8,10},{14,12},{12,14},{3,1},{1,3},... | collective-permute-start | bytes 1179656 | tf_op jit(solution)/shard_map/ppermute | solution.py:423
  70.9 1.9 %collective-permute-done.17.refs_3_ = bf16[6,64,128]{2,1,0:T(8,128)(2,1)S(1)} collective-permute-done((bf16[6,64,128]{2,1,0:T(8,128)(2,1)S(1)}, bf16[6,64,128]{2,1,0:T(8,128)(2,1)S(1)}, u32[]{:S(2)}, u32[]{:S(2)}) %collective-permute-start.17) | collective-permute-done | bytes 98336 | tf_op jit(solution)/shard_map/ppermute | solution.py:423
  73.7 1.6 %collective-permute-start.23 = (bf16[4,2,16,1536]{3,2,1,0:T(8,128)(2,1)S(1)}, bf16[4,2,16,1536]{3,2,1,0:T(8,128)(2,1)S(1)}, u32[]{:S(2)}, u32[]{:S(2)}) collective-permute-start(bf16[4,2,16,1536]{3,2,1,0:T(8,128)(2,1)S(1)} %get-tuple-element.66.refs_2_), channel_id=1, source_target_pairs={{2,0},{0,2},{6,4},{4,6},{10,8},{8,10},{14,12},{12,14},{3,1},{1,3},... | collective-permute-start | bytes 1179656 | tf_op jit(solution)/shard_map/ppermute | solution.py:423
  75.2 2.2 %elementals_own.1 = (f32[48,768]{1,0:T(8,128)S(1)}, bf16[48,768]{1,0:T(8,128)(2,1)S(1)}, bf16[48,768]{1,0:T(8,128)(2,1)S(1)}, bf16[48,768]{1,0:T(8,128)(2,1)S(1)}, bf16[2,384,3072]{2,1,0:T(8,128)(2,1)S(1)}) custom-call(s32[2]{0:T(128)S(1)} %pad_add_fusion.place_ref, bf16[4,2,16,1536]{3,2,1,0:T(8,128)(2,1)S(1)} %get-tuple-element.52.refs_0_, ...), custom_call_target="tpu_custom_call" | custom-call | flops 905969664 | bytes 2359296 | tf_op jit(solution)/shard_map/elementals_own/pallas_call | solution.py:317
  77.5 2.3 %collective-permute-start.19 = (bf16[48,768]{1,0:T(8,128)(2,1)S(1)}, bf16[48,768]{1,0:T(8,128)(2,1)S(1)}, u32[]{:S(2)}, u32[]{:S(2)}) collective-permute-start(bf16[48,768]{1,0:T(8,128)(2,1)S(1)} %get-tuple-element.70), channel_id=1, source_target_pairs={{8,0},{10,2},{12,4},{14,6},{0,8},{2,10},{4,12},{6,14},{9,1},{11,3}... | collective-permute-start | bytes 221192 | tf_op jit(solution)/shard_map/ppermute | solution.py:423
  79.9 2.1 %collective-permute-start.20 = (bf16[48,768]{1,0:T(8,128)(2,1)S(1)}, bf16[48,768]{1,0:T(8,128)(2,1)S(1)}, u32[]{:S(2)}, u32[]{:S(2)}) collective-permute-start(bf16[48,768]{1,0:T(8,128)(2,1)S(1)} %get-tuple-element.71), channel_id=1, source_target_pairs={{4,0},{6,2},{8,4},{10,6},{12,8},{14,10},{0,12},{2,14},{5,1},{7,3},... | collective-permute-start | bytes 221192 | tf_op jit(solution)/shard_map/ppermute | solution.py:423
  82.0 6.1 %collective-permute-done.21.refs_0_ = bf16[4,2,16,1536]{3,2,1,0:T(8,128)(2,1)S(1)} collective-permute-done((bf16[4,2,16,1536]{3,2,1,0:T(8,128)(2,1)S(1)}, bf16[4,2,16,1536]{3,2,1,0:T(8,128)(2,1)S(1)}, u32[]{:S(2)}, u32[]{:S(2)}) %collective-permute-start.21) | collective-permute-done | bytes 393248 | tf_op jit(solution)/shard_map/ppermute | solution.py:423
  88.1 4.3 %collective-permute-done.23.refs_2_ = bf16[4,2,16,1536]{3,2,1,0:T(8,128)(2,1)S(1)} collective-permute-done((bf16[4,2,16,1536]{3,2,1,0:T(8,128)(2,1)S(1)}, bf16[4,2,16,1536]{3,2,1,0:T(8,128)(2,1)S(1)}, u32[]{:S(2)}, u32[]{:S(2)}) %collective-permute-start.23) | collective-permute-done | bytes 393248 | tf_op jit(solution)/shard_map/ppermute | solution.py:423
  92.5 2.2 %elementals_other.1 = (f32[48,768]{1,0:T(8,128)S(1)}, bf16[48,768]{1,0:T(8,128)(2,1)S(1)}, bf16[48,768]{1,0:T(8,128)(2,1)S(1)}, bf16[48,768]{1,0:T(8,128)(2,1)S(1)}) custom-call(s32[2]{0:T(128)S(1)} %pad_add_fusion.place_ref, bf16[4,2,16,1536]{3,2,1,0:T(8,128)(2,1)S(1)} %collective-permute-done.21.refs_0_, ...), custom_call_target="tpu_custom_call" | custom-call | flops 905969664 | bytes 2359296 | tf_op jit(solution)/shard_map/elementals_other/pallas_call | solution.py:317
  95.9 1.5 %collective-permute-start.25 = (bf16[48,768]{1,0:T(8,128)(2,1)S(1)}, bf16[48,768]{1,0:T(8,128)(2,1)S(1)}, u32[]{:S(2)}, u32[]{:S(2)}) collective-permute-start(bf16[48,768]{1,0:T(8,128)(2,1)S(1)} %get-tuple-element.75), channel_id=1, source_target_pairs={{8,0},{10,2},{12,4},{14,6},{0,8},{2,10},{4,12},{6,14},{9,1},{11,3}... | collective-permute-start | bytes 221192 | tf_op jit(solution)/shard_map/ppermute | solution.py:423
  98.6 2.6 %collective-permute-done.24 = bf16[48,768]{1,0:T(8,128)(2,1)S(1)} collective-permute-done((bf16[48,768]{1,0:T(8,128)(2,1)S(1)}, bf16[48,768]{1,0:T(8,128)(2,1)S(1)}, u32[]{:S(2)}, u32[]{:S(2)}) %collective-permute-start.24) | collective-permute-done | bytes 73760 | tf_op jit(solution)/shard_map/ppermute | solution.py:423
  101.2 2.0 %collective-permute-done.25 = bf16[48,768]{1,0:T(8,128)(2,1)S(1)} collective-permute-done((bf16[48,768]{1,0:T(8,128)(2,1)S(1)}, bf16[48,768]{1,0:T(8,128)(2,1)S(1)}, u32[]{:S(2)}, u32[]{:S(2)}) %collective-permute-start.25) | collective-permute-done | bytes 73760 | tf_op jit(solution)/shard_map/ppermute | solution.py:423
  103.4 5.8 %collective-permute-start.27 = (bf16[96,768]{1,0:T(8,128)(2,1)S(1)}, bf16[96,768]{1,0:T(8,128)(2,1)S(1)}, u32[]{:S(2)}, u32[]{:S(2)}) collective-permute-start(bf16[96,768]{1,0:T(8,128)(2,1)S(1)} %pad_maximum_fusion.refs_0_), channel_id=1, source_target_pairs={{4,0},{6,2},{8,4},{10,6},{12,8},{14,10},{0,12},{2,14},{5,1},{7,3},... | collective-permute-start | bytes 442376 | tf_op jit(solution)/shard_map/ppermute | solution.py:423
  110.1 1.5 %collective-permute-start.30 = (bf16[96,768]{1,0:T(8,128)(2,1)S(1)}, bf16[96,768]{1,0:T(8,128)(2,1)S(1)}, u32[]{:S(2)}, u32[]{:S(2)}) collective-permute-start(bf16[96,768]{1,0:T(8,128)(2,1)S(1)} %pad_maximum_fusion.refs_0_), channel_id=1, source_target_pairs={{2,0},{0,2},{6,4},{4,6},{10,8},{8,10},{14,12},{12,14},{3,1},{1,3},... | collective-permute-start | bytes 442376 | tf_op jit(solution)/shard_map/ppermute | solution.py:423
  112.0 1.5 %collective-permute-start.31 = (bf16[96,768]{1,0:T(8,128)(2,1)S(1)}, bf16[96,768]{1,0:T(8,128)(2,1)S(1)}, u32[]{:S(2)}, u32[]{:S(2)}) collective-permute-start(bf16[96,768]{1,0:T(8,128)(2,1)S(1)} %collective-permute-done.27.refs_1_), channel_id=1, source_target_pairs={{2,0},{0,2},{6,4},{4,6},{10,8},{8,10},{14,12},{12,14},{3,1},{1,3},... | collective-permute-start | bytes 442376 | tf_op jit(solution)/shard_map/ppermute | solution.py:423
  113.5 4.5 %collective-permute-done.28.refs_2_ = bf16[96,768]{1,0:T(8,128)(2,1)S(1)} collective-permute-done((bf16[96,768]{1,0:T(8,128)(2,1)S(1)}, bf16[96,768]{1,0:T(8,128)(2,1)S(1)}, u32[]{:S(2)}, u32[]{:S(2)}) %collective-permute-start.28) | collective-permute-done | bytes 147488 | tf_op jit(solution)/shard_map/ppermute | solution.py:423
  120.0 4.7 %project_first.1.first_ref = bf16[8,2,192,384]{3,2,1,0:T(8,128)(2,1)S(1)} custom-call(s32[2]{0:T(128)S(1)} %pad_add_fusion.place_ref, s32[2]{0:T(128)S(1)} %copy-done.5, bf16[8,2,192,384]{3,2,1,0:T(8,128)(2,1)S(1)} %bitcast.15, bf16[96,768]{1,0:T(8,128)(2,1)S(1)} %pad_maximum_fusion.refs_0_, bf16[96,768]{1,0:T(8,128)(2,1)S(1)} %collective-permute-done.27.refs_1_, ...), custom_call_target="tpu_custom_call" | custom-call | flops 1811939328 | bytes 4718592 | tf_op jit(solution)/shard_map/project_first/pallas_call | solution.py:385
  124.8 7.0 %project_second.1 = bf16[8,2,2,192,384]{4,3,2,1,0:T(8,128)(2,1)} custom-call(s32[2]{0:T(128)S(1)} %pad_add_fusion.place_ref, s32[2]{0:T(128)S(1)} %copy-done.5, bf16[8,2,192,384]{3,2,1,0:T(8,128)(2,1)S(1)} %bitcast.16, bf16[8,2,192,384]{3,2,1,0:T(8,128)(2,1)S(1)} %project_first.1.first_ref, bf16[96,768]{1,0:T(8,128)(2,1)S(1)} %collective-permute-done.30.refs_0_, ...), custom_call_target="tpu_custom_call" | custom-call | flops 1811939328 | bytes 7077888 | tf_op jit(solution)/shard_map/project_second/pallas_call | solution.py:401
  (73 shorter events, 19.2 us)
Async XLA Ops:
  3.2 10.1 %collective-permute-start = (bf16[600,128]{1,0:T(8,128)(2,1)S(1)}, bf16[600,128]{1,0:T(8,128)(2,1)S(1)}, u32[]{:S(2)}, u32[]{:S(2)}) collective-permute-start(bf16[600,128]{1,0:T(8,128)(2,1)S(1)} %get-tuple-element.41.refs_0_), channel_id=1, source_target_pairs={{12,0},{14,2},{0,4},{2,6},{4,8},{6,10},{8,12},{10,14},{13,1},{15,3... | collective-permute-start | bytes 460808 | tf_op jit(solution)/shard_map/ppermute | solution.py:423
  6.3 13.6 %collective-permute-start.1 = (bf16[600,128]{1,0:T(8,128)(2,1)S(1)}, bf16[600,128]{1,0:T(8,128)(2,1)S(1)}, u32[]{:S(2)}, u32[]{:S(2)}) collective-permute-start(bf16[600,128]{1,0:T(8,128)(2,1)S(1)} %get-tuple-element.42), channel_id=1, source_target_pairs={{8,0},{10,2},{12,4},{14,6},{0,8},{2,10},{4,12},{6,14},{9,1},{11,3}... | collective-permute-start | bytes 460808 | tf_op jit(solution)/shard_map/ppermute | solution.py:423
  8.9 12.0 %collective-permute-start.2 = (bf16[600,128]{1,0:T(8,128)(2,1)S(1)}, bf16[600,128]{1,0:T(8,128)(2,1)S(1)}, u32[]{:S(2)}, u32[]{:S(2)}) collective-permute-start(bf16[600,128]{1,0:T(8,128)(2,1)S(1)} %get-tuple-element.43), channel_id=1, source_target_pairs={{4,0},{6,2},{8,4},{10,6},{12,8},{14,10},{0,12},{2,14},{5,1},{7,3},... | collective-permute-start | bytes 460808 | tf_op jit(solution)/shard_map/ppermute | solution.py:423
  10.9 24.7 %collective-permute-start.6 = (bf16[384,128]{1,0:T(8,128)(2,1)S(1)}, bf16[384,128]{1,0:T(8,128)(2,1)S(1)}, u32[]{:S(2)}, u32[]{:S(2)}) collective-permute-start(bf16[384,128]{1,0:T(8,128)(2,1)S(1)} %get-tuple-element.48.refs_0_), channel_id=1, source_target_pairs={{12,0},{14,2},{0,4},{2,6},{4,8},{6,10},{8,12},{10,14},{13,1},{15,3... | collective-permute-start | bytes 294920 | tf_op jit(solution)/shard_map/ppermute | solution.py:423
  11.6 24.7 %collective-permute-start.7 = (bf16[384,128]{1,0:T(8,128)(2,1)S(1)}, bf16[384,128]{1,0:T(8,128)(2,1)S(1)}, u32[]{:S(2)}, u32[]{:S(2)}) collective-permute-start(bf16[384,128]{1,0:T(8,128)(2,1)S(1)} %get-tuple-element.49), channel_id=1, source_target_pairs={{8,0},{10,2},{12,4},{14,6},{0,8},{2,10},{4,12},{6,14},{9,1},{11,3}... | collective-permute-start | bytes 294920 | tf_op jit(solution)/shard_map/ppermute | solution.py:423
  13.3 25.3 %collective-permute-start.8 = (bf16[384,128]{1,0:T(8,128)(2,1)S(1)}, bf16[384,128]{1,0:T(8,128)(2,1)S(1)}, u32[]{:S(2)}, u32[]{:S(2)}) collective-permute-start(bf16[384,128]{1,0:T(8,128)(2,1)S(1)} %get-tuple-element.50), channel_id=1, source_target_pairs={{4,0},{6,2},{8,4},{10,6},{12,8},{14,10},{0,12},{2,14},{5,1},{7,3},... | collective-permute-start | bytes 294920 | tf_op jit(solution)/shard_map/ppermute | solution.py:423
  27.1 20.2 %collective-permute-start.3 = (bf16[6,64,128]{2,1,0:T(8,128)(2,1)S(1)}, bf16[6,64,128]{2,1,0:T(8,128)(2,1)S(1)}, u32[]{:S(2)}, u32[]{:S(2)}) collective-permute-start(bf16[6,64,128]{2,1,0:T(8,128)(2,1)S(1)} %get-tuple-element.45), channel_id=1, source_target_pairs={{4,0},{6,2},{8,4},{10,6},{12,8},{14,10},{0,12},{2,14},{5,1},{7,3},... | collective-permute-start | bytes 294920 | tf_op jit(solution)/shard_map/ppermute | solution.py:423
  35.4 12.0 %collective-permute-start.4 = (bf16[6,64,128]{2,1,0:T(8,128)(2,1)S(1)}, bf16[6,64,128]{2,1,0:T(8,128)(2,1)S(1)}, u32[]{:S(2)}, u32[]{:S(2)}) collective-permute-start(bf16[6,64,128]{2,1,0:T(8,128)(2,1)S(1)} %get-tuple-element.46), channel_id=1, source_target_pairs={{8,0},{10,2},{12,4},{14,6},{0,8},{2,10},{4,12},{6,14},{9,1},{11,3}... | collective-permute-start | bytes 294920 | tf_op jit(solution)/shard_map/ppermute | solution.py:423
  35.5 19.4 %collective-permute-start.12 = (bf16[384,128]{1,0:T(8,128)(2,1)S(1)}, bf16[384,128]{1,0:T(8,128)(2,1)S(1)}, u32[]{:S(2)}, u32[]{:S(2)}) collective-permute-start(bf16[384,128]{1,0:T(8,128)(2,1)S(1)} %get-tuple-element.56), channel_id=1, source_target_pairs={{12,0},{14,2},{0,4},{2,6},{4,8},{6,10},{8,12},{10,14},{13,1},{15,3... | collective-permute-start | bytes 294920 | tf_op jit(solution)/shard_map/ppermute | solution.py:423
  36.2 22.6 %collective-permute-start.13 = (bf16[384,128]{1,0:T(8,128)(2,1)S(1)}, bf16[384,128]{1,0:T(8,128)(2,1)S(1)}, u32[]{:S(2)}, u32[]{:S(2)}) collective-permute-start(bf16[384,128]{1,0:T(8,128)(2,1)S(1)} %get-tuple-element.57), channel_id=1, source_target_pairs={{8,0},{10,2},{12,4},{14,6},{0,8},{2,10},{4,12},{6,14},{9,1},{11,3}... | collective-permute-start | bytes 294920 | tf_op jit(solution)/shard_map/ppermute | solution.py:423
  38.6 20.2 %collective-permute-start.14 = (bf16[384,128]{1,0:T(8,128)(2,1)S(1)}, bf16[384,128]{1,0:T(8,128)(2,1)S(1)}, u32[]{:S(2)}, u32[]{:S(2)}) collective-permute-start(bf16[384,128]{1,0:T(8,128)(2,1)S(1)} %get-tuple-element.58), channel_id=1, source_target_pairs={{4,0},{6,2},{8,4},{10,6},{12,8},{14,10},{0,12},{2,14},{5,1},{7,3},... | collective-permute-start | bytes 294920 | tf_op jit(solution)/shard_map/ppermute | solution.py:423
  47.3 6.8 %collective-permute-start.5 = (bf16[6,64,128]{2,1,0:T(8,128)(2,1)S(1)}, bf16[6,64,128]{2,1,0:T(8,128)(2,1)S(1)}, u32[]{:S(2)}, u32[]{:S(2)}) collective-permute-start(bf16[6,64,128]{2,1,0:T(8,128)(2,1)S(1)} %get-tuple-element.47), channel_id=1, source_target_pairs={{12,0},{14,2},{0,4},{2,6},{4,8},{6,10},{8,12},{10,14},{13,1},{15,3... | collective-permute-start | bytes 294920 | tf_op jit(solution)/shard_map/ppermute | solution.py:423
  47.3 17.4 %collective-permute-start.10 = (bf16[6,64,128]{2,1,0:T(8,128)(2,1)S(1)}, bf16[6,64,128]{2,1,0:T(8,128)(2,1)S(1)}, u32[]{:S(2)}, u32[]{:S(2)}) collective-permute-start(bf16[6,64,128]{2,1,0:T(8,128)(2,1)S(1)} %get-tuple-element.54), channel_id=1, source_target_pairs={{8,0},{10,2},{12,4},{14,6},{0,8},{2,10},{4,12},{6,14},{9,1},{11,3}... | collective-permute-start | bytes 294920 | tf_op jit(solution)/shard_map/ppermute | solution.py:423
  54.0 12.7 %collective-permute-start.11 = (bf16[6,64,128]{2,1,0:T(8,128)(2,1)S(1)}, bf16[6,64,128]{2,1,0:T(8,128)(2,1)S(1)}, u32[]{:S(2)}, u32[]{:S(2)}) collective-permute-start(bf16[6,64,128]{2,1,0:T(8,128)(2,1)S(1)} %get-tuple-element.55), channel_id=1, source_target_pairs={{12,0},{14,2},{0,4},{2,6},{4,8},{6,10},{8,12},{10,14},{13,1},{15,3... | collective-permute-start | bytes 294920 | tf_op jit(solution)/shard_map/ppermute | solution.py:423
  54.9 11.8 %collective-permute-start.9 = (bf16[6,64,128]{2,1,0:T(8,128)(2,1)S(1)}, bf16[6,64,128]{2,1,0:T(8,128)(2,1)S(1)}, u32[]{:S(2)}, u32[]{:S(2)}) collective-permute-start(bf16[6,64,128]{2,1,0:T(8,128)(2,1)S(1)} %get-tuple-element.53), channel_id=1, source_target_pairs={{4,0},{6,2},{8,4},{10,6},{12,8},{14,10},{0,12},{2,14},{5,1},{7,3},... | collective-permute-start | bytes 294920 | tf_op jit(solution)/shard_map/ppermute | solution.py:423
  64.6 6.3 %collective-permute-start.15 = (bf16[6,64,128]{2,1,0:T(8,128)(2,1)S(1)}, bf16[6,64,128]{2,1,0:T(8,128)(2,1)S(1)}, u32[]{:S(2)}, u32[]{:S(2)}) collective-permute-start(bf16[6,64,128]{2,1,0:T(8,128)(2,1)S(1)} %get-tuple-element.62), channel_id=1, source_target_pairs={{4,0},{6,2},{8,4},{10,6},{12,8},{14,10},{0,12},{2,14},{5,1},{7,3},... | collective-permute-start | bytes 294920 | tf_op jit(solution)/shard_map/ppermute | solution.py:423
  64.7 6.2 %collective-permute-start.16 = (bf16[6,64,128]{2,1,0:T(8,128)(2,1)S(1)}, bf16[6,64,128]{2,1,0:T(8,128)(2,1)S(1)}, u32[]{:S(2)}, u32[]{:S(2)}) collective-permute-start(bf16[6,64,128]{2,1,0:T(8,128)(2,1)S(1)} %get-tuple-element.63), channel_id=1, source_target_pairs={{8,0},{10,2},{12,4},{14,6},{0,8},{2,10},{4,12},{6,14},{9,1},{11,3}... | collective-permute-start | bytes 294920 | tf_op jit(solution)/shard_map/ppermute | solution.py:423
  64.8 8.0 %collective-permute-start.17 = (bf16[6,64,128]{2,1,0:T(8,128)(2,1)S(1)}, bf16[6,64,128]{2,1,0:T(8,128)(2,1)S(1)}, u32[]{:S(2)}, u32[]{:S(2)}) collective-permute-start(bf16[6,64,128]{2,1,0:T(8,128)(2,1)S(1)} %get-tuple-element.64), channel_id=1, source_target_pairs={{12,0},{14,2},{0,4},{2,6},{4,8},{6,10},{8,12},{10,14},{13,1},{15,3... | collective-permute-start | bytes 294920 | tf_op jit(solution)/shard_map/ppermute | solution.py:423
  67.6 12.3 %collective-permute-start.22 = (bf16[4,2,16,1536]{3,2,1,0:T(8,128)(2,1)S(1)}, bf16[4,2,16,1536]{3,2,1,0:T(8,128)(2,1)S(1)}, u32[]{:S(2)}, u32[]{:S(2)}) collective-permute-start(bf16[4,2,16,1536]{3,2,1,0:T(8,128)(2,1)S(1)} %get-tuple-element.61.refs_1_), channel_id=1, source_target_pairs={{2,0},{0,2},{6,4},{4,6},{10,8},{8,10},{14,12},{12,14},{3,1},{1,3},... | collective-permute-start | bytes 1179656 | tf_op jit(solution)/shard_map/ppermute | solution.py:423
  69.2 18.9 %collective-permute-start.21 = (bf16[4,2,16,1536]{3,2,1,0:T(8,128)(2,1)S(1)}, bf16[4,2,16,1536]{3,2,1,0:T(8,128)(2,1)S(1)}, u32[]{:S(2)}, u32[]{:S(2)}) collective-permute-start(bf16[4,2,16,1536]{3,2,1,0:T(8,128)(2,1)S(1)} %get-tuple-element.52.refs_0_), channel_id=1, source_target_pairs={{2,0},{0,2},{6,4},{4,6},{10,8},{8,10},{14,12},{12,14},{3,1},{1,3},... | collective-permute-start | bytes 1179656 | tf_op jit(solution)/shard_map/ppermute | solution.py:423
  73.7 18.8 %collective-permute-start.23 = (bf16[4,2,16,1536]{3,2,1,0:T(8,128)(2,1)S(1)}, bf16[4,2,16,1536]{3,2,1,0:T(8,128)(2,1)S(1)}, u32[]{:S(2)}, u32[]{:S(2)}) collective-permute-start(bf16[4,2,16,1536]{3,2,1,0:T(8,128)(2,1)S(1)} %get-tuple-element.66.refs_2_), channel_id=1, source_target_pairs={{2,0},{0,2},{6,4},{4,6},{10,8},{8,10},{14,12},{12,14},{3,1},{1,3},... | collective-permute-start | bytes 1179656 | tf_op jit(solution)/shard_map/ppermute | solution.py:423
  77.5 20.0 %collective-permute-start.18 = (bf16[48,768]{1,0:T(8,128)(2,1)S(1)}, bf16[48,768]{1,0:T(8,128)(2,1)S(1)}, u32[]{:S(2)}, u32[]{:S(2)}) collective-permute-start(bf16[48,768]{1,0:T(8,128)(2,1)S(1)} %get-tuple-element.69), channel_id=1, source_target_pairs={{12,0},{14,2},{0,4},{2,6},{4,8},{6,10},{8,12},{10,14},{13,1},{15,3... | collective-permute-start | bytes 221192 | tf_op jit(solution)/shard_map/ppermute | solution.py:423
  77.5 21.1 %collective-permute-start.19 = (bf16[48,768]{1,0:T(8,128)(2,1)S(1)}, bf16[48,768]{1,0:T(8,128)(2,1)S(1)}, u32[]{:S(2)}, u32[]{:S(2)}) collective-permute-start(bf16[48,768]{1,0:T(8,128)(2,1)S(1)} %get-tuple-element.70), channel_id=1, source_target_pairs={{8,0},{10,2},{12,4},{14,6},{0,8},{2,10},{4,12},{6,14},{9,1},{11,3}... | collective-permute-start | bytes 221192 | tf_op jit(solution)/shard_map/ppermute | solution.py:423
  79.9 18.7 %collective-permute-start.20 = (bf16[48,768]{1,0:T(8,128)(2,1)S(1)}, bf16[48,768]{1,0:T(8,128)(2,1)S(1)}, u32[]{:S(2)}, u32[]{:S(2)}) collective-permute-start(bf16[48,768]{1,0:T(8,128)(2,1)S(1)} %get-tuple-element.71), channel_id=1, source_target_pairs={{4,0},{6,2},{8,4},{10,6},{12,8},{14,10},{0,12},{2,14},{5,1},{7,3},... | collective-permute-start | bytes 221192 | tf_op jit(solution)/shard_map/ppermute | solution.py:423
  94.7 6.5 %collective-permute-start.24 = (bf16[48,768]{1,0:T(8,128)(2,1)S(1)}, bf16[48,768]{1,0:T(8,128)(2,1)S(1)}, u32[]{:S(2)}, u32[]{:S(2)}) collective-permute-start(bf16[48,768]{1,0:T(8,128)(2,1)S(1)} %get-tuple-element.74), channel_id=1, source_target_pairs={{12,0},{14,2},{0,4},{2,6},{4,8},{6,10},{8,12},{10,14},{13,1},{15,3... | collective-permute-start | bytes 221192 | tf_op jit(solution)/shard_map/ppermute | solution.py:423
  95.9 7.3 %collective-permute-start.25 = (bf16[48,768]{1,0:T(8,128)(2,1)S(1)}, bf16[48,768]{1,0:T(8,128)(2,1)S(1)}, u32[]{:S(2)}, u32[]{:S(2)}) collective-permute-start(bf16[48,768]{1,0:T(8,128)(2,1)S(1)} %get-tuple-element.75), channel_id=1, source_target_pairs={{8,0},{10,2},{12,4},{14,6},{0,8},{2,10},{4,12},{6,14},{9,1},{11,3}... | collective-permute-start | bytes 221192 | tf_op jit(solution)/shard_map/ppermute | solution.py:423
  103.4 8.6 %collective-permute-start.27 = (bf16[96,768]{1,0:T(8,128)(2,1)S(1)}, bf16[96,768]{1,0:T(8,128)(2,1)S(1)}, u32[]{:S(2)}, u32[]{:S(2)}) collective-permute-start(bf16[96,768]{1,0:T(8,128)(2,1)S(1)} %pad_maximum_fusion.refs_0_), channel_id=1, source_target_pairs={{4,0},{6,2},{8,4},{10,6},{12,8},{14,10},{0,12},{2,14},{5,1},{7,3},... | collective-permute-start | bytes 442376 | tf_op jit(solution)/shard_map/ppermute | solution.py:423
  109.3 8.7 %collective-permute-start.28 = (bf16[96,768]{1,0:T(8,128)(2,1)S(1)}, bf16[96,768]{1,0:T(8,128)(2,1)S(1)}, u32[]{:S(2)}, u32[]{:S(2)}) collective-permute-start(bf16[96,768]{1,0:T(8,128)(2,1)S(1)} %pad_maximum_fusion.refs_0_), channel_id=1, source_target_pairs={{8,0},{10,2},{12,4},{14,6},{0,8},{2,10},{4,12},{6,14},{9,1},{11,3}... | collective-permute-start | bytes 442376 | tf_op jit(solution)/shard_map/ppermute | solution.py:423
  110.1 9.3 %collective-permute-start.29 = (bf16[96,768]{1,0:T(8,128)(2,1)S(1)}, bf16[96,768]{1,0:T(8,128)(2,1)S(1)}, u32[]{:S(2)}, u32[]{:S(2)}) collective-permute-start(bf16[96,768]{1,0:T(8,128)(2,1)S(1)} %pad_maximum_fusion.refs_0_), channel_id=1, source_target_pairs={{12,0},{14,2},{0,4},{2,6},{4,8},{6,10},{8,12},{10,14},{13,1},{15,3... | collective-permute-start | bytes 442376 | tf_op jit(solution)/shard_map/ppermute | solution.py:423
  110.1 14.6 %collective-permute-start.30 = (bf16[96,768]{1,0:T(8,128)(2,1)S(1)}, bf16[96,768]{1,0:T(8,128)(2,1)S(1)}, u32[]{:S(2)}, u32[]{:S(2)}) collective-permute-start(bf16[96,768]{1,0:T(8,128)(2,1)S(1)} %pad_maximum_fusion.refs_0_), channel_id=1, source_target_pairs={{2,0},{0,2},{6,4},{4,6},{10,8},{8,10},{14,12},{12,14},{3,1},{1,3},... | collective-permute-start | bytes 442376 | tf_op jit(solution)/shard_map/ppermute | solution.py:423
  112.0 12.7 %collective-permute-start.31 = (bf16[96,768]{1,0:T(8,128)(2,1)S(1)}, bf16[96,768]{1,0:T(8,128)(2,1)S(1)}, u32[]{:S(2)}, u32[]{:S(2)}) collective-permute-start(bf16[96,768]{1,0:T(8,128)(2,1)S(1)} %collective-permute-done.27.refs_1_), channel_id=1, source_target_pairs={{2,0},{0,2},{6,4},{4,6},{10,8},{8,10},{14,12},{12,14},{3,1},{1,3},... | collective-permute-start | bytes 442376 | tf_op jit(solution)/shard_map/ppermute | solution.py:423
  118.0 6.8 %collective-permute-start.32 = (bf16[96,768]{1,0:T(8,128)(2,1)S(1)}, bf16[96,768]{1,0:T(8,128)(2,1)S(1)}, u32[]{:S(2)}, u32[]{:S(2)}) collective-permute-start(bf16[96,768]{1,0:T(8,128)(2,1)S(1)} %collective-permute-done.28.refs_2_), channel_id=1, source_target_pairs={{2,0},{0,2},{6,4},{4,6},{10,8},{8,10},{14,12},{12,14},{3,1},{1,3},... | collective-permute-start | bytes 442376 | tf_op jit(solution)/shard_map/ppermute | solution.py:423
  (9 other events, 93.8 us)

commit v2 on v1

--- a/solution.py
+++ b/solution.py
@@ -332,9 +332,19 @@
 
 def fill_right(right_ref, pieces, across, place_ref, owner_ref):
     sites = len(pieces)
-    momenta, nvec, block = right_ref.shape[0], right_ref.shape[1] // 2, right_ref.shape[2] // 2
+    momenta, nvec = right_ref.shape[0], right_ref.shape[1] // 2
+    block = nvec // 2
+    half = block - LANES
     rows = block // sites
     v = lax.rem(place_ref[1] + across, 2)
+    leads = owner_ref[v] == 0
+
+    def tiles(value):
+        zeros = jnp.zeros((value.shape[0], LANES - half), value.dtype)
+        first = jnp.concatenate([value[:, :LANES], value[:, LANES:], zeros], axis=1)
+        second = jnp.concatenate([value[:, half:], zeros, value[:, :half]], axis=1)
+        return jnp.where(leads, first, second)
+
     for up, piece in enumerate(pieces):
         z = lax.rem(place_ref[0] + up, sites)
         for part, owner in ((0, owner_ref[v]), (1, owner_ref[1 - v])):
@@ -342,9 +352,11 @@
             low = pl.multiple_of(nvec + owner * block + z * rows, 16)
             for p in range(momenta):
                 value = piece[part * rows : (part + 1) * rows, p * 2 * block : (p + 1) * 2 * block]
-                right_ref[p, pl.ds(row, rows), :] = value
-                turned = jnp.concatenate([-value[:, block:], value[:, :block]], axis=1)
-                right_ref[p, pl.ds(low, rows), :] = turned
+                re, im = tiles(value[:, :block]), tiles(value[:, block:])
+                right_ref[p, pl.ds(row, rows), : 2 * LANES] = re
+                right_ref[p, pl.ds(row, rows), 2 * LANES :] = im
+                right_ref[p, pl.ds(low, rows), : 2 * LANES] = -im
+                right_ref[p, pl.ds(low, rows), 2 * LANES :] = re
 
 
 def first_kernel(sites, place_ref, owner_ref, tau_ref, *refs):
@@ -368,26 +380,27 @@
     def assemble():
         fill_right(right_ref, pieces, 1, place_ref, owner_ref)
 
-    block = right_ref.shape[2] // 2
+    leads = owner_ref[place_ref[1]] == 0
     left = jnp.concatenate([tau_ref[0, 0], tau_ref[0, 1]], axis=1)
-    leads = owner_ref[place_ref[1]] == 0
     for p in range(right_ref.shape[0]):
-        mine = first_ref[0, p]
         product = jnp.dot(left, right_ref[p], preferred_element_type=jnp.float32).astype(jnp.bfloat16)
-        low, high = jnp.where(leads, mine, product), jnp.where(leads, product, mine)
-        out_ref[0, p, 0] = jnp.concatenate([low[:, :block], high[:, :block]], axis=1)
-        out_ref[0, p, 1] = jnp.concatenate([low[:, block:], high[:, block:]], axis=1)
+        for c in range(2):
+            at = 2 * c * LANES
+            mine, theirs = first_ref[0, p, :, at : at + LANES], product[:, at : at + LANES]
+            middle = first_ref[0, p, :, at + LANES : at + 2 * LANES] + product[:, at + LANES : at + 2 * LANES]
+            out_ref[0, p, c, :, :LANES] = jnp.where(leads, mine, theirs)
+            out_ref[0, p, c, :, LANES : 2 * LANES] = middle
+            out_ref[0, p, c, :, 2 * LANES :] = jnp.where(leads, theirs, mine)
 
 
 def project_first(tau, place, owner, pieces, momenta):
     outer, _, rows, nvec = tau.shape
-    block = nvec // 2
     return pl.pallas_call(
         functools.partial(first_kernel, len(pieces)),
-        out_shape=pltpu.VMEM((outer, momenta, rows, 2 * block), jnp.bfloat16),
+        out_shape=pltpu.VMEM((outer, momenta, rows, 4 * LANES), jnp.bfloat16),
         in_specs=[SMEM, SMEM] + [VMEM] * (1 + len(pieces)),
         out_specs=VMEM,
-        scratch_shapes=[pltpu.VMEM((momenta, 2 * nvec, 2 * block), jnp.bfloat16)],
+        scratch_shapes=[pltpu.VMEM((momenta, 2 * nvec, 4 * LANES), jnp.bfloat16)],
         cost_estimate=pl.CostEstimate(
             flops=2 * outer * rows * 2 * nvec * nvec * momenta, bytes_accessed=outer * rows * nvec * 8,
             transcendentals=0),
@@ -405,7 +418,7 @@
         in_specs=[SMEM, SMEM, pl.BlockSpec((1, 2, rows, nvec), lambda i: (i, 0, 0, 0)),
                   pl.BlockSpec((1, *first.shape[1:]), lambda i: (i, 0, 0, 0))] + [VMEM] * len(pieces),
         out_specs=pl.BlockSpec((1, momenta, 2, rows, nvec), lambda i: (i, 0, 0, 0, 0)),
-        scratch_shapes=[pltpu.VMEM((momenta, 2 * nvec, nvec), jnp.bfloat16)],
+        scratch_shapes=[pltpu.VMEM((momenta, 2 * nvec, 4 * LANES), jnp.bfloat16)],
         cost_estimate=pl.CostEstimate(
             flops=2 * outer * rows * 2 * nvec * nvec * momenta, bytes_accessed=outer * rows * nvec * 12,
             transcendentals=0),
@@ -436,7 +449,12 @@
 
     received, packed = [], []
     for chunk in range(len(CHUNKS)):
-        packed = pack(own, place, chunk, sites, own_links, packed[:1])
+        after = packed[:1]
+        if chunk == 1:
+            after = received[0][:1]
+        if chunk == 2:
+            after = [*received[0], packed[0]]
+        packed = pack(own, place, chunk, sites, own_links, after)
         received.append([from_place(packed[d - 1], -d, 0) for d in range(1, sites)])
 
     flat = lax.broadcasted_iota(jnp.int32, (4, LANES), 0) * LANES + lax.broadcasted_iota(jnp.int32, (4, LANES), 1)
@@ -621,7 +639,7 @@
     block, layers, plane = eigvecs.shape[3:]
     sites, groups = lax.axis_size("site"), lax.axis_size("vec")
     fits = layers == 1 and plane == LX * LY == 4 * LANES and sites == 4 and groups == 2
-    fits = fits and block == sites * sum(CHUNKS) and (2 * block) % (32 * sites) == 0 and block % (2 * block // sites) == 0
+    fits = fits and block == sites * sum(CHUNKS) and LANES < block < 2 * LANES and (2 * block) % (32 * sites) == 0 and block % (2 * block // sites) == 0
     device = per_device if fits else general_device
     return device(eigvecs, links, peramb, block_owner, momenta)
 

time: 132 us -> 128 us (0.970)
  waiting for transfers between devices: 34.9 us -> 25.7 us
  starting transfers between devices: 55.1 us -> 60 us
    ppermute x34, waiting for transfers between devices: 34.9 us -> 25.7 us  [from_place(): return lax.ppermute(block, ('site', 'vec'), route)]
    ppermute x34, starting transfers between devices: 55.1 us -> 60 us  [from_place(): return lax.ppermute(block, ('site', 'vec'), route)]
  transfers between devices with their start and end apart: 34 -> 34, of which waited for: 13 -> 13; matrix products, arithmetic and copies ran while one was open for 0% -> 1% of each run, Pallas kernels for 23% -> 24%
where the time goes in v2:
time: 128 us
  starting transfers between devices  60 us (47%)
  Pallas kernels  37.9 us (30%)
  waiting for transfers between devices  25.7 us (20%)
  local copies, waits for them, and re-layouts  2.75 us (2%)
    ppermute x34, starting transfers between devices, from_place(): return lax.ppermute(block, ('site', 'vec'), route)  60 us
    ppermute x34, waiting for transfers between devices, from_place(): return lax.ppermute(block, ('site', 'vec'), route)  25.7 us
    pallas_call x3, Pallas kernels, filter_chunk(): pl.pallas_call(functools.partial(filter_kernel, sites, chunk), out_shape=...  17.4 us
    pallas_call x1, Pallas kernels, project_second(): pl.pallas_call(functools.partial(second_kernel, len(pieces)), grid=(outer...  6.67 us
    pallas_call x1, Pallas kernels, project_first(): pl.pallas_call(functools.partial(first_kernel, len(pieces)), out_shape=pl...  4.65 us
    pallas_call x2, Pallas kernels, elementals(): pl.pallas_call(functools.partial(own_kernel if own else other_kernel, seg...  4.47 us
    pallas_call x3, Pallas kernels, finish(): pl.pallas_call(functools.partial(finish_kernel, sites, chunk), out_shape=...  2.66 us
    unnamed x14, local copies, waits for them, and re-layouts  2.58 us
  transfers between devices with their start and end apart: 34, of which 13 were waited for; matrix products, arithmetic and copies ran while one was open for 1% of the time, Pallas kernels for 24%

profile of v2, /device:TPU:0, one launch (start us, length us, event | category | flops | bytes accessed | tf_op | source)
XLA Modules:
  0.0 127.8 jit_solution(7301087521591182166)
XLA Ops:
  0.1 1.7 %copy-done = f32[1,2,3,192,1,512]{5,4,3,2,1,0:T(1,128)S(1)} copy-done((f32[1,2,3,192,1,512]{5,4,3,2,1,0:T(1,128)S(1)}, f32[1,2,3,192,1,512]{5,4,3,2,1,0:T(1,128)}, u32[]{:S(2)}) %copy-start) | copy-done | bytes 2359320
  3.2 3.1 %collective-permute-start = (bf16[600,128]{1,0:T(8,128)(2,1)S(1)}, bf16[600,128]{1,0:T(8,128)(2,1)S(1)}, u32[]{:S(2)}, u32[]{:S(2)}) collective-permute-start(bf16[600,128]{1,0:T(8,128)(2,1)S(1)} %get-tuple-element.41), channel_id=1, source_target_pairs={{12,0},{14,2},{0,4},{2,6},{4,8},{6,10},{8,12},{10,14},{13,1},{15,3... | collective-permute-start | bytes 460808 | tf_op jit(solution)/shard_map/ppermute | solution.py:436
  6.3 2.6 %collective-permute-start.1 = (bf16[600,128]{1,0:T(8,128)(2,1)S(1)}, bf16[600,128]{1,0:T(8,128)(2,1)S(1)}, u32[]{:S(2)}, u32[]{:S(2)}) collective-permute-start(bf16[600,128]{1,0:T(8,128)(2,1)S(1)} %get-tuple-element.42), channel_id=1, source_target_pairs={{8,0},{10,2},{12,4},{14,6},{0,8},{2,10},{4,12},{6,14},{9,1},{11,3}... | collective-permute-start | bytes 460808 | tf_op jit(solution)/shard_map/ppermute | solution.py:436
  11.2 2.1 %collective-permute-done.refs_1_.refs_0_ = bf16[600,128]{1,0:T(8,128)(2,1)S(1)} collective-permute-done((bf16[600,128]{1,0:T(8,128)(2,1)S(1)}, bf16[600,128]{1,0:T(8,128)(2,1)S(1)}, u32[]{:S(2)}, u32[]{:S(2)}) %collective-permute-start) | collective-permute-done | bytes 153632 | tf_op jit(solution)/shard_map/ppermute | solution.py:436
  13.9 5.4 %collective-permute-start.6 = (bf16[384,128]{1,0:T(8,128)(2,1)S(1)}, bf16[384,128]{1,0:T(8,128)(2,1)S(1)}, u32[]{:S(2)}, u32[]{:S(2)}) collective-permute-start(bf16[384,128]{1,0:T(8,128)(2,1)S(1)} %get-tuple-element.48.refs_3_), channel_id=1, source_target_pairs={{12,0},{14,2},{0,4},{2,6},{4,8},{6,10},{8,12},{10,14},{13,1},{15,3... | collective-permute-start | bytes 294920 | tf_op jit(solution)/shard_map/ppermute | solution.py:436
  19.3 4.3 %collective-permute-start.7 = (bf16[384,128]{1,0:T(8,128)(2,1)S(1)}, bf16[384,128]{1,0:T(8,128)(2,1)S(1)}, u32[]{:S(2)}, u32[]{:S(2)}) collective-permute-start(bf16[384,128]{1,0:T(8,128)(2,1)S(1)} %get-tuple-element.49), channel_id=1, source_target_pairs={{8,0},{10,2},{12,4},{14,6},{0,8},{2,10},{4,12},{6,14},{9,1},{11,3}... | collective-permute-start | bytes 294920 | tf_op jit(solution)/shard_map/ppermute | solution.py:436
  23.7 2.8 %collective-permute-start.8 = (bf16[384,128]{1,0:T(8,128)(2,1)S(1)}, bf16[384,128]{1,0:T(8,128)(2,1)S(1)}, u32[]{:S(2)}, u32[]{:S(2)}) collective-permute-start(bf16[384,128]{1,0:T(8,128)(2,1)S(1)} %get-tuple-element.50), channel_id=1, source_target_pairs={{4,0},{6,2},{8,4},{10,6},{12,8},{14,10},{0,12},{2,14},{5,1},{7,3},... | collective-permute-start | bytes 294920 | tf_op jit(solution)/shard_map/ppermute | solution.py:436
  26.8 5.8 %shard_map.56 = (bf16[6,64,128]{2,1,0:T(8,128)(2,1)S(1)}, bf16[6,64,128]{2,1,0:T(8,128)(2,1)S(1)}, bf16[6,64,128]{2,1,0:T(8,128)(2,1)S(1)}, bf16[6,64,128]{2,1,0:T(8,128)(2,1)S(1)}) custom-call(s32[2]{0:T(128)S(1)} %pad_add_fusion.place_ref, f32[6,768,128]{2,1,0:T(8,128)S(1)} %bitcast.8, bf16[600,128]{1,0:T(8,128)(2,1)S(1)} %collective-permute-done.refs_1_.refs_0_, ...), custom_call_target="tpu_custom_call" | custom-call | flops 28311552 | bytes 786432 | tf_op jit(solution)/shard_map/pallas_call | solution.py:202
  35.6 2.2 %collective-permute-start.12 = (bf16[384,128]{1,0:T(8,128)(2,1)S(1)}, bf16[384,128]{1,0:T(8,128)(2,1)S(1)}, u32[]{:S(2)}, u32[]{:S(2)}) collective-permute-start(bf16[384,128]{1,0:T(8,128)(2,1)S(1)} %get-tuple-element.56), channel_id=1, source_target_pairs={{12,0},{14,2},{0,4},{2,6},{4,8},{6,10},{8,12},{10,14},{13,1},{15,3... | collective-permute-start | bytes 294920 | tf_op jit(solution)/shard_map/ppermute | solution.py:436
  38.9 5.8 %shard_map.58 = (bf16[6,64,128]{2,1,0:T(8,128)(2,1)S(1)}, bf16[6,64,128]{2,1,0:T(8,128)(2,1)S(1)}, bf16[6,64,128]{2,1,0:T(8,128)(2,1)S(1)}, bf16[6,64,128]{2,1,0:T(8,128)(2,1)S(1)}) custom-call(s32[2]{0:T(128)S(1)} %pad_add_fusion.place_ref, f32[6,768,128]{2,1,0:T(8,128)S(1)} %bitcast.10, bf16[384,128]{1,0:T(8,128)(2,1)S(1)} %collective-permute-done.6.refs_1_, ...), custom_call_target="tpu_custom_call" | custom-call | flops 28311552 | bytes 786432 | tf_op jit(solution)/shard_map/pallas_call | solution.py:202
  44.8 2.5 %collective-permute-start.14 = (bf16[384,128]{1,0:T(8,128)(2,1)S(1)}, bf16[384,128]{1,0:T(8,128)(2,1)S(1)}, u32[]{:S(2)}, u32[]{:S(2)}) collective-permute-start(bf16[384,128]{1,0:T(8,128)(2,1)S(1)} %get-tuple-element.58), channel_id=1, source_target_pairs={{4,0},{6,2},{8,4},{10,6},{12,8},{14,10},{0,12},{2,14},{5,1},{7,3},... | collective-permute-start | bytes 294920 | tf_op jit(solution)/shard_map/ppermute | solution.py:436
  49.7 3.3 %collective-permute-start.9 = (bf16[6,64,128]{2,1,0:T(8,128)(2,1)S(1)}, bf16[6,64,128]{2,1,0:T(8,128)(2,1)S(1)}, u32[]{:S(2)}, u32[]{:S(2)}) collective-permute-start(bf16[6,64,128]{2,1,0:T(8,128)(2,1)S(1)} %get-tuple-element.53), channel_id=1, source_target_pairs={{4,0},{6,2},{8,4},{10,6},{12,8},{14,10},{0,12},{2,14},{5,1},{7,3},... | collective-permute-start | bytes 294920 | tf_op jit(solution)/shard_map/ppermute | solution.py:436
  53.2 5.8 %shard_map.61 = (bf16[6,64,128]{2,1,0:T(8,128)(2,1)S(1)}, bf16[6,64,128]{2,1,0:T(8,128)(2,1)S(1)}, bf16[6,64,128]{2,1,0:T(8,128)(2,1)S(1)}, bf16[6,64,128]{2,1,0:T(8,128)(2,1)S(1)}) custom-call(s32[2]{0:T(128)S(1)} %pad_add_fusion.place_ref, f32[6,768,128]{2,1,0:T(8,128)S(1)} %bitcast.12, bf16[384,128]{1,0:T(8,128)(2,1)S(1)} %collective-permute-done.12.refs_1_, ...), custom_call_target="tpu_custom_call" | custom-call | flops 28311552 | bytes 786432 | tf_op jit(solution)/shard_map/pallas_call | solution.py:202
  59.0 3.5 %collective-permute-start.15 = (bf16[6,64,128]{2,1,0:T(8,128)(2,1)S(1)}, bf16[6,64,128]{2,1,0:T(8,128)(2,1)S(1)}, u32[]{:S(2)}, u32[]{:S(2)}) collective-permute-start(bf16[6,64,128]{2,1,0:T(8,128)(2,1)S(1)} %get-tuple-element.62), channel_id=1, source_target_pairs={{4,0},{6,2},{8,4},{10,6},{12,8},{14,10},{0,12},{2,14},{5,1},{7,3},... | collective-permute-start | bytes 294920 | tf_op jit(solution)/shard_map/ppermute | solution.py:436
  62.4 1.8 %collective-permute-start.16 = (bf16[6,64,128]{2,1,0:T(8,128)(2,1)S(1)}, bf16[6,64,128]{2,1,0:T(8,128)(2,1)S(1)}, u32[]{:S(2)}, u32[]{:S(2)}) collective-permute-start(bf16[6,64,128]{2,1,0:T(8,128)(2,1)S(1)} %get-tuple-element.63), channel_id=1, source_target_pairs={{8,0},{10,2},{12,4},{14,6},{0,8},{2,10},{4,12},{6,14},{9,1},{11,3}... | collective-permute-start | bytes 294920 | tf_op jit(solution)/shard_map/ppermute | solution.py:436
  64.2 1.6 %collective-permute-start.21 = (bf16[4,2,16,1536]{3,2,1,0:T(8,128)(2,1)S(1)}, bf16[4,2,16,1536]{3,2,1,0:T(8,128)(2,1)S(1)}, u32[]{:S(2)}, u32[]{:S(2)}) collective-permute-start(bf16[4,2,16,1536]{3,2,1,0:T(8,128)(2,1)S(1)} %get-tuple-element.52.refs_0_), channel_id=1, source_target_pairs={{2,0},{0,2},{6,4},{4,6},{10,8},{8,10},{14,12},{12,14},{3,1},{1,3},... | collective-permute-start | bytes 1179656 | tf_op jit(solution)/shard_map/ppermute | solution.py:436
  67.1 2.6 %collective-permute-done.16.refs_2_ = bf16[6,64,128]{2,1,0:T(8,128)(2,1)S(1)} collective-permute-done((bf16[6,64,128]{2,1,0:T(8,128)(2,1)S(1)}, bf16[6,64,128]{2,1,0:T(8,128)(2,1)S(1)}, u32[]{:S(2)}, u32[]{:S(2)}) %collective-permute-start.16) | collective-permute-done | bytes 98336 | tf_op jit(solution)/shard_map/ppermute | solution.py:436
  71.6 1.6 %collective-permute-start.23 = (bf16[4,2,16,1536]{3,2,1,0:T(8,128)(2,1)S(1)}, bf16[4,2,16,1536]{3,2,1,0:T(8,128)(2,1)S(1)}, u32[]{:S(2)}, u32[]{:S(2)}) collective-permute-start(bf16[4,2,16,1536]{3,2,1,0:T(8,128)(2,1)S(1)} %get-tuple-element.66.refs_2_), channel_id=1, source_target_pairs={{2,0},{0,2},{6,4},{4,6},{10,8},{8,10},{14,12},{12,14},{3,1},{1,3},... | collective-permute-start | bytes 1179656 | tf_op jit(solution)/shard_map/ppermute | solution.py:436
  73.7 2.2 %elementals_own.1 = (f32[48,768]{1,0:T(8,128)S(1)}, bf16[48,768]{1,0:T(8,128)(2,1)S(1)}, bf16[48,768]{1,0:T(8,128)(2,1)S(1)}, bf16[48,768]{1,0:T(8,128)(2,1)S(1)}, bf16[2,384,3072]{2,1,0:T(8,128)(2,1)S(1)}) custom-call(s32[2]{0:T(128)S(1)} %pad_add_fusion.place_ref, bf16[4,2,16,1536]{3,2,1,0:T(8,128)(2,1)S(1)} %get-tuple-element.52.refs_0_, ...), custom_call_target="tpu_custom_call" | custom-call | flops 905969664 | bytes 2359296 | tf_op jit(solution)/shard_map/elementals_own/pallas_call | solution.py:317
  76.7 3.4 %collective-permute-start.20 = (bf16[48,768]{1,0:T(8,128)(2,1)S(1)}, bf16[48,768]{1,0:T(8,128)(2,1)S(1)}, u32[]{:S(2)}, u32[]{:S(2)}) collective-permute-start(bf16[48,768]{1,0:T(8,128)(2,1)S(1)} %get-tuple-element.71), channel_id=1, source_target_pairs={{4,0},{6,2},{8,4},{10,6},{12,8},{14,10},{0,12},{2,14},{5,1},{7,3},... | collective-permute-start | bytes 221192 | tf_op jit(solution)/shard_map/ppermute | solution.py:436
  80.0 3.6 %collective-permute-done.23.refs_2_ = bf16[4,2,16,1536]{3,2,1,0:T(8,128)(2,1)S(1)} collective-permute-done((bf16[4,2,16,1536]{3,2,1,0:T(8,128)(2,1)S(1)}, bf16[4,2,16,1536]{3,2,1,0:T(8,128)(2,1)S(1)}, u32[]{:S(2)}, u32[]{:S(2)}) %collective-permute-start.23) | collective-permute-done | bytes 393248 | tf_op jit(solution)/shard_map/ppermute | solution.py:436
  83.6 5.3 %collective-permute-done.22.refs_1_ = bf16[4,2,16,1536]{3,2,1,0:T(8,128)(2,1)S(1)} collective-permute-done((bf16[4,2,16,1536]{3,2,1,0:T(8,128)(2,1)S(1)}, bf16[4,2,16,1536]{3,2,1,0:T(8,128)(2,1)S(1)}, u32[]{:S(2)}, u32[]{:S(2)}) %collective-permute-start.22) | collective-permute-done | bytes 393248 | tf_op jit(solution)/shard_map/ppermute | solution.py:436
  88.9 2.2 %elementals_other.1 = (f32[48,768]{1,0:T(8,128)S(1)}, bf16[48,768]{1,0:T(8,128)(2,1)S(1)}, bf16[48,768]{1,0:T(8,128)(2,1)S(1)}, bf16[48,768]{1,0:T(8,128)(2,1)S(1)}) custom-call(s32[2]{0:T(128)S(1)} %pad_add_fusion.place_ref, bf16[4,2,16,1536]{3,2,1,0:T(8,128)(2,1)S(1)} %collective-permute-done.21.refs_0_, ...), custom_call_target="tpu_custom_call" | custom-call | flops 905969664 | bytes 2359296 | tf_op jit(solution)/shard_map/elementals_other/pallas_call | solution.py:317
  92.4 2.5 %collective-permute-start.25 = (bf16[48,768]{1,0:T(8,128)(2,1)S(1)}, bf16[48,768]{1,0:T(8,128)(2,1)S(1)}, u32[]{:S(2)}, u32[]{:S(2)}) collective-permute-start(bf16[48,768]{1,0:T(8,128)(2,1)S(1)} %get-tuple-element.75), channel_id=1, source_target_pairs={{8,0},{10,2},{12,4},{14,6},{0,8},{2,10},{4,12},{6,14},{9,1},{11,3}... | collective-permute-start | bytes 221192 | tf_op jit(solution)/shard_map/ppermute | solution.py:436
  95.7 1.8 %collective-permute-done.24 = bf16[48,768]{1,0:T(8,128)(2,1)S(1)} collective-permute-done((bf16[48,768]{1,0:T(8,128)(2,1)S(1)}, bf16[48,768]{1,0:T(8,128)(2,1)S(1)}, u32[]{:S(2)}, u32[]{:S(2)}) %collective-permute-start.24) | collective-permute-done | bytes 73760 | tf_op jit(solution)/shard_map/ppermute | solution.py:436
  97.5 2.2 %collective-permute-done.25 = bf16[48,768]{1,0:T(8,128)(2,1)S(1)} collective-permute-done((bf16[48,768]{1,0:T(8,128)(2,1)S(1)}, bf16[48,768]{1,0:T(8,128)(2,1)S(1)}, u32[]{:S(2)}, u32[]{:S(2)}) %collective-permute-start.25) | collective-permute-done | bytes 73760 | tf_op jit(solution)/shard_map/ppermute | solution.py:436
  100.6 2.3 %collective-permute-start.27 = (bf16[96,768]{1,0:T(8,128)(2,1)S(1)}, bf16[96,768]{1,0:T(8,128)(2,1)S(1)}, u32[]{:S(2)}, u32[]{:S(2)}) collective-permute-start(bf16[96,768]{1,0:T(8,128)(2,1)S(1)} %pad_maximum_fusion.refs_0_), channel_id=1, source_target_pairs={{4,0},{6,2},{8,4},{10,6},{12,8},{14,10},{0,12},{2,14},{5,1},{7,3},... | collective-permute-start | bytes 442376 | tf_op jit(solution)/shard_map/ppermute | solution.py:436
  102.9 3.7 %collective-permute-start.28 = (bf16[96,768]{1,0:T(8,128)(2,1)S(1)}, bf16[96,768]{1,0:T(8,128)(2,1)S(1)}, u32[]{:S(2)}, u32[]{:S(2)}) collective-permute-start(bf16[96,768]{1,0:T(8,128)(2,1)S(1)} %pad_maximum_fusion.refs_0_), channel_id=1, source_target_pairs={{8,0},{10,2},{12,4},{14,6},{0,8},{2,10},{4,12},{6,14},{9,1},{11,3}... | collective-permute-start | bytes 442376 | tf_op jit(solution)/shard_map/ppermute | solution.py:436
  106.6 1.5 %collective-permute-start.30 = (bf16[96,768]{1,0:T(8,128)(2,1)S(1)}, bf16[96,768]{1,0:T(8,128)(2,1)S(1)}, u32[]{:S(2)}, u32[]{:S(2)}) collective-permute-start(bf16[96,768]{1,0:T(8,128)(2,1)S(1)} %pad_maximum_fusion.refs_0_), channel_id=1, source_target_pairs={{2,0},{0,2},{6,4},{4,6},{10,8},{8,10},{14,12},{12,14},{3,1},{1,3},... | collective-permute-start | bytes 442376 | tf_op jit(solution)/shard_map/ppermute | solution.py:436
  109.7 4.7 %collective-permute-done.28.refs_2_ = bf16[96,768]{1,0:T(8,128)(2,1)S(1)} collective-permute-done((bf16[96,768]{1,0:T(8,128)(2,1)S(1)}, bf16[96,768]{1,0:T(8,128)(2,1)S(1)}, u32[]{:S(2)}, u32[]{:S(2)}) %collective-permute-start.28) | collective-permute-done | bytes 147488 | tf_op jit(solution)/shard_map/ppermute | solution.py:436
  116.4 4.7 %project_first.1.first_ref = bf16[8,2,192,512]{3,2,1,0:T(8,128)(2,1)S(1)} custom-call(s32[2]{0:T(128)S(1)} %pad_add_fusion.place_ref, s32[2]{0:T(128)S(1)} %copy-done.5, bf16[8,2,192,384]{3,2,1,0:T(8,128)(2,1)S(1)} %bitcast.15, bf16[96,768]{1,0:T(8,128)(2,1)S(1)} %pad_maximum_fusion.refs_0_, bf16[96,768]{1,0:T(8,128)(2,1)S(1)} %collective-permute-done.27.refs_1_, ...), custom_call_target="tpu_custom_call" | custom-call | flops 1811939328 | bytes 4718592 | tf_op jit(solution)/shard_map/project_first/pallas_call | solution.py:398
  121.1 6.7 %project_second.1 = bf16[8,2,2,192,384]{4,3,2,1,0:T(8,128)(2,1)} custom-call(s32[2]{0:T(128)S(1)} %pad_add_fusion.place_ref, s32[2]{0:T(128)S(1)} %copy-done.5, bf16[8,2,192,384]{3,2,1,0:T(8,128)(2,1)S(1)} %bitcast.16, bf16[8,2,192,512]{3,2,1,0:T(8,128)(2,1)S(1)} %project_first.1.first_ref, bf16[96,768]{1,0:T(8,128)(2,1)S(1)} %collective-permute-done.30.refs_0_, ...), custom_call_target="tpu_custom_call" | custom-call | flops 1811939328 | bytes 7077888 | tf_op jit(solution)/shard_map/project_second/pallas_call | solution.py:414
  (73 shorter events, 22.5 us)
Async XLA Ops:
  3.2 10.1 %collective-permute-start = (bf16[600,128]{1,0:T(8,128)(2,1)S(1)}, bf16[600,128]{1,0:T(8,128)(2,1)S(1)}, u32[]{:S(2)}, u32[]{:S(2)}) collective-permute-start(bf16[600,128]{1,0:T(8,128)(2,1)S(1)} %get-tuple-element.41), channel_id=1, source_target_pairs={{12,0},{14,2},{0,4},{2,6},{4,8},{6,10},{8,12},{10,14},{13,1},{15,3... | collective-permute-start | bytes 460808 | tf_op jit(solution)/shard_map/ppermute | solution.py:436
  6.3 20.2 %collective-permute-start.1 = (bf16[600,128]{1,0:T(8,128)(2,1)S(1)}, bf16[600,128]{1,0:T(8,128)(2,1)S(1)}, u32[]{:S(2)}, u32[]{:S(2)}) collective-permute-start(bf16[600,128]{1,0:T(8,128)(2,1)S(1)} %get-tuple-element.42), channel_id=1, source_target_pairs={{8,0},{10,2},{12,4},{14,6},{0,8},{2,10},{4,12},{6,14},{9,1},{11,3}... | collective-permute-start | bytes 460808 | tf_op jit(solution)/shard_map/ppermute | solution.py:436
  8.9 17.6 %collective-permute-start.2 = (bf16[600,128]{1,0:T(8,128)(2,1)S(1)}, bf16[600,128]{1,0:T(8,128)(2,1)S(1)}, u32[]{:S(2)}, u32[]{:S(2)}) collective-permute-start(bf16[600,128]{1,0:T(8,128)(2,1)S(1)} %get-tuple-element.43), channel_id=1, source_target_pairs={{4,0},{6,2},{8,4},{10,6},{12,8},{14,10},{0,12},{2,14},{5,1},{7,3},... | collective-permute-start | bytes 460808 | tf_op jit(solution)/shard_map/ppermute | solution.py:436
  13.9 20.6 %collective-permute-start.6 = (bf16[384,128]{1,0:T(8,128)(2,1)S(1)}, bf16[384,128]{1,0:T(8,128)(2,1)S(1)}, u32[]{:S(2)}, u32[]{:S(2)}) collective-permute-start(bf16[384,128]{1,0:T(8,128)(2,1)S(1)} %get-tuple-element.48.refs_3_), channel_id=1, source_target_pairs={{12,0},{14,2},{0,4},{2,6},{4,8},{6,10},{8,12},{10,14},{13,1},{15,3... | collective-permute-start | bytes 294920 | tf_op jit(solution)/shard_map/ppermute | solution.py:436
  19.3 16.2 %collective-permute-start.7 = (bf16[384,128]{1,0:T(8,128)(2,1)S(1)}, bf16[384,128]{1,0:T(8,128)(2,1)S(1)}, u32[]{:S(2)}, u32[]{:S(2)}) collective-permute-start(bf16[384,128]{1,0:T(8,128)(2,1)S(1)} %get-tuple-element.49), channel_id=1, source_target_pairs={{8,0},{10,2},{12,4},{14,6},{0,8},{2,10},{4,12},{6,14},{9,1},{11,3}... | collective-permute-start | bytes 294920 | tf_op jit(solution)/shard_map/ppermute | solution.py:436
  23.7 14.1 %collective-permute-start.8 = (bf16[384,128]{1,0:T(8,128)(2,1)S(1)}, bf16[384,128]{1,0:T(8,128)(2,1)S(1)}, u32[]{:S(2)}, u32[]{:S(2)}) collective-permute-start(bf16[384,128]{1,0:T(8,128)(2,1)S(1)} %get-tuple-element.50), channel_id=1, source_target_pairs={{4,0},{6,2},{8,4},{10,6},{12,8},{14,10},{0,12},{2,14},{5,1},{7,3},... | collective-permute-start | bytes 294920 | tf_op jit(solution)/shard_map/ppermute | solution.py:436
  32.6 12.1 %collective-permute-start.3 = (bf16[6,64,128]{2,1,0:T(8,128)(2,1)S(1)}, bf16[6,64,128]{2,1,0:T(8,128)(2,1)S(1)}, u32[]{:S(2)}, u32[]{:S(2)}) collective-permute-start(bf16[6,64,128]{2,1,0:T(8,128)(2,1)S(1)} %get-tuple-element.45), channel_id=1, source_target_pairs={{4,0},{6,2},{8,4},{10,6},{12,8},{14,10},{0,12},{2,14},{5,1},{7,3},... | collective-permute-start | bytes 294920 | tf_op jit(solution)/shard_map/ppermute | solution.py:436
  33.4 14.5 %collective-permute-start.4 = (bf16[6,64,128]{2,1,0:T(8,128)(2,1)S(1)}, bf16[6,64,128]{2,1,0:T(8,128)(2,1)S(1)}, u32[]{:S(2)}, u32[]{:S(2)}) collective-permute-start(bf16[6,64,128]{2,1,0:T(8,128)(2,1)S(1)} %get-tuple-element.46), channel_id=1, source_target_pairs={{8,0},{10,2},{12,4},{14,6},{0,8},{2,10},{4,12},{6,14},{9,1},{11,3}... | collective-permute-start | bytes 294920 | tf_op jit(solution)/shard_map/ppermute | solution.py:436
  34.5 13.6 %collective-permute-start.5 = (bf16[6,64,128]{2,1,0:T(8,128)(2,1)S(1)}, bf16[6,64,128]{2,1,0:T(8,128)(2,1)S(1)}, u32[]{:S(2)}, u32[]{:S(2)}) collective-permute-start(bf16[6,64,128]{2,1,0:T(8,128)(2,1)S(1)} %get-tuple-element.47), channel_id=1, source_target_pairs={{12,0},{14,2},{0,4},{2,6},{4,8},{6,10},{8,12},{10,14},{13,1},{15,3... | collective-permute-start | bytes 294920 | tf_op jit(solution)/shard_map/ppermute | solution.py:436
  35.6 14.1 %collective-permute-start.12 = (bf16[384,128]{1,0:T(8,128)(2,1)S(1)}, bf16[384,128]{1,0:T(8,128)(2,1)S(1)}, u32[]{:S(2)}, u32[]{:S(2)}) collective-permute-start(bf16[384,128]{1,0:T(8,128)(2,1)S(1)} %get-tuple-element.56), channel_id=1, source_target_pairs={{12,0},{14,2},{0,4},{2,6},{4,8},{6,10},{8,12},{10,14},{13,1},{15,3... | collective-permute-start | bytes 294920 | tf_op jit(solution)/shard_map/ppermute | solution.py:436
  37.7 15.4 %collective-permute-start.13 = (bf16[384,128]{1,0:T(8,128)(2,1)S(1)}, bf16[384,128]{1,0:T(8,128)(2,1)S(1)}, u32[]{:S(2)}, u32[]{:S(2)}) collective-permute-start(bf16[384,128]{1,0:T(8,128)(2,1)S(1)} %get-tuple-element.57), channel_id=1, source_target_pairs={{8,0},{10,2},{12,4},{14,6},{0,8},{2,10},{4,12},{6,14},{9,1},{11,3}... | collective-permute-start | bytes 294920 | tf_op jit(solution)/shard_map/ppermute | solution.py:436
  44.8 8.4 %collective-permute-start.14 = (bf16[384,128]{1,0:T(8,128)(2,1)S(1)}, bf16[384,128]{1,0:T(8,128)(2,1)S(1)}, u32[]{:S(2)}, u32[]{:S(2)}) collective-permute-start(bf16[384,128]{1,0:T(8,128)(2,1)S(1)} %get-tuple-element.58), channel_id=1, source_target_pairs={{4,0},{6,2},{8,4},{10,6},{12,8},{14,10},{0,12},{2,14},{5,1},{7,3},... | collective-permute-start | bytes 294920 | tf_op jit(solution)/shard_map/ppermute | solution.py:436
  48.0 16.3 %collective-permute-start.10 = (bf16[6,64,128]{2,1,0:T(8,128)(2,1)S(1)}, bf16[6,64,128]{2,1,0:T(8,128)(2,1)S(1)}, u32[]{:S(2)}, u32[]{:S(2)}) collective-permute-start(bf16[6,64,128]{2,1,0:T(8,128)(2,1)S(1)} %get-tuple-element.54), channel_id=1, source_target_pairs={{8,0},{10,2},{12,4},{14,6},{0,8},{2,10},{4,12},{6,14},{9,1},{11,3}... | collective-permute-start | bytes 294920 | tf_op jit(solution)/shard_map/ppermute | solution.py:436
  48.1 16.1 %collective-permute-start.11 = (bf16[6,64,128]{2,1,0:T(8,128)(2,1)S(1)}, bf16[6,64,128]{2,1,0:T(8,128)(2,1)S(1)}, u32[]{:S(2)}, u32[]{:S(2)}) collective-permute-start(bf16[6,64,128]{2,1,0:T(8,128)(2,1)S(1)} %get-tuple-element.55), channel_id=1, source_target_pairs={{12,0},{14,2},{0,4},{2,6},{4,8},{6,10},{8,12},{10,14},{13,1},{15,3... | collective-permute-start | bytes 294920 | tf_op jit(solution)/shard_map/ppermute | solution.py:436
  49.7 16.1 %collective-permute-start.9 = (bf16[6,64,128]{2,1,0:T(8,128)(2,1)S(1)}, bf16[6,64,128]{2,1,0:T(8,128)(2,1)S(1)}, u32[]{:S(2)}, u32[]{:S(2)}) collective-permute-start(bf16[6,64,128]{2,1,0:T(8,128)(2,1)S(1)} %get-tuple-element.53), channel_id=1, source_target_pairs={{4,0},{6,2},{8,4},{10,6},{12,8},{14,10},{0,12},{2,14},{5,1},{7,3},... | collective-permute-start | bytes 294920 | tf_op jit(solution)/shard_map/ppermute | solution.py:436
  59.0 8.1 %collective-permute-start.15 = (bf16[6,64,128]{2,1,0:T(8,128)(2,1)S(1)}, bf16[6,64,128]{2,1,0:T(8,128)(2,1)S(1)}, u32[]{:S(2)}, u32[]{:S(2)}) collective-permute-start(bf16[6,64,128]{2,1,0:T(8,128)(2,1)S(1)} %get-tuple-element.62), channel_id=1, source_target_pairs={{4,0},{6,2},{8,4},{10,6},{12,8},{14,10},{0,12},{2,14},{5,1},{7,3},... | collective-permute-start | bytes 294920 | tf_op jit(solution)/shard_map/ppermute | solution.py:436
  62.4 7.2 %collective-permute-start.16 = (bf16[6,64,128]{2,1,0:T(8,128)(2,1)S(1)}, bf16[6,64,128]{2,1,0:T(8,128)(2,1)S(1)}, u32[]{:S(2)}, u32[]{:S(2)}) collective-permute-start(bf16[6,64,128]{2,1,0:T(8,128)(2,1)S(1)} %get-tuple-element.63), channel_id=1, source_target_pairs={{8,0},{10,2},{12,4},{14,6},{0,8},{2,10},{4,12},{6,14},{9,1},{11,3}... | collective-permute-start | bytes 294920 | tf_op jit(solution)/shard_map/ppermute | solution.py:436
  64.2 6.5 %collective-permute-start.17 = (bf16[6,64,128]{2,1,0:T(8,128)(2,1)S(1)}, bf16[6,64,128]{2,1,0:T(8,128)(2,1)S(1)}, u32[]{:S(2)}, u32[]{:S(2)}) collective-permute-start(bf16[6,64,128]{2,1,0:T(8,128)(2,1)S(1)} %get-tuple-element.64), channel_id=1, source_target_pairs={{12,0},{14,2},{0,4},{2,6},{4,8},{6,10},{8,12},{10,14},{13,1},{15,3... | collective-permute-start | bytes 294920 | tf_op jit(solution)/shard_map/ppermute | solution.py:436
  64.2 12.5 %collective-permute-start.21 = (bf16[4,2,16,1536]{3,2,1,0:T(8,128)(2,1)S(1)}, bf16[4,2,16,1536]{3,2,1,0:T(8,128)(2,1)S(1)}, u32[]{:S(2)}, u32[]{:S(2)}) collective-permute-start(bf16[4,2,16,1536]{3,2,1,0:T(8,128)(2,1)S(1)} %get-tuple-element.52.refs_0_), channel_id=1, source_target_pairs={{2,0},{0,2},{6,4},{4,6},{10,8},{8,10},{14,12},{12,14},{3,1},{1,3},... | collective-permute-start | bytes 1179656 | tf_op jit(solution)/shard_map/ppermute | solution.py:436
  71.6 12.1 %collective-permute-start.23 = (bf16[4,2,16,1536]{3,2,1,0:T(8,128)(2,1)S(1)}, bf16[4,2,16,1536]{3,2,1,0:T(8,128)(2,1)S(1)}, u32[]{:S(2)}, u32[]{:S(2)}) collective-permute-start(bf16[4,2,16,1536]{3,2,1,0:T(8,128)(2,1)S(1)} %get-tuple-element.66.refs_2_), channel_id=1, source_target_pairs={{2,0},{0,2},{6,4},{4,6},{10,8},{8,10},{14,12},{12,14},{3,1},{1,3},... | collective-permute-start | bytes 1179656 | tf_op jit(solution)/shard_map/ppermute | solution.py:436
  73.1 15.8 %collective-permute-start.22 = (bf16[4,2,16,1536]{3,2,1,0:T(8,128)(2,1)S(1)}, bf16[4,2,16,1536]{3,2,1,0:T(8,128)(2,1)S(1)}, u32[]{:S(2)}, u32[]{:S(2)}) collective-permute-start(bf16[4,2,16,1536]{3,2,1,0:T(8,128)(2,1)S(1)} %get-tuple-element.61.refs_1_), channel_id=1, source_target_pairs={{2,0},{0,2},{6,4},{4,6},{10,8},{8,10},{14,12},{12,14},{3,1},{1,3},... | collective-permute-start | bytes 1179656 | tf_op jit(solution)/shard_map/ppermute | solution.py:436
  75.9 19.1 %collective-permute-start.18 = (bf16[48,768]{1,0:T(8,128)(2,1)S(1)}, bf16[48,768]{1,0:T(8,128)(2,1)S(1)}, u32[]{:S(2)}, u32[]{:S(2)}) collective-permute-start(bf16[48,768]{1,0:T(8,128)(2,1)S(1)} %get-tuple-element.69), channel_id=1, source_target_pairs={{12,0},{14,2},{0,4},{2,6},{4,8},{6,10},{8,12},{10,14},{13,1},{15,3... | collective-permute-start | bytes 221192 | tf_op jit(solution)/shard_map/ppermute | solution.py:436
  76.0 19.6 %collective-permute-start.19 = (bf16[48,768]{1,0:T(8,128)(2,1)S(1)}, bf16[48,768]{1,0:T(8,128)(2,1)S(1)}, u32[]{:S(2)}, u32[]{:S(2)}) collective-permute-start(bf16[48,768]{1,0:T(8,128)(2,1)S(1)} %get-tuple-element.70), channel_id=1, source_target_pairs={{8,0},{10,2},{12,4},{14,6},{0,8},{2,10},{4,12},{6,14},{9,1},{11,3}... | collective-permute-start | bytes 221192 | tf_op jit(solution)/shard_map/ppermute | solution.py:436
  76.7 18.9 %collective-permute-start.20 = (bf16[48,768]{1,0:T(8,128)(2,1)S(1)}, bf16[48,768]{1,0:T(8,128)(2,1)S(1)}, u32[]{:S(2)}, u32[]{:S(2)}) collective-permute-start(bf16[48,768]{1,0:T(8,128)(2,1)S(1)} %get-tuple-element.71), channel_id=1, source_target_pairs={{4,0},{6,2},{8,4},{10,6},{12,8},{14,10},{0,12},{2,14},{5,1},{7,3},... | collective-permute-start | bytes 221192 | tf_op jit(solution)/shard_map/ppermute | solution.py:436
  91.1 6.3 %collective-permute-start.24 = (bf16[48,768]{1,0:T(8,128)(2,1)S(1)}, bf16[48,768]{1,0:T(8,128)(2,1)S(1)}, u32[]{:S(2)}, u32[]{:S(2)}) collective-permute-start(bf16[48,768]{1,0:T(8,128)(2,1)S(1)} %get-tuple-element.74), channel_id=1, source_target_pairs={{12,0},{14,2},{0,4},{2,6},{4,8},{6,10},{8,12},{10,14},{13,1},{15,3... | collective-permute-start | bytes 221192 | tf_op jit(solution)/shard_map/ppermute | solution.py:436
  92.4 7.2 %collective-permute-start.25 = (bf16[48,768]{1,0:T(8,128)(2,1)S(1)}, bf16[48,768]{1,0:T(8,128)(2,1)S(1)}, u32[]{:S(2)}, u32[]{:S(2)}) collective-permute-start(bf16[48,768]{1,0:T(8,128)(2,1)S(1)} %get-tuple-element.75), channel_id=1, source_target_pairs={{8,0},{10,2},{12,4},{14,6},{0,8},{2,10},{4,12},{6,14},{9,1},{11,3}... | collective-permute-start | bytes 221192 | tf_op jit(solution)/shard_map/ppermute | solution.py:436
  100.6 7.6 %collective-permute-start.27 = (bf16[96,768]{1,0:T(8,128)(2,1)S(1)}, bf16[96,768]{1,0:T(8,128)(2,1)S(1)}, u32[]{:S(2)}, u32[]{:S(2)}) collective-permute-start(bf16[96,768]{1,0:T(8,128)(2,1)S(1)} %pad_maximum_fusion.refs_0_), channel_id=1, source_target_pairs={{4,0},{6,2},{8,4},{10,6},{12,8},{14,10},{0,12},{2,14},{5,1},{7,3},... | collective-permute-start | bytes 442376 | tf_op jit(solution)/shard_map/ppermute | solution.py:436
  102.9 11.5 %collective-permute-start.28 = (bf16[96,768]{1,0:T(8,128)(2,1)S(1)}, bf16[96,768]{1,0:T(8,128)(2,1)S(1)}, u32[]{:S(2)}, u32[]{:S(2)}) collective-permute-start(bf16[96,768]{1,0:T(8,128)(2,1)S(1)} %pad_maximum_fusion.refs_0_), channel_id=1, source_target_pairs={{8,0},{10,2},{12,4},{14,6},{0,8},{2,10},{4,12},{6,14},{9,1},{11,3}... | collective-permute-start | bytes 442376 | tf_op jit(solution)/shard_map/ppermute | solution.py:436
  106.5 9.3 %collective-permute-start.29 = (bf16[96,768]{1,0:T(8,128)(2,1)S(1)}, bf16[96,768]{1,0:T(8,128)(2,1)S(1)}, u32[]{:S(2)}, u32[]{:S(2)}) collective-permute-start(bf16[96,768]{1,0:T(8,128)(2,1)S(1)} %pad_maximum_fusion.refs_0_), channel_id=1, source_target_pairs={{12,0},{14,2},{0,4},{2,6},{4,8},{6,10},{8,12},{10,14},{13,1},{15,3... | collective-permute-start | bytes 442376 | tf_op jit(solution)/shard_map/ppermute | solution.py:436
  106.6 14.6 %collective-permute-start.30 = (bf16[96,768]{1,0:T(8,128)(2,1)S(1)}, bf16[96,768]{1,0:T(8,128)(2,1)S(1)}, u32[]{:S(2)}, u32[]{:S(2)}) collective-permute-start(bf16[96,768]{1,0:T(8,128)(2,1)S(1)} %pad_maximum_fusion.refs_0_), channel_id=1, source_target_pairs={{2,0},{0,2},{6,4},{4,6},{10,8},{8,10},{14,12},{12,14},{3,1},{1,3},... | collective-permute-start | bytes 442376 | tf_op jit(solution)/shard_map/ppermute | solution.py:436
  108.2 12.9 %collective-permute-start.31 = (bf16[96,768]{1,0:T(8,128)(2,1)S(1)}, bf16[96,768]{1,0:T(8,128)(2,1)S(1)}, u32[]{:S(2)}, u32[]{:S(2)}) collective-permute-start(bf16[96,768]{1,0:T(8,128)(2,1)S(1)} %collective-permute-done.27.refs_1_), channel_id=1, source_target_pairs={{2,0},{0,2},{6,4},{4,6},{10,8},{8,10},{14,12},{12,14},{3,1},{1,3},... | collective-permute-start | bytes 442376 | tf_op jit(solution)/shard_map/ppermute | solution.py:436
  114.4 6.7 %collective-permute-start.32 = (bf16[96,768]{1,0:T(8,128)(2,1)S(1)}, bf16[96,768]{1,0:T(8,128)(2,1)S(1)}, u32[]{:S(2)}, u32[]{:S(2)}) collective-permute-start(bf16[96,768]{1,0:T(8,128)(2,1)S(1)} %collective-permute-done.28.refs_2_), channel_id=1, source_target_pairs={{2,0},{0,2},{6,4},{4,6},{10,8},{8,10},{14,12},{12,14},{3,1},{1,3},... | collective-permute-start | bytes 442376 | tf_op jit(solution)/shard_map/ppermute | solution.py:436
  (9 other events, 126.5 us)

commit v3 on v2

--- a/solution.py
+++ b/solution.py
@@ -255,11 +255,12 @@
 
 def fill_left(left_ref, chunks):
     slots, _, _, depth = chunks[0].shape
+    sizes = [ref.shape[2] for ref in chunks]
     for n, ref in enumerate(chunks):
         for slot in range(slots):
-            at = slot * sum(CHUNKS) + sum(CHUNKS[:n])
+            at = slot * sum(sizes) + sum(sizes[:n])
             for part in range(2):
-                left_ref[at : at + CHUNKS[n], part * depth : (part + 1) * depth] = ref[slot, part]
+                left_ref[at : at + sizes[n], part * depth : (part + 1) * depth] = ref[slot, part]
 
 
 def multiply(left_ref, right_ref, total_ref, place_ref, outs):
@@ -274,14 +275,14 @@
         outs[d][...] = total_ref[lax.rem(place_ref[0] + d, segments)].astype(outs[d].dtype)
 
 
-def own_kernel(segments, place_ref, *refs):
+def early_kernel(segments, count, place_ref, *refs):
     chunks = len(CHUNKS)
-    own, shifted = refs[:chunks], refs[chunks : 2 * chunks]
-    outs = refs[2 * chunks : 2 * chunks + segments]
-    right_ref, left_ref, total_ref = refs[2 * chunks + segments :]
-    slots, _, _, depth = own[0].shape
-    block = left_ref.shape[0]
-    fill_left(left_ref, own)
+    left, shifted = refs[:count], refs[count : count + chunks]
+    outs = refs[count + chunks : count + chunks + segments]
+    right_ref, left_ref, total_ref = refs[count + chunks + segments :]
+    slots, _, _, depth = left[0].shape
+    block = right_ref.shape[1] // 2
+    fill_left(left_ref, left)
     for p in range(right_ref.shape[0]):
         for n, ref in enumerate(shifted):
             for slot in range(slots):
@@ -295,39 +296,61 @@
     multiply(left_ref, right_ref, total_ref, place_ref, outs)
 
 
-def other_kernel(segments, place_ref, *refs):
-    chunks = len(CHUNKS)
-    other, right_ref = refs[:chunks], refs[chunks]
-    outs = refs[chunks + 1 : chunks + 1 + segments]
-    left_ref, total_ref = refs[chunks + 1 + segments :]
-    fill_left(left_ref, other)
+def late_kernel(segments, count, place_ref, *refs):
+    left, right_ref = refs[:count], refs[count]
+    outs = refs[count + 1 : count + 1 + segments]
+    left_ref, total_ref = refs[count + 1 + segments :]
+    fill_left(left_ref, left)
     multiply(left_ref, right_ref, total_ref, place_ref, outs)
 
 
 def elementals(place, left, shifted, right, segments):
     _, _, _, depth = left[0].shape
     block = segments * sum(CHUNKS)
-    own = right is None
-    momenta = shifted[0].shape[0] if own else right.shape[0]
-    rows, columns = block // segments, momenta * 2 * block
+    rows = sum(ref.shape[2] for ref in left)
+    early = right is None
+    momenta = shifted[0].shape[0] if early else right.shape[0]
+    columns = momenta * 2 * block
     shapes = [pltpu.VMEM((rows, columns), jnp.float32 if d == 0 else jnp.bfloat16) for d in range(segments)]
-    if own:
+    if early:
         shapes.append(pltpu.VMEM((momenta, 2 * block, 2 * depth), jnp.bfloat16))
-    operands = [*left, *shifted] if own else [*left, right]
-    return pl.pallas_call(
-        functools.partial(own_kernel if own else other_kernel, segments),
+    operands = [*left, *shifted] if early else [*left, right]
+    return pl.pallas_call(
+        functools.partial(early_kernel if early else late_kernel, segments, len(left)),
         out_shape=shapes,
         in_specs=[SMEM] + [VMEM] * len(operands),
         out_specs=[VMEM] * len(shapes),
         scratch_shapes=[
-            pltpu.VMEM((block, 2 * depth), jnp.bfloat16),
+            pltpu.VMEM((segments * rows, 2 * depth), jnp.bfloat16),
             pltpu.VMEM((segments, rows, columns), jnp.float32),
         ],
         cost_estimate=pl.CostEstimate(
-            flops=2 * block * columns * 2 * depth, bytes_accessed=8 * block * depth, transcendentals=0),
-        compiler_params=GRANT,
-        name="elementals_own" if own else "elementals_other",
+            flops=2 * segments * rows * columns * 2 * depth, bytes_accessed=8 * block * depth, transcendentals=0),
+        compiler_params=GRANT,
+        name="elementals_early" if early else "elementals_late",
     )(place, *operands)
+
+
+def add_kernel(count, *refs):
+    out_ref, at = refs[-1], 0
+    for group in (refs[:count], refs[count:-1]):
+        total = group[0][...]
+        for ref in group[1:]:
+            total = total + ref[...].astype(jnp.float32)
+        out_ref[at : at + total.shape[0]] = total.astype(jnp.bfloat16)
+        at += total.shape[0]
+
+
+def add_parts(early, late):
+    rows = early[0].shape[0] + late[0].shape[0]
+    return pl.pallas_call(
+        functools.partial(add_kernel, len(early)),
+        out_shape=pltpu.VMEM((rows, early[0].shape[1]), jnp.bfloat16),
+        in_specs=[VMEM] * (len(early) + len(late)),
+        out_specs=VMEM,
+        compiler_params=GRANT,
+        name="add_parts",
+    )(*early, *late)
 
 
 def fill_right(right_ref, pieces, across, place_ref, owner_ref):
@@ -359,18 +382,25 @@
                 right_ref[p, pl.ds(low, rows), 2 * LANES :] = re
 
 
+def pair_of(tau_ref, n):
+    left = [jnp.concatenate([tau_ref[n + k, 0], tau_ref[n + k, 1]], axis=1) for k in range(2)]
+    return jnp.concatenate(left, axis=0)
+
+
 def first_kernel(sites, place_ref, owner_ref, tau_ref, *refs):
     pieces, (out_ref, right_ref) = refs[:sites], refs[sites:]
     fill_right(right_ref, pieces, 0, place_ref, owner_ref)
 
     def step(n, carry):
-        left = jnp.concatenate([tau_ref[n, 0], tau_ref[n, 1]], axis=1)
+        left = pair_of(tau_ref, 2 * n)
         for p in range(right_ref.shape[0]):
-            product = jnp.dot(left, right_ref[p], preferred_element_type=jnp.float32)
-            out_ref[n, p] = product.astype(jnp.bfloat16)
+            product = jnp.dot(left, right_ref[p], preferred_element_type=jnp.float32).astype(jnp.bfloat16)
+            for k in range(2):
+                out_ref[2 * n + k, p] = product[k * rows : (k + 1) * rows]
         return carry
 
-    lax.fori_loop(0, tau_ref.shape[0], step, 0)
+    rows = tau_ref.shape[2]
+    lax.fori_loop(0, tau_ref.shape[0] // 2, step, 0)
 
 
 def second_kernel(sites, place_ref, owner_ref, tau_ref, first_ref, *refs):
@@ -381,16 +411,19 @@
         fill_right(right_ref, pieces, 1, place_ref, owner_ref)
 
     leads = owner_ref[place_ref[1]] == 0
-    left = jnp.concatenate([tau_ref[0, 0], tau_ref[0, 1]], axis=1)
+    left = pair_of(tau_ref, 0)
+    rows = tau_ref.shape[2]
     for p in range(right_ref.shape[0]):
-        product = jnp.dot(left, right_ref[p], preferred_element_type=jnp.float32).astype(jnp.bfloat16)
-        for c in range(2):
-            at = 2 * c * LANES
-            mine, theirs = first_ref[0, p, :, at : at + LANES], product[:, at : at + LANES]
-            middle = first_ref[0, p, :, at + LANES : at + 2 * LANES] + product[:, at + LANES : at + 2 * LANES]
-            out_ref[0, p, c, :, :LANES] = jnp.where(leads, mine, theirs)
-            out_ref[0, p, c, :, LANES : 2 * LANES] = middle
-            out_ref[0, p, c, :, 2 * LANES :] = jnp.where(leads, theirs, mine)
+        both = jnp.dot(left, right_ref[p], preferred_element_type=jnp.float32).astype(jnp.bfloat16)
+        for k in range(2):
+            product = both[k * rows : (k + 1) * rows]
+            for c in range(2):
+                at = 2 * c * LANES
+                mine, theirs = first_ref[k, p, :, at : at + LANES], product[:, at : at + LANES]
+                middle = first_ref[k, p, :, at + LANES : at + 2 * LANES] + product[:, at + LANES : at + 2 * LANES]
+                out_ref[k, p, c, :, :LANES] = jnp.where(leads, mine, theirs)
+                out_ref[k, p, c, :, LANES : 2 * LANES] = middle
+                out_ref[k, p, c, :, 2 * LANES :] = jnp.where(leads, theirs, mine)
 
 
 def project_first(tau, place, owner, pieces, momenta):
@@ -413,11 +446,11 @@
     outer, _, rows, nvec = tau.shape
     return pl.pallas_call(
         functools.partial(second_kernel, len(pieces)),
-        grid=(outer,),
+        grid=(outer // 2,),
         out_shape=jax.ShapeDtypeStruct((outer, momenta, 2, rows, nvec), jnp.bfloat16),
-        in_specs=[SMEM, SMEM, pl.BlockSpec((1, 2, rows, nvec), lambda i: (i, 0, 0, 0)),
-                  pl.BlockSpec((1, *first.shape[1:]), lambda i: (i, 0, 0, 0))] + [VMEM] * len(pieces),
-        out_specs=pl.BlockSpec((1, momenta, 2, rows, nvec), lambda i: (i, 0, 0, 0, 0)),
+        in_specs=[SMEM, SMEM, pl.BlockSpec((2, 2, rows, nvec), lambda i: (i, 0, 0, 0)),
+                  pl.BlockSpec((2, *first.shape[1:]), lambda i: (i, 0, 0, 0))] + [VMEM] * len(pieces),
+        out_specs=pl.BlockSpec((2, momenta, 2, rows, nvec), lambda i: (i, 0, 0, 0, 0)),
         scratch_shapes=[pltpu.VMEM((momenta, 2 * nvec, 4 * LANES), jnp.bfloat16)],
         cost_estimate=pl.CostEstimate(
             flops=2 * outer * rows * 2 * nvec * nvec * momenta, bytes_accessed=outer * rows * nvec * 12,
@@ -477,13 +510,12 @@
             last = s
     filtered, shifted, other = ([group_of[n] for n in range(len(CHUNKS))] for group_of in (filtered, shifted, other))
 
-    *parts, right = elementals(place, filtered, shifted, None, sites)
+    *parts, right = elementals(place, filtered + other[:-1], shifted, None, sites)
     sent = [from_place(parts[d], -d, 0) for d in range(1, sites)]
-    own_sum = functools.reduce(lambda total, part: total + part.astype(jnp.float32), sent, parts[0])
-    parts = elementals(place, other, None, right, sites)
+    early = [parts[0], *sent]
+    parts = elementals(place, other[-1:], None, right, sites)
     sent = [from_place(parts[d], -d, 0) for d in range(1, sites)]
-    other_sum = functools.reduce(lambda total, part: total + part.astype(jnp.float32), sent, parts[0])
-    mine = jnp.concatenate([own_sum, other_sum], axis=0).astype(jnp.bfloat16)
+    mine = add_parts(early, [parts[0], *sent])
 
     across = [from_place(mine, 0, 1)]
     pieces = [mine] + [from_place(mine, up, 0) for up in range(1, sites)]
@@ -639,7 +671,8 @@
     block, layers, plane = eigvecs.shape[3:]
     sites, groups = lax.axis_size("site"), lax.axis_size("vec")
     fits = layers == 1 and plane == LX * LY == 4 * LANES and sites == 4 and groups == 2
-    fits = fits and block == sites * sum(CHUNKS) and LANES < block < 2 * LANES and (2 * block) % (32 * sites) == 0 and block % (2 * block // sites) == 0
+    fits = fits and block == sites * sum(CHUNKS) and LANES < block < 2 * LANES
+    fits = fits and peramb.shape[1] * peramb.shape[2] % 2 == 0 and (2 * block) % (32 * sites) == 0 and block % (2 * block // sites) == 0
     device = per_device if fits else general_device
     return device(eigvecs, links, peramb, block_owner, momenta)
 

time: 128 us -> 116 us (0.906)
  starting transfers between devices: 60 us -> 53.5 us
  waiting for transfers between devices: 25.7 us -> 23 us
  Pallas kernels: 37.9 us -> 36.3 us
    ppermute x34, starting transfers between devices: 60 us -> 53.5 us  [from_place(): return lax.ppermute(block, ('site', 'vec'), route)]
    ppermute x34, waiting for transfers between devices: 25.7 us -> 23 us  [from_place(): return lax.ppermute(block, ('site', 'vec'), route)]
    pallas_call x1, Pallas kernels: 6.67 us -> 5.28 us  [project_second(): pl.pallas_call(functools.partial(second_kernel, len(pieces)), grid=(outer...]
    pallas_call x2 -> x3, Pallas kernels: 4.47 us -> 5.05 us  [the longest x2 4.97 us: elementals(): pl.pallas_call(functools.partial(early_kernel if early else late_kernel,...]
  transfers between devices with their start and end apart: 34 -> 34, of which waited for: 13 -> 11; matrix products, arithmetic and copies ran while one was open for 1% -> 0% of each run, Pallas kernels for 24% -> 26%
where the time goes in v3:
time: 116 us
  starting transfers between devices  53.5 us (46%)
  Pallas kernels  36.3 us (31%)
  waiting for transfers between devices  23 us (20%)
  local copies, waits for them, and re-layouts  2.76 us (2%)
    ppermute x34, starting transfers between devices, from_place(): return lax.ppermute(block, ('site', 'vec'), route)  53.5 us
    ppermute x34, waiting for transfers between devices, from_place(): return lax.ppermute(block, ('site', 'vec'), route)  23 us
    pallas_call x3, Pallas kernels, filter_chunk(): pl.pallas_call(functools.partial(filter_kernel, sites, chunk), out_shape=...  17.4 us
    pallas_call x1, Pallas kernels, project_second(): pl.pallas_call(functools.partial(second_kernel, len(pieces)), grid=(outer...  5.28 us
    pallas_call x2, Pallas kernels, elementals(): pl.pallas_call(functools.partial(early_kernel if early else late_kernel,...  4.97 us
    pallas_call x1, Pallas kernels, project_first(): pl.pallas_call(functools.partial(first_kernel, len(pieces)), out_shape=pl...  3.89 us
    pallas_call x3, Pallas kernels, finish(): pl.pallas_call(functools.partial(finish_kernel, sites, chunk), out_shape=...  2.67 us
    unnamed x14, local copies, waits for them, and re-layouts  2.58 us
  transfers between devices with their start and end apart: 34, of which 11 were waited for; matrix products, arithmetic and copies ran while one was open for 0% of the time, Pallas kernels for 26%

profile of v3, /device:TPU:0, one launch (start us, length us, event | category | flops | bytes accessed | tf_op | source)
XLA Modules:
  0.0 116.3 jit_solution(2871348087303153989)
XLA Ops:
  0.1 1.7 %copy-done = f32[1,2,3,192,1,512]{5,4,3,2,1,0:T(1,128)S(1)} copy-done((f32[1,2,3,192,1,512]{5,4,3,2,1,0:T(1,128)S(1)}, f32[1,2,3,192,1,512]{5,4,3,2,1,0:T(1,128)}, u32[]{:S(2)}) %copy-start) | copy-done | bytes 2359320
  3.2 3.1 %collective-permute-start = (bf16[600,128]{1,0:T(8,128)(2,1)S(1)}, bf16[600,128]{1,0:T(8,128)(2,1)S(1)}, u32[]{:S(2)}, u32[]{:S(2)}) collective-permute-start(bf16[600,128]{1,0:T(8,128)(2,1)S(1)} %get-tuple-element.41), channel_id=1, source_target_pairs={{12,0},{14,2},{0,4},{2,6},{4,8},{6,10},{8,12},{10,14},{13,1},{15,3... | collective-permute-start | bytes 460808 | tf_op jit(solution)/shard_map/ppermute | solution.py:469
  6.3 2.6 %collective-permute-start.1 = (bf16[600,128]{1,0:T(8,128)(2,1)S(1)}, bf16[600,128]{1,0:T(8,128)(2,1)S(1)}, u32[]{:S(2)}, u32[]{:S(2)}) collective-permute-start(bf16[600,128]{1,0:T(8,128)(2,1)S(1)} %get-tuple-element.42), channel_id=1, source_target_pairs={{8,0},{10,2},{12,4},{14,6},{0,8},{2,10},{4,12},{6,14},{9,1},{11,3}... | collective-permute-start | bytes 460808 | tf_op jit(solution)/shard_map/ppermute | solution.py:469
  8.9 1.3 %collective-permute-start.2 = (bf16[600,128]{1,0:T(8,128)(2,1)S(1)}, bf16[600,128]{1,0:T(8,128)(2,1)S(1)}, u32[]{:S(2)}, u32[]{:S(2)}) collective-permute-start(bf16[600,128]{1,0:T(8,128)(2,1)S(1)} %get-tuple-element.43), channel_id=1, source_target_pairs={{4,0},{6,2},{8,4},{10,6},{12,8},{14,10},{0,12},{2,14},{5,1},{7,3},... | collective-permute-start | bytes 460808 | tf_op jit(solution)/shard_map/ppermute | solution.py:469
  10.4 2.9 %collective-permute-done.refs_1_.refs_0_ = bf16[600,128]{1,0:T(8,128)(2,1)S(1)} collective-permute-done((bf16[600,128]{1,0:T(8,128)(2,1)S(1)}, bf16[600,128]{1,0:T(8,128)(2,1)S(1)}, u32[]{:S(2)}, u32[]{:S(2)}) %collective-permute-start) | collective-permute-done | bytes 153632 | tf_op jit(solution)/shard_map/ppermute | solution.py:469
  13.9 5.4 %collective-permute-start.6 = (bf16[384,128]{1,0:T(8,128)(2,1)S(1)}, bf16[384,128]{1,0:T(8,128)(2,1)S(1)}, u32[]{:S(2)}, u32[]{:S(2)}) collective-permute-start(bf16[384,128]{1,0:T(8,128)(2,1)S(1)} %get-tuple-element.48.refs_3_), channel_id=1, source_target_pairs={{12,0},{14,2},{0,4},{2,6},{4,8},{6,10},{8,12},{10,14},{13,1},{15,3... | collective-permute-start | bytes 294920 | tf_op jit(solution)/shard_map/ppermute | solution.py:469
  19.3 4.3 %collective-permute-start.7 = (bf16[384,128]{1,0:T(8,128)(2,1)S(1)}, bf16[384,128]{1,0:T(8,128)(2,1)S(1)}, u32[]{:S(2)}, u32[]{:S(2)}) collective-permute-start(bf16[384,128]{1,0:T(8,128)(2,1)S(1)} %get-tuple-element.49), channel_id=1, source_target_pairs={{8,0},{10,2},{12,4},{14,6},{0,8},{2,10},{4,12},{6,14},{9,1},{11,3}... | collective-permute-start | bytes 294920 | tf_op jit(solution)/shard_map/ppermute | solution.py:469
  23.8 2.9 %collective-permute-start.8 = (bf16[384,128]{1,0:T(8,128)(2,1)S(1)}, bf16[384,128]{1,0:T(8,128)(2,1)S(1)}, u32[]{:S(2)}, u32[]{:S(2)}) collective-permute-start(bf16[384,128]{1,0:T(8,128)(2,1)S(1)} %get-tuple-element.50), channel_id=1, source_target_pairs={{4,0},{6,2},{8,4},{10,6},{12,8},{14,10},{0,12},{2,14},{5,1},{7,3},... | collective-permute-start | bytes 294920 | tf_op jit(solution)/shard_map/ppermute | solution.py:469
  27.1 5.8 %shard_map.56 = (bf16[6,64,128]{2,1,0:T(8,128)(2,1)S(1)}, bf16[6,64,128]{2,1,0:T(8,128)(2,1)S(1)}, bf16[6,64,128]{2,1,0:T(8,128)(2,1)S(1)}, bf16[6,64,128]{2,1,0:T(8,128)(2,1)S(1)}) custom-call(s32[2]{0:T(128)S(1)} %pad_add_fusion.place_ref, f32[6,768,128]{2,1,0:T(8,128)S(1)} %bitcast.8, bf16[600,128]{1,0:T(8,128)(2,1)S(1)} %collective-permute-done.refs_1_.refs_0_, ...), custom_call_target="tpu_custom_call" | custom-call | flops 28311552 | bytes 786432 | tf_op jit(solution)/shard_map/pallas_call | solution.py:202
  34.3 1.3 %collective-permute-start.5 = (bf16[6,64,128]{2,1,0:T(8,128)(2,1)S(1)}, bf16[6,64,128]{2,1,0:T(8,128)(2,1)S(1)}, u32[]{:S(2)}, u32[]{:S(2)}) collective-permute-start(bf16[6,64,128]{2,1,0:T(8,128)(2,1)S(1)} %get-tuple-element.47), channel_id=1, source_target_pairs={{12,0},{14,2},{0,4},{2,6},{4,8},{6,10},{8,12},{10,14},{13,1},{15,3... | collective-permute-start | bytes 294920 | tf_op jit(solution)/shard_map/ppermute | solution.py:469
  35.6 1.9 %collective-permute-start.12 = (bf16[384,128]{1,0:T(8,128)(2,1)S(1)}, bf16[384,128]{1,0:T(8,128)(2,1)S(1)}, u32[]{:S(2)}, u32[]{:S(2)}) collective-permute-start(bf16[384,128]{1,0:T(8,128)(2,1)S(1)} %get-tuple-element.56), channel_id=1, source_target_pairs={{12,0},{14,2},{0,4},{2,6},{4,8},{6,10},{8,12},{10,14},{13,1},{15,3... | collective-permute-start | bytes 294920 | tf_op jit(solution)/shard_map/ppermute | solution.py:469
  39.0 5.8 %shard_map.58 = (bf16[6,64,128]{2,1,0:T(8,128)(2,1)S(1)}, bf16[6,64,128]{2,1,0:T(8,128)(2,1)S(1)}, bf16[6,64,128]{2,1,0:T(8,128)(2,1)S(1)}, bf16[6,64,128]{2,1,0:T(8,128)(2,1)S(1)}) custom-call(s32[2]{0:T(128)S(1)} %pad_add_fusion.place_ref, f32[6,768,128]{2,1,0:T(8,128)S(1)} %bitcast.10, bf16[384,128]{1,0:T(8,128)(2,1)S(1)} %collective-permute-done.6.refs_1_, ...), custom_call_target="tpu_custom_call" | custom-call | flops 28311552 | bytes 786432 | tf_op jit(solution)/shard_map/pallas_call | solution.py:202
  44.8 2.7 %collective-permute-start.14 = (bf16[384,128]{1,0:T(8,128)(2,1)S(1)}, bf16[384,128]{1,0:T(8,128)(2,1)S(1)}, u32[]{:S(2)}, u32[]{:S(2)}) collective-permute-start(bf16[384,128]{1,0:T(8,128)(2,1)S(1)} %get-tuple-element.58), channel_id=1, source_target_pairs={{4,0},{6,2},{8,4},{10,6},{12,8},{14,10},{0,12},{2,14},{5,1},{7,3},... | collective-permute-start | bytes 294920 | tf_op jit(solution)/shard_map/ppermute | solution.py:469
  48.6 3.2 %collective-permute-start.9 = (bf16[6,64,128]{2,1,0:T(8,128)(2,1)S(1)}, bf16[6,64,128]{2,1,0:T(8,128)(2,1)S(1)}, u32[]{:S(2)}, u32[]{:S(2)}) collective-permute-start(bf16[6,64,128]{2,1,0:T(8,128)(2,1)S(1)} %get-tuple-element.53), channel_id=1, source_target_pairs={{4,0},{6,2},{8,4},{10,6},{12,8},{14,10},{0,12},{2,14},{5,1},{7,3},... | collective-permute-start | bytes 294920 | tf_op jit(solution)/shard_map/ppermute | solution.py:469
  53.2 1.5 %collective-permute-start.18 = (bf16[4,2,16,1536]{3,2,1,0:T(8,128)(2,1)S(1)}, bf16[4,2,16,1536]{3,2,1,0:T(8,128)(2,1)S(1)}, u32[]{:S(2)}, u32[]{:S(2)}) collective-permute-start(bf16[4,2,16,1536]{3,2,1,0:T(8,128)(2,1)S(1)} %get-tuple-element.52.refs_0_), channel_id=1, source_target_pairs={{2,0},{0,2},{6,4},{4,6},{10,8},{8,10},{14,12},{12,14},{3,1},{1,3},... | collective-permute-start | bytes 1179656 | tf_op jit(solution)/shard_map/ppermute | solution.py:469
  54.7 5.8 %shard_map.61 = (bf16[6,64,128]{2,1,0:T(8,128)(2,1)S(1)}, bf16[6,64,128]{2,1,0:T(8,128)(2,1)S(1)}, bf16[6,64,128]{2,1,0:T(8,128)(2,1)S(1)}, bf16[6,64,128]{2,1,0:T(8,128)(2,1)S(1)}) custom-call(s32[2]{0:T(128)S(1)} %pad_add_fusion.place_ref, f32[6,768,128]{2,1,0:T(8,128)S(1)} %bitcast.12, bf16[384,128]{1,0:T(8,128)(2,1)S(1)} %collective-permute-done.12.refs_1_, ...), custom_call_target="tpu_custom_call" | custom-call | flops 28311552 | bytes 786432 | tf_op jit(solution)/shard_map/pallas_call | solution.py:202
  62.0 3.7 %collective-permute-start.15 = (bf16[6,64,128]{2,1,0:T(8,128)(2,1)S(1)}, bf16[6,64,128]{2,1,0:T(8,128)(2,1)S(1)}, u32[]{:S(2)}, u32[]{:S(2)}) collective-permute-start(bf16[6,64,128]{2,1,0:T(8,128)(2,1)S(1)} %get-tuple-element.62), channel_id=1, source_target_pairs={{4,0},{6,2},{8,4},{10,6},{12,8},{14,10},{0,12},{2,14},{5,1},{7,3},... | collective-permute-start | bytes 294920 | tf_op jit(solution)/shard_map/ppermute | solution.py:469
  66.6 2.5 %collective-permute-done.15.refs_1_ = bf16[6,64,128]{2,1,0:T(8,128)(2,1)S(1)} collective-permute-done((bf16[6,64,128]{2,1,0:T(8,128)(2,1)S(1)}, bf16[6,64,128]{2,1,0:T(8,128)(2,1)S(1)}, u32[]{:S(2)}, u32[]{:S(2)}) %collective-permute-start.15) | collective-permute-done | bytes 98336 | tf_op jit(solution)/shard_map/ppermute | solution.py:469
  69.1 2.8 %collective-permute-done.16.refs_2_ = bf16[6,64,128]{2,1,0:T(8,128)(2,1)S(1)} collective-permute-done((bf16[6,64,128]{2,1,0:T(8,128)(2,1)S(1)}, bf16[6,64,128]{2,1,0:T(8,128)(2,1)S(1)}, u32[]{:S(2)}, u32[]{:S(2)}) %collective-permute-start.16) | collective-permute-done | bytes 98336 | tf_op jit(solution)/shard_map/ppermute | solution.py:469
  74.7 2.9 %elementals_early.1 = (f32[80,768]{1,0:T(8,128)S(1)}, bf16[80,768]{1,0:T(8,128)(2,1)S(1)}, bf16[80,768]{1,0:T(8,128)(2,1)S(1)}, bf16[80,768]{1,0:T(8,128)(2,1)S(1)}, bf16[2,384,3072]{2,1,0:T(8,128)(2,1)S(1)}) custom-call(s32[2]{0:T(128)S(1)} %pad_add_fusion.place_ref, bf16[4,2,16,1536]{3,2,1,0:T(8,128)(2,1)S(1)} %get-tuple-element.52.refs_0_, ...), custom_call_target="tpu_custom_call" | custom-call | flops 1509949440 | bytes 2359296 | tf_op jit(solution)/shard_map/elementals_early/pallas_call | solution.py:318
  77.9 1.4 %collective-permute-start.21 = (bf16[80,768]{1,0:T(8,128)(2,1)S(1)}, bf16[80,768]{1,0:T(8,128)(2,1)S(1)}, u32[]{:S(2)}, u32[]{:S(2)}) collective-permute-start(bf16[80,768]{1,0:T(8,128)(2,1)S(1)} %get-tuple-element.70), channel_id=1, source_target_pairs={{8,0},{10,2},{12,4},{14,6},{0,8},{2,10},{4,12},{6,14},{9,1},{11,3}... | collective-permute-start | bytes 368648 | tf_op jit(solution)/shard_map/ppermute | solution.py:469
  79.3 2.5 %collective-permute-start.22 = (bf16[80,768]{1,0:T(8,128)(2,1)S(1)}, bf16[80,768]{1,0:T(8,128)(2,1)S(1)}, u32[]{:S(2)}, u32[]{:S(2)}) collective-permute-start(bf16[80,768]{1,0:T(8,128)(2,1)S(1)} %get-tuple-element.71), channel_id=1, source_target_pairs={{4,0},{6,2},{8,4},{10,6},{12,8},{14,10},{0,12},{2,14},{5,1},{7,3},... | collective-permute-start | bytes 368648 | tf_op jit(solution)/shard_map/ppermute | solution.py:469
  81.8 2.1 %elementals_late.1 = (f32[16,768]{1,0:T(8,128)S(1)}, bf16[16,768]{1,0:T(8,128)(2,1)S(1)}, bf16[16,768]{1,0:T(8,128)(2,1)S(1)}, bf16[16,768]{1,0:T(8,128)(2,1)S(1)}) custom-call(s32[2]{0:T(128)S(1)} %pad_add_fusion.place_ref, bf16[4,2,16,1536]{3,2,1,0:T(8,128)(2,1)S(1)} %collective-permute-done.23.refs_0_, bf16[2,384,3072]{2,1,0:T(8,128)(2,1)S(1)} %get-tuple-element.72.refs_1_), custom_call_target="tpu_custom_call" | custom-call | flops 301989888 | bytes 2359296 | tf_op jit(solution)/shard_map/elementals_late/pallas_call | solution.py:318
  84.2 1.5 %collective-permute-start.25 = (bf16[16,768]{1,0:T(8,128)(2,1)S(1)}, bf16[16,768]{1,0:T(8,128)(2,1)S(1)}, u32[]{:S(2)}, u32[]{:S(2)}) collective-permute-start(bf16[16,768]{1,0:T(8,128)(2,1)S(1)} %get-tuple-element.75), channel_id=1, source_target_pairs={{8,0},{10,2},{12,4},{14,6},{0,8},{2,10},{4,12},{6,14},{9,1},{11,3}... | collective-permute-start | bytes 73736 | tf_op jit(solution)/shard_map/ppermute | solution.py:469
  85.7 3.9 %collective-permute-done.24.refs_5_ = bf16[16,768]{1,0:T(8,128)(2,1)S(1)} collective-permute-done((bf16[16,768]{1,0:T(8,128)(2,1)S(1)}, bf16[16,768]{1,0:T(8,128)(2,1)S(1)}, u32[]{:S(2)}, u32[]{:S(2)}) %collective-permute-start.24) | collective-permute-done | bytes 24608 | tf_op jit(solution)/shard_map/ppermute | solution.py:469
  89.9 3.5 %collective-permute-done.26.refs_7_ = bf16[16,768]{1,0:T(8,128)(2,1)S(1)} collective-permute-done((bf16[16,768]{1,0:T(8,128)(2,1)S(1)}, bf16[16,768]{1,0:T(8,128)(2,1)S(1)}, u32[]{:S(2)}, u32[]{:S(2)}) %collective-permute-start.26) | collective-permute-done | bytes 24608 | tf_op jit(solution)/shard_map/ppermute | solution.py:469
  93.5 2.5 %collective-permute-start.27 = (bf16[96,768]{1,0:T(8,128)(2,1)S(1)}, bf16[96,768]{1,0:T(8,128)(2,1)S(1)}, u32[]{:S(2)}, u32[]{:S(2)}) collective-permute-start(bf16[96,768]{1,0:T(8,128)(2,1)S(1)} %add_parts.1.refs_0_), channel_id=1, source_target_pairs={{4,0},{6,2},{8,4},{10,6},{12,8},{14,10},{0,12},{2,14},{5,1},{7,3},... | collective-permute-start | bytes 442376 | tf_op jit(solution)/shard_map/ppermute | solution.py:469
  96.6 1.5 %collective-permute-start.30 = (bf16[96,768]{1,0:T(8,128)(2,1)S(1)}, bf16[96,768]{1,0:T(8,128)(2,1)S(1)}, u32[]{:S(2)}, u32[]{:S(2)}) collective-permute-start(bf16[96,768]{1,0:T(8,128)(2,1)S(1)} %add_parts.1.refs_0_), channel_id=1, source_target_pairs={{2,0},{0,2},{6,4},{4,6},{10,8},{8,10},{14,12},{12,14},{3,1},{1,3},... | collective-permute-start | bytes 442376 | tf_op jit(solution)/shard_map/ppermute | solution.py:469
  98.9 1.3 %collective-permute-start.31 = (bf16[96,768]{1,0:T(8,128)(2,1)S(1)}, bf16[96,768]{1,0:T(8,128)(2,1)S(1)}, u32[]{:S(2)}, u32[]{:S(2)}) collective-permute-start(bf16[96,768]{1,0:T(8,128)(2,1)S(1)} %collective-permute-done.27.refs_1_), channel_id=1, source_target_pairs={{2,0},{0,2},{6,4},{4,6},{10,8},{8,10},{14,12},{12,14},{3,1},{1,3},... | collective-permute-start | bytes 442376 | tf_op jit(solution)/shard_map/ppermute | solution.py:469
  100.2 4.0 %collective-permute-done.28.refs_2_ = bf16[96,768]{1,0:T(8,128)(2,1)S(1)} collective-permute-done((bf16[96,768]{1,0:T(8,128)(2,1)S(1)}, bf16[96,768]{1,0:T(8,128)(2,1)S(1)}, u32[]{:S(2)}, u32[]{:S(2)}) %collective-permute-start.28) | collective-permute-done | bytes 147488 | tf_op jit(solution)/shard_map/ppermute | solution.py:469
  106.3 3.9 %project_first.1.first_ref = bf16[8,2,192,512]{3,2,1,0:T(8,128)(2,1)S(1)} custom-call(s32[2]{0:T(128)S(1)} %pad_add_fusion.place_ref, s32[2]{0:T(128)S(1)} %copy-done.5, bf16[8,2,192,384]{3,2,1,0:T(8,128)(2,1)S(1)} %bitcast.15, bf16[96,768]{1,0:T(8,128)(2,1)S(1)} %add_parts.1.refs_0_, bf16[96,768]{1,0:T(8,128)(2,1)S(1)} %collective-permute-done.27.refs_1_, ...), custom_call_target="tpu_custom_call" | custom-call | flops 1811939328 | bytes 4718592 | tf_op jit(solution)/shard_map/project_first/pallas_call | solution.py:431
  111.0 5.3 %project_second.1 = bf16[8,2,2,192,384]{4,3,2,1,0:T(8,128)(2,1)} custom-call(s32[2]{0:T(128)S(1)} %pad_add_fusion.place_ref, s32[2]{0:T(128)S(1)} %copy-done.5, bf16[8,2,192,384]{3,2,1,0:T(8,128)(2,1)S(1)} %bitcast.16, bf16[8,2,192,512]{3,2,1,0:T(8,128)(2,1)S(1)} %project_first.1.first_ref, bf16[96,768]{1,0:T(8,128)(2,1)S(1)} %collective-permute-done.30.refs_0_, ...), custom_call_target="tpu_custom_call" | custom-call | flops 1811939328 | bytes 7077888 | tf_op jit(solution)/shard_map/project_second/pallas_call | solution.py:447
  (71 shorter events, 18.4 us)
Async XLA Ops:
  3.2 10.1 %collective-permute-start = (bf16[600,128]{1,0:T(8,128)(2,1)S(1)}, bf16[600,128]{1,0:T(8,128)(2,1)S(1)}, u32[]{:S(2)}, u32[]{:S(2)}) collective-permute-start(bf16[600,128]{1,0:T(8,128)(2,1)S(1)} %get-tuple-element.41), channel_id=1, source_target_pairs={{12,0},{14,2},{0,4},{2,6},{4,8},{6,10},{8,12},{10,14},{13,1},{15,3... | collective-permute-start | bytes 460808 | tf_op jit(solution)/shard_map/ppermute | solution.py:469
  6.3 20.4 %collective-permute-start.1 = (bf16[600,128]{1,0:T(8,128)(2,1)S(1)}, bf16[600,128]{1,0:T(8,128)(2,1)S(1)}, u32[]{:S(2)}, u32[]{:S(2)}) collective-permute-start(bf16[600,128]{1,0:T(8,128)(2,1)S(1)} %get-tuple-element.42), channel_id=1, source_target_pairs={{8,0},{10,2},{12,4},{14,6},{0,8},{2,10},{4,12},{6,14},{9,1},{11,3}... | collective-permute-start | bytes 460808 | tf_op jit(solution)/shard_map/ppermute | solution.py:469
  8.9 17.8 %collective-permute-start.2 = (bf16[600,128]{1,0:T(8,128)(2,1)S(1)}, bf16[600,128]{1,0:T(8,128)(2,1)S(1)}, u32[]{:S(2)}, u32[]{:S(2)}) collective-permute-start(bf16[600,128]{1,0:T(8,128)(2,1)S(1)} %get-tuple-element.43), channel_id=1, source_target_pairs={{4,0},{6,2},{8,4},{10,6},{12,8},{14,10},{0,12},{2,14},{5,1},{7,3},... | collective-permute-start | bytes 460808 | tf_op jit(solution)/shard_map/ppermute | solution.py:469
  13.9 20.4 %collective-permute-start.6 = (bf16[384,128]{1,0:T(8,128)(2,1)S(1)}, bf16[384,128]{1,0:T(8,128)(2,1)S(1)}, u32[]{:S(2)}, u32[]{:S(2)}) collective-permute-start(bf16[384,128]{1,0:T(8,128)(2,1)S(1)} %get-tuple-element.48.refs_3_), channel_id=1, source_target_pairs={{12,0},{14,2},{0,4},{2,6},{4,8},{6,10},{8,12},{10,14},{13,1},{15,3... | collective-permute-start | bytes 294920 | tf_op jit(solution)/shard_map/ppermute | solution.py:469
  19.3 16.3 %collective-permute-start.7 = (bf16[384,128]{1,0:T(8,128)(2,1)S(1)}, bf16[384,128]{1,0:T(8,128)(2,1)S(1)}, u32[]{:S(2)}, u32[]{:S(2)}) collective-permute-start(bf16[384,128]{1,0:T(8,128)(2,1)S(1)} %get-tuple-element.49), channel_id=1, source_target_pairs={{8,0},{10,2},{12,4},{14,6},{0,8},{2,10},{4,12},{6,14},{9,1},{11,3}... | collective-permute-start | bytes 294920 | tf_op jit(solution)/shard_map/ppermute | solution.py:469
  23.8 13.9 %collective-permute-start.8 = (bf16[384,128]{1,0:T(8,128)(2,1)S(1)}, bf16[384,128]{1,0:T(8,128)(2,1)S(1)}, u32[]{:S(2)}, u32[]{:S(2)}) collective-permute-start(bf16[384,128]{1,0:T(8,128)(2,1)S(1)} %get-tuple-element.50), channel_id=1, source_target_pairs={{4,0},{6,2},{8,4},{10,6},{12,8},{14,10},{0,12},{2,14},{5,1},{7,3},... | collective-permute-start | bytes 294920 | tf_op jit(solution)/shard_map/ppermute | solution.py:469
  32.9 11.9 %collective-permute-start.3 = (bf16[6,64,128]{2,1,0:T(8,128)(2,1)S(1)}, bf16[6,64,128]{2,1,0:T(8,128)(2,1)S(1)}, u32[]{:S(2)}, u32[]{:S(2)}) collective-permute-start(bf16[6,64,128]{2,1,0:T(8,128)(2,1)S(1)} %get-tuple-element.45), channel_id=1, source_target_pairs={{4,0},{6,2},{8,4},{10,6},{12,8},{14,10},{0,12},{2,14},{5,1},{7,3},... | collective-permute-start | bytes 294920 | tf_op jit(solution)/shard_map/ppermute | solution.py:469
  33.4 14.5 %collective-permute-start.4 = (bf16[6,64,128]{2,1,0:T(8,128)(2,1)S(1)}, bf16[6,64,128]{2,1,0:T(8,128)(2,1)S(1)}, u32[]{:S(2)}, u32[]{:S(2)}) collective-permute-start(bf16[6,64,128]{2,1,0:T(8,128)(2,1)S(1)} %get-tuple-element.46), channel_id=1, source_target_pairs={{8,0},{10,2},{12,4},{14,6},{0,8},{2,10},{4,12},{6,14},{9,1},{11,3}... | collective-permute-start | bytes 294920 | tf_op jit(solution)/shard_map/ppermute | solution.py:469
  34.3 13.6 %collective-permute-start.5 = (bf16[6,64,128]{2,1,0:T(8,128)(2,1)S(1)}, bf16[6,64,128]{2,1,0:T(8,128)(2,1)S(1)}, u32[]{:S(2)}, u32[]{:S(2)}) collective-permute-start(bf16[6,64,128]{2,1,0:T(8,128)(2,1)S(1)} %get-tuple-element.47), channel_id=1, source_target_pairs={{12,0},{14,2},{0,4},{2,6},{4,8},{6,10},{8,12},{10,14},{13,1},{15,3... | collective-permute-start | bytes 294920 | tf_op jit(solution)/shard_map/ppermute | solution.py:469
  35.6 13.0 %collective-permute-start.12 = (bf16[384,128]{1,0:T(8,128)(2,1)S(1)}, bf16[384,128]{1,0:T(8,128)(2,1)S(1)}, u32[]{:S(2)}, u32[]{:S(2)}) collective-permute-start(bf16[384,128]{1,0:T(8,128)(2,1)S(1)} %get-tuple-element.56), channel_id=1, source_target_pairs={{12,0},{14,2},{0,4},{2,6},{4,8},{6,10},{8,12},{10,14},{13,1},{15,3... | collective-permute-start | bytes 294920 | tf_op jit(solution)/shard_map/ppermute | solution.py:469
  37.7 15.4 %collective-permute-start.13 = (bf16[384,128]{1,0:T(8,128)(2,1)S(1)}, bf16[384,128]{1,0:T(8,128)(2,1)S(1)}, u32[]{:S(2)}, u32[]{:S(2)}) collective-permute-start(bf16[384,128]{1,0:T(8,128)(2,1)S(1)} %get-tuple-element.57), channel_id=1, source_target_pairs={{8,0},{10,2},{12,4},{14,6},{0,8},{2,10},{4,12},{6,14},{9,1},{11,3}... | collective-permute-start | bytes 294920 | tf_op jit(solution)/shard_map/ppermute | solution.py:469
  44.8 9.8 %collective-permute-start.14 = (bf16[384,128]{1,0:T(8,128)(2,1)S(1)}, bf16[384,128]{1,0:T(8,128)(2,1)S(1)}, u32[]{:S(2)}, u32[]{:S(2)}) collective-permute-start(bf16[384,128]{1,0:T(8,128)(2,1)S(1)} %get-tuple-element.58), channel_id=1, source_target_pairs={{4,0},{6,2},{8,4},{10,6},{12,8},{14,10},{0,12},{2,14},{5,1},{7,3},... | collective-permute-start | bytes 294920 | tf_op jit(solution)/shard_map/ppermute | solution.py:469
  48.0 12.5 %collective-permute-start.10 = (bf16[6,64,128]{2,1,0:T(8,128)(2,1)S(1)}, bf16[6,64,128]{2,1,0:T(8,128)(2,1)S(1)}, u32[]{:S(2)}, u32[]{:S(2)}) collective-permute-start(bf16[6,64,128]{2,1,0:T(8,128)(2,1)S(1)} %get-tuple-element.54), channel_id=1, source_target_pairs={{8,0},{10,2},{12,4},{14,6},{0,8},{2,10},{4,12},{6,14},{9,1},{11,3}... | collective-permute-start | bytes 294920 | tf_op jit(solution)/shard_map/ppermute | solution.py:469
  48.0 12.5 %collective-permute-start.11 = (bf16[6,64,128]{2,1,0:T(8,128)(2,1)S(1)}, bf16[6,64,128]{2,1,0:T(8,128)(2,1)S(1)}, u32[]{:S(2)}, u32[]{:S(2)}) collective-permute-start(bf16[6,64,128]{2,1,0:T(8,128)(2,1)S(1)} %get-tuple-element.55), channel_id=1, source_target_pairs={{12,0},{14,2},{0,4},{2,6},{4,8},{6,10},{8,12},{10,14},{13,1},{15,3... | collective-permute-start | bytes 294920 | tf_op jit(solution)/shard_map/ppermute | solution.py:469
  48.6 11.9 %collective-permute-start.9 = (bf16[6,64,128]{2,1,0:T(8,128)(2,1)S(1)}, bf16[6,64,128]{2,1,0:T(8,128)(2,1)S(1)}, u32[]{:S(2)}, u32[]{:S(2)}) collective-permute-start(bf16[6,64,128]{2,1,0:T(8,128)(2,1)S(1)} %get-tuple-element.53), channel_id=1, source_target_pairs={{4,0},{6,2},{8,4},{10,6},{12,8},{14,10},{0,12},{2,14},{5,1},{7,3},... | collective-permute-start | bytes 294920 | tf_op jit(solution)/shard_map/ppermute | solution.py:469
  53.2 21.5 %collective-permute-start.18 = (bf16[4,2,16,1536]{3,2,1,0:T(8,128)(2,1)S(1)}, bf16[4,2,16,1536]{3,2,1,0:T(8,128)(2,1)S(1)}, u32[]{:S(2)}, u32[]{:S(2)}) collective-permute-start(bf16[4,2,16,1536]{3,2,1,0:T(8,128)(2,1)S(1)} %get-tuple-element.52.refs_0_), channel_id=1, source_target_pairs={{2,0},{0,2},{6,4},{4,6},{10,8},{8,10},{14,12},{12,14},{3,1},{1,3},... | collective-permute-start | bytes 1179656 | tf_op jit(solution)/shard_map/ppermute | solution.py:469
  61.4 13.3 %collective-permute-start.19 = (bf16[4,2,16,1536]{3,2,1,0:T(8,128)(2,1)S(1)}, bf16[4,2,16,1536]{3,2,1,0:T(8,128)(2,1)S(1)}, u32[]{:S(2)}, u32[]{:S(2)}) collective-permute-start(bf16[4,2,16,1536]{3,2,1,0:T(8,128)(2,1)S(1)} %get-tuple-element.61.refs_1_), channel_id=1, source_target_pairs={{2,0},{0,2},{6,4},{4,6},{10,8},{8,10},{14,12},{12,14},{3,1},{1,3},... | collective-permute-start | bytes 1179656 | tf_op jit(solution)/shard_map/ppermute | solution.py:469
  62.0 7.1 %collective-permute-start.15 = (bf16[6,64,128]{2,1,0:T(8,128)(2,1)S(1)}, bf16[6,64,128]{2,1,0:T(8,128)(2,1)S(1)}, u32[]{:S(2)}, u32[]{:S(2)}) collective-permute-start(bf16[6,64,128]{2,1,0:T(8,128)(2,1)S(1)} %get-tuple-element.62), channel_id=1, source_target_pairs={{4,0},{6,2},{8,4},{10,6},{12,8},{14,10},{0,12},{2,14},{5,1},{7,3},... | collective-permute-start | bytes 294920 | tf_op jit(solution)/shard_map/ppermute | solution.py:469
  65.7 6.2 %collective-permute-start.16 = (bf16[6,64,128]{2,1,0:T(8,128)(2,1)S(1)}, bf16[6,64,128]{2,1,0:T(8,128)(2,1)S(1)}, u32[]{:S(2)}, u32[]{:S(2)}) collective-permute-start(bf16[6,64,128]{2,1,0:T(8,128)(2,1)S(1)} %get-tuple-element.63), channel_id=1, source_target_pairs={{8,0},{10,2},{12,4},{14,6},{0,8},{2,10},{4,12},{6,14},{9,1},{11,3}... | collective-permute-start | bytes 294920 | tf_op jit(solution)/shard_map/ppermute | solution.py:469
  66.6 6.4 %collective-permute-start.17 = (bf16[6,64,128]{2,1,0:T(8,128)(2,1)S(1)}, bf16[6,64,128]{2,1,0:T(8,128)(2,1)S(1)}, u32[]{:S(2)}, u32[]{:S(2)}) collective-permute-start(bf16[6,64,128]{2,1,0:T(8,128)(2,1)S(1)} %get-tuple-element.64), channel_id=1, source_target_pairs={{12,0},{14,2},{0,4},{2,6},{4,8},{6,10},{8,12},{10,14},{13,1},{15,3... | collective-permute-start | bytes 294920 | tf_op jit(solution)/shard_map/ppermute | solution.py:469
  73.9 7.9 %collective-permute-start.23 = (bf16[4,2,16,1536]{3,2,1,0:T(8,128)(2,1)S(1)}, bf16[4,2,16,1536]{3,2,1,0:T(8,128)(2,1)S(1)}, u32[]{:S(2)}, u32[]{:S(2)}) collective-permute-start(bf16[4,2,16,1536]{3,2,1,0:T(8,128)(2,1)S(1)} %get-tuple-element.66.refs_2_), channel_id=1, source_target_pairs={{2,0},{0,2},{6,4},{4,6},{10,8},{8,10},{14,12},{12,14},{3,1},{1,3},... | collective-permute-start | bytes 1179656 | tf_op jit(solution)/shard_map/ppermute | solution.py:469
  77.6 15.8 %collective-permute-start.20 = (bf16[80,768]{1,0:T(8,128)(2,1)S(1)}, bf16[80,768]{1,0:T(8,128)(2,1)S(1)}, u32[]{:S(2)}, u32[]{:S(2)}) collective-permute-start(bf16[80,768]{1,0:T(8,128)(2,1)S(1)} %get-tuple-element.69), channel_id=1, source_target_pairs={{12,0},{14,2},{0,4},{2,6},{4,8},{6,10},{8,12},{10,14},{13,1},{15,3... | collective-permute-start | bytes 368648 | tf_op jit(solution)/shard_map/ppermute | solution.py:469
  77.9 15.6 %collective-permute-start.21 = (bf16[80,768]{1,0:T(8,128)(2,1)S(1)}, bf16[80,768]{1,0:T(8,128)(2,1)S(1)}, u32[]{:S(2)}, u32[]{:S(2)}) collective-permute-start(bf16[80,768]{1,0:T(8,128)(2,1)S(1)} %get-tuple-element.70), channel_id=1, source_target_pairs={{8,0},{10,2},{12,4},{14,6},{0,8},{2,10},{4,12},{6,14},{9,1},{11,3}... | collective-permute-start | bytes 368648 | tf_op jit(solution)/shard_map/ppermute | solution.py:469
  79.3 14.2 %collective-permute-start.22 = (bf16[80,768]{1,0:T(8,128)(2,1)S(1)}, bf16[80,768]{1,0:T(8,128)(2,1)S(1)}, u32[]{:S(2)}, u32[]{:S(2)}) collective-permute-start(bf16[80,768]{1,0:T(8,128)(2,1)S(1)} %get-tuple-element.71), channel_id=1, source_target_pairs={{4,0},{6,2},{8,4},{10,6},{12,8},{14,10},{0,12},{2,14},{5,1},{7,3},... | collective-permute-start | bytes 368648 | tf_op jit(solution)/shard_map/ppermute | solution.py:469
  83.9 5.7 %collective-permute-start.24 = (bf16[16,768]{1,0:T(8,128)(2,1)S(1)}, bf16[16,768]{1,0:T(8,128)(2,1)S(1)}, u32[]{:S(2)}, u32[]{:S(2)}) collective-permute-start(bf16[16,768]{1,0:T(8,128)(2,1)S(1)} %get-tuple-element.74), channel_id=1, source_target_pairs={{12,0},{14,2},{0,4},{2,6},{4,8},{6,10},{8,12},{10,14},{13,1},{15,3... | collective-permute-start | bytes 73736 | tf_op jit(solution)/shard_map/ppermute | solution.py:469
  84.2 5.7 %collective-permute-start.25 = (bf16[16,768]{1,0:T(8,128)(2,1)S(1)}, bf16[16,768]{1,0:T(8,128)(2,1)S(1)}, u32[]{:S(2)}, u32[]{:S(2)}) collective-permute-start(bf16[16,768]{1,0:T(8,128)(2,1)S(1)} %get-tuple-element.75), channel_id=1, source_target_pairs={{8,0},{10,2},{12,4},{14,6},{0,8},{2,10},{4,12},{6,14},{9,1},{11,3}... | collective-permute-start | bytes 73736 | tf_op jit(solution)/shard_map/ppermute | solution.py:469
  96.0 8.2 %collective-permute-start.28 = (bf16[96,768]{1,0:T(8,128)(2,1)S(1)}, bf16[96,768]{1,0:T(8,128)(2,1)S(1)}, u32[]{:S(2)}, u32[]{:S(2)}) collective-permute-start(bf16[96,768]{1,0:T(8,128)(2,1)S(1)} %add_parts.1.refs_0_), channel_id=1, source_target_pairs={{8,0},{10,2},{12,4},{14,6},{0,8},{2,10},{4,12},{6,14},{9,1},{11,3}... | collective-permute-start | bytes 442376 | tf_op jit(solution)/shard_map/ppermute | solution.py:469
  96.0 9.4 %collective-permute-start.29 = (bf16[96,768]{1,0:T(8,128)(2,1)S(1)}, bf16[96,768]{1,0:T(8,128)(2,1)S(1)}, u32[]{:S(2)}, u32[]{:S(2)}) collective-permute-start(bf16[96,768]{1,0:T(8,128)(2,1)S(1)} %add_parts.1.refs_0_), channel_id=1, source_target_pairs={{12,0},{14,2},{0,4},{2,6},{4,8},{6,10},{8,12},{10,14},{13,1},{15,3... | collective-permute-start | bytes 442376 | tf_op jit(solution)/shard_map/ppermute | solution.py:469
  96.6 13.5 %collective-permute-start.30 = (bf16[96,768]{1,0:T(8,128)(2,1)S(1)}, bf16[96,768]{1,0:T(8,128)(2,1)S(1)}, u32[]{:S(2)}, u32[]{:S(2)}) collective-permute-start(bf16[96,768]{1,0:T(8,128)(2,1)S(1)} %add_parts.1.refs_0_), channel_id=1, source_target_pairs={{2,0},{0,2},{6,4},{4,6},{10,8},{8,10},{14,12},{12,14},{3,1},{1,3},... | collective-permute-start | bytes 442376 | tf_op jit(solution)/shard_map/ppermute | solution.py:469
  98.9 11.3 %collective-permute-start.31 = (bf16[96,768]{1,0:T(8,128)(2,1)S(1)}, bf16[96,768]{1,0:T(8,128)(2,1)S(1)}, u32[]{:S(2)}, u32[]{:S(2)}) collective-permute-start(bf16[96,768]{1,0:T(8,128)(2,1)S(1)} %collective-permute-done.27.refs_1_), channel_id=1, source_target_pairs={{2,0},{0,2},{6,4},{4,6},{10,8},{8,10},{14,12},{12,14},{3,1},{1,3},... | collective-permute-start | bytes 442376 | tf_op jit(solution)/shard_map/ppermute | solution.py:469
  104.3 6.0 %collective-permute-start.32 = (bf16[96,768]{1,0:T(8,128)(2,1)S(1)}, bf16[96,768]{1,0:T(8,128)(2,1)S(1)}, u32[]{:S(2)}, u32[]{:S(2)}) collective-permute-start(bf16[96,768]{1,0:T(8,128)(2,1)S(1)} %collective-permute-done.28.refs_2_), channel_id=1, source_target_pairs={{2,0},{0,2},{6,4},{4,6},{10,8},{8,10},{14,12},{12,14},{3,1},{1,3},... | collective-permute-start | bytes 442376 | tf_op jit(solution)/shard_map/ppermute | solution.py:469
  105.4 5.6 %collective-permute-start.33 = (bf16[96,768]{1,0:T(8,128)(2,1)S(1)}, bf16[96,768]{1,0:T(8,128)(2,1)S(1)}, u32[]{:S(2)}, u32[]{:S(2)}) collective-permute-start(bf16[96,768]{1,0:T(8,128)(2,1)S(1)} %collective-permute-done.29.refs_3_), channel_id=1, source_target_pairs={{2,0},{0,2},{6,4},{4,6},{10,8},{8,10},{14,12},{12,14},{3,1},{1,3},... | collective-permute-start | bytes 442376 | tf_op jit(solution)/shard_map/ppermute | solution.py:469
  (9 other events, 141.4 us)

commit v4 on v3

--- a/solution.py
+++ b/solution.py
@@ -29,6 +29,7 @@
 VMEM = pl.BlockSpec(memory_space=pltpu.VMEM)
 SMEM = pl.BlockSpec(memory_space=pltpu.SMEM)
 ANY = pl.BlockSpec(memory_space=pl.ANY)
+HBM = pl.BlockSpec(memory_space=pltpu.HBM)
 GRANT = pltpu.CompilerParams(vmem_limit_bytes=16 * 2**20)
 
 
@@ -64,7 +65,7 @@
 def tables_kernel(*refs):
     table_ref = refs[-1]
     shifts = Shifts()
-    scale = jnp.float32(-1.0 / 6.0)
+    scale = jnp.float32(-math.sqrt(2.0) / 6.0)
     size = refs[0].shape[0]
     links = [ref[ref.shape[0] - size :].astype(jnp.float32) for ref in refs[:-1]]
     count = len(links)
@@ -78,10 +79,13 @@
         for direction in range(3):
             for target in range(3):
                 for source in range(3):
-                    slot = (2 * direction) * 18 + (target * 3 + source) * 2
-                    table_ref[plane, slot] = entry(plane, direction, 0, target, source)
-                    table_ref[plane, slot + 1] = entry(plane, direction, 1, target, source)
-                    slot = (2 * direction + 1) * 18 + (target * 3 + source) * 2
+                    slot = (2 * direction) * 27 + (target * 3 + source) * 3
+                    re = entry(plane, direction, 0, target, source)
+                    im = entry(plane, direction, 1, target, source)
+                    table_ref[plane, slot] = re
+                    table_ref[plane, slot + 1] = im
+                    table_ref[plane, slot + 2] = re + im
+                    slot = (2 * direction + 1) * 27 + (target * 3 + source) * 3
                     below = plane + 1 if direction == 2 else plane
                     re = entry(below, direction, 0, source, target)
                     im = entry(below, direction, 1, source, target)
@@ -90,12 +94,13 @@
                         re, im = move(re), move(im)
                     table_ref[plane, slot] = re
                     table_ref[plane, slot + 1] = -im
+                    table_ref[plane, slot + 2] = re - im
 
 
 def link_tables(links):
     return pl.pallas_call(
         tables_kernel,
-        out_shape=pltpu.VMEM((len(links), 108, 8, LANES), jnp.float32),
+        out_shape=pltpu.VMEM((len(links), 162, 8, LANES), jnp.float32),
         in_specs=[VMEM] * len(links),
         out_specs=VMEM,
         compiler_params=GRANT,
@@ -111,24 +116,56 @@
         out = outs[d - 1]
         for c in range(6):
             out[c * rows : (c + 1) * rows] = own_ref[c, pl.ds(start, rows), :].astype(jnp.bfloat16)
-        if out.shape[0] > 6 * rows:
-            out[6 * rows :] = refs[0][...].astype(jnp.bfloat16)
+
+
+def first_pack_kernel(sites, place_ref, own_ref, links_ref, *refs):
+    outs, block_ref, link_ref, sems = refs[: sites - 1], refs[sites - 1], refs[sites], refs[sites + 1]
+    rows = CHUNKS[0] * 4
+    copies = [pltpu.make_async_copy(links_ref, link_ref, sems.at[0])]
+    for d in range(1, sites):
+        start = row_of(lax.rem(place_ref[0] + d, sites), own_ref.shape[1] // sites, 0)
+        copies.append(pltpu.make_async_copy(own_ref.at[:, pl.ds(start, rows), :], block_ref.at[d - 1], sems.at[d]))
+    for copy in copies:
+        copy.start()
+    copies[0].wait()
+    links = link_ref[...].astype(jnp.bfloat16)
+    for d in range(1, sites):
+        copies[d].wait()
+        for c in range(6):
+            outs[d - 1][c * rows : (c + 1) * rows] = block_ref[d - 1, c].astype(jnp.bfloat16)
+        outs[d - 1][6 * rows :] = links
+
+
+def first_pack(own, place, sites, links):
+    rows = CHUNKS[0] * 4
+    return pl.pallas_call(
+        functools.partial(first_pack_kernel, sites),
+        out_shape=[pltpu.VMEM((6 * rows + links.shape[0], LANES), jnp.bfloat16)] * (sites - 1),
+        in_specs=[SMEM, HBM, HBM],
+        out_specs=[VMEM] * (sites - 1),
+        scratch_shapes=[
+            pltpu.VMEM((sites - 1, 6, rows, LANES), jnp.float32),
+            pltpu.VMEM(links.shape, jnp.float32),
+            pltpu.SemaphoreType.DMA((sites,)),
+        ],
+        compiler_params=pltpu.CompilerParams(vmem_limit_bytes=66 * 10**6),
+        name="pack0",
+    )(place, own, links)
 
 
 def row_of(slot, rows_per_slot, chunk):
     return pl.multiple_of(slot * rows_per_slot + 4 * sum(CHUNKS[:chunk]), 32)
 
 
-def pack(own, place, chunk, sites, links, after):
-    extra = [links] if chunk == 0 else []
-    length = 24 * CHUNKS[chunk] + sum(e.shape[0] for e in extra)
+def pack(own, place, chunk, sites, after):
+    length = 24 * CHUNKS[chunk]
     return pl.pallas_call(
         functools.partial(pack_kernel, sites, chunk),
         out_shape=[pltpu.VMEM((length, LANES), jnp.bfloat16)] * (sites - 1),
-        in_specs=[SMEM] + [VMEM] * (1 + len(extra)) + [ANY] * len(after),
+        in_specs=[SMEM, VMEM] + [ANY] * len(after),
         out_specs=[VMEM] * (sites - 1),
         compiler_params=GRANT,
-    )(place, own, *extra, *after)
+    )(place, own, *after)
 
 
 def filter_kernel(sites, chunk, place_ref, *refs):
@@ -140,7 +177,7 @@
 
     def hop(plane, here, ahead_z, behind_z):
         count = len(here(0))
-        total = [[None] * count for _ in range(6)]
+        sums = [[[None] * count for _ in range(3)] for _ in range(3)]
         moves = (shifts.ahead_x, shifts.behind_x, shifts.ahead_y, shifts.behind_y, None, None)
         for direction in range(6):
             if direction < 4:
@@ -148,21 +185,20 @@
             else:
                 take = ahead_z if direction == 4 else behind_z
                 field = [take(c) for c in range(6)]
-            for target in range(3):
-                for source in range(3):
-                    slot = direction * 18 + (target * 3 + source) * 2
-                    re = table_ref[plane, slot]
-                    im = table_ref[plane, slot + 1]
-                    for n in range(count):
-                        f_re, f_im = field[source][n], field[3 + source][n]
-                        add_re = re * f_re - im * f_im
-                        add_im = re * f_im + im * f_re
-                        if total[target][n] is None:
-                            total[target][n], total[3 + target][n] = add_re, add_im
-                        else:
-                            total[target][n] = total[target][n] + add_re
-                            total[3 + target][n] = total[3 + target][n] + add_im
-        return total
+            for source in range(3):
+                re, im = field[source], field[3 + source]
+                factors = ([im[n] - re[n] for n in range(count)], [im[n] + re[n] for n in range(count)], re)
+                for target in range(3):
+                    slot = direction * 27 + (target * 3 + source) * 3
+                    for k in range(3):
+                        link = table_ref[plane, slot + k]
+                        for n in range(count):
+                            add = link * factors[k][n]
+                            old = sums[target][k][n]
+                            sums[target][k][n] = add if old is None else old + add
+        total_re = [[sums[t][2][n] - sums[t][1][n] for n in range(count)] for t in range(3)]
+        total_im = [[sums[t][2][n] + sums[t][0][n] for n in range(count)] for t in range(3)]
+        return total_re + total_im
 
     def step(index, carry):
         base = pl.multiple_of(index * 16, 16)
@@ -189,7 +225,7 @@
         for plane in range(sites):
             out = hop(plane, first(plane), first(plane - 1), first(plane + 1))
             for c in range(6):
-                value = 2.0 * jnp.concatenate(out[c], axis=0)
+                value = jnp.concatenate(out[c], axis=0)
                 outs[plane][c, pl.ds(base, 16), :] = value.astype(jnp.bfloat16)
         return carry
 
@@ -483,11 +519,12 @@
     received, packed = [], []
     for chunk in range(len(CHUNKS)):
         after = packed[:1]
-        if chunk == 1:
-            after = received[0][:1]
         if chunk == 2:
-            after = [*received[0], packed[0]]
-        packed = pack(own, place, chunk, sites, own_links, after)
+            after = [received[0][0], packed[0]]
+        if chunk == 0:
+            packed = first_pack(own, place, sites, own_links)
+        else:
+            packed = pack(own, place, chunk, sites, after)
         received.append([from_place(packed[d - 1], -d, 0) for d in range(1, sites)])
 
     flat = lax.broadcasted_iota(jnp.int32, (4, LANES), 0) * LANES + lax.broadcasted_iota(jnp.int32, (4, LANES), 1)
@@ -510,10 +547,10 @@
             last = s
     filtered, shifted, other = ([group_of[n] for n in range(len(CHUNKS))] for group_of in (filtered, shifted, other))
 
-    *parts, right = elementals(place, filtered + other[:-1], shifted, None, sites)
+    *parts, right = elementals(place, filtered + other[:1], shifted, None, sites)
     sent = [from_place(parts[d], -d, 0) for d in range(1, sites)]
     early = [parts[0], *sent]
-    parts = elementals(place, other[-1:], None, right, sites)
+    parts = elementals(place, other[1:], None, right, sites)
     sent = [from_place(parts[d], -d, 0) for d in range(1, sites)]
     mine = add_parts(early, [parts[0], *sent])
 

time: 116 us -> 115 us (level)
  starting transfers between devices: 53.5 us -> 48.9 us
  waiting for transfers between devices: 23 us -> 27.1 us
  Pallas kernels: 36.3 us -> 35 us
    ppermute x34, starting transfers between devices: 53.5 us -> 48.9 us  [from_place(): return lax.ppermute(block, ('site', 'vec'), route)]
    ppermute x34, waiting for transfers between devices: 23 us -> 27.1 us  [from_place(): return lax.ppermute(block, ('site', 'vec'), route)]
    pallas_call x3, Pallas kernels: 17.4 us -> 15.2 us  [filter_chunk(): pl.pallas_call(functools.partial(filter_kernel, sites, chunk), out_shape=...]
    pallas_call x1 -> x2, Pallas kernels: 0.3 us -> 2.19 us  [the longest x1 1.88 us: first_pack(): pl.pallas_call(functools.partial(first_pack_kernel, sites), out_shape=[pl...]
  transfers between devices with their start and end apart: 34 -> 34, of which waited for: 11 -> 13; matrix products, arithmetic and copies ran while one was open for 0% -> 0% of each run, Pallas kernels for 26% -> 24%
where the time goes in v4:
time: 115 us
  starting transfers between devices  48.9 us (43%)
  Pallas kernels  35 us (30%)
  waiting for transfers between devices  27.1 us (24%)
  local copies, waits for them, and re-layouts  2.52 us (2%)
    ppermute x34, starting transfers between devices, from_place(): return lax.ppermute(block, ('site', 'vec'), route)  48.9 us
    ppermute x34, waiting for transfers between devices, from_place(): return lax.ppermute(block, ('site', 'vec'), route)  27.1 us
    pallas_call x3, Pallas kernels, filter_chunk(): pl.pallas_call(functools.partial(filter_kernel, sites, chunk), out_shape=...  15.2 us
    pallas_call x1, Pallas kernels, project_second(): pl.pallas_call(functools.partial(second_kernel, len(pieces)), grid=(outer...  5.29 us
    pallas_call x2, Pallas kernels, elementals(): pl.pallas_call(functools.partial(early_kernel if early else late_kernel,...  4.53 us
    pallas_call x1, Pallas kernels, project_first(): pl.pallas_call(functools.partial(first_kernel, len(pieces)), out_shape=pl...  3.89 us
    pallas_call x3, Pallas kernels, finish(): pl.pallas_call(functools.partial(finish_kernel, sites, chunk), out_shape=...  2.67 us
    unnamed x14, local copies, waits for them, and re-layouts  2.35 us
  transfers between devices with their start and end apart: 34, of which 13 were waited for; matrix products, arithmetic and copies ran while one was open for 0% of the time, Pallas kernels for 24%

profile of v4, /device:TPU:0, one launch (start us, length us, event | category | flops | bytes accessed | tf_op | source)
XLA Modules:
  0.0 114.7 jit_solution(4786989623441124360)
XLA Ops:
  0.7 1.9 %pack0.1 = (bf16[600,128]{1,0:T(8,128)(2,1)S(1)}, bf16[600,128]{1,0:T(8,128)(2,1)S(1)}, bf16[600,128]{1,0:T(8,128)(2,1)S(1)}) custom-call(s32[2]{0:T(128)} %pad_add_fusion.place_ref, f32[6,768,128]{2,1,0:T(8,128)} %bitcast.6, f32[216,128]{1,0:T(8,128)} %bitcast.17), custom_call_target="tpu_custom_call" | custom-call | tf_op jit(solution)/shard_map/pack0/pallas_call | solution.py:141
  2.5 3.1 %collective-permute-start = (bf16[600,128]{1,0:T(8,128)(2,1)S(1)}, bf16[600,128]{1,0:T(8,128)(2,1)S(1)}, u32[]{:S(2)}, u32[]{:S(2)}) collective-permute-start(bf16[600,128]{1,0:T(8,128)(2,1)S(1)} %get-tuple-element.41.refs_0_), channel_id=1, source_target_pairs={{12,0},{14,2},{0,4},{2,6},{4,8},{6,10},{8,12},{10,14},{13,1},{15,3... | collective-permute-start | bytes 460808 | tf_op jit(solution)/shard_map/ppermute | solution.py:505
  5.6 2.6 %collective-permute-start.1 = (bf16[600,128]{1,0:T(8,128)(2,1)S(1)}, bf16[600,128]{1,0:T(8,128)(2,1)S(1)}, u32[]{:S(2)}, u32[]{:S(2)}) collective-permute-start(bf16[600,128]{1,0:T(8,128)(2,1)S(1)} %get-tuple-element.42), channel_id=1, source_target_pairs={{8,0},{10,2},{12,4},{14,6},{0,8},{2,10},{4,12},{6,14},{9,1},{11,3}... | collective-permute-start | bytes 460808 | tf_op jit(solution)/shard_map/ppermute | solution.py:505
  9.6 1.7 %copy-done = f32[1,2,3,192,1,512]{5,4,3,2,1,0:T(1,128)S(1)} copy-done((f32[1,2,3,192,1,512]{5,4,3,2,1,0:T(1,128)S(1)}, f32[1,2,3,192,1,512]{5,4,3,2,1,0:T(1,128)}, u32[]{:S(2)}) %copy-start) | copy-done | bytes 2359320
  13.9 2.9 %collective-permute-start.8 = (bf16[384,128]{1,0:T(8,128)(2,1)S(1)}, bf16[384,128]{1,0:T(8,128)(2,1)S(1)}, u32[]{:S(2)}, u32[]{:S(2)}) collective-permute-start(bf16[384,128]{1,0:T(8,128)(2,1)S(1)} %get-tuple-element.50), channel_id=1, source_target_pairs={{4,0},{6,2},{8,4},{10,6},{12,8},{14,10},{0,12},{2,14},{5,1},{7,3},... | collective-permute-start | bytes 294920 | tf_op jit(solution)/shard_map/ppermute | solution.py:505
  16.7 5.1 %collective-permute-done.1.refs_2_ = bf16[600,128]{1,0:T(8,128)(2,1)S(1)} collective-permute-done((bf16[600,128]{1,0:T(8,128)(2,1)S(1)}, bf16[600,128]{1,0:T(8,128)(2,1)S(1)}, u32[]{:S(2)}, u32[]{:S(2)}) %collective-permute-start.1) | collective-permute-done | bytes 153632 | tf_op jit(solution)/shard_map/ppermute | solution.py:505
  22.1 5.1 %shard_map.55 = (bf16[6,64,128]{2,1,0:T(8,128)(2,1)S(1)}, bf16[6,64,128]{2,1,0:T(8,128)(2,1)S(1)}, bf16[6,64,128]{2,1,0:T(8,128)(2,1)S(1)}, bf16[6,64,128]{2,1,0:T(8,128)(2,1)S(1)}) custom-call(s32[2]{0:T(128)S(1)} %copy-done.4, f32[6,768,128]{2,1,0:T(8,128)S(1)} %bitcast.8, bf16[600,128]{1,0:T(8,128)(2,1)S(1)} %collective-permute-done.refs_1_.refs_0_, ...), custom_call_target="tpu_custom_call" | custom-call | flops 28311552 | bytes 786432 | tf_op jit(solution)/shard_map/pallas_call | solution.py:238
  27.2 6.8 %collective-permute-start.3 = (bf16[6,64,128]{2,1,0:T(8,128)(2,1)S(1)}, bf16[6,64,128]{2,1,0:T(8,128)(2,1)S(1)}, u32[]{:S(2)}, u32[]{:S(2)}) collective-permute-start(bf16[6,64,128]{2,1,0:T(8,128)(2,1)S(1)} %get-tuple-element.45), channel_id=1, source_target_pairs={{4,0},{6,2},{8,4},{10,6},{12,8},{14,10},{0,12},{2,14},{5,1},{7,3},... | collective-permute-start | bytes 294920 | tf_op jit(solution)/shard_map/ppermute | solution.py:505
  35.4 2.9 %collective-permute-start.12 = (bf16[384,128]{1,0:T(8,128)(2,1)S(1)}, bf16[384,128]{1,0:T(8,128)(2,1)S(1)}, u32[]{:S(2)}, u32[]{:S(2)}) collective-permute-start(bf16[384,128]{1,0:T(8,128)(2,1)S(1)} %get-tuple-element.56), channel_id=1, source_target_pairs={{12,0},{14,2},{0,4},{2,6},{4,8},{6,10},{8,12},{10,14},{13,1},{15,3... | collective-permute-start | bytes 294920 | tf_op jit(solution)/shard_map/ppermute | solution.py:505
  39.2 5.1 %shard_map.57 = (bf16[6,64,128]{2,1,0:T(8,128)(2,1)S(1)}, bf16[6,64,128]{2,1,0:T(8,128)(2,1)S(1)}, bf16[6,64,128]{2,1,0:T(8,128)(2,1)S(1)}, bf16[6,64,128]{2,1,0:T(8,128)(2,1)S(1)}) custom-call(s32[2]{0:T(128)S(1)} %copy-done.4, f32[6,768,128]{2,1,0:T(8,128)S(1)} %bitcast.10, bf16[384,128]{1,0:T(8,128)(2,1)S(1)} %collective-permute-done.6.refs_1_, ...), custom_call_target="tpu_custom_call" | custom-call | flops 28311552 | bytes 786432 | tf_op jit(solution)/shard_map/pallas_call | solution.py:238
  44.3 1.6 %collective-permute-start.14 = (bf16[384,128]{1,0:T(8,128)(2,1)S(1)}, bf16[384,128]{1,0:T(8,128)(2,1)S(1)}, u32[]{:S(2)}, u32[]{:S(2)}) collective-permute-start(bf16[384,128]{1,0:T(8,128)(2,1)S(1)} %get-tuple-element.58), channel_id=1, source_target_pairs={{4,0},{6,2},{8,4},{10,6},{12,8},{14,10},{0,12},{2,14},{5,1},{7,3},... | collective-permute-start | bytes 294920 | tf_op jit(solution)/shard_map/ppermute | solution.py:505
  45.9 2.8 %collective-permute-done.4.refs_2_ = bf16[6,64,128]{2,1,0:T(8,128)(2,1)S(1)} collective-permute-done((bf16[6,64,128]{2,1,0:T(8,128)(2,1)S(1)}, bf16[6,64,128]{2,1,0:T(8,128)(2,1)S(1)}, u32[]{:S(2)}, u32[]{:S(2)}) %collective-permute-start.4) | collective-permute-done | bytes 98336 | tf_op jit(solution)/shard_map/ppermute | solution.py:505
  49.8 1.6 %collective-permute-start.18 = (bf16[4,2,16,1536]{3,2,1,0:T(8,128)(2,1)S(1)}, bf16[4,2,16,1536]{3,2,1,0:T(8,128)(2,1)S(1)}, u32[]{:S(2)}, u32[]{:S(2)}) collective-permute-start(bf16[4,2,16,1536]{3,2,1,0:T(8,128)(2,1)S(1)} %get-tuple-element.52.refs_0_), channel_id=1, source_target_pairs={{2,0},{0,2},{6,4},{4,6},{10,8},{8,10},{14,12},{12,14},{3,1},{1,3},... | collective-permute-start | bytes 1179656 | tf_op jit(solution)/shard_map/ppermute | solution.py:505
  51.3 1.5 %collective-permute-done.13.refs_2_ = bf16[384,128]{1,0:T(8,128)(2,1)S(1)} collective-permute-done((bf16[384,128]{1,0:T(8,128)(2,1)S(1)}, bf16[384,128]{1,0:T(8,128)(2,1)S(1)}, u32[]{:S(2)}, u32[]{:S(2)}) %collective-permute-start.13) | collective-permute-done | bytes 98336 | tf_op jit(solution)/shard_map/ppermute | solution.py:505
  52.8 2.7 %collective-permute-start.9 = (bf16[6,64,128]{2,1,0:T(8,128)(2,1)S(1)}, bf16[6,64,128]{2,1,0:T(8,128)(2,1)S(1)}, u32[]{:S(2)}, u32[]{:S(2)}) collective-permute-start(bf16[6,64,128]{2,1,0:T(8,128)(2,1)S(1)} %get-tuple-element.53), channel_id=1, source_target_pairs={{4,0},{6,2},{8,4},{10,6},{12,8},{14,10},{0,12},{2,14},{5,1},{7,3},... | collective-permute-start | bytes 294920 | tf_op jit(solution)/shard_map/ppermute | solution.py:505
  55.5 5.1 %shard_map.60 = (bf16[6,64,128]{2,1,0:T(8,128)(2,1)S(1)}, bf16[6,64,128]{2,1,0:T(8,128)(2,1)S(1)}, bf16[6,64,128]{2,1,0:T(8,128)(2,1)S(1)}, bf16[6,64,128]{2,1,0:T(8,128)(2,1)S(1)}) custom-call(s32[2]{0:T(128)S(1)} %copy-done.4, f32[6,768,128]{2,1,0:T(8,128)S(1)} %bitcast.12, bf16[384,128]{1,0:T(8,128)(2,1)S(1)} %collective-permute-done.12.refs_1_, ...), custom_call_target="tpu_custom_call" | custom-call | flops 28311552 | bytes 786432 | tf_op jit(solution)/shard_map/pallas_call | solution.py:238
  60.8 2.3 %collective-permute-start.16 = (bf16[6,64,128]{2,1,0:T(8,128)(2,1)S(1)}, bf16[6,64,128]{2,1,0:T(8,128)(2,1)S(1)}, u32[]{:S(2)}, u32[]{:S(2)}) collective-permute-start(bf16[6,64,128]{2,1,0:T(8,128)(2,1)S(1)} %get-tuple-element.63), channel_id=1, source_target_pairs={{8,0},{10,2},{12,4},{14,6},{0,8},{2,10},{4,12},{6,14},{9,1},{11,3}... | collective-permute-start | bytes 294920 | tf_op jit(solution)/shard_map/ppermute | solution.py:505
  64.3 1.4 %collective-permute-start.22 = (bf16[4,2,16,1536]{3,2,1,0:T(8,128)(2,1)S(1)}, bf16[4,2,16,1536]{3,2,1,0:T(8,128)(2,1)S(1)}, u32[]{:S(2)}, u32[]{:S(2)}) collective-permute-start(bf16[4,2,16,1536]{3,2,1,0:T(8,128)(2,1)S(1)} %get-tuple-element.61.refs_1_), channel_id=1, source_target_pairs={{2,0},{0,2},{6,4},{4,6},{10,8},{8,10},{14,12},{12,14},{3,1},{1,3},... | collective-permute-start | bytes 1179656 | tf_op jit(solution)/shard_map/ppermute | solution.py:505
  66.1 2.2 %collective-permute-done.16.refs_2_ = bf16[6,64,128]{2,1,0:T(8,128)(2,1)S(1)} collective-permute-done((bf16[6,64,128]{2,1,0:T(8,128)(2,1)S(1)}, bf16[6,64,128]{2,1,0:T(8,128)(2,1)S(1)}, u32[]{:S(2)}, u32[]{:S(2)}) %collective-permute-start.16) | collective-permute-done | bytes 98336 | tf_op jit(solution)/shard_map/ppermute | solution.py:505
  70.4 1.6 %collective-permute-start.23 = (bf16[4,2,16,1536]{3,2,1,0:T(8,128)(2,1)S(1)}, bf16[4,2,16,1536]{3,2,1,0:T(8,128)(2,1)S(1)}, u32[]{:S(2)}, u32[]{:S(2)}) collective-permute-start(bf16[4,2,16,1536]{3,2,1,0:T(8,128)(2,1)S(1)} %get-tuple-element.66.refs_2_), channel_id=1, source_target_pairs={{2,0},{0,2},{6,4},{4,6},{10,8},{8,10},{14,12},{12,14},{3,1},{1,3},... | collective-permute-start | bytes 1179656 | tf_op jit(solution)/shard_map/ppermute | solution.py:505
  72.0 2.5 %elementals_early.1 = (f32[64,768]{1,0:T(8,128)S(1)}, bf16[64,768]{1,0:T(8,128)(2,1)S(1)}, bf16[64,768]{1,0:T(8,128)(2,1)S(1)}, bf16[64,768]{1,0:T(8,128)(2,1)S(1)}, bf16[2,384,3072]{2,1,0:T(8,128)(2,1)S(1)}) custom-call(s32[2]{0:T(128)S(1)} %copy-done.4, bf16[4,2,16,1536]{3,2,1,0:T(8,128)(2,1)S(1)} %get-tuple-element.52.refs_0_, ...), custom_call_target="tpu_custom_call" | custom-call | flops 1207959552 | bytes 2359296 | tf_op jit(solution)/shard_map/elementals_early/pallas_call | solution.py:354
  75.8 2.6 %collective-permute-start.21 = (bf16[64,768]{1,0:T(8,128)(2,1)S(1)}, bf16[64,768]{1,0:T(8,128)(2,1)S(1)}, u32[]{:S(2)}, u32[]{:S(2)}) collective-permute-start(bf16[64,768]{1,0:T(8,128)(2,1)S(1)} %get-tuple-element.71), channel_id=1, source_target_pairs={{4,0},{6,2},{8,4},{10,6},{12,8},{14,10},{0,12},{2,14},{5,1},{7,3},... | collective-permute-start | bytes 294920 | tf_op jit(solution)/shard_map/ppermute | solution.py:505
  78.4 2.2 %collective-permute-done.23.refs_1_ = bf16[4,2,16,1536]{3,2,1,0:T(8,128)(2,1)S(1)} collective-permute-done((bf16[4,2,16,1536]{3,2,1,0:T(8,128)(2,1)S(1)}, bf16[4,2,16,1536]{3,2,1,0:T(8,128)(2,1)S(1)}, u32[]{:S(2)}, u32[]{:S(2)}) %collective-permute-start.23) | collective-permute-done | bytes 393248 | tf_op jit(solution)/shard_map/ppermute | solution.py:505
  80.6 2.1 %elementals_late.1 = (f32[32,768]{1,0:T(8,128)S(1)}, bf16[32,768]{1,0:T(8,128)(2,1)S(1)}, bf16[32,768]{1,0:T(8,128)(2,1)S(1)}, bf16[32,768]{1,0:T(8,128)(2,1)S(1)}) custom-call(s32[2]{0:T(128)S(1)} %copy-done.4, bf16[4,2,16,1536]{3,2,1,0:T(8,128)(2,1)S(1)} %collective-permute-done.22.refs_0_, bf16[4,2,16,1536]{3,2,1,0:T(8,128)(2,1)S(1)} %collective-permute-done.23.refs_1_, ...), custom_call_target="tpu_custom_call" | custom-call | flops 603979776 | bytes 2359296 | tf_op jit(solution)/shard_map/elementals_late/pallas_call | solution.py:354
  83.0 3.3 %collective-permute-start.25 = (bf16[32,768]{1,0:T(8,128)(2,1)S(1)}, bf16[32,768]{1,0:T(8,128)(2,1)S(1)}, u32[]{:S(2)}, u32[]{:S(2)}) collective-permute-start(bf16[32,768]{1,0:T(8,128)(2,1)S(1)} %get-tuple-element.75), channel_id=1, source_target_pairs={{8,0},{10,2},{12,4},{14,6},{0,8},{2,10},{4,12},{6,14},{9,1},{11,3}... | collective-permute-start | bytes 147464 | tf_op jit(solution)/shard_map/ppermute | solution.py:505
  86.6 2.2 %collective-permute-done.24.refs_5_ = bf16[32,768]{1,0:T(8,128)(2,1)S(1)} collective-permute-done((bf16[32,768]{1,0:T(8,128)(2,1)S(1)}, bf16[32,768]{1,0:T(8,128)(2,1)S(1)}, u32[]{:S(2)}, u32[]{:S(2)}) %collective-permute-start.24) | collective-permute-done | bytes 49184 | tf_op jit(solution)/shard_map/ppermute | solution.py:505
  90.9 2.1 %collective-permute-start.27 = (bf16[96,768]{1,0:T(8,128)(2,1)S(1)}, bf16[96,768]{1,0:T(8,128)(2,1)S(1)}, u32[]{:S(2)}, u32[]{:S(2)}) collective-permute-start(bf16[96,768]{1,0:T(8,128)(2,1)S(1)} %add_parts.1.refs_0_), channel_id=1, source_target_pairs={{4,0},{6,2},{8,4},{10,6},{12,8},{14,10},{0,12},{2,14},{5,1},{7,3},... | collective-permute-start | bytes 442376 | tf_op jit(solution)/shard_map/ppermute | solution.py:505
  94.8 2.7 %collective-permute-done.27.refs_1_ = bf16[96,768]{1,0:T(8,128)(2,1)S(1)} collective-permute-done((bf16[96,768]{1,0:T(8,128)(2,1)S(1)}, bf16[96,768]{1,0:T(8,128)(2,1)S(1)}, u32[]{:S(2)}, u32[]{:S(2)}) %collective-permute-start.27) | collective-permute-done | bytes 147488 | tf_op jit(solution)/shard_map/ppermute | solution.py:505
  97.4 1.4 %collective-permute-start.31 = (bf16[96,768]{1,0:T(8,128)(2,1)S(1)}, bf16[96,768]{1,0:T(8,128)(2,1)S(1)}, u32[]{:S(2)}, u32[]{:S(2)}) collective-permute-start(bf16[96,768]{1,0:T(8,128)(2,1)S(1)} %collective-permute-done.27.refs_1_), channel_id=1, source_target_pairs={{2,0},{0,2},{6,4},{4,6},{10,8},{8,10},{14,12},{12,14},{3,1},{1,3},... | collective-permute-start | bytes 442376 | tf_op jit(solution)/shard_map/ppermute | solution.py:505
  98.8 3.7 %collective-permute-done.28.refs_2_ = bf16[96,768]{1,0:T(8,128)(2,1)S(1)} collective-permute-done((bf16[96,768]{1,0:T(8,128)(2,1)S(1)}, bf16[96,768]{1,0:T(8,128)(2,1)S(1)}, u32[]{:S(2)}, u32[]{:S(2)}) %collective-permute-start.28) | collective-permute-done | bytes 147488 | tf_op jit(solution)/shard_map/ppermute | solution.py:505
  104.6 3.9 %project_first.1.first_ref = bf16[8,2,192,512]{3,2,1,0:T(8,128)(2,1)S(1)} custom-call(s32[2]{0:T(128)S(1)} %copy-done.4, s32[2]{0:T(128)S(1)} %copy-done.5, bf16[8,2,192,384]{3,2,1,0:T(8,128)(2,1)S(1)} %bitcast.15, bf16[96,768]{1,0:T(8,128)(2,1)S(1)} %add_parts.1.refs_0_, bf16[96,768]{1,0:T(8,128)(2,1)S(1)} %collective-permute-done.27.refs_1_, ...), custom_call_target="tpu_custom_call" | custom-call | flops 1811939328 | bytes 4718592 | tf_op jit(solution)/shard_map/project_first/pallas_call | solution.py:467
  109.4 5.3 %project_second.1 = bf16[8,2,2,192,384]{4,3,2,1,0:T(8,128)(2,1)} custom-call(s32[2]{0:T(128)S(1)} %copy-done.4, s32[2]{0:T(128)S(1)} %copy-done.5, bf16[8,2,192,384]{3,2,1,0:T(8,128)(2,1)S(1)} %bitcast.16, bf16[8,2,192,512]{3,2,1,0:T(8,128)(2,1)S(1)} %project_first.1.first_ref, bf16[96,768]{1,0:T(8,128)(2,1)S(1)} %collective-permute-done.30.refs_0_, ...), custom_call_target="tpu_custom_call" | custom-call | flops 1811939328 | bytes 7077888 | tf_op jit(solution)/shard_map/project_second/pallas_call | solution.py:483
  (71 shorter events, 21.0 us)
Async XLA Ops:
  2.5 11.3 %collective-permute-start = (bf16[600,128]{1,0:T(8,128)(2,1)S(1)}, bf16[600,128]{1,0:T(8,128)(2,1)S(1)}, u32[]{:S(2)}, u32[]{:S(2)}) collective-permute-start(bf16[600,128]{1,0:T(8,128)(2,1)S(1)} %get-tuple-element.41.refs_0_), channel_id=1, source_target_pairs={{12,0},{14,2},{0,4},{2,6},{4,8},{6,10},{8,12},{10,14},{13,1},{15,3... | collective-permute-start | bytes 460808 | tf_op jit(solution)/shard_map/ppermute | solution.py:505
  5.6 16.2 %collective-permute-start.1 = (bf16[600,128]{1,0:T(8,128)(2,1)S(1)}, bf16[600,128]{1,0:T(8,128)(2,1)S(1)}, u32[]{:S(2)}, u32[]{:S(2)}) collective-permute-start(bf16[600,128]{1,0:T(8,128)(2,1)S(1)} %get-tuple-element.42), channel_id=1, source_target_pairs={{8,0},{10,2},{12,4},{14,6},{0,8},{2,10},{4,12},{6,14},{9,1},{11,3}... | collective-permute-start | bytes 460808 | tf_op jit(solution)/shard_map/ppermute | solution.py:505
  8.2 13.6 %collective-permute-start.2 = (bf16[600,128]{1,0:T(8,128)(2,1)S(1)}, bf16[600,128]{1,0:T(8,128)(2,1)S(1)}, u32[]{:S(2)}, u32[]{:S(2)}) collective-permute-start(bf16[600,128]{1,0:T(8,128)(2,1)S(1)} %get-tuple-element.43), channel_id=1, source_target_pairs={{4,0},{6,2},{8,4},{10,6},{12,8},{14,10},{0,12},{2,14},{5,1},{7,3},... | collective-permute-start | bytes 460808 | tf_op jit(solution)/shard_map/ppermute | solution.py:505
  12.5 21.5 %collective-permute-start.6 = (bf16[384,128]{1,0:T(8,128)(2,1)S(1)}, bf16[384,128]{1,0:T(8,128)(2,1)S(1)}, u32[]{:S(2)}, u32[]{:S(2)}) collective-permute-start(bf16[384,128]{1,0:T(8,128)(2,1)S(1)} %get-tuple-element.48.refs_1_), channel_id=1, source_target_pairs={{12,0},{14,2},{0,4},{2,6},{4,8},{6,10},{8,12},{10,14},{13,1},{15,3... | collective-permute-start | bytes 294920 | tf_op jit(solution)/shard_map/ppermute | solution.py:505
  13.2 22.2 %collective-permute-start.7 = (bf16[384,128]{1,0:T(8,128)(2,1)S(1)}, bf16[384,128]{1,0:T(8,128)(2,1)S(1)}, u32[]{:S(2)}, u32[]{:S(2)}) collective-permute-start(bf16[384,128]{1,0:T(8,128)(2,1)S(1)} %get-tuple-element.49), channel_id=1, source_target_pairs={{8,0},{10,2},{12,4},{14,6},{0,8},{2,10},{4,12},{6,14},{9,1},{11,3}... | collective-permute-start | bytes 294920 | tf_op jit(solution)/shard_map/ppermute | solution.py:505
  13.9 24.5 %collective-permute-start.8 = (bf16[384,128]{1,0:T(8,128)(2,1)S(1)}, bf16[384,128]{1,0:T(8,128)(2,1)S(1)}, u32[]{:S(2)}, u32[]{:S(2)}) collective-permute-start(bf16[384,128]{1,0:T(8,128)(2,1)S(1)} %get-tuple-element.50), channel_id=1, source_target_pairs={{4,0},{6,2},{8,4},{10,6},{12,8},{14,10},{0,12},{2,14},{5,1},{7,3},... | collective-permute-start | bytes 294920 | tf_op jit(solution)/shard_map/ppermute | solution.py:505
  27.2 17.1 %collective-permute-start.3 = (bf16[6,64,128]{2,1,0:T(8,128)(2,1)S(1)}, bf16[6,64,128]{2,1,0:T(8,128)(2,1)S(1)}, u32[]{:S(2)}, u32[]{:S(2)}) collective-permute-start(bf16[6,64,128]{2,1,0:T(8,128)(2,1)S(1)} %get-tuple-element.45), channel_id=1, source_target_pairs={{4,0},{6,2},{8,4},{10,6},{12,8},{14,10},{0,12},{2,14},{5,1},{7,3},... | collective-permute-start | bytes 294920 | tf_op jit(solution)/shard_map/ppermute | solution.py:505
  34.0 14.7 %collective-permute-start.4 = (bf16[6,64,128]{2,1,0:T(8,128)(2,1)S(1)}, bf16[6,64,128]{2,1,0:T(8,128)(2,1)S(1)}, u32[]{:S(2)}, u32[]{:S(2)}) collective-permute-start(bf16[6,64,128]{2,1,0:T(8,128)(2,1)S(1)} %get-tuple-element.46), channel_id=1, source_target_pairs={{8,0},{10,2},{12,4},{14,6},{0,8},{2,10},{4,12},{6,14},{9,1},{11,3}... | collective-permute-start | bytes 294920 | tf_op jit(solution)/shard_map/ppermute | solution.py:505
  34.0 14.7 %collective-permute-start.5 = (bf16[6,64,128]{2,1,0:T(8,128)(2,1)S(1)}, bf16[6,64,128]{2,1,0:T(8,128)(2,1)S(1)}, u32[]{:S(2)}, u32[]{:S(2)}) collective-permute-start(bf16[6,64,128]{2,1,0:T(8,128)(2,1)S(1)} %get-tuple-element.47), channel_id=1, source_target_pairs={{12,0},{14,2},{0,4},{2,6},{4,8},{6,10},{8,12},{10,14},{13,1},{15,3... | collective-permute-start | bytes 294920 | tf_op jit(solution)/shard_map/ppermute | solution.py:505
  35.4 14.3 %collective-permute-start.12 = (bf16[384,128]{1,0:T(8,128)(2,1)S(1)}, bf16[384,128]{1,0:T(8,128)(2,1)S(1)}, u32[]{:S(2)}, u32[]{:S(2)}) collective-permute-start(bf16[384,128]{1,0:T(8,128)(2,1)S(1)} %get-tuple-element.56), channel_id=1, source_target_pairs={{12,0},{14,2},{0,4},{2,6},{4,8},{6,10},{8,12},{10,14},{13,1},{15,3... | collective-permute-start | bytes 294920 | tf_op jit(solution)/shard_map/ppermute | solution.py:505
  38.3 14.5 %collective-permute-start.13 = (bf16[384,128]{1,0:T(8,128)(2,1)S(1)}, bf16[384,128]{1,0:T(8,128)(2,1)S(1)}, u32[]{:S(2)}, u32[]{:S(2)}) collective-permute-start(bf16[384,128]{1,0:T(8,128)(2,1)S(1)} %get-tuple-element.57), channel_id=1, source_target_pairs={{8,0},{10,2},{12,4},{14,6},{0,8},{2,10},{4,12},{6,14},{9,1},{11,3}... | collective-permute-start | bytes 294920 | tf_op jit(solution)/shard_map/ppermute | solution.py:505
  44.3 11.2 %collective-permute-start.14 = (bf16[384,128]{1,0:T(8,128)(2,1)S(1)}, bf16[384,128]{1,0:T(8,128)(2,1)S(1)}, u32[]{:S(2)}, u32[]{:S(2)}) collective-permute-start(bf16[384,128]{1,0:T(8,128)(2,1)S(1)} %get-tuple-element.58), channel_id=1, source_target_pairs={{4,0},{6,2},{8,4},{10,6},{12,8},{14,10},{0,12},{2,14},{5,1},{7,3},... | collective-permute-start | bytes 294920 | tf_op jit(solution)/shard_map/ppermute | solution.py:505
  48.7 12.1 %collective-permute-start.10 = (bf16[6,64,128]{2,1,0:T(8,128)(2,1)S(1)}, bf16[6,64,128]{2,1,0:T(8,128)(2,1)S(1)}, u32[]{:S(2)}, u32[]{:S(2)}) collective-permute-start(bf16[6,64,128]{2,1,0:T(8,128)(2,1)S(1)} %get-tuple-element.54), channel_id=1, source_target_pairs={{8,0},{10,2},{12,4},{14,6},{0,8},{2,10},{4,12},{6,14},{9,1},{11,3}... | collective-permute-start | bytes 294920 | tf_op jit(solution)/shard_map/ppermute | solution.py:505
  48.7 14.4 %collective-permute-start.11 = (bf16[6,64,128]{2,1,0:T(8,128)(2,1)S(1)}, bf16[6,64,128]{2,1,0:T(8,128)(2,1)S(1)}, u32[]{:S(2)}, u32[]{:S(2)}) collective-permute-start(bf16[6,64,128]{2,1,0:T(8,128)(2,1)S(1)} %get-tuple-element.55), channel_id=1, source_target_pairs={{12,0},{14,2},{0,4},{2,6},{4,8},{6,10},{8,12},{10,14},{13,1},{15,3... | collective-permute-start | bytes 294920 | tf_op jit(solution)/shard_map/ppermute | solution.py:505
  49.8 22.2 %collective-permute-start.18 = (bf16[4,2,16,1536]{3,2,1,0:T(8,128)(2,1)S(1)}, bf16[4,2,16,1536]{3,2,1,0:T(8,128)(2,1)S(1)}, u32[]{:S(2)}, u32[]{:S(2)}) collective-permute-start(bf16[4,2,16,1536]{3,2,1,0:T(8,128)(2,1)S(1)} %get-tuple-element.52.refs_0_), channel_id=1, source_target_pairs={{2,0},{0,2},{6,4},{4,6},{10,8},{8,10},{14,12},{12,14},{3,1},{1,3},... | collective-permute-start | bytes 1179656 | tf_op jit(solution)/shard_map/ppermute | solution.py:505
  52.8 10.6 %collective-permute-start.9 = (bf16[6,64,128]{2,1,0:T(8,128)(2,1)S(1)}, bf16[6,64,128]{2,1,0:T(8,128)(2,1)S(1)}, u32[]{:S(2)}, u32[]{:S(2)}) collective-permute-start(bf16[6,64,128]{2,1,0:T(8,128)(2,1)S(1)} %get-tuple-element.53), channel_id=1, source_target_pairs={{4,0},{6,2},{8,4},{10,6},{12,8},{14,10},{0,12},{2,14},{5,1},{7,3},... | collective-permute-start | bytes 294920 | tf_op jit(solution)/shard_map/ppermute | solution.py:505
  60.8 7.5 %collective-permute-start.16 = (bf16[6,64,128]{2,1,0:T(8,128)(2,1)S(1)}, bf16[6,64,128]{2,1,0:T(8,128)(2,1)S(1)}, u32[]{:S(2)}, u32[]{:S(2)}) collective-permute-start(bf16[6,64,128]{2,1,0:T(8,128)(2,1)S(1)} %get-tuple-element.63), channel_id=1, source_target_pairs={{8,0},{10,2},{12,4},{14,6},{0,8},{2,10},{4,12},{6,14},{9,1},{11,3}... | collective-permute-start | bytes 294920 | tf_op jit(solution)/shard_map/ppermute | solution.py:505
  63.1 6.4 %collective-permute-start.17 = (bf16[6,64,128]{2,1,0:T(8,128)(2,1)S(1)}, bf16[6,64,128]{2,1,0:T(8,128)(2,1)S(1)}, u32[]{:S(2)}, u32[]{:S(2)}) collective-permute-start(bf16[6,64,128]{2,1,0:T(8,128)(2,1)S(1)} %get-tuple-element.64), channel_id=1, source_target_pairs={{12,0},{14,2},{0,4},{2,6},{4,8},{6,10},{8,12},{10,14},{13,1},{15,3... | collective-permute-start | bytes 294920 | tf_op jit(solution)/shard_map/ppermute | solution.py:505
  64.3 14.0 %collective-permute-start.22 = (bf16[4,2,16,1536]{3,2,1,0:T(8,128)(2,1)S(1)}, bf16[4,2,16,1536]{3,2,1,0:T(8,128)(2,1)S(1)}, u32[]{:S(2)}, u32[]{:S(2)}) collective-permute-start(bf16[4,2,16,1536]{3,2,1,0:T(8,128)(2,1)S(1)} %get-tuple-element.61.refs_1_), channel_id=1, source_target_pairs={{2,0},{0,2},{6,4},{4,6},{10,8},{8,10},{14,12},{12,14},{3,1},{1,3},... | collective-permute-start | bytes 1179656 | tf_op jit(solution)/shard_map/ppermute | solution.py:505
  70.4 10.1 %collective-permute-start.23 = (bf16[4,2,16,1536]{3,2,1,0:T(8,128)(2,1)S(1)}, bf16[4,2,16,1536]{3,2,1,0:T(8,128)(2,1)S(1)}, u32[]{:S(2)}, u32[]{:S(2)}) collective-permute-start(bf16[4,2,16,1536]{3,2,1,0:T(8,128)(2,1)S(1)} %get-tuple-element.66.refs_2_), channel_id=1, source_target_pairs={{2,0},{0,2},{6,4},{4,6},{10,8},{8,10},{14,12},{12,14},{3,1},{1,3},... | collective-permute-start | bytes 1179656 | tf_op jit(solution)/shard_map/ppermute | solution.py:505
  74.5 11.8 %collective-permute-start.19 = (bf16[64,768]{1,0:T(8,128)(2,1)S(1)}, bf16[64,768]{1,0:T(8,128)(2,1)S(1)}, u32[]{:S(2)}, u32[]{:S(2)}) collective-permute-start(bf16[64,768]{1,0:T(8,128)(2,1)S(1)} %get-tuple-element.69), channel_id=1, source_target_pairs={{12,0},{14,2},{0,4},{2,6},{4,8},{6,10},{8,12},{10,14},{13,1},{15,3... | collective-permute-start | bytes 294920 | tf_op jit(solution)/shard_map/ppermute | solution.py:505
  74.5 12.1 %collective-permute-start.20 = (bf16[64,768]{1,0:T(8,128)(2,1)S(1)}, bf16[64,768]{1,0:T(8,128)(2,1)S(1)}, u32[]{:S(2)}, u32[]{:S(2)}) collective-permute-start(bf16[64,768]{1,0:T(8,128)(2,1)S(1)} %get-tuple-element.70), channel_id=1, source_target_pairs={{8,0},{10,2},{12,4},{14,6},{0,8},{2,10},{4,12},{6,14},{9,1},{11,3}... | collective-permute-start | bytes 294920 | tf_op jit(solution)/shard_map/ppermute | solution.py:505
  75.8 10.9 %collective-permute-start.21 = (bf16[64,768]{1,0:T(8,128)(2,1)S(1)}, bf16[64,768]{1,0:T(8,128)(2,1)S(1)}, u32[]{:S(2)}, u32[]{:S(2)}) collective-permute-start(bf16[64,768]{1,0:T(8,128)(2,1)S(1)} %get-tuple-element.71), channel_id=1, source_target_pairs={{4,0},{6,2},{8,4},{10,6},{12,8},{14,10},{0,12},{2,14},{5,1},{7,3},... | collective-permute-start | bytes 294920 | tf_op jit(solution)/shard_map/ppermute | solution.py:505
  82.7 6.1 %collective-permute-start.24 = (bf16[32,768]{1,0:T(8,128)(2,1)S(1)}, bf16[32,768]{1,0:T(8,128)(2,1)S(1)}, u32[]{:S(2)}, u32[]{:S(2)}) collective-permute-start(bf16[32,768]{1,0:T(8,128)(2,1)S(1)} %get-tuple-element.74), channel_id=1, source_target_pairs={{12,0},{14,2},{0,4},{2,6},{4,8},{6,10},{8,12},{10,14},{13,1},{15,3... | collective-permute-start | bytes 147464 | tf_op jit(solution)/shard_map/ppermute | solution.py:505
  83.0 6.5 %collective-permute-start.25 = (bf16[32,768]{1,0:T(8,128)(2,1)S(1)}, bf16[32,768]{1,0:T(8,128)(2,1)S(1)}, u32[]{:S(2)}, u32[]{:S(2)}) collective-permute-start(bf16[32,768]{1,0:T(8,128)(2,1)S(1)} %get-tuple-element.75), channel_id=1, source_target_pairs={{8,0},{10,2},{12,4},{14,6},{0,8},{2,10},{4,12},{6,14},{9,1},{11,3}... | collective-permute-start | bytes 147464 | tf_op jit(solution)/shard_map/ppermute | solution.py:505
  90.9 6.5 %collective-permute-start.27 = (bf16[96,768]{1,0:T(8,128)(2,1)S(1)}, bf16[96,768]{1,0:T(8,128)(2,1)S(1)}, u32[]{:S(2)}, u32[]{:S(2)}) collective-permute-start(bf16[96,768]{1,0:T(8,128)(2,1)S(1)} %add_parts.1.refs_0_), channel_id=1, source_target_pairs={{4,0},{6,2},{8,4},{10,6},{12,8},{14,10},{0,12},{2,14},{5,1},{7,3},... | collective-permute-start | bytes 442376 | tf_op jit(solution)/shard_map/ppermute | solution.py:505
  93.0 9.5 %collective-permute-start.28 = (bf16[96,768]{1,0:T(8,128)(2,1)S(1)}, bf16[96,768]{1,0:T(8,128)(2,1)S(1)}, u32[]{:S(2)}, u32[]{:S(2)}) collective-permute-start(bf16[96,768]{1,0:T(8,128)(2,1)S(1)} %add_parts.1.refs_0_), channel_id=1, source_target_pairs={{8,0},{10,2},{12,4},{14,6},{0,8},{2,10},{4,12},{6,14},{9,1},{11,3}... | collective-permute-start | bytes 442376 | tf_op jit(solution)/shard_map/ppermute | solution.py:505
  93.3 10.5 %collective-permute-start.29 = (bf16[96,768]{1,0:T(8,128)(2,1)S(1)}, bf16[96,768]{1,0:T(8,128)(2,1)S(1)}, u32[]{:S(2)}, u32[]{:S(2)}) collective-permute-start(bf16[96,768]{1,0:T(8,128)(2,1)S(1)} %add_parts.1.refs_0_), channel_id=1, source_target_pairs={{12,0},{14,2},{0,4},{2,6},{4,8},{6,10},{8,12},{10,14},{13,1},{15,3... | collective-permute-start | bytes 442376 | tf_op jit(solution)/shard_map/ppermute | solution.py:505
  93.6 14.8 %collective-permute-start.30 = (bf16[96,768]{1,0:T(8,128)(2,1)S(1)}, bf16[96,768]{1,0:T(8,128)(2,1)S(1)}, u32[]{:S(2)}, u32[]{:S(2)}) collective-permute-start(bf16[96,768]{1,0:T(8,128)(2,1)S(1)} %add_parts.1.refs_0_), channel_id=1, source_target_pairs={{2,0},{0,2},{6,4},{4,6},{10,8},{8,10},{14,12},{12,14},{3,1},{1,3},... | collective-permute-start | bytes 442376 | tf_op jit(solution)/shard_map/ppermute | solution.py:505
  97.4 11.0 %collective-permute-start.31 = (bf16[96,768]{1,0:T(8,128)(2,1)S(1)}, bf16[96,768]{1,0:T(8,128)(2,1)S(1)}, u32[]{:S(2)}, u32[]{:S(2)}) collective-permute-start(bf16[96,768]{1,0:T(8,128)(2,1)S(1)} %collective-permute-done.27.refs_1_), channel_id=1, source_target_pairs={{2,0},{0,2},{6,4},{4,6},{10,8},{8,10},{14,12},{12,14},{3,1},{1,3},... | collective-permute-start | bytes 442376 | tf_op jit(solution)/shard_map/ppermute | solution.py:505
  102.5 6.0 %collective-permute-start.32 = (bf16[96,768]{1,0:T(8,128)(2,1)S(1)}, bf16[96,768]{1,0:T(8,128)(2,1)S(1)}, u32[]{:S(2)}, u32[]{:S(2)}) collective-permute-start(bf16[96,768]{1,0:T(8,128)(2,1)S(1)} %collective-permute-done.28.refs_2_), channel_id=1, source_target_pairs={{2,0},{0,2},{6,4},{4,6},{10,8},{8,10},{14,12},{12,14},{3,1},{1,3},... | collective-permute-start | bytes 442376 | tf_op jit(solution)/shard_map/ppermute | solution.py:505
  103.8 5.6 %collective-permute-start.33 = (bf16[96,768]{1,0:T(8,128)(2,1)S(1)}, bf16[96,768]{1,0:T(8,128)(2,1)S(1)}, u32[]{:S(2)}, u32[]{:S(2)}) collective-permute-start(bf16[96,768]{1,0:T(8,128)(2,1)S(1)} %collective-permute-done.29.refs_3_), channel_id=1, source_target_pairs={{2,0},{0,2},{6,4},{4,6},{10,8},{8,10},{14,12},{12,14},{3,1},{1,3},... | collective-permute-start | bytes 442376 | tf_op jit(solution)/shard_map/ppermute | solution.py:505
  (9 other events, 106.1 us)

commit v5 on v4

--- a/solution.py
+++ b/solution.py
@@ -118,12 +118,12 @@
             out[c * rows : (c + 1) * rows] = own_ref[c, pl.ds(start, rows), :].astype(jnp.bfloat16)
 
 
-def first_pack_kernel(sites, place_ref, own_ref, links_ref, *refs):
+def first_pack_kernel(sites, own_ref, links_ref, *refs):
     outs, block_ref, link_ref, sems = refs[: sites - 1], refs[sites - 1], refs[sites], refs[sites + 1]
     rows = CHUNKS[0] * 4
     copies = [pltpu.make_async_copy(links_ref, link_ref, sems.at[0])]
     for d in range(1, sites):
-        start = row_of(lax.rem(place_ref[0] + d, sites), own_ref.shape[1] // sites, 0)
+        start = row_of(lax.rem(lax.axis_index("site") + d, sites), own_ref.shape[1] // sites, 0)
         copies.append(pltpu.make_async_copy(own_ref.at[:, pl.ds(start, rows), :], block_ref.at[d - 1], sems.at[d]))
     for copy in copies:
         copy.start()
@@ -136,12 +136,12 @@
         outs[d - 1][6 * rows :] = links
 
 
-def first_pack(own, place, sites, links):
+def first_pack(own, sites, links):
     rows = CHUNKS[0] * 4
     return pl.pallas_call(
         functools.partial(first_pack_kernel, sites),
         out_shape=[pltpu.VMEM((6 * rows + links.shape[0], LANES), jnp.bfloat16)] * (sites - 1),
-        in_specs=[SMEM, HBM, HBM],
+        in_specs=[HBM, HBM],
         out_specs=[VMEM] * (sites - 1),
         scratch_shapes=[
             pltpu.VMEM((sites - 1, 6, rows, LANES), jnp.float32),
@@ -150,7 +150,7 @@
         ],
         compiler_params=pltpu.CompilerParams(vmem_limit_bytes=66 * 10**6),
         name="pack0",
-    )(place, own, links)
+    )(own, links)
 
 
 def row_of(slot, rows_per_slot, chunk):
@@ -391,18 +391,18 @@
 
 def fill_right(right_ref, pieces, across, place_ref, owner_ref):
     sites = len(pieces)
-    momenta, nvec = right_ref.shape[0], right_ref.shape[1] // 2
+    nvec = right_ref.shape[0] // 2
+    momenta = right_ref.shape[1] // (3 * LANES)
     block = nvec // 2
     half = block - LANES
     rows = block // sites
     v = lax.rem(place_ref[1] + across, 2)
     leads = owner_ref[v] == 0
 
-    def tiles(value):
-        zeros = jnp.zeros((value.shape[0], LANES - half), value.dtype)
-        first = jnp.concatenate([value[:, :LANES], value[:, LANES:], zeros], axis=1)
-        second = jnp.concatenate([value[:, half:], zeros, value[:, :half]], axis=1)
-        return jnp.where(leads, first, second)
+    def tiles(re, im):
+        lead = (re[:, :LANES], im[:, :LANES], jnp.concatenate([re[:, LANES:], im[:, LANES:]], axis=1))
+        other = (re[:, half:], im[:, half:], jnp.concatenate([im[:, :half], re[:, :half]], axis=1))
+        return [jnp.where(leads, x, y) for x, y in zip(lead, other)]
 
     for up, piece in enumerate(pieces):
         z = lax.rem(place_ref[0] + up, sites)
@@ -411,11 +411,12 @@
             low = pl.multiple_of(nvec + owner * block + z * rows, 16)
             for p in range(momenta):
                 value = piece[part * rows : (part + 1) * rows, p * 2 * block : (p + 1) * 2 * block]
-                re, im = tiles(value[:, :block]), tiles(value[:, block:])
-                right_ref[p, pl.ds(row, rows), : 2 * LANES] = re
-                right_ref[p, pl.ds(row, rows), 2 * LANES :] = im
-                right_ref[p, pl.ds(low, rows), : 2 * LANES] = -im
-                right_ref[p, pl.ds(low, rows), 2 * LANES :] = re
+                re, im = value[:, :block], value[:, block:]
+                for at, (first, second, ends) in ((row, tiles(re, im)), (low, tiles(-im, re))):
+                    right_ref[pl.ds(at, rows), 2 * p * LANES : (2 * p + 1) * LANES] = first
+                    right_ref[pl.ds(at, rows), (2 * p + 1) * LANES : (2 * p + 2) * LANES] = second
+                    last = (2 * momenta + p) * LANES
+                    right_ref[pl.ds(at, rows), last : last + LANES] = ends
 
 
 def pair_of(tau_ref, n):
@@ -426,16 +427,14 @@
 def first_kernel(sites, place_ref, owner_ref, tau_ref, *refs):
     pieces, (out_ref, right_ref) = refs[:sites], refs[sites:]
     fill_right(right_ref, pieces, 0, place_ref, owner_ref)
+    rows = tau_ref.shape[2]
 
     def step(n, carry):
-        left = pair_of(tau_ref, 2 * n)
-        for p in range(right_ref.shape[0]):
-            product = jnp.dot(left, right_ref[p], preferred_element_type=jnp.float32).astype(jnp.bfloat16)
-            for k in range(2):
-                out_ref[2 * n + k, p] = product[k * rows : (k + 1) * rows]
+        product = jnp.dot(pair_of(tau_ref, 2 * n), right_ref[...], preferred_element_type=jnp.float32)
+        for k in range(2):
+            out_ref[2 * n + k] = product[k * rows : (k + 1) * rows].astype(jnp.bfloat16)
         return carry
 
-    rows = tau_ref.shape[2]
     lax.fori_loop(0, tau_ref.shape[0] // 2, step, 0)
 
 
@@ -447,29 +446,36 @@
         fill_right(right_ref, pieces, 1, place_ref, owner_ref)
 
     leads = owner_ref[place_ref[1]] == 0
-    left = pair_of(tau_ref, 0)
     rows = tau_ref.shape[2]
-    for p in range(right_ref.shape[0]):
-        both = jnp.dot(left, right_ref[p], preferred_element_type=jnp.float32).astype(jnp.bfloat16)
-        for k in range(2):
-            product = both[k * rows : (k + 1) * rows]
+    momenta = out_ref.shape[1]
+    lower = lax.broadcasted_iota(jnp.int32, (rows, LANES), 1) < LANES // 2
+    both = jnp.dot(pair_of(tau_ref, 0), right_ref[...], preferred_element_type=jnp.float32)
+    for k in range(2):
+
+        def ordered(tile):
+            mine = first_ref[k, :, tile * LANES : (tile + 1) * LANES].astype(jnp.float32)
+            theirs = both[k * rows : (k + 1) * rows, tile * LANES : (tile + 1) * LANES]
+            return jnp.where(leads, mine, theirs), jnp.where(leads, theirs, mine)
+
+        for p in range(momenta):
+            low_ends, high_ends = ordered(2 * momenta + p)
+            middles = (jnp.where(lower, low_ends, high_ends),
+                       pltpu.roll(jnp.where(lower, high_ends, low_ends), LANES // 2, 1))
             for c in range(2):
-                at = 2 * c * LANES
-                mine, theirs = first_ref[k, p, :, at : at + LANES], product[:, at : at + LANES]
-                middle = first_ref[k, p, :, at + LANES : at + 2 * LANES] + product[:, at + LANES : at + 2 * LANES]
-                out_ref[k, p, c, :, :LANES] = jnp.where(leads, mine, theirs)
-                out_ref[k, p, c, :, LANES : 2 * LANES] = middle
-                out_ref[k, p, c, :, 2 * LANES :] = jnp.where(leads, theirs, mine)
+                low, high = ordered(2 * p + c)
+                out_ref[k, p, c, :, :LANES] = low.astype(jnp.bfloat16)
+                out_ref[k, p, c, :, LANES : 2 * LANES] = middles[c].astype(jnp.bfloat16)
+                out_ref[k, p, c, :, 2 * LANES :] = high.astype(jnp.bfloat16)
 
 
 def project_first(tau, place, owner, pieces, momenta):
     outer, _, rows, nvec = tau.shape
     return pl.pallas_call(
         functools.partial(first_kernel, len(pieces)),
-        out_shape=pltpu.VMEM((outer, momenta, rows, 4 * LANES), jnp.bfloat16),
+        out_shape=pltpu.VMEM((outer, rows, momenta * 3 * LANES), jnp.bfloat16),
         in_specs=[SMEM, SMEM] + [VMEM] * (1 + len(pieces)),
         out_specs=VMEM,
-        scratch_shapes=[pltpu.VMEM((momenta, 2 * nvec, 4 * LANES), jnp.bfloat16)],
+        scratch_shapes=[pltpu.VMEM((2 * nvec, momenta * 3 * LANES), jnp.bfloat16)],
         cost_estimate=pl.CostEstimate(
             flops=2 * outer * rows * 2 * nvec * nvec * momenta, bytes_accessed=outer * rows * nvec * 8,
             transcendentals=0),
@@ -485,9 +491,9 @@
         grid=(outer // 2,),
         out_shape=jax.ShapeDtypeStruct((outer, momenta, 2, rows, nvec), jnp.bfloat16),
         in_specs=[SMEM, SMEM, pl.BlockSpec((2, 2, rows, nvec), lambda i: (i, 0, 0, 0)),
-                  pl.BlockSpec((2, *first.shape[1:]), lambda i: (i, 0, 0, 0))] + [VMEM] * len(pieces),
+                  pl.BlockSpec((2, *first.shape[1:]), lambda i: (i, 0, 0))] + [VMEM] * len(pieces),
         out_specs=pl.BlockSpec((2, momenta, 2, rows, nvec), lambda i: (i, 0, 0, 0, 0)),
-        scratch_shapes=[pltpu.VMEM((momenta, 2 * nvec, 4 * LANES), jnp.bfloat16)],
+        scratch_shapes=[pltpu.VMEM((2 * nvec, momenta * 3 * LANES), jnp.bfloat16)],
         cost_estimate=pl.CostEstimate(
             flops=2 * outer * rows * 2 * nvec * nvec * momenta, bytes_accessed=outer * rows * nvec * 12,
             transcendentals=0),
@@ -522,7 +528,7 @@
         if chunk == 2:
             after = [received[0][0], packed[0]]
         if chunk == 0:
-            packed = first_pack(own, place, sites, own_links)
+            packed = first_pack(own, sites, own_links)
         else:
             packed = pack(own, place, chunk, sites, after)
         received.append([from_place(packed[d - 1], -d, 0) for d in range(1, sites)])
@@ -708,7 +714,7 @@
     block, layers, plane = eigvecs.shape[3:]
     sites, groups = lax.axis_size("site"), lax.axis_size("vec")
     fits = layers == 1 and plane == LX * LY == 4 * LANES and sites == 4 and groups == 2
-    fits = fits and block == sites * sum(CHUNKS) and LANES < block < 2 * LANES
+    fits = fits and block == sites * sum(CHUNKS) and 2 * block == 3 * LANES
     fits = fits and peramb.shape[1] * peramb.shape[2] % 2 == 0 and (2 * block) % (32 * sites) == 0 and block % (2 * block // sites) == 0
     device = per_device if fits else general_device
     return device(eigvecs, links, peramb, block_owner, momenta)

time: 115 us -> 115 us (level)
    unnamed x14 -> x12, local copies, waits for them, and re-layouts: 2.35 us -> 1.68 us
  transfers between devices with their start and end apart: 34 -> 34, of which waited for: 13 -> 13; matrix products, arithmetic and copies ran while one was open for 0% -> 1% of each run, Pallas kernels for 24% -> 25%
where the time goes in v5:
time: 115 us
  starting transfers between devices  48.9 us (43%)
  Pallas kernels  36 us (31%)
  waiting for transfers between devices  27.1 us (24%)
  local copies, waits for them, and re-layouts  1.85 us (2%)
    ppermute x34, starting transfers between devices, from_place(): return lax.ppermute(block, ('site', 'vec'), route)  48.9 us
    ppermute x34, waiting for transfers between devices, from_place(): return lax.ppermute(block, ('site', 'vec'), route)  27.1 us
    pallas_call x3, Pallas kernels, filter_chunk(): pl.pallas_call(functools.partial(filter_kernel, sites, chunk), out_shape=...  15.2 us
    pallas_call x1, Pallas kernels, project_second(): pl.pallas_call(functools.partial(second_kernel, len(pieces)), grid=(outer...  6.36 us
    pallas_call x2, Pallas kernels, elementals(): pl.pallas_call(functools.partial(early_kernel if early else late_kernel,...  4.55 us
    pallas_call x1, Pallas kernels, project_first(): pl.pallas_call(functools.partial(first_kernel, len(pieces)), out_shape=pl...  4.47 us
    pallas_call x3, Pallas kernels, finish(): pl.pallas_call(functools.partial(finish_kernel, sites, chunk), out_shape=...  2.67 us
  transfers between devices with their start and end apart: 34, of which 13 were waited for; matrix products, arithmetic and copies ran while one was open for 1% of the time, Pallas kernels for 25%

profile of v5, /device:TPU:0, one launch (start us, length us, event | category | flops | bytes accessed | tf_op | source)
XLA Modules:
  0.0 114.5 jit_solution(12869021445151044486)
XLA Ops:
  1.3 3.1 %collective-permute-start = (bf16[600,128]{1,0:T(8,128)(2,1)S(1)}, bf16[600,128]{1,0:T(8,128)(2,1)S(1)}, u32[]{:S(2)}, u32[]{:S(2)}) collective-permute-start(bf16[600,128]{1,0:T(8,128)(2,1)S(1)} %get-tuple-element.41.refs_0_), channel_id=1, source_target_pairs={{12,0},{14,2},{0,4},{2,6},{4,8},{6,10},{8,12},{10,14},{13,1},{15,3... | collective-permute-start | bytes 460808 | tf_op jit(solution)/shard_map/ppermute | solution.py:511
  4.4 2.6 %collective-permute-start.1 = (bf16[600,128]{1,0:T(8,128)(2,1)S(1)}, bf16[600,128]{1,0:T(8,128)(2,1)S(1)}, u32[]{:S(2)}, u32[]{:S(2)}) collective-permute-start(bf16[600,128]{1,0:T(8,128)(2,1)S(1)} %get-tuple-element.42), channel_id=1, source_target_pairs={{8,0},{10,2},{12,4},{14,6},{0,8},{2,10},{4,12},{6,14},{9,1},{11,3}... | collective-permute-start | bytes 460808 | tf_op jit(solution)/shard_map/ppermute | solution.py:511
  8.4 1.7 %copy-done = f32[1,2,3,192,1,512]{5,4,3,2,1,0:T(1,128)S(1)} copy-done((f32[1,2,3,192,1,512]{5,4,3,2,1,0:T(1,128)S(1)}, f32[1,2,3,192,1,512]{5,4,3,2,1,0:T(1,128)}, u32[]{:S(2)}) %copy-start) | copy-done | bytes 2359320
  12.0 2.9 %collective-permute-start.8 = (bf16[384,128]{1,0:T(8,128)(2,1)S(1)}, bf16[384,128]{1,0:T(8,128)(2,1)S(1)}, u32[]{:S(2)}, u32[]{:S(2)}) collective-permute-start(bf16[384,128]{1,0:T(8,128)(2,1)S(1)} %get-tuple-element.50), channel_id=1, source_target_pairs={{4,0},{6,2},{8,4},{10,6},{12,8},{14,10},{0,12},{2,14},{5,1},{7,3},... | collective-permute-start | bytes 294920 | tf_op jit(solution)/shard_map/ppermute | solution.py:511
  14.9 5.7 %collective-permute-done.1.refs_2_ = bf16[600,128]{1,0:T(8,128)(2,1)S(1)} collective-permute-done((bf16[600,128]{1,0:T(8,128)(2,1)S(1)}, bf16[600,128]{1,0:T(8,128)(2,1)S(1)}, u32[]{:S(2)}, u32[]{:S(2)}) %collective-permute-start.1) | collective-permute-done | bytes 153632 | tf_op jit(solution)/shard_map/ppermute | solution.py:511
  20.9 5.1 %shard_map.55 = (bf16[6,64,128]{2,1,0:T(8,128)(2,1)S(1)}, bf16[6,64,128]{2,1,0:T(8,128)(2,1)S(1)}, bf16[6,64,128]{2,1,0:T(8,128)(2,1)S(1)}, bf16[6,64,128]{2,1,0:T(8,128)(2,1)S(1)}) custom-call(s32[2]{0:T(128)S(1)} %pad_add_fusion.place_ref, f32[6,768,128]{2,1,0:T(8,128)S(1)} %bitcast.8, bf16[600,128]{1,0:T(8,128)(2,1)S(1)} %collective-permute-done.refs_1_.refs_0_, ...), custom_call_target="tpu_custom_call" | custom-call | flops 28311552 | bytes 786432 | tf_op jit(solution)/shard_map/pallas_call | solution.py:238
  26.0 6.8 %collective-permute-start.3 = (bf16[6,64,128]{2,1,0:T(8,128)(2,1)S(1)}, bf16[6,64,128]{2,1,0:T(8,128)(2,1)S(1)}, u32[]{:S(2)}, u32[]{:S(2)}) collective-permute-start(bf16[6,64,128]{2,1,0:T(8,128)(2,1)S(1)} %get-tuple-element.45), channel_id=1, source_target_pairs={{4,0},{6,2},{8,4},{10,6},{12,8},{14,10},{0,12},{2,14},{5,1},{7,3},... | collective-permute-start | bytes 294920 | tf_op jit(solution)/shard_map/ppermute | solution.py:511
  34.2 2.9 %collective-permute-start.12 = (bf16[384,128]{1,0:T(8,128)(2,1)S(1)}, bf16[384,128]{1,0:T(8,128)(2,1)S(1)}, u32[]{:S(2)}, u32[]{:S(2)}) collective-permute-start(bf16[384,128]{1,0:T(8,128)(2,1)S(1)} %get-tuple-element.56), channel_id=1, source_target_pairs={{12,0},{14,2},{0,4},{2,6},{4,8},{6,10},{8,12},{10,14},{13,1},{15,3... | collective-permute-start | bytes 294920 | tf_op jit(solution)/shard_map/ppermute | solution.py:511
  38.0 5.1 %shard_map.57 = (bf16[6,64,128]{2,1,0:T(8,128)(2,1)S(1)}, bf16[6,64,128]{2,1,0:T(8,128)(2,1)S(1)}, bf16[6,64,128]{2,1,0:T(8,128)(2,1)S(1)}, bf16[6,64,128]{2,1,0:T(8,128)(2,1)S(1)}) custom-call(s32[2]{0:T(128)S(1)} %pad_add_fusion.place_ref, f32[6,768,128]{2,1,0:T(8,128)S(1)} %bitcast.10, bf16[384,128]{1,0:T(8,128)(2,1)S(1)} %collective-permute-done.6.refs_1_, ...), custom_call_target="tpu_custom_call" | custom-call | flops 28311552 | bytes 786432 | tf_op jit(solution)/shard_map/pallas_call | solution.py:238
  43.0 1.6 %collective-permute-start.14 = (bf16[384,128]{1,0:T(8,128)(2,1)S(1)}, bf16[384,128]{1,0:T(8,128)(2,1)S(1)}, u32[]{:S(2)}, u32[]{:S(2)}) collective-permute-start(bf16[384,128]{1,0:T(8,128)(2,1)S(1)} %get-tuple-element.58), channel_id=1, source_target_pairs={{4,0},{6,2},{8,4},{10,6},{12,8},{14,10},{0,12},{2,14},{5,1},{7,3},... | collective-permute-start | bytes 294920 | tf_op jit(solution)/shard_map/ppermute | solution.py:511
  44.6 2.8 %collective-permute-done.4.refs_2_ = bf16[6,64,128]{2,1,0:T(8,128)(2,1)S(1)} collective-permute-done((bf16[6,64,128]{2,1,0:T(8,128)(2,1)S(1)}, bf16[6,64,128]{2,1,0:T(8,128)(2,1)S(1)}, u32[]{:S(2)}, u32[]{:S(2)}) %collective-permute-start.4) | collective-permute-done | bytes 98336 | tf_op jit(solution)/shard_map/ppermute | solution.py:511
  48.5 1.6 %collective-permute-start.18 = (bf16[4,2,16,1536]{3,2,1,0:T(8,128)(2,1)S(1)}, bf16[4,2,16,1536]{3,2,1,0:T(8,128)(2,1)S(1)}, u32[]{:S(2)}, u32[]{:S(2)}) collective-permute-start(bf16[4,2,16,1536]{3,2,1,0:T(8,128)(2,1)S(1)} %get-tuple-element.52.refs_0_), channel_id=1, source_target_pairs={{2,0},{0,2},{6,4},{4,6},{10,8},{8,10},{14,12},{12,14},{3,1},{1,3},... | collective-permute-start | bytes 1179656 | tf_op jit(solution)/shard_map/ppermute | solution.py:511
  50.1 1.5 %collective-permute-done.13.refs_2_ = bf16[384,128]{1,0:T(8,128)(2,1)S(1)} collective-permute-done((bf16[384,128]{1,0:T(8,128)(2,1)S(1)}, bf16[384,128]{1,0:T(8,128)(2,1)S(1)}, u32[]{:S(2)}, u32[]{:S(2)}) %collective-permute-start.13) | collective-permute-done | bytes 98336 | tf_op jit(solution)/shard_map/ppermute | solution.py:511
  51.6 2.7 %collective-permute-start.9 = (bf16[6,64,128]{2,1,0:T(8,128)(2,1)S(1)}, bf16[6,64,128]{2,1,0:T(8,128)(2,1)S(1)}, u32[]{:S(2)}, u32[]{:S(2)}) collective-permute-start(bf16[6,64,128]{2,1,0:T(8,128)(2,1)S(1)} %get-tuple-element.53), channel_id=1, source_target_pairs={{4,0},{6,2},{8,4},{10,6},{12,8},{14,10},{0,12},{2,14},{5,1},{7,3},... | collective-permute-start | bytes 294920 | tf_op jit(solution)/shard_map/ppermute | solution.py:511
  54.3 5.1 %shard_map.60 = (bf16[6,64,128]{2,1,0:T(8,128)(2,1)S(1)}, bf16[6,64,128]{2,1,0:T(8,128)(2,1)S(1)}, bf16[6,64,128]{2,1,0:T(8,128)(2,1)S(1)}, bf16[6,64,128]{2,1,0:T(8,128)(2,1)S(1)}) custom-call(s32[2]{0:T(128)S(1)} %pad_add_fusion.place_ref, f32[6,768,128]{2,1,0:T(8,128)S(1)} %bitcast.12, bf16[384,128]{1,0:T(8,128)(2,1)S(1)} %collective-permute-done.12.refs_1_, ...), custom_call_target="tpu_custom_call" | custom-call | flops 28311552 | bytes 786432 | tf_op jit(solution)/shard_map/pallas_call | solution.py:238
  59.6 2.3 %collective-permute-start.16 = (bf16[6,64,128]{2,1,0:T(8,128)(2,1)S(1)}, bf16[6,64,128]{2,1,0:T(8,128)(2,1)S(1)}, u32[]{:S(2)}, u32[]{:S(2)}) collective-permute-start(bf16[6,64,128]{2,1,0:T(8,128)(2,1)S(1)} %get-tuple-element.63), channel_id=1, source_target_pairs={{8,0},{10,2},{12,4},{14,6},{0,8},{2,10},{4,12},{6,14},{9,1},{11,3}... | collective-permute-start | bytes 294920 | tf_op jit(solution)/shard_map/ppermute | solution.py:511
  63.0 1.4 %collective-permute-start.22 = (bf16[4,2,16,1536]{3,2,1,0:T(8,128)(2,1)S(1)}, bf16[4,2,16,1536]{3,2,1,0:T(8,128)(2,1)S(1)}, u32[]{:S(2)}, u32[]{:S(2)}) collective-permute-start(bf16[4,2,16,1536]{3,2,1,0:T(8,128)(2,1)S(1)} %get-tuple-element.61.refs_1_), channel_id=1, source_target_pairs={{2,0},{0,2},{6,4},{4,6},{10,8},{8,10},{14,12},{12,14},{3,1},{1,3},... | collective-permute-start | bytes 1179656 | tf_op jit(solution)/shard_map/ppermute | solution.py:511
  64.8 2.2 %collective-permute-done.16.refs_2_ = bf16[6,64,128]{2,1,0:T(8,128)(2,1)S(1)} collective-permute-done((bf16[6,64,128]{2,1,0:T(8,128)(2,1)S(1)}, bf16[6,64,128]{2,1,0:T(8,128)(2,1)S(1)}, u32[]{:S(2)}, u32[]{:S(2)}) %collective-permute-start.16) | collective-permute-done | bytes 98336 | tf_op jit(solution)/shard_map/ppermute | solution.py:511
  69.2 1.6 %collective-permute-start.23 = (bf16[4,2,16,1536]{3,2,1,0:T(8,128)(2,1)S(1)}, bf16[4,2,16,1536]{3,2,1,0:T(8,128)(2,1)S(1)}, u32[]{:S(2)}, u32[]{:S(2)}) collective-permute-start(bf16[4,2,16,1536]{3,2,1,0:T(8,128)(2,1)S(1)} %get-tuple-element.66.refs_2_), channel_id=1, source_target_pairs={{2,0},{0,2},{6,4},{4,6},{10,8},{8,10},{14,12},{12,14},{3,1},{1,3},... | collective-permute-start | bytes 1179656 | tf_op jit(solution)/shard_map/ppermute | solution.py:511
  70.7 2.5 %elementals_early.1 = (f32[64,768]{1,0:T(8,128)S(1)}, bf16[64,768]{1,0:T(8,128)(2,1)S(1)}, bf16[64,768]{1,0:T(8,128)(2,1)S(1)}, bf16[64,768]{1,0:T(8,128)(2,1)S(1)}, bf16[2,384,3072]{2,1,0:T(8,128)(2,1)S(1)}) custom-call(s32[2]{0:T(128)S(1)} %pad_add_fusion.place_ref, bf16[4,2,16,1536]{3,2,1,0:T(8,128)(2,1)S(1)} %get-tuple-element.52.refs_0_, ...), custom_call_target="tpu_custom_call" | custom-call | flops 1207959552 | bytes 2359296 | tf_op jit(solution)/shard_map/elementals_early/pallas_call | solution.py:354
  74.5 2.6 %collective-permute-start.21 = (bf16[64,768]{1,0:T(8,128)(2,1)S(1)}, bf16[64,768]{1,0:T(8,128)(2,1)S(1)}, u32[]{:S(2)}, u32[]{:S(2)}) collective-permute-start(bf16[64,768]{1,0:T(8,128)(2,1)S(1)} %get-tuple-element.71), channel_id=1, source_target_pairs={{4,0},{6,2},{8,4},{10,6},{12,8},{14,10},{0,12},{2,14},{5,1},{7,3},... | collective-permute-start | bytes 294920 | tf_op jit(solution)/shard_map/ppermute | solution.py:511
  77.1 2.2 %collective-permute-done.23.refs_1_ = bf16[4,2,16,1536]{3,2,1,0:T(8,128)(2,1)S(1)} collective-permute-done((bf16[4,2,16,1536]{3,2,1,0:T(8,128)(2,1)S(1)}, bf16[4,2,16,1536]{3,2,1,0:T(8,128)(2,1)S(1)}, u32[]{:S(2)}, u32[]{:S(2)}) %collective-permute-start.23) | collective-permute-done | bytes 393248 | tf_op jit(solution)/shard_map/ppermute | solution.py:511
  79.3 2.1 %elementals_late.1 = (f32[32,768]{1,0:T(8,128)S(1)}, bf16[32,768]{1,0:T(8,128)(2,1)S(1)}, bf16[32,768]{1,0:T(8,128)(2,1)S(1)}, bf16[32,768]{1,0:T(8,128)(2,1)S(1)}) custom-call(s32[2]{0:T(128)S(1)} %pad_add_fusion.place_ref, bf16[4,2,16,1536]{3,2,1,0:T(8,128)(2,1)S(1)} %collective-permute-done.22.refs_0_, ...), custom_call_target="tpu_custom_call" | custom-call | flops 603979776 | bytes 2359296 | tf_op jit(solution)/shard_map/elementals_late/pallas_call | solution.py:354
  81.7 3.3 %collective-permute-start.25 = (bf16[32,768]{1,0:T(8,128)(2,1)S(1)}, bf16[32,768]{1,0:T(8,128)(2,1)S(1)}, u32[]{:S(2)}, u32[]{:S(2)}) collective-permute-start(bf16[32,768]{1,0:T(8,128)(2,1)S(1)} %get-tuple-element.75), channel_id=1, source_target_pairs={{8,0},{10,2},{12,4},{14,6},{0,8},{2,10},{4,12},{6,14},{9,1},{11,3}... | collective-permute-start | bytes 147464 | tf_op jit(solution)/shard_map/ppermute | solution.py:511
  85.4 2.2 %collective-permute-done.24.refs_5_ = bf16[32,768]{1,0:T(8,128)(2,1)S(1)} collective-permute-done((bf16[32,768]{1,0:T(8,128)(2,1)S(1)}, bf16[32,768]{1,0:T(8,128)(2,1)S(1)}, u32[]{:S(2)}, u32[]{:S(2)}) %collective-permute-start.24) | collective-permute-done | bytes 49184 | tf_op jit(solution)/shard_map/ppermute | solution.py:511
  88.2 1.4 %collective-permute-done.26.refs_7_ = bf16[32,768]{1,0:T(8,128)(2,1)S(1)} collective-permute-done((bf16[32,768]{1,0:T(8,128)(2,1)S(1)}, bf16[32,768]{1,0:T(8,128)(2,1)S(1)}, u32[]{:S(2)}, u32[]{:S(2)}) %collective-permute-start.26) | collective-permute-done | bytes 49184 | tf_op jit(solution)/shard_map/ppermute | solution.py:511
  89.7 2.1 %collective-permute-start.27 = (bf16[96,768]{1,0:T(8,128)(2,1)S(1)}, bf16[96,768]{1,0:T(8,128)(2,1)S(1)}, u32[]{:S(2)}, u32[]{:S(2)}) collective-permute-start(bf16[96,768]{1,0:T(8,128)(2,1)S(1)} %add_parts.1.refs_0_), channel_id=1, source_target_pairs={{4,0},{6,2},{8,4},{10,6},{12,8},{14,10},{0,12},{2,14},{5,1},{7,3},... | collective-permute-start | bytes 442376 | tf_op jit(solution)/shard_map/ppermute | solution.py:511
  93.5 2.7 %collective-permute-done.27.refs_1_ = bf16[96,768]{1,0:T(8,128)(2,1)S(1)} collective-permute-done((bf16[96,768]{1,0:T(8,128)(2,1)S(1)}, bf16[96,768]{1,0:T(8,128)(2,1)S(1)}, u32[]{:S(2)}, u32[]{:S(2)}) %collective-permute-start.27) | collective-permute-done | bytes 147488 | tf_op jit(solution)/shard_map/ppermute | solution.py:511
  96.2 1.4 %collective-permute-start.31 = (bf16[96,768]{1,0:T(8,128)(2,1)S(1)}, bf16[96,768]{1,0:T(8,128)(2,1)S(1)}, u32[]{:S(2)}, u32[]{:S(2)}) collective-permute-start(bf16[96,768]{1,0:T(8,128)(2,1)S(1)} %collective-permute-done.27.refs_1_), channel_id=1, source_target_pairs={{2,0},{0,2},{6,4},{4,6},{10,8},{8,10},{14,12},{12,14},{3,1},{1,3},... | collective-permute-start | bytes 442376 | tf_op jit(solution)/shard_map/ppermute | solution.py:511
  97.6 3.7 %collective-permute-done.28.refs_2_ = bf16[96,768]{1,0:T(8,128)(2,1)S(1)} collective-permute-done((bf16[96,768]{1,0:T(8,128)(2,1)S(1)}, bf16[96,768]{1,0:T(8,128)(2,1)S(1)}, u32[]{:S(2)}, u32[]{:S(2)}) %collective-permute-start.28) | collective-permute-done | bytes 147488 | tf_op jit(solution)/shard_map/ppermute | solution.py:511
  103.3 4.5 %project_first.1.first_ref = bf16[8,192,768]{2,1,0:T(8,128)(2,1)S(1)} custom-call(s32[2]{0:T(128)S(1)} %pad_add_fusion.place_ref, s32[2]{0:T(128)S(1)} %copy-done.4, bf16[8,2,192,384]{3,2,1,0:T(8,128)(2,1)S(1)} %bitcast.15, bf16[96,768]{1,0:T(8,128)(2,1)S(1)} %add_parts.1.refs_0_, bf16[96,768]{1,0:T(8,128)(2,1)S(1)} %collective-permute-done.27.refs_1_, ...), custom_call_target="tpu_custom_call" | custom-call | flops 1811939328 | bytes 4718592 | tf_op jit(solution)/shard_map/project_first/pallas_call | solution.py:473
  108.2 6.4 %project_second.1 = bf16[8,2,2,192,384]{4,3,2,1,0:T(8,128)(2,1)} custom-call(s32[2]{0:T(128)S(1)} %pad_add_fusion.place_ref, s32[2]{0:T(128)S(1)} %copy-done.4, bf16[8,2,192,384]{3,2,1,0:T(8,128)(2,1)S(1)} %bitcast.16, bf16[8,192,768]{2,1,0:T(8,128)(2,1)S(1)} %project_first.1.first_ref, bf16[96,768]{1,0:T(8,128)(2,1)S(1)} %collective-permute-done.30.refs_0_, ...), custom_call_target="tpu_custom_call" | custom-call | flops 1811939328 | bytes 7077888 | tf_op jit(solution)/shard_map/project_second/pallas_call | solution.py:489
  (69 shorter events, 19.1 us)
Async XLA Ops:
  1.3 10.7 %collective-permute-start = (bf16[600,128]{1,0:T(8,128)(2,1)S(1)}, bf16[600,128]{1,0:T(8,128)(2,1)S(1)}, u32[]{:S(2)}, u32[]{:S(2)}) collective-permute-start(bf16[600,128]{1,0:T(8,128)(2,1)S(1)} %get-tuple-element.41.refs_0_), channel_id=1, source_target_pairs={{12,0},{14,2},{0,4},{2,6},{4,8},{6,10},{8,12},{10,14},{13,1},{15,3... | collective-permute-start | bytes 460808 | tf_op jit(solution)/shard_map/ppermute | solution.py:511
  4.4 16.2 %collective-permute-start.1 = (bf16[600,128]{1,0:T(8,128)(2,1)S(1)}, bf16[600,128]{1,0:T(8,128)(2,1)S(1)}, u32[]{:S(2)}, u32[]{:S(2)}) collective-permute-start(bf16[600,128]{1,0:T(8,128)(2,1)S(1)} %get-tuple-element.42), channel_id=1, source_target_pairs={{8,0},{10,2},{12,4},{14,6},{0,8},{2,10},{4,12},{6,14},{9,1},{11,3}... | collective-permute-start | bytes 460808 | tf_op jit(solution)/shard_map/ppermute | solution.py:511
  7.0 13.6 %collective-permute-start.2 = (bf16[600,128]{1,0:T(8,128)(2,1)S(1)}, bf16[600,128]{1,0:T(8,128)(2,1)S(1)}, u32[]{:S(2)}, u32[]{:S(2)}) collective-permute-start(bf16[600,128]{1,0:T(8,128)(2,1)S(1)} %get-tuple-element.43), channel_id=1, source_target_pairs={{4,0},{6,2},{8,4},{10,6},{12,8},{14,10},{0,12},{2,14},{5,1},{7,3},... | collective-permute-start | bytes 460808 | tf_op jit(solution)/shard_map/ppermute | solution.py:511
  10.6 22.1 %collective-permute-start.6 = (bf16[384,128]{1,0:T(8,128)(2,1)S(1)}, bf16[384,128]{1,0:T(8,128)(2,1)S(1)}, u32[]{:S(2)}, u32[]{:S(2)}) collective-permute-start(bf16[384,128]{1,0:T(8,128)(2,1)S(1)} %get-tuple-element.48.refs_1_), channel_id=1, source_target_pairs={{12,0},{14,2},{0,4},{2,6},{4,8},{6,10},{8,12},{10,14},{13,1},{15,3... | collective-permute-start | bytes 294920 | tf_op jit(solution)/shard_map/ppermute | solution.py:511
  11.4 22.8 %collective-permute-start.7 = (bf16[384,128]{1,0:T(8,128)(2,1)S(1)}, bf16[384,128]{1,0:T(8,128)(2,1)S(1)}, u32[]{:S(2)}, u32[]{:S(2)}) collective-permute-start(bf16[384,128]{1,0:T(8,128)(2,1)S(1)} %get-tuple-element.49), channel_id=1, source_target_pairs={{8,0},{10,2},{12,4},{14,6},{0,8},{2,10},{4,12},{6,14},{9,1},{11,3}... | collective-permute-start | bytes 294920 | tf_op jit(solution)/shard_map/ppermute | solution.py:511
  12.0 25.1 %collective-permute-start.8 = (bf16[384,128]{1,0:T(8,128)(2,1)S(1)}, bf16[384,128]{1,0:T(8,128)(2,1)S(1)}, u32[]{:S(2)}, u32[]{:S(2)}) collective-permute-start(bf16[384,128]{1,0:T(8,128)(2,1)S(1)} %get-tuple-element.50), channel_id=1, source_target_pairs={{4,0},{6,2},{8,4},{10,6},{12,8},{14,10},{0,12},{2,14},{5,1},{7,3},... | collective-permute-start | bytes 294920 | tf_op jit(solution)/shard_map/ppermute | solution.py:511
  26.0 17.1 %collective-permute-start.3 = (bf16[6,64,128]{2,1,0:T(8,128)(2,1)S(1)}, bf16[6,64,128]{2,1,0:T(8,128)(2,1)S(1)}, u32[]{:S(2)}, u32[]{:S(2)}) collective-permute-start(bf16[6,64,128]{2,1,0:T(8,128)(2,1)S(1)} %get-tuple-element.45), channel_id=1, source_target_pairs={{4,0},{6,2},{8,4},{10,6},{12,8},{14,10},{0,12},{2,14},{5,1},{7,3},... | collective-permute-start | bytes 294920 | tf_op jit(solution)/shard_map/ppermute | solution.py:511
  32.7 14.7 %collective-permute-start.4 = (bf16[6,64,128]{2,1,0:T(8,128)(2,1)S(1)}, bf16[6,64,128]{2,1,0:T(8,128)(2,1)S(1)}, u32[]{:S(2)}, u32[]{:S(2)}) collective-permute-start(bf16[6,64,128]{2,1,0:T(8,128)(2,1)S(1)} %get-tuple-element.46), channel_id=1, source_target_pairs={{8,0},{10,2},{12,4},{14,6},{0,8},{2,10},{4,12},{6,14},{9,1},{11,3}... | collective-permute-start | bytes 294920 | tf_op jit(solution)/shard_map/ppermute | solution.py:511
  32.7 14.7 %collective-permute-start.5 = (bf16[6,64,128]{2,1,0:T(8,128)(2,1)S(1)}, bf16[6,64,128]{2,1,0:T(8,128)(2,1)S(1)}, u32[]{:S(2)}, u32[]{:S(2)}) collective-permute-start(bf16[6,64,128]{2,1,0:T(8,128)(2,1)S(1)} %get-tuple-element.47), channel_id=1, source_target_pairs={{12,0},{14,2},{0,4},{2,6},{4,8},{6,10},{8,12},{10,14},{13,1},{15,3... | collective-permute-start | bytes 294920 | tf_op jit(solution)/shard_map/ppermute | solution.py:511
  34.2 14.3 %collective-permute-start.12 = (bf16[384,128]{1,0:T(8,128)(2,1)S(1)}, bf16[384,128]{1,0:T(8,128)(2,1)S(1)}, u32[]{:S(2)}, u32[]{:S(2)}) collective-permute-start(bf16[384,128]{1,0:T(8,128)(2,1)S(1)} %get-tuple-element.56), channel_id=1, source_target_pairs={{12,0},{14,2},{0,4},{2,6},{4,8},{6,10},{8,12},{10,14},{13,1},{15,3... | collective-permute-start | bytes 294920 | tf_op jit(solution)/shard_map/ppermute | solution.py:511
  37.1 14.5 %collective-permute-start.13 = (bf16[384,128]{1,0:T(8,128)(2,1)S(1)}, bf16[384,128]{1,0:T(8,128)(2,1)S(1)}, u32[]{:S(2)}, u32[]{:S(2)}) collective-permute-start(bf16[384,128]{1,0:T(8,128)(2,1)S(1)} %get-tuple-element.57), channel_id=1, source_target_pairs={{8,0},{10,2},{12,4},{14,6},{0,8},{2,10},{4,12},{6,14},{9,1},{11,3}... | collective-permute-start | bytes 294920 | tf_op jit(solution)/shard_map/ppermute | solution.py:511
  43.0 11.2 %collective-permute-start.14 = (bf16[384,128]{1,0:T(8,128)(2,1)S(1)}, bf16[384,128]{1,0:T(8,128)(2,1)S(1)}, u32[]{:S(2)}, u32[]{:S(2)}) collective-permute-start(bf16[384,128]{1,0:T(8,128)(2,1)S(1)} %get-tuple-element.58), channel_id=1, source_target_pairs={{4,0},{6,2},{8,4},{10,6},{12,8},{14,10},{0,12},{2,14},{5,1},{7,3},... | collective-permute-start | bytes 294920 | tf_op jit(solution)/shard_map/ppermute | solution.py:511
  47.4 12.1 %collective-permute-start.10 = (bf16[6,64,128]{2,1,0:T(8,128)(2,1)S(1)}, bf16[6,64,128]{2,1,0:T(8,128)(2,1)S(1)}, u32[]{:S(2)}, u32[]{:S(2)}) collective-permute-start(bf16[6,64,128]{2,1,0:T(8,128)(2,1)S(1)} %get-tuple-element.54), channel_id=1, source_target_pairs={{8,0},{10,2},{12,4},{14,6},{0,8},{2,10},{4,12},{6,14},{9,1},{11,3}... | collective-permute-start | bytes 294920 | tf_op jit(solution)/shard_map/ppermute | solution.py:511
  47.5 14.4 %collective-permute-start.11 = (bf16[6,64,128]{2,1,0:T(8,128)(2,1)S(1)}, bf16[6,64,128]{2,1,0:T(8,128)(2,1)S(1)}, u32[]{:S(2)}, u32[]{:S(2)}) collective-permute-start(bf16[6,64,128]{2,1,0:T(8,128)(2,1)S(1)} %get-tuple-element.55), channel_id=1, source_target_pairs={{12,0},{14,2},{0,4},{2,6},{4,8},{6,10},{8,12},{10,14},{13,1},{15,3... | collective-permute-start | bytes 294920 | tf_op jit(solution)/shard_map/ppermute | solution.py:511
  48.5 22.2 %collective-permute-start.18 = (bf16[4,2,16,1536]{3,2,1,0:T(8,128)(2,1)S(1)}, bf16[4,2,16,1536]{3,2,1,0:T(8,128)(2,1)S(1)}, u32[]{:S(2)}, u32[]{:S(2)}) collective-permute-start(bf16[4,2,16,1536]{3,2,1,0:T(8,128)(2,1)S(1)} %get-tuple-element.52.refs_0_), channel_id=1, source_target_pairs={{2,0},{0,2},{6,4},{4,6},{10,8},{8,10},{14,12},{12,14},{3,1},{1,3},... | collective-permute-start | bytes 1179656 | tf_op jit(solution)/shard_map/ppermute | solution.py:511
  51.6 10.6 %collective-permute-start.9 = (bf16[6,64,128]{2,1,0:T(8,128)(2,1)S(1)}, bf16[6,64,128]{2,1,0:T(8,128)(2,1)S(1)}, u32[]{:S(2)}, u32[]{:S(2)}) collective-permute-start(bf16[6,64,128]{2,1,0:T(8,128)(2,1)S(1)} %get-tuple-element.53), channel_id=1, source_target_pairs={{4,0},{6,2},{8,4},{10,6},{12,8},{14,10},{0,12},{2,14},{5,1},{7,3},... | collective-permute-start | bytes 294920 | tf_op jit(solution)/shard_map/ppermute | solution.py:511
  59.6 7.5 %collective-permute-start.16 = (bf16[6,64,128]{2,1,0:T(8,128)(2,1)S(1)}, bf16[6,64,128]{2,1,0:T(8,128)(2,1)S(1)}, u32[]{:S(2)}, u32[]{:S(2)}) collective-permute-start(bf16[6,64,128]{2,1,0:T(8,128)(2,1)S(1)} %get-tuple-element.63), channel_id=1, source_target_pairs={{8,0},{10,2},{12,4},{14,6},{0,8},{2,10},{4,12},{6,14},{9,1},{11,3}... | collective-permute-start | bytes 294920 | tf_op jit(solution)/shard_map/ppermute | solution.py:511
  61.9 6.4 %collective-permute-start.17 = (bf16[6,64,128]{2,1,0:T(8,128)(2,1)S(1)}, bf16[6,64,128]{2,1,0:T(8,128)(2,1)S(1)}, u32[]{:S(2)}, u32[]{:S(2)}) collective-permute-start(bf16[6,64,128]{2,1,0:T(8,128)(2,1)S(1)} %get-tuple-element.64), channel_id=1, source_target_pairs={{12,0},{14,2},{0,4},{2,6},{4,8},{6,10},{8,12},{10,14},{13,1},{15,3... | collective-permute-start | bytes 294920 | tf_op jit(solution)/shard_map/ppermute | solution.py:511
  63.0 14.1 %collective-permute-start.22 = (bf16[4,2,16,1536]{3,2,1,0:T(8,128)(2,1)S(1)}, bf16[4,2,16,1536]{3,2,1,0:T(8,128)(2,1)S(1)}, u32[]{:S(2)}, u32[]{:S(2)}) collective-permute-start(bf16[4,2,16,1536]{3,2,1,0:T(8,128)(2,1)S(1)} %get-tuple-element.61.refs_1_), channel_id=1, source_target_pairs={{2,0},{0,2},{6,4},{4,6},{10,8},{8,10},{14,12},{12,14},{3,1},{1,3},... | collective-permute-start | bytes 1179656 | tf_op jit(solution)/shard_map/ppermute | solution.py:511
  69.2 10.1 %collective-permute-start.23 = (bf16[4,2,16,1536]{3,2,1,0:T(8,128)(2,1)S(1)}, bf16[4,2,16,1536]{3,2,1,0:T(8,128)(2,1)S(1)}, u32[]{:S(2)}, u32[]{:S(2)}) collective-permute-start(bf16[4,2,16,1536]{3,2,1,0:T(8,128)(2,1)S(1)} %get-tuple-element.66.refs_2_), channel_id=1, source_target_pairs={{2,0},{0,2},{6,4},{4,6},{10,8},{8,10},{14,12},{12,14},{3,1},{1,3},... | collective-permute-start | bytes 1179656 | tf_op jit(solution)/shard_map/ppermute | solution.py:511
  73.2 11.8 %collective-permute-start.19 = (bf16[64,768]{1,0:T(8,128)(2,1)S(1)}, bf16[64,768]{1,0:T(8,128)(2,1)S(1)}, u32[]{:S(2)}, u32[]{:S(2)}) collective-permute-start(bf16[64,768]{1,0:T(8,128)(2,1)S(1)} %get-tuple-element.69), channel_id=1, source_target_pairs={{12,0},{14,2},{0,4},{2,6},{4,8},{6,10},{8,12},{10,14},{13,1},{15,3... | collective-permute-start | bytes 294920 | tf_op jit(solution)/shard_map/ppermute | solution.py:511
  73.3 12.1 %collective-permute-start.20 = (bf16[64,768]{1,0:T(8,128)(2,1)S(1)}, bf16[64,768]{1,0:T(8,128)(2,1)S(1)}, u32[]{:S(2)}, u32[]{:S(2)}) collective-permute-start(bf16[64,768]{1,0:T(8,128)(2,1)S(1)} %get-tuple-element.70), channel_id=1, source_target_pairs={{8,0},{10,2},{12,4},{14,6},{0,8},{2,10},{4,12},{6,14},{9,1},{11,3}... | collective-permute-start | bytes 294920 | tf_op jit(solution)/shard_map/ppermute | solution.py:511
  74.5 10.9 %collective-permute-start.21 = (bf16[64,768]{1,0:T(8,128)(2,1)S(1)}, bf16[64,768]{1,0:T(8,128)(2,1)S(1)}, u32[]{:S(2)}, u32[]{:S(2)}) collective-permute-start(bf16[64,768]{1,0:T(8,128)(2,1)S(1)} %get-tuple-element.71), channel_id=1, source_target_pairs={{4,0},{6,2},{8,4},{10,6},{12,8},{14,10},{0,12},{2,14},{5,1},{7,3},... | collective-permute-start | bytes 294920 | tf_op jit(solution)/shard_map/ppermute | solution.py:511
  81.4 6.1 %collective-permute-start.24 = (bf16[32,768]{1,0:T(8,128)(2,1)S(1)}, bf16[32,768]{1,0:T(8,128)(2,1)S(1)}, u32[]{:S(2)}, u32[]{:S(2)}) collective-permute-start(bf16[32,768]{1,0:T(8,128)(2,1)S(1)} %get-tuple-element.74), channel_id=1, source_target_pairs={{12,0},{14,2},{0,4},{2,6},{4,8},{6,10},{8,12},{10,14},{13,1},{15,3... | collective-permute-start | bytes 147464 | tf_op jit(solution)/shard_map/ppermute | solution.py:511
  81.7 6.5 %collective-permute-start.25 = (bf16[32,768]{1,0:T(8,128)(2,1)S(1)}, bf16[32,768]{1,0:T(8,128)(2,1)S(1)}, u32[]{:S(2)}, u32[]{:S(2)}) collective-permute-start(bf16[32,768]{1,0:T(8,128)(2,1)S(1)} %get-tuple-element.75), channel_id=1, source_target_pairs={{8,0},{10,2},{12,4},{14,6},{0,8},{2,10},{4,12},{6,14},{9,1},{11,3}... | collective-permute-start | bytes 147464 | tf_op jit(solution)/shard_map/ppermute | solution.py:511
  89.7 6.5 %collective-permute-start.27 = (bf16[96,768]{1,0:T(8,128)(2,1)S(1)}, bf16[96,768]{1,0:T(8,128)(2,1)S(1)}, u32[]{:S(2)}, u32[]{:S(2)}) collective-permute-start(bf16[96,768]{1,0:T(8,128)(2,1)S(1)} %add_parts.1.refs_0_), channel_id=1, source_target_pairs={{4,0},{6,2},{8,4},{10,6},{12,8},{14,10},{0,12},{2,14},{5,1},{7,3},... | collective-permute-start | bytes 442376 | tf_op jit(solution)/shard_map/ppermute | solution.py:511
  91.8 9.5 %collective-permute-start.28 = (bf16[96,768]{1,0:T(8,128)(2,1)S(1)}, bf16[96,768]{1,0:T(8,128)(2,1)S(1)}, u32[]{:S(2)}, u32[]{:S(2)}) collective-permute-start(bf16[96,768]{1,0:T(8,128)(2,1)S(1)} %add_parts.1.refs_0_), channel_id=1, source_target_pairs={{8,0},{10,2},{12,4},{14,6},{0,8},{2,10},{4,12},{6,14},{9,1},{11,3}... | collective-permute-start | bytes 442376 | tf_op jit(solution)/shard_map/ppermute | solution.py:511
  92.1 10.5 %collective-permute-start.29 = (bf16[96,768]{1,0:T(8,128)(2,1)S(1)}, bf16[96,768]{1,0:T(8,128)(2,1)S(1)}, u32[]{:S(2)}, u32[]{:S(2)}) collective-permute-start(bf16[96,768]{1,0:T(8,128)(2,1)S(1)} %add_parts.1.refs_0_), channel_id=1, source_target_pairs={{12,0},{14,2},{0,4},{2,6},{4,8},{6,10},{8,12},{10,14},{13,1},{15,3... | collective-permute-start | bytes 442376 | tf_op jit(solution)/shard_map/ppermute | solution.py:511
  92.4 15.4 %collective-permute-start.30 = (bf16[96,768]{1,0:T(8,128)(2,1)S(1)}, bf16[96,768]{1,0:T(8,128)(2,1)S(1)}, u32[]{:S(2)}, u32[]{:S(2)}) collective-permute-start(bf16[96,768]{1,0:T(8,128)(2,1)S(1)} %add_parts.1.refs_0_), channel_id=1, source_target_pairs={{2,0},{0,2},{6,4},{4,6},{10,8},{8,10},{14,12},{12,14},{3,1},{1,3},... | collective-permute-start | bytes 442376 | tf_op jit(solution)/shard_map/ppermute | solution.py:511
  96.2 11.6 %collective-permute-start.31 = (bf16[96,768]{1,0:T(8,128)(2,1)S(1)}, bf16[96,768]{1,0:T(8,128)(2,1)S(1)}, u32[]{:S(2)}, u32[]{:S(2)}) collective-permute-start(bf16[96,768]{1,0:T(8,128)(2,1)S(1)} %collective-permute-done.27.refs_1_), channel_id=1, source_target_pairs={{2,0},{0,2},{6,4},{4,6},{10,8},{8,10},{14,12},{12,14},{3,1},{1,3},... | collective-permute-start | bytes 442376 | tf_op jit(solution)/shard_map/ppermute | solution.py:511
  101.3 6.5 %collective-permute-start.32 = (bf16[96,768]{1,0:T(8,128)(2,1)S(1)}, bf16[96,768]{1,0:T(8,128)(2,1)S(1)}, u32[]{:S(2)}, u32[]{:S(2)}) collective-permute-start(bf16[96,768]{1,0:T(8,128)(2,1)S(1)} %collective-permute-done.28.refs_2_), channel_id=1, source_target_pairs={{2,0},{0,2},{6,4},{4,6},{10,8},{8,10},{14,12},{12,14},{3,1},{1,3},... | collective-permute-start | bytes 442376 | tf_op jit(solution)/shard_map/ppermute | solution.py:511
  102.6 5.6 %collective-permute-start.33 = (bf16[96,768]{1,0:T(8,128)(2,1)S(1)}, bf16[96,768]{1,0:T(8,128)(2,1)S(1)}, u32[]{:S(2)}, u32[]{:S(2)}) collective-permute-start(bf16[96,768]{1,0:T(8,128)(2,1)S(1)} %collective-permute-done.29.refs_3_), channel_id=1, source_target_pairs={{2,0},{0,2},{6,4},{4,6},{10,8},{8,10},{14,12},{12,14},{3,1},{1,3},... | collective-permute-start | bytes 442376 | tf_op jit(solution)/shard_map/ppermute | solution.py:511
  (8 other events, 102.9 us)

commit v6 on v5

--- a/solution.py
+++ b/solution.py
@@ -311,7 +311,21 @@
         outs[d][...] = total_ref[lax.rem(place_ref[0] + d, segments)].astype(outs[d].dtype)
 
 
-def early_kernel(segments, count, place_ref, *refs):
+def column_of(unit, units, leads):
+    tile, half = LANES // 16, LANES // 32
+    if unit < tile:
+        first = (unit * 16, LANES + unit * 16)
+    else:
+        first = (2 * LANES + (unit - tile) * 16, 2 * LANES + (unit - tile + half) * 16)
+    if unit < units - tile:
+        second = (2 * LANES + (unit + half) * 16, 2 * LANES + unit * 16)
+    else:
+        at = (unit - units + tile) * 16
+        second = (at, LANES + at)
+    return [pl.multiple_of(jnp.where(leads, x, y), 16) for x, y in zip(first, second)]
+
+
+def early_kernel(segments, count, place_ref, owner_ref, *refs):
     chunks = len(CHUNKS)
     left, shifted = refs[:count], refs[count : count + chunks]
     outs = refs[count + chunks : count + chunks + segments]
@@ -319,16 +333,19 @@
     slots, _, _, depth = left[0].shape
     block = right_ref.shape[1] // 2
     fill_left(left_ref, left)
-    for p in range(right_ref.shape[0]):
-        for n, ref in enumerate(shifted):
-            for slot in range(slots):
-                re, im = ref[p, slot, 0], ref[p, slot, 1]
-                at = slot * sum(CHUNKS) + sum(CHUNKS[:n])
-                low, high = slice(at, at + CHUNKS[n]), slice(block + at, block + at + CHUNKS[n])
-                right_ref[p, low, :depth] = re
-                right_ref[p, low, depth:] = im
-                right_ref[p, high, :depth] = im
-                right_ref[p, high, depth:] = -re
+    leads = owner_ref[place_ref[1]] == 0
+    for n, ref in enumerate(shifted):
+        for slot in range(slots):
+            for part in range(CHUNKS[n] // 16):
+                unit = (slot * sum(CHUNKS) + sum(CHUNKS[:n])) // 16 + part
+                real, imaginary = column_of(unit, block // 16, leads)
+                for p in range(right_ref.shape[0]):
+                    re = ref[p, slot, 0, part * 16 : part * 16 + 16]
+                    im = ref[p, slot, 1, part * 16 : part * 16 + 16]
+                    right_ref[p, pl.ds(real, 16), :depth] = re
+                    right_ref[p, pl.ds(real, 16), depth:] = im
+                    right_ref[p, pl.ds(imaginary, 16), :depth] = im
+                    right_ref[p, pl.ds(imaginary, 16), depth:] = -re
     multiply(left_ref, right_ref, total_ref, place_ref, outs)
 
 
@@ -340,7 +357,7 @@
     multiply(left_ref, right_ref, total_ref, place_ref, outs)
 
 
-def elementals(place, left, shifted, right, segments):
+def elementals(place, owner, left, shifted, right, segments):
     _, _, _, depth = left[0].shape
     block = segments * sum(CHUNKS)
     rows = sum(ref.shape[2] for ref in left)
@@ -351,10 +368,11 @@
     if early:
         shapes.append(pltpu.VMEM((momenta, 2 * block, 2 * depth), jnp.bfloat16))
     operands = [*left, *shifted] if early else [*left, right]
+    scalars = [place, owner] if early else [place]
     return pl.pallas_call(
         functools.partial(early_kernel if early else late_kernel, segments, len(left)),
         out_shape=shapes,
-        in_specs=[SMEM] + [VMEM] * len(operands),
+        in_specs=[SMEM] * len(scalars) + [VMEM] * len(operands),
         out_specs=[VMEM] * len(shapes),
         scratch_shapes=[
             pltpu.VMEM((segments * rows, 2 * depth), jnp.bfloat16),
@@ -364,7 +382,7 @@
             flops=2 * segments * rows * columns * 2 * depth, bytes_accessed=8 * block * depth, transcendentals=0),
         compiler_params=GRANT,
         name="elementals_early" if early else "elementals_late",
-    )(place, *operands)
+    )(*scalars, *operands)
 
 
 def add_kernel(count, *refs):
@@ -394,29 +412,25 @@
     nvec = right_ref.shape[0] // 2
     momenta = right_ref.shape[1] // (3 * LANES)
     block = nvec // 2
-    half = block - LANES
     rows = block // sites
     v = lax.rem(place_ref[1] + across, 2)
     leads = owner_ref[v] == 0
-
-    def tiles(re, im):
-        lead = (re[:, :LANES], im[:, :LANES], jnp.concatenate([re[:, LANES:], im[:, LANES:]], axis=1))
-        other = (re[:, half:], im[:, half:], jnp.concatenate([im[:, :half], re[:, :half]], axis=1))
-        return [jnp.where(leads, x, y) for x, y in zip(lead, other)]
-
+    lower = lax.broadcasted_iota(jnp.int32, (rows, LANES), 1) < LANES // 2
+    sign = jnp.where(lower == leads, -1.0, 1.0).astype(jnp.bfloat16)
     for up, piece in enumerate(pieces):
         z = lax.rem(place_ref[0] + up, sites)
         for part, owner in ((0, owner_ref[v]), (1, owner_ref[1 - v])):
             row = pl.multiple_of(owner * block + z * rows, 16)
             low = pl.multiple_of(nvec + owner * block + z * rows, 16)
+            here = slice(part * rows, (part + 1) * rows)
+            right_ref[pl.ds(row, rows), :] = piece[here, :]
             for p in range(momenta):
-                value = piece[part * rows : (part + 1) * rows, p * 2 * block : (p + 1) * 2 * block]
-                re, im = value[:, :block], value[:, block:]
-                for at, (first, second, ends) in ((row, tiles(re, im)), (low, tiles(-im, re))):
-                    right_ref[pl.ds(at, rows), 2 * p * LANES : (2 * p + 1) * LANES] = first
-                    right_ref[pl.ds(at, rows), (2 * p + 1) * LANES : (2 * p + 2) * LANES] = second
-                    last = (2 * momenta + p) * LANES
-                    right_ref[pl.ds(at, rows), last : last + LANES] = ends
+                first, second, ends = (3 * p * LANES + k * LANES for k in range(3))
+                halves = piece[here, ends : ends + LANES]
+                swapped = jnp.concatenate([halves[:, LANES // 2 :], halves[:, : LANES // 2]], axis=1)
+                right_ref[pl.ds(low, rows), first : first + LANES] = -piece[here, second : second + LANES]
+                right_ref[pl.ds(low, rows), second : second + LANES] = piece[here, first : first + LANES]
+                right_ref[pl.ds(low, rows), ends : ends + LANES] = swapped * sign
 
 
 def pair_of(tau_ref, n):
@@ -458,11 +472,11 @@
             return jnp.where(leads, mine, theirs), jnp.where(leads, theirs, mine)
 
         for p in range(momenta):
-            low_ends, high_ends = ordered(2 * momenta + p)
+            low_ends, high_ends = ordered(3 * p + 2)
             middles = (jnp.where(lower, low_ends, high_ends),
                        pltpu.roll(jnp.where(lower, high_ends, low_ends), LANES // 2, 1))
             for c in range(2):
-                low, high = ordered(2 * p + c)
+                low, high = ordered(3 * p + c)
                 out_ref[k, p, c, :, :LANES] = low.astype(jnp.bfloat16)
                 out_ref[k, p, c, :, LANES : 2 * LANES] = middles[c].astype(jnp.bfloat16)
                 out_ref[k, p, c, :, 2 * LANES :] = high.astype(jnp.bfloat16)
@@ -553,10 +567,10 @@
             last = s
     filtered, shifted, other = ([group_of[n] for n in range(len(CHUNKS))] for group_of in (filtered, shifted, other))
 
-    *parts, right = elementals(place, filtered + other[:1], shifted, None, sites)
+    *parts, right = elementals(place, block_owner, filtered + other[:1], shifted, None, sites)
     sent = [from_place(parts[d], -d, 0) for d in range(1, sites)]
     early = [parts[0], *sent]
-    parts = elementals(place, other[1:], None, right, sites)
+    parts = elementals(place, block_owner, other[1:], None, right, sites)
     sent = [from_place(parts[d], -d, 0) for d in range(1, sites)]
     mine = add_parts(early, [parts[0], *sent])
 
@@ -714,7 +728,7 @@
     block, layers, plane = eigvecs.shape[3:]
     sites, groups = lax.axis_size("site"), lax.axis_size("vec")
     fits = layers == 1 and plane == LX * LY == 4 * LANES and sites == 4 and groups == 2
-    fits = fits and block == sites * sum(CHUNKS) and 2 * block == 3 * LANES
+    fits = fits and block == sites * sum(CHUNKS) and 2 * block == 3 * LANES and set(CHUNKS) == {16}
     fits = fits and peramb.shape[1] * peramb.shape[2] % 2 == 0 and (2 * block) % (32 * sites) == 0 and block % (2 * block // sites) == 0
     device = per_device if fits else general_device
     return device(eigvecs, links, peramb, block_owner, momenta)

time: 115 us -> 113 us (0.983)
  Pallas kernels: 36 us -> 34 us
    pallas_call x1, Pallas kernels: 6.36 us -> 5.14 us  [project_second(): pl.pallas_call(functools.partial(second_kernel, len(pieces)), grid=(outer...]
    pallas_call x1, Pallas kernels: 4.47 us -> 3.3 us  [project_first(): pl.pallas_call(functools.partial(first_kernel, len(pieces)), out_shape=pl...]
  transfers between devices with their start and end apart: 34 -> 34, of which waited for: 13 -> 13; matrix products, arithmetic and copies ran while one was open for 1% -> 1% of each run, Pallas kernels for 25% -> 24%
where the time goes in v6:
time: 113 us
  starting transfers between devices  48.9 us (43%)
  Pallas kernels  34 us (30%)
  waiting for transfers between devices  27.8 us (25%)
  local copies, waits for them, and re-layouts  1.85 us (2%)
    ppermute x34, starting transfers between devices, from_place(): return lax.ppermute(block, ('site', 'vec'), route)  48.9 us
    ppermute x34, waiting for transfers between devices, from_place(): return lax.ppermute(block, ('site', 'vec'), route)  27.8 us
    pallas_call x3, Pallas kernels, filter_chunk(): pl.pallas_call(functools.partial(filter_kernel, sites, chunk), out_shape=...  15.2 us
    pallas_call x1, Pallas kernels, project_second(): pl.pallas_call(functools.partial(second_kernel, len(pieces)), grid=(outer...  5.14 us
    pallas_call x2, Pallas kernels, elementals(): pl.pallas_call(functools.partial(early_kernel if early else late_kernel,...  4.9 us
    pallas_call x1, Pallas kernels, project_first(): pl.pallas_call(functools.partial(first_kernel, len(pieces)), out_shape=pl...  3.3 us
    pallas_call x3, Pallas kernels, finish(): pl.pallas_call(functools.partial(finish_kernel, sites, chunk), out_shape=...  2.67 us
  transfers between devices with their start and end apart: 34, of which 13 were waited for; matrix products, arithmetic and copies ran while one was open for 1% of the time, Pallas kernels for 24%

profile of v6, /device:TPU:0, one launch (start us, length us, event | category | flops | bytes accessed | tf_op | source)
XLA Modules:
  0.0 113.3 jit_solution(2040057109349482036)
XLA Ops:
  1.3 3.1 %collective-permute-start = (bf16[600,128]{1,0:T(8,128)(2,1)S(1)}, bf16[600,128]{1,0:T(8,128)(2,1)S(1)}, u32[]{:S(2)}, u32[]{:S(2)}) collective-permute-start(bf16[600,128]{1,0:T(8,128)(2,1)S(1)} %get-tuple-element.41.refs_0_), channel_id=1, source_target_pairs={{12,0},{14,2},{0,4},{2,6},{4,8},{6,10},{8,12},{10,14},{13,1},{15,3... | collective-permute-start | bytes 460808 | tf_op jit(solution)/shard_map/ppermute | solution.py:525
  4.4 2.6 %collective-permute-start.1 = (bf16[600,128]{1,0:T(8,128)(2,1)S(1)}, bf16[600,128]{1,0:T(8,128)(2,1)S(1)}, u32[]{:S(2)}, u32[]{:S(2)}) collective-permute-start(bf16[600,128]{1,0:T(8,128)(2,1)S(1)} %get-tuple-element.42), channel_id=1, source_target_pairs={{8,0},{10,2},{12,4},{14,6},{0,8},{2,10},{4,12},{6,14},{9,1},{11,3}... | collective-permute-start | bytes 460808 | tf_op jit(solution)/shard_map/ppermute | solution.py:525
  8.4 1.7 %copy-done = f32[1,2,3,192,1,512]{5,4,3,2,1,0:T(1,128)S(1)} copy-done((f32[1,2,3,192,1,512]{5,4,3,2,1,0:T(1,128)S(1)}, f32[1,2,3,192,1,512]{5,4,3,2,1,0:T(1,128)}, u32[]{:S(2)}) %copy-start) | copy-done | bytes 2359320
  12.0 2.9 %collective-permute-start.8 = (bf16[384,128]{1,0:T(8,128)(2,1)S(1)}, bf16[384,128]{1,0:T(8,128)(2,1)S(1)}, u32[]{:S(2)}, u32[]{:S(2)}) collective-permute-start(bf16[384,128]{1,0:T(8,128)(2,1)S(1)} %get-tuple-element.50), channel_id=1, source_target_pairs={{4,0},{6,2},{8,4},{10,6},{12,8},{14,10},{0,12},{2,14},{5,1},{7,3},... | collective-permute-start | bytes 294920 | tf_op jit(solution)/shard_map/ppermute | solution.py:525
  14.9 5.7 %collective-permute-done.1.refs_2_ = bf16[600,128]{1,0:T(8,128)(2,1)S(1)} collective-permute-done((bf16[600,128]{1,0:T(8,128)(2,1)S(1)}, bf16[600,128]{1,0:T(8,128)(2,1)S(1)}, u32[]{:S(2)}, u32[]{:S(2)}) %collective-permute-start.1) | collective-permute-done | bytes 153632 | tf_op jit(solution)/shard_map/ppermute | solution.py:525
  20.9 5.1 %shard_map.55 = (bf16[6,64,128]{2,1,0:T(8,128)(2,1)S(1)}, bf16[6,64,128]{2,1,0:T(8,128)(2,1)S(1)}, bf16[6,64,128]{2,1,0:T(8,128)(2,1)S(1)}, bf16[6,64,128]{2,1,0:T(8,128)(2,1)S(1)}) custom-call(s32[2]{0:T(128)S(1)} %pad_add_fusion.place_ref, f32[6,768,128]{2,1,0:T(8,128)S(1)} %bitcast.8, bf16[600,128]{1,0:T(8,128)(2,1)S(1)} %collective-permute-done.refs_1_.refs_0_, ...), custom_call_target="tpu_custom_call" | custom-call | flops 28311552 | bytes 786432 | tf_op jit(solution)/shard_map/pallas_call | solution.py:238
  26.0 6.8 %collective-permute-start.3 = (bf16[6,64,128]{2,1,0:T(8,128)(2,1)S(1)}, bf16[6,64,128]{2,1,0:T(8,128)(2,1)S(1)}, u32[]{:S(2)}, u32[]{:S(2)}) collective-permute-start(bf16[6,64,128]{2,1,0:T(8,128)(2,1)S(1)} %get-tuple-element.45), channel_id=1, source_target_pairs={{4,0},{6,2},{8,4},{10,6},{12,8},{14,10},{0,12},{2,14},{5,1},{7,3},... | collective-permute-start | bytes 294920 | tf_op jit(solution)/shard_map/ppermute | solution.py:525
  34.2 2.9 %collective-permute-start.12 = (bf16[384,128]{1,0:T(8,128)(2,1)S(1)}, bf16[384,128]{1,0:T(8,128)(2,1)S(1)}, u32[]{:S(2)}, u32[]{:S(2)}) collective-permute-start(bf16[384,128]{1,0:T(8,128)(2,1)S(1)} %get-tuple-element.56), channel_id=1, source_target_pairs={{12,0},{14,2},{0,4},{2,6},{4,8},{6,10},{8,12},{10,14},{13,1},{15,3... | collective-permute-start | bytes 294920 | tf_op jit(solution)/shard_map/ppermute | solution.py:525
  38.0 5.1 %shard_map.57 = (bf16[6,64,128]{2,1,0:T(8,128)(2,1)S(1)}, bf16[6,64,128]{2,1,0:T(8,128)(2,1)S(1)}, bf16[6,64,128]{2,1,0:T(8,128)(2,1)S(1)}, bf16[6,64,128]{2,1,0:T(8,128)(2,1)S(1)}) custom-call(s32[2]{0:T(128)S(1)} %pad_add_fusion.place_ref, f32[6,768,128]{2,1,0:T(8,128)S(1)} %bitcast.10, bf16[384,128]{1,0:T(8,128)(2,1)S(1)} %collective-permute-done.6.refs_1_, ...), custom_call_target="tpu_custom_call" | custom-call | flops 28311552 | bytes 786432 | tf_op jit(solution)/shard_map/pallas_call | solution.py:238
  43.0 1.6 %collective-permute-start.14 = (bf16[384,128]{1,0:T(8,128)(2,1)S(1)}, bf16[384,128]{1,0:T(8,128)(2,1)S(1)}, u32[]{:S(2)}, u32[]{:S(2)}) collective-permute-start(bf16[384,128]{1,0:T(8,128)(2,1)S(1)} %get-tuple-element.58), channel_id=1, source_target_pairs={{4,0},{6,2},{8,4},{10,6},{12,8},{14,10},{0,12},{2,14},{5,1},{7,3},... | collective-permute-start | bytes 294920 | tf_op jit(solution)/shard_map/ppermute | solution.py:525
  44.6 2.8 %collective-permute-done.4.refs_2_ = bf16[6,64,128]{2,1,0:T(8,128)(2,1)S(1)} collective-permute-done((bf16[6,64,128]{2,1,0:T(8,128)(2,1)S(1)}, bf16[6,64,128]{2,1,0:T(8,128)(2,1)S(1)}, u32[]{:S(2)}, u32[]{:S(2)}) %collective-permute-start.4) | collective-permute-done | bytes 98336 | tf_op jit(solution)/shard_map/ppermute | solution.py:525
  48.5 1.6 %collective-permute-start.18 = (bf16[4,2,16,1536]{3,2,1,0:T(8,128)(2,1)S(1)}, bf16[4,2,16,1536]{3,2,1,0:T(8,128)(2,1)S(1)}, u32[]{:S(2)}, u32[]{:S(2)}) collective-permute-start(bf16[4,2,16,1536]{3,2,1,0:T(8,128)(2,1)S(1)} %get-tuple-element.52.refs_0_), channel_id=1, source_target_pairs={{2,0},{0,2},{6,4},{4,6},{10,8},{8,10},{14,12},{12,14},{3,1},{1,3},... | collective-permute-start | bytes 1179656 | tf_op jit(solution)/shard_map/ppermute | solution.py:525
  50.1 1.5 %collective-permute-done.13.refs_2_ = bf16[384,128]{1,0:T(8,128)(2,1)S(1)} collective-permute-done((bf16[384,128]{1,0:T(8,128)(2,1)S(1)}, bf16[384,128]{1,0:T(8,128)(2,1)S(1)}, u32[]{:S(2)}, u32[]{:S(2)}) %collective-permute-start.13) | collective-permute-done | bytes 98336 | tf_op jit(solution)/shard_map/ppermute | solution.py:525
  51.6 2.7 %collective-permute-start.9 = (bf16[6,64,128]{2,1,0:T(8,128)(2,1)S(1)}, bf16[6,64,128]{2,1,0:T(8,128)(2,1)S(1)}, u32[]{:S(2)}, u32[]{:S(2)}) collective-permute-start(bf16[6,64,128]{2,1,0:T(8,128)(2,1)S(1)} %get-tuple-element.53), channel_id=1, source_target_pairs={{4,0},{6,2},{8,4},{10,6},{12,8},{14,10},{0,12},{2,14},{5,1},{7,3},... | collective-permute-start | bytes 294920 | tf_op jit(solution)/shard_map/ppermute | solution.py:525
  54.3 5.1 %shard_map.60 = (bf16[6,64,128]{2,1,0:T(8,128)(2,1)S(1)}, bf16[6,64,128]{2,1,0:T(8,128)(2,1)S(1)}, bf16[6,64,128]{2,1,0:T(8,128)(2,1)S(1)}, bf16[6,64,128]{2,1,0:T(8,128)(2,1)S(1)}) custom-call(s32[2]{0:T(128)S(1)} %pad_add_fusion.place_ref, f32[6,768,128]{2,1,0:T(8,128)S(1)} %bitcast.12, bf16[384,128]{1,0:T(8,128)(2,1)S(1)} %collective-permute-done.12.refs_1_, ...), custom_call_target="tpu_custom_call" | custom-call | flops 28311552 | bytes 786432 | tf_op jit(solution)/shard_map/pallas_call | solution.py:238
  59.6 2.3 %collective-permute-start.16 = (bf16[6,64,128]{2,1,0:T(8,128)(2,1)S(1)}, bf16[6,64,128]{2,1,0:T(8,128)(2,1)S(1)}, u32[]{:S(2)}, u32[]{:S(2)}) collective-permute-start(bf16[6,64,128]{2,1,0:T(8,128)(2,1)S(1)} %get-tuple-element.63), channel_id=1, source_target_pairs={{8,0},{10,2},{12,4},{14,6},{0,8},{2,10},{4,12},{6,14},{9,1},{11,3}... | collective-permute-start | bytes 294920 | tf_op jit(solution)/shard_map/ppermute | solution.py:525
  63.0 1.4 %collective-permute-start.22 = (bf16[4,2,16,1536]{3,2,1,0:T(8,128)(2,1)S(1)}, bf16[4,2,16,1536]{3,2,1,0:T(8,128)(2,1)S(1)}, u32[]{:S(2)}, u32[]{:S(2)}) collective-permute-start(bf16[4,2,16,1536]{3,2,1,0:T(8,128)(2,1)S(1)} %get-tuple-element.61.refs_1_), channel_id=1, source_target_pairs={{2,0},{0,2},{6,4},{4,6},{10,8},{8,10},{14,12},{12,14},{3,1},{1,3},... | collective-permute-start | bytes 1179656 | tf_op jit(solution)/shard_map/ppermute | solution.py:525
  64.8 2.2 %collective-permute-done.16.refs_2_ = bf16[6,64,128]{2,1,0:T(8,128)(2,1)S(1)} collective-permute-done((bf16[6,64,128]{2,1,0:T(8,128)(2,1)S(1)}, bf16[6,64,128]{2,1,0:T(8,128)(2,1)S(1)}, u32[]{:S(2)}, u32[]{:S(2)}) %collective-permute-start.16) | collective-permute-done | bytes 98336 | tf_op jit(solution)/shard_map/ppermute | solution.py:525
  69.2 1.6 %collective-permute-start.23 = (bf16[4,2,16,1536]{3,2,1,0:T(8,128)(2,1)S(1)}, bf16[4,2,16,1536]{3,2,1,0:T(8,128)(2,1)S(1)}, u32[]{:S(2)}, u32[]{:S(2)}) collective-permute-start(bf16[4,2,16,1536]{3,2,1,0:T(8,128)(2,1)S(1)} %get-tuple-element.66.refs_2_), channel_id=1, source_target_pairs={{2,0},{0,2},{6,4},{4,6},{10,8},{8,10},{14,12},{12,14},{3,1},{1,3},... | collective-permute-start | bytes 1179656 | tf_op jit(solution)/shard_map/ppermute | solution.py:525
  70.7 2.8 %elementals_early.1 = (f32[64,768]{1,0:T(8,128)S(1)}, bf16[64,768]{1,0:T(8,128)(2,1)S(1)}, bf16[64,768]{1,0:T(8,128)(2,1)S(1)}, bf16[64,768]{1,0:T(8,128)(2,1)S(1)}, bf16[2,384,3072]{2,1,0:T(8,128)(2,1)S(1)}) custom-call(s32[2]{0:T(128)S(1)} %pad_add_fusion.place_ref, s32[2]{0:T(128)S(1)} %copy-done.4, ...), custom_call_target="tpu_custom_call" | custom-call | flops 1207959552 | bytes 2359296 | tf_op jit(solution)/shard_map/elementals_early/pallas_call | solution.py:372
  74.9 2.6 %collective-permute-start.21 = (bf16[64,768]{1,0:T(8,128)(2,1)S(1)}, bf16[64,768]{1,0:T(8,128)(2,1)S(1)}, u32[]{:S(2)}, u32[]{:S(2)}) collective-permute-start(bf16[64,768]{1,0:T(8,128)(2,1)S(1)} %get-tuple-element.71), channel_id=1, source_target_pairs={{4,0},{6,2},{8,4},{10,6},{12,8},{14,10},{0,12},{2,14},{5,1},{7,3},... | collective-permute-start | bytes 294920 | tf_op jit(solution)/shard_map/ppermute | solution.py:525
  77.5 1.9 %collective-permute-done.23.refs_1_ = bf16[4,2,16,1536]{3,2,1,0:T(8,128)(2,1)S(1)} collective-permute-done((bf16[4,2,16,1536]{3,2,1,0:T(8,128)(2,1)S(1)}, bf16[4,2,16,1536]{3,2,1,0:T(8,128)(2,1)S(1)}, u32[]{:S(2)}, u32[]{:S(2)}) %collective-permute-start.23) | collective-permute-done | bytes 393248 | tf_op jit(solution)/shard_map/ppermute | solution.py:525
  79.3 2.1 %elementals_late.1 = (f32[32,768]{1,0:T(8,128)S(1)}, bf16[32,768]{1,0:T(8,128)(2,1)S(1)}, bf16[32,768]{1,0:T(8,128)(2,1)S(1)}, bf16[32,768]{1,0:T(8,128)(2,1)S(1)}) custom-call(s32[2]{0:T(128)S(1)} %pad_add_fusion.place_ref, bf16[4,2,16,1536]{3,2,1,0:T(8,128)(2,1)S(1)} %collective-permute-done.22.refs_0_, ...), custom_call_target="tpu_custom_call" | custom-call | flops 603979776 | bytes 2359296 | tf_op jit(solution)/shard_map/elementals_late/pallas_call | solution.py:372
  81.7 3.3 %collective-permute-start.25 = (bf16[32,768]{1,0:T(8,128)(2,1)S(1)}, bf16[32,768]{1,0:T(8,128)(2,1)S(1)}, u32[]{:S(2)}, u32[]{:S(2)}) collective-permute-start(bf16[32,768]{1,0:T(8,128)(2,1)S(1)} %get-tuple-element.75), channel_id=1, source_target_pairs={{8,0},{10,2},{12,4},{14,6},{0,8},{2,10},{4,12},{6,14},{9,1},{11,3}... | collective-permute-start | bytes 147464 | tf_op jit(solution)/shard_map/ppermute | solution.py:525
  85.4 2.2 %collective-permute-done.24.refs_5_ = bf16[32,768]{1,0:T(8,128)(2,1)S(1)} collective-permute-done((bf16[32,768]{1,0:T(8,128)(2,1)S(1)}, bf16[32,768]{1,0:T(8,128)(2,1)S(1)}, u32[]{:S(2)}, u32[]{:S(2)}) %collective-permute-start.24) | collective-permute-done | bytes 49184 | tf_op jit(solution)/shard_map/ppermute | solution.py:525
  89.7 2.1 %collective-permute-start.27 = (bf16[96,768]{1,0:T(8,128)(2,1)S(1)}, bf16[96,768]{1,0:T(8,128)(2,1)S(1)}, u32[]{:S(2)}, u32[]{:S(2)}) collective-permute-start(bf16[96,768]{1,0:T(8,128)(2,1)S(1)} %add_parts.1.refs_0_), channel_id=1, source_target_pairs={{4,0},{6,2},{8,4},{10,6},{12,8},{14,10},{0,12},{2,14},{5,1},{7,3},... | collective-permute-start | bytes 442376 | tf_op jit(solution)/shard_map/ppermute | solution.py:525
  93.5 2.7 %collective-permute-done.27.refs_1_ = bf16[96,768]{1,0:T(8,128)(2,1)S(1)} collective-permute-done((bf16[96,768]{1,0:T(8,128)(2,1)S(1)}, bf16[96,768]{1,0:T(8,128)(2,1)S(1)}, u32[]{:S(2)}, u32[]{:S(2)}) %collective-permute-start.27) | collective-permute-done | bytes 147488 | tf_op jit(solution)/shard_map/ppermute | solution.py:525
  96.2 1.4 %collective-permute-start.31 = (bf16[96,768]{1,0:T(8,128)(2,1)S(1)}, bf16[96,768]{1,0:T(8,128)(2,1)S(1)}, u32[]{:S(2)}, u32[]{:S(2)}) collective-permute-start(bf16[96,768]{1,0:T(8,128)(2,1)S(1)} %collective-permute-done.27.refs_1_), channel_id=1, source_target_pairs={{2,0},{0,2},{6,4},{4,6},{10,8},{8,10},{14,12},{12,14},{3,1},{1,3},... | collective-permute-start | bytes 442376 | tf_op jit(solution)/shard_map/ppermute | solution.py:525
  97.6 3.7 %collective-permute-done.28.refs_2_ = bf16[96,768]{1,0:T(8,128)(2,1)S(1)} collective-permute-done((bf16[96,768]{1,0:T(8,128)(2,1)S(1)}, bf16[96,768]{1,0:T(8,128)(2,1)S(1)}, u32[]{:S(2)}, u32[]{:S(2)}) %collective-permute-start.28) | collective-permute-done | bytes 147488 | tf_op jit(solution)/shard_map/ppermute | solution.py:525
  103.3 3.3 %project_first.1.first_ref = bf16[8,192,768]{2,1,0:T(8,128)(2,1)S(1)} custom-call(s32[2]{0:T(128)S(1)} %pad_add_fusion.place_ref, s32[2]{0:T(128)S(1)} %copy-done.4, bf16[8,2,192,384]{3,2,1,0:T(8,128)(2,1)S(1)} %bitcast.15, bf16[96,768]{1,0:T(8,128)(2,1)S(1)} %add_parts.1.refs_0_, bf16[96,768]{1,0:T(8,128)(2,1)S(1)} %collective-permute-done.27.refs_1_, ...), custom_call_target="tpu_custom_call" | custom-call | flops 1811939328 | bytes 4718592 | tf_op jit(solution)/shard_map/project_first/pallas_call | solution.py:487
  106.6 1.5 %collective-permute-done.33.refs_3_ = bf16[96,768]{1,0:T(8,128)(2,1)S(1)} collective-permute-done((bf16[96,768]{1,0:T(8,128)(2,1)S(1)}, bf16[96,768]{1,0:T(8,128)(2,1)S(1)}, u32[]{:S(2)}, u32[]{:S(2)}) %collective-permute-start.33) | collective-permute-done | bytes 147488 | tf_op jit(solution)/shard_map/ppermute | solution.py:525
  108.2 5.1 %project_second.1 = bf16[8,2,2,192,384]{4,3,2,1,0:T(8,128)(2,1)} custom-call(s32[2]{0:T(128)S(1)} %pad_add_fusion.place_ref, s32[2]{0:T(128)S(1)} %copy-done.4, bf16[8,2,192,384]{3,2,1,0:T(8,128)(2,1)S(1)} %bitcast.16, bf16[8,192,768]{2,1,0:T(8,128)(2,1)S(1)} %project_first.1.first_ref, bf16[96,768]{1,0:T(8,128)(2,1)S(1)} %collective-permute-done.30.refs_0_, ...), custom_call_target="tpu_custom_call" | custom-call | flops 1811939328 | bytes 7077888 | tf_op jit(solution)/shard_map/project_second/pallas_call | solution.py:503
  (69 shorter events, 20.1 us)
Async XLA Ops:
  1.3 10.7 %collective-permute-start = (bf16[600,128]{1,0:T(8,128)(2,1)S(1)}, bf16[600,128]{1,0:T(8,128)(2,1)S(1)}, u32[]{:S(2)}, u32[]{:S(2)}) collective-permute-start(bf16[600,128]{1,0:T(8,128)(2,1)S(1)} %get-tuple-element.41.refs_0_), channel_id=1, source_target_pairs={{12,0},{14,2},{0,4},{2,6},{4,8},{6,10},{8,12},{10,14},{13,1},{15,3... | collective-permute-start | bytes 460808 | tf_op jit(solution)/shard_map/ppermute | solution.py:525
  4.4 16.2 %collective-permute-start.1 = (bf16[600,128]{1,0:T(8,128)(2,1)S(1)}, bf16[600,128]{1,0:T(8,128)(2,1)S(1)}, u32[]{:S(2)}, u32[]{:S(2)}) collective-permute-start(bf16[600,128]{1,0:T(8,128)(2,1)S(1)} %get-tuple-element.42), channel_id=1, source_target_pairs={{8,0},{10,2},{12,4},{14,6},{0,8},{2,10},{4,12},{6,14},{9,1},{11,3}... | collective-permute-start | bytes 460808 | tf_op jit(solution)/shard_map/ppermute | solution.py:525
  7.0 13.6 %collective-permute-start.2 = (bf16[600,128]{1,0:T(8,128)(2,1)S(1)}, bf16[600,128]{1,0:T(8,128)(2,1)S(1)}, u32[]{:S(2)}, u32[]{:S(2)}) collective-permute-start(bf16[600,128]{1,0:T(8,128)(2,1)S(1)} %get-tuple-element.43), channel_id=1, source_target_pairs={{4,0},{6,2},{8,4},{10,6},{12,8},{14,10},{0,12},{2,14},{5,1},{7,3},... | collective-permute-start | bytes 460808 | tf_op jit(solution)/shard_map/ppermute | solution.py:525
  10.6 22.1 %collective-permute-start.6 = (bf16[384,128]{1,0:T(8,128)(2,1)S(1)}, bf16[384,128]{1,0:T(8,128)(2,1)S(1)}, u32[]{:S(2)}, u32[]{:S(2)}) collective-permute-start(bf16[384,128]{1,0:T(8,128)(2,1)S(1)} %get-tuple-element.48.refs_1_), channel_id=1, source_target_pairs={{12,0},{14,2},{0,4},{2,6},{4,8},{6,10},{8,12},{10,14},{13,1},{15,3... | collective-permute-start | bytes 294920 | tf_op jit(solution)/shard_map/ppermute | solution.py:525
  11.4 22.8 %collective-permute-start.7 = (bf16[384,128]{1,0:T(8,128)(2,1)S(1)}, bf16[384,128]{1,0:T(8,128)(2,1)S(1)}, u32[]{:S(2)}, u32[]{:S(2)}) collective-permute-start(bf16[384,128]{1,0:T(8,128)(2,1)S(1)} %get-tuple-element.49), channel_id=1, source_target_pairs={{8,0},{10,2},{12,4},{14,6},{0,8},{2,10},{4,12},{6,14},{9,1},{11,3}... | collective-permute-start | bytes 294920 | tf_op jit(solution)/shard_map/ppermute | solution.py:525
  12.0 25.1 %collective-permute-start.8 = (bf16[384,128]{1,0:T(8,128)(2,1)S(1)}, bf16[384,128]{1,0:T(8,128)(2,1)S(1)}, u32[]{:S(2)}, u32[]{:S(2)}) collective-permute-start(bf16[384,128]{1,0:T(8,128)(2,1)S(1)} %get-tuple-element.50), channel_id=1, source_target_pairs={{4,0},{6,2},{8,4},{10,6},{12,8},{14,10},{0,12},{2,14},{5,1},{7,3},... | collective-permute-start | bytes 294920 | tf_op jit(solution)/shard_map/ppermute | solution.py:525
  26.0 17.1 %collective-permute-start.3 = (bf16[6,64,128]{2,1,0:T(8,128)(2,1)S(1)}, bf16[6,64,128]{2,1,0:T(8,128)(2,1)S(1)}, u32[]{:S(2)}, u32[]{:S(2)}) collective-permute-start(bf16[6,64,128]{2,1,0:T(8,128)(2,1)S(1)} %get-tuple-element.45), channel_id=1, source_target_pairs={{4,0},{6,2},{8,4},{10,6},{12,8},{14,10},{0,12},{2,14},{5,1},{7,3},... | collective-permute-start | bytes 294920 | tf_op jit(solution)/shard_map/ppermute | solution.py:525
  32.7 14.7 %collective-permute-start.4 = (bf16[6,64,128]{2,1,0:T(8,128)(2,1)S(1)}, bf16[6,64,128]{2,1,0:T(8,128)(2,1)S(1)}, u32[]{:S(2)}, u32[]{:S(2)}) collective-permute-start(bf16[6,64,128]{2,1,0:T(8,128)(2,1)S(1)} %get-tuple-element.46), channel_id=1, source_target_pairs={{8,0},{10,2},{12,4},{14,6},{0,8},{2,10},{4,12},{6,14},{9,1},{11,3}... | collective-permute-start | bytes 294920 | tf_op jit(solution)/shard_map/ppermute | solution.py:525
  32.7 14.7 %collective-permute-start.5 = (bf16[6,64,128]{2,1,0:T(8,128)(2,1)S(1)}, bf16[6,64,128]{2,1,0:T(8,128)(2,1)S(1)}, u32[]{:S(2)}, u32[]{:S(2)}) collective-permute-start(bf16[6,64,128]{2,1,0:T(8,128)(2,1)S(1)} %get-tuple-element.47), channel_id=1, source_target_pairs={{12,0},{14,2},{0,4},{2,6},{4,8},{6,10},{8,12},{10,14},{13,1},{15,3... | collective-permute-start | bytes 294920 | tf_op jit(solution)/shard_map/ppermute | solution.py:525
  34.2 14.3 %collective-permute-start.12 = (bf16[384,128]{1,0:T(8,128)(2,1)S(1)}, bf16[384,128]{1,0:T(8,128)(2,1)S(1)}, u32[]{:S(2)}, u32[]{:S(2)}) collective-permute-start(bf16[384,128]{1,0:T(8,128)(2,1)S(1)} %get-tuple-element.56), channel_id=1, source_target_pairs={{12,0},{14,2},{0,4},{2,6},{4,8},{6,10},{8,12},{10,14},{13,1},{15,3... | collective-permute-start | bytes 294920 | tf_op jit(solution)/shard_map/ppermute | solution.py:525
  37.1 14.5 %collective-permute-start.13 = (bf16[384,128]{1,0:T(8,128)(2,1)S(1)}, bf16[384,128]{1,0:T(8,128)(2,1)S(1)}, u32[]{:S(2)}, u32[]{:S(2)}) collective-permute-start(bf16[384,128]{1,0:T(8,128)(2,1)S(1)} %get-tuple-element.57), channel_id=1, source_target_pairs={{8,0},{10,2},{12,4},{14,6},{0,8},{2,10},{4,12},{6,14},{9,1},{11,3}... | collective-permute-start | bytes 294920 | tf_op jit(solution)/shard_map/ppermute | solution.py:525
  43.0 11.2 %collective-permute-start.14 = (bf16[384,128]{1,0:T(8,128)(2,1)S(1)}, bf16[384,128]{1,0:T(8,128)(2,1)S(1)}, u32[]{:S(2)}, u32[]{:S(2)}) collective-permute-start(bf16[384,128]{1,0:T(8,128)(2,1)S(1)} %get-tuple-element.58), channel_id=1, source_target_pairs={{4,0},{6,2},{8,4},{10,6},{12,8},{14,10},{0,12},{2,14},{5,1},{7,3},... | collective-permute-start | bytes 294920 | tf_op jit(solution)/shard_map/ppermute | solution.py:525
  47.4 12.1 %collective-permute-start.10 = (bf16[6,64,128]{2,1,0:T(8,128)(2,1)S(1)}, bf16[6,64,128]{2,1,0:T(8,128)(2,1)S(1)}, u32[]{:S(2)}, u32[]{:S(2)}) collective-permute-start(bf16[6,64,128]{2,1,0:T(8,128)(2,1)S(1)} %get-tuple-element.54), channel_id=1, source_target_pairs={{8,0},{10,2},{12,4},{14,6},{0,8},{2,10},{4,12},{6,14},{9,1},{11,3}... | collective-permute-start | bytes 294920 | tf_op jit(solution)/shard_map/ppermute | solution.py:525
  47.5 14.4 %collective-permute-start.11 = (bf16[6,64,128]{2,1,0:T(8,128)(2,1)S(1)}, bf16[6,64,128]{2,1,0:T(8,128)(2,1)S(1)}, u32[]{:S(2)}, u32[]{:S(2)}) collective-permute-start(bf16[6,64,128]{2,1,0:T(8,128)(2,1)S(1)} %get-tuple-element.55), channel_id=1, source_target_pairs={{12,0},{14,2},{0,4},{2,6},{4,8},{6,10},{8,12},{10,14},{13,1},{15,3... | collective-permute-start | bytes 294920 | tf_op jit(solution)/shard_map/ppermute | solution.py:525
  48.5 22.2 %collective-permute-start.18 = (bf16[4,2,16,1536]{3,2,1,0:T(8,128)(2,1)S(1)}, bf16[4,2,16,1536]{3,2,1,0:T(8,128)(2,1)S(1)}, u32[]{:S(2)}, u32[]{:S(2)}) collective-permute-start(bf16[4,2,16,1536]{3,2,1,0:T(8,128)(2,1)S(1)} %get-tuple-element.52.refs_0_), channel_id=1, source_target_pairs={{2,0},{0,2},{6,4},{4,6},{10,8},{8,10},{14,12},{12,14},{3,1},{1,3},... | collective-permute-start | bytes 1179656 | tf_op jit(solution)/shard_map/ppermute | solution.py:525
  51.6 10.6 %collective-permute-start.9 = (bf16[6,64,128]{2,1,0:T(8,128)(2,1)S(1)}, bf16[6,64,128]{2,1,0:T(8,128)(2,1)S(1)}, u32[]{:S(2)}, u32[]{:S(2)}) collective-permute-start(bf16[6,64,128]{2,1,0:T(8,128)(2,1)S(1)} %get-tuple-element.53), channel_id=1, source_target_pairs={{4,0},{6,2},{8,4},{10,6},{12,8},{14,10},{0,12},{2,14},{5,1},{7,3},... | collective-permute-start | bytes 294920 | tf_op jit(solution)/shard_map/ppermute | solution.py:525
  59.3 5.5 %collective-permute-start.15 = (bf16[6,64,128]{2,1,0:T(8,128)(2,1)S(1)}, bf16[6,64,128]{2,1,0:T(8,128)(2,1)S(1)}, u32[]{:S(2)}, u32[]{:S(2)}) collective-permute-start(bf16[6,64,128]{2,1,0:T(8,128)(2,1)S(1)} %get-tuple-element.62), channel_id=1, source_target_pairs={{4,0},{6,2},{8,4},{10,6},{12,8},{14,10},{0,12},{2,14},{5,1},{7,3},... | collective-permute-start | bytes 294920 | tf_op jit(solution)/shard_map/ppermute | solution.py:525
  59.6 7.5 %collective-permute-start.16 = (bf16[6,64,128]{2,1,0:T(8,128)(2,1)S(1)}, bf16[6,64,128]{2,1,0:T(8,128)(2,1)S(1)}, u32[]{:S(2)}, u32[]{:S(2)}) collective-permute-start(bf16[6,64,128]{2,1,0:T(8,128)(2,1)S(1)} %get-tuple-element.63), channel_id=1, source_target_pairs={{8,0},{10,2},{12,4},{14,6},{0,8},{2,10},{4,12},{6,14},{9,1},{11,3}... | collective-permute-start | bytes 294920 | tf_op jit(solution)/shard_map/ppermute | solution.py:525
  61.9 6.4 %collective-permute-start.17 = (bf16[6,64,128]{2,1,0:T(8,128)(2,1)S(1)}, bf16[6,64,128]{2,1,0:T(8,128)(2,1)S(1)}, u32[]{:S(2)}, u32[]{:S(2)}) collective-permute-start(bf16[6,64,128]{2,1,0:T(8,128)(2,1)S(1)} %get-tuple-element.64), channel_id=1, source_target_pairs={{12,0},{14,2},{0,4},{2,6},{4,8},{6,10},{8,12},{10,14},{13,1},{15,3... | collective-permute-start | bytes 294920 | tf_op jit(solution)/shard_map/ppermute | solution.py:525
  63.0 14.4 %collective-permute-start.22 = (bf16[4,2,16,1536]{3,2,1,0:T(8,128)(2,1)S(1)}, bf16[4,2,16,1536]{3,2,1,0:T(8,128)(2,1)S(1)}, u32[]{:S(2)}, u32[]{:S(2)}) collective-permute-start(bf16[4,2,16,1536]{3,2,1,0:T(8,128)(2,1)S(1)} %get-tuple-element.61.refs_1_), channel_id=1, source_target_pairs={{2,0},{0,2},{6,4},{4,6},{10,8},{8,10},{14,12},{12,14},{3,1},{1,3},... | collective-permute-start | bytes 1179656 | tf_op jit(solution)/shard_map/ppermute | solution.py:525
  69.2 10.1 %collective-permute-start.23 = (bf16[4,2,16,1536]{3,2,1,0:T(8,128)(2,1)S(1)}, bf16[4,2,16,1536]{3,2,1,0:T(8,128)(2,1)S(1)}, u32[]{:S(2)}, u32[]{:S(2)}) collective-permute-start(bf16[4,2,16,1536]{3,2,1,0:T(8,128)(2,1)S(1)} %get-tuple-element.66.refs_2_), channel_id=1, source_target_pairs={{2,0},{0,2},{6,4},{4,6},{10,8},{8,10},{14,12},{12,14},{3,1},{1,3},... | collective-permute-start | bytes 1179656 | tf_op jit(solution)/shard_map/ppermute | solution.py:525
  73.6 11.4 %collective-permute-start.19 = (bf16[64,768]{1,0:T(8,128)(2,1)S(1)}, bf16[64,768]{1,0:T(8,128)(2,1)S(1)}, u32[]{:S(2)}, u32[]{:S(2)}) collective-permute-start(bf16[64,768]{1,0:T(8,128)(2,1)S(1)} %get-tuple-element.69), channel_id=1, source_target_pairs={{12,0},{14,2},{0,4},{2,6},{4,8},{6,10},{8,12},{10,14},{13,1},{15,3... | collective-permute-start | bytes 294920 | tf_op jit(solution)/shard_map/ppermute | solution.py:525
  73.6 11.7 %collective-permute-start.20 = (bf16[64,768]{1,0:T(8,128)(2,1)S(1)}, bf16[64,768]{1,0:T(8,128)(2,1)S(1)}, u32[]{:S(2)}, u32[]{:S(2)}) collective-permute-start(bf16[64,768]{1,0:T(8,128)(2,1)S(1)} %get-tuple-element.70), channel_id=1, source_target_pairs={{8,0},{10,2},{12,4},{14,6},{0,8},{2,10},{4,12},{6,14},{9,1},{11,3}... | collective-permute-start | bytes 294920 | tf_op jit(solution)/shard_map/ppermute | solution.py:525
  74.9 10.5 %collective-permute-start.21 = (bf16[64,768]{1,0:T(8,128)(2,1)S(1)}, bf16[64,768]{1,0:T(8,128)(2,1)S(1)}, u32[]{:S(2)}, u32[]{:S(2)}) collective-permute-start(bf16[64,768]{1,0:T(8,128)(2,1)S(1)} %get-tuple-element.71), channel_id=1, source_target_pairs={{4,0},{6,2},{8,4},{10,6},{12,8},{14,10},{0,12},{2,14},{5,1},{7,3},... | collective-permute-start | bytes 294920 | tf_op jit(solution)/shard_map/ppermute | solution.py:525
  81.4 6.1 %collective-permute-start.24 = (bf16[32,768]{1,0:T(8,128)(2,1)S(1)}, bf16[32,768]{1,0:T(8,128)(2,1)S(1)}, u32[]{:S(2)}, u32[]{:S(2)}) collective-permute-start(bf16[32,768]{1,0:T(8,128)(2,1)S(1)} %get-tuple-element.74), channel_id=1, source_target_pairs={{12,0},{14,2},{0,4},{2,6},{4,8},{6,10},{8,12},{10,14},{13,1},{15,3... | collective-permute-start | bytes 147464 | tf_op jit(solution)/shard_map/ppermute | solution.py:525
  81.7 6.5 %collective-permute-start.25 = (bf16[32,768]{1,0:T(8,128)(2,1)S(1)}, bf16[32,768]{1,0:T(8,128)(2,1)S(1)}, u32[]{:S(2)}, u32[]{:S(2)}) collective-permute-start(bf16[32,768]{1,0:T(8,128)(2,1)S(1)} %get-tuple-element.75), channel_id=1, source_target_pairs={{8,0},{10,2},{12,4},{14,6},{0,8},{2,10},{4,12},{6,14},{9,1},{11,3}... | collective-permute-start | bytes 147464 | tf_op jit(solution)/shard_map/ppermute | solution.py:525
  89.7 6.5 %collective-permute-start.27 = (bf16[96,768]{1,0:T(8,128)(2,1)S(1)}, bf16[96,768]{1,0:T(8,128)(2,1)S(1)}, u32[]{:S(2)}, u32[]{:S(2)}) collective-permute-start(bf16[96,768]{1,0:T(8,128)(2,1)S(1)} %add_parts.1.refs_0_), channel_id=1, source_target_pairs={{4,0},{6,2},{8,4},{10,6},{12,8},{14,10},{0,12},{2,14},{5,1},{7,3},... | collective-permute-start | bytes 442376 | tf_op jit(solution)/shard_map/ppermute | solution.py:525
  91.7 9.5 %collective-permute-start.28 = (bf16[96,768]{1,0:T(8,128)(2,1)S(1)}, bf16[96,768]{1,0:T(8,128)(2,1)S(1)}, u32[]{:S(2)}, u32[]{:S(2)}) collective-permute-start(bf16[96,768]{1,0:T(8,128)(2,1)S(1)} %add_parts.1.refs_0_), channel_id=1, source_target_pairs={{8,0},{10,2},{12,4},{14,6},{0,8},{2,10},{4,12},{6,14},{9,1},{11,3}... | collective-permute-start | bytes 442376 | tf_op jit(solution)/shard_map/ppermute | solution.py:525
  92.1 10.5 %collective-permute-start.29 = (bf16[96,768]{1,0:T(8,128)(2,1)S(1)}, bf16[96,768]{1,0:T(8,128)(2,1)S(1)}, u32[]{:S(2)}, u32[]{:S(2)}) collective-permute-start(bf16[96,768]{1,0:T(8,128)(2,1)S(1)} %add_parts.1.refs_0_), channel_id=1, source_target_pairs={{12,0},{14,2},{0,4},{2,6},{4,8},{6,10},{8,12},{10,14},{13,1},{15,3... | collective-permute-start | bytes 442376 | tf_op jit(solution)/shard_map/ppermute | solution.py:525
  92.4 14.2 %collective-permute-start.30 = (bf16[96,768]{1,0:T(8,128)(2,1)S(1)}, bf16[96,768]{1,0:T(8,128)(2,1)S(1)}, u32[]{:S(2)}, u32[]{:S(2)}) collective-permute-start(bf16[96,768]{1,0:T(8,128)(2,1)S(1)} %add_parts.1.refs_0_), channel_id=1, source_target_pairs={{2,0},{0,2},{6,4},{4,6},{10,8},{8,10},{14,12},{12,14},{3,1},{1,3},... | collective-permute-start | bytes 442376 | tf_op jit(solution)/shard_map/ppermute | solution.py:525
  96.2 10.4 %collective-permute-start.31 = (bf16[96,768]{1,0:T(8,128)(2,1)S(1)}, bf16[96,768]{1,0:T(8,128)(2,1)S(1)}, u32[]{:S(2)}, u32[]{:S(2)}) collective-permute-start(bf16[96,768]{1,0:T(8,128)(2,1)S(1)} %collective-permute-done.27.refs_1_), channel_id=1, source_target_pairs={{2,0},{0,2},{6,4},{4,6},{10,8},{8,10},{14,12},{12,14},{3,1},{1,3},... | collective-permute-start | bytes 442376 | tf_op jit(solution)/shard_map/ppermute | solution.py:525
  102.6 5.6 %collective-permute-start.33 = (bf16[96,768]{1,0:T(8,128)(2,1)S(1)}, bf16[96,768]{1,0:T(8,128)(2,1)S(1)}, u32[]{:S(2)}, u32[]{:S(2)}) collective-permute-start(bf16[96,768]{1,0:T(8,128)(2,1)S(1)} %collective-permute-done.29.refs_3_), channel_id=1, source_target_pairs={{2,0},{0,2},{6,4},{4,6},{10,8},{8,10},{14,12},{12,14},{3,1},{1,3},... | collective-permute-start | bytes 442376 | tf_op jit(solution)/shard_map/ppermute | solution.py:525
  (8 other events, 87.4 us)

commit v7 on v6

--- a/solution.py
+++ b/solution.py
@@ -516,7 +516,7 @@
     )(place, owner, tau, first, *pieces)
 
 
-def from_place(block, up, across):
+def permuted(block, up, across):
     sites, groups = lax.axis_size("site"), lax.axis_size("vec")
     route = []
     for z in range(sites):
@@ -545,7 +545,7 @@
             packed = first_pack(own, sites, own_links)
         else:
             packed = pack(own, place, chunk, sites, after)
-        received.append([from_place(packed[d - 1], -d, 0) for d in range(1, sites)])
+        received.append([permuted(packed[d - 1], -d, 0) for d in range(1, sites)])
 
     flat = lax.broadcasted_iota(jnp.int32, (4, LANES), 0) * LANES + lax.broadcasted_iota(jnp.int32, (4, LANES), 1)
     theta = phase_angle(momenta, flat % LX, flat // LX, jnp.full_like(flat, site), sites)
@@ -558,25 +558,25 @@
         after = [] if last is None else [last]
         if kind == "filter":
             out = filter_chunk(own, place, chunk, received[chunk], table, after)
-            hops[chunk] = [out[0]] + [from_place(out[d], d, 0) for d in range(1, sites)]
+            hops[chunk] = [out[0]] + [permuted(out[d], d, 0) for d in range(1, sites)]
             last = out[0]
         else:
             f, s = finish(own, place, chunk, hops[chunk], cosine, sine, after)
-            other[chunk] = from_place(f, 0, 1)
+            other[chunk] = permuted(f, 0, 1)
             filtered[chunk], shifted[chunk] = f, s
             last = s
     filtered, shifted, other = ([group_of[n] for n in range(len(CHUNKS))] for group_of in (filtered, shifted, other))
 
     *parts, right = elementals(place, block_owner, filtered + other[:1], shifted, None, sites)
-    sent = [from_place(parts[d], -d, 0) for d in range(1, sites)]
+    sent = [permuted(parts[d], -d, 0) for d in range(1, sites)]
     early = [parts[0], *sent]
     parts = elementals(place, block_owner, other[1:], None, right, sites)
-    sent = [from_place(parts[d], -d, 0) for d in range(1, sites)]
+    sent = [permuted(parts[d], -d, 0) for d in range(1, sites)]
     mine = add_parts(early, [parts[0], *sent])
 
-    across = [from_place(mine, 0, 1)]
-    pieces = [mine] + [from_place(mine, up, 0) for up in range(1, sites)]
-    across += [from_place(piece, 0, 1) for piece in pieces[1:]]
+    across = [permuted(mine, 0, 1)]
+    pieces = [mine] + [permuted(mine, up, 0) for up in range(1, sites)]
+    across += [permuted(piece, 0, 1) for piece in pieces[1:]]
     sinks, spins = peramb.shape[1], peramb.shape[2]
     tau = peramb.reshape(sinks * spins, 2, block, peramb.shape[5])
     first = project_first(tau, place, block_owner, pieces, momenta.shape[0])

time: 113 us -> 113 us (level)
  no operation moved by 1% of the time
where the time goes in v7:
time: 113 us
  starting transfers between devices  48.9 us (43%)
  Pallas kernels  34 us (30%)
  waiting for transfers between devices  27.8 us (25%)
  local copies, waits for them, and re-layouts  1.85 us (2%)
    ppermute x34, starting transfers between devices, permuted(): return lax.ppermute(block, ('site', 'vec'), route)  48.9 us
    ppermute x34, waiting for transfers between devices, permuted(): return lax.ppermute(block, ('site', 'vec'), route)  27.8 us
    pallas_call x3, Pallas kernels, filter_chunk(): pl.pallas_call(functools.partial(filter_kernel, sites, chunk), out_shape=...  15.2 us
    pallas_call x1, Pallas kernels, project_second(): pl.pallas_call(functools.partial(second_kernel, len(pieces)), grid=(outer...  5.14 us
    pallas_call x2, Pallas kernels, elementals(): pl.pallas_call(functools.partial(early_kernel if early else late_kernel,...  4.9 us
    pallas_call x1, Pallas kernels, project_first(): pl.pallas_call(functools.partial(first_kernel, len(pieces)), out_shape=pl...  3.3 us
    pallas_call x3, Pallas kernels, finish(): pl.pallas_call(functools.partial(finish_kernel, sites, chunk), out_shape=...  2.67 us
  transfers between devices with their start and end apart: 34, of which 13 were waited for; matrix products, arithmetic and copies ran while one was open for 1% of the time, Pallas kernels for 24%

profile of v7, /device:TPU:0, one launch (start us, length us, event | category | flops | bytes accessed | tf_op | source)
XLA Modules:
  0.0 113.3 jit_solution(2040057109349482036)
XLA Ops:
  1.3 3.1 %collective-permute-start = (bf16[600,128]{1,0:T(8,128)(2,1)S(1)}, bf16[600,128]{1,0:T(8,128)(2,1)S(1)}, u32[]{:S(2)}, u32[]{:S(2)}) collective-permute-start(bf16[600,128]{1,0:T(8,128)(2,1)S(1)} %get-tuple-element.41.refs_0_), channel_id=1, source_target_pairs={{12,0},{14,2},{0,4},{2,6},{4,8},{6,10},{8,12},{10,14},{13,1},{15,3... | collective-permute-start | bytes 460808 | tf_op jit(solution)/shard_map/ppermute | solution.py:525
  4.4 2.6 %collective-permute-start.1 = (bf16[600,128]{1,0:T(8,128)(2,1)S(1)}, bf16[600,128]{1,0:T(8,128)(2,1)S(1)}, u32[]{:S(2)}, u32[]{:S(2)}) collective-permute-start(bf16[600,128]{1,0:T(8,128)(2,1)S(1)} %get-tuple-element.42), channel_id=1, source_target_pairs={{8,0},{10,2},{12,4},{14,6},{0,8},{2,10},{4,12},{6,14},{9,1},{11,3}... | collective-permute-start | bytes 460808 | tf_op jit(solution)/shard_map/ppermute | solution.py:525
  8.4 1.7 %copy-done = f32[1,2,3,192,1,512]{5,4,3,2,1,0:T(1,128)S(1)} copy-done((f32[1,2,3,192,1,512]{5,4,3,2,1,0:T(1,128)S(1)}, f32[1,2,3,192,1,512]{5,4,3,2,1,0:T(1,128)}, u32[]{:S(2)}) %copy-start) | copy-done | bytes 2359320
  12.0 2.9 %collective-permute-start.8 = (bf16[384,128]{1,0:T(8,128)(2,1)S(1)}, bf16[384,128]{1,0:T(8,128)(2,1)S(1)}, u32[]{:S(2)}, u32[]{:S(2)}) collective-permute-start(bf16[384,128]{1,0:T(8,128)(2,1)S(1)} %get-tuple-element.50), channel_id=1, source_target_pairs={{4,0},{6,2},{8,4},{10,6},{12,8},{14,10},{0,12},{2,14},{5,1},{7,3},... | collective-permute-start | bytes 294920 | tf_op jit(solution)/shard_map/ppermute | solution.py:525
  14.9 5.7 %collective-permute-done.1.refs_2_ = bf16[600,128]{1,0:T(8,128)(2,1)S(1)} collective-permute-done((bf16[600,128]{1,0:T(8,128)(2,1)S(1)}, bf16[600,128]{1,0:T(8,128)(2,1)S(1)}, u32[]{:S(2)}, u32[]{:S(2)}) %collective-permute-start.1) | collective-permute-done | bytes 153632 | tf_op jit(solution)/shard_map/ppermute | solution.py:525
  20.9 5.1 %shard_map.55 = (bf16[6,64,128]{2,1,0:T(8,128)(2,1)S(1)}, bf16[6,64,128]{2,1,0:T(8,128)(2,1)S(1)}, bf16[6,64,128]{2,1,0:T(8,128)(2,1)S(1)}, bf16[6,64,128]{2,1,0:T(8,128)(2,1)S(1)}) custom-call(s32[2]{0:T(128)S(1)} %pad_add_fusion.place_ref, f32[6,768,128]{2,1,0:T(8,128)S(1)} %bitcast.8, bf16[600,128]{1,0:T(8,128)(2,1)S(1)} %collective-permute-done.refs_1_.refs_0_, ...), custom_call_target="tpu_custom_call" | custom-call | flops 28311552 | bytes 786432 | tf_op jit(solution)/shard_map/pallas_call | solution.py:238
  26.0 6.8 %collective-permute-start.3 = (bf16[6,64,128]{2,1,0:T(8,128)(2,1)S(1)}, bf16[6,64,128]{2,1,0:T(8,128)(2,1)S(1)}, u32[]{:S(2)}, u32[]{:S(2)}) collective-permute-start(bf16[6,64,128]{2,1,0:T(8,128)(2,1)S(1)} %get-tuple-element.45), channel_id=1, source_target_pairs={{4,0},{6,2},{8,4},{10,6},{12,8},{14,10},{0,12},{2,14},{5,1},{7,3},... | collective-permute-start | bytes 294920 | tf_op jit(solution)/shard_map/ppermute | solution.py:525
  34.2 2.9 %collective-permute-start.12 = (bf16[384,128]{1,0:T(8,128)(2,1)S(1)}, bf16[384,128]{1,0:T(8,128)(2,1)S(1)}, u32[]{:S(2)}, u32[]{:S(2)}) collective-permute-start(bf16[384,128]{1,0:T(8,128)(2,1)S(1)} %get-tuple-element.56), channel_id=1, source_target_pairs={{12,0},{14,2},{0,4},{2,6},{4,8},{6,10},{8,12},{10,14},{13,1},{15,3... | collective-permute-start | bytes 294920 | tf_op jit(solution)/shard_map/ppermute | solution.py:525
  38.0 5.1 %shard_map.57 = (bf16[6,64,128]{2,1,0:T(8,128)(2,1)S(1)}, bf16[6,64,128]{2,1,0:T(8,128)(2,1)S(1)}, bf16[6,64,128]{2,1,0:T(8,128)(2,1)S(1)}, bf16[6,64,128]{2,1,0:T(8,128)(2,1)S(1)}) custom-call(s32[2]{0:T(128)S(1)} %pad_add_fusion.place_ref, f32[6,768,128]{2,1,0:T(8,128)S(1)} %bitcast.10, bf16[384,128]{1,0:T(8,128)(2,1)S(1)} %collective-permute-done.6.refs_1_, ...), custom_call_target="tpu_custom_call" | custom-call | flops 28311552 | bytes 786432 | tf_op jit(solution)/shard_map/pallas_call | solution.py:238
  43.0 1.6 %collective-permute-start.14 = (bf16[384,128]{1,0:T(8,128)(2,1)S(1)}, bf16[384,128]{1,0:T(8,128)(2,1)S(1)}, u32[]{:S(2)}, u32[]{:S(2)}) collective-permute-start(bf16[384,128]{1,0:T(8,128)(2,1)S(1)} %get-tuple-element.58), channel_id=1, source_target_pairs={{4,0},{6,2},{8,4},{10,6},{12,8},{14,10},{0,12},{2,14},{5,1},{7,3},... | collective-permute-start | bytes 294920 | tf_op jit(solution)/shard_map/ppermute | solution.py:525
  44.6 2.8 %collective-permute-done.4.refs_2_ = bf16[6,64,128]{2,1,0:T(8,128)(2,1)S(1)} collective-permute-done((bf16[6,64,128]{2,1,0:T(8,128)(2,1)S(1)}, bf16[6,64,128]{2,1,0:T(8,128)(2,1)S(1)}, u32[]{:S(2)}, u32[]{:S(2)}) %collective-permute-start.4) | collective-permute-done | bytes 98336 | tf_op jit(solution)/shard_map/ppermute | solution.py:525
  48.5 1.6 %collective-permute-start.18 = (bf16[4,2,16,1536]{3,2,1,0:T(8,128)(2,1)S(1)}, bf16[4,2,16,1536]{3,2,1,0:T(8,128)(2,1)S(1)}, u32[]{:S(2)}, u32[]{:S(2)}) collective-permute-start(bf16[4,2,16,1536]{3,2,1,0:T(8,128)(2,1)S(1)} %get-tuple-element.52.refs_0_), channel_id=1, source_target_pairs={{2,0},{0,2},{6,4},{4,6},{10,8},{8,10},{14,12},{12,14},{3,1},{1,3},... | collective-permute-start | bytes 1179656 | tf_op jit(solution)/shard_map/ppermute | solution.py:525
  50.1 1.5 %collective-permute-done.13.refs_2_ = bf16[384,128]{1,0:T(8,128)(2,1)S(1)} collective-permute-done((bf16[384,128]{1,0:T(8,128)(2,1)S(1)}, bf16[384,128]{1,0:T(8,128)(2,1)S(1)}, u32[]{:S(2)}, u32[]{:S(2)}) %collective-permute-start.13) | collective-permute-done | bytes 98336 | tf_op jit(solution)/shard_map/ppermute | solution.py:525
  51.6 2.7 %collective-permute-start.9 = (bf16[6,64,128]{2,1,0:T(8,128)(2,1)S(1)}, bf16[6,64,128]{2,1,0:T(8,128)(2,1)S(1)}, u32[]{:S(2)}, u32[]{:S(2)}) collective-permute-start(bf16[6,64,128]{2,1,0:T(8,128)(2,1)S(1)} %get-tuple-element.53), channel_id=1, source_target_pairs={{4,0},{6,2},{8,4},{10,6},{12,8},{14,10},{0,12},{2,14},{5,1},{7,3},... | collective-permute-start | bytes 294920 | tf_op jit(solution)/shard_map/ppermute | solution.py:525
  54.3 5.1 %shard_map.60 = (bf16[6,64,128]{2,1,0:T(8,128)(2,1)S(1)}, bf16[6,64,128]{2,1,0:T(8,128)(2,1)S(1)}, bf16[6,64,128]{2,1,0:T(8,128)(2,1)S(1)}, bf16[6,64,128]{2,1,0:T(8,128)(2,1)S(1)}) custom-call(s32[2]{0:T(128)S(1)} %pad_add_fusion.place_ref, f32[6,768,128]{2,1,0:T(8,128)S(1)} %bitcast.12, bf16[384,128]{1,0:T(8,128)(2,1)S(1)} %collective-permute-done.12.refs_1_, ...), custom_call_target="tpu_custom_call" | custom-call | flops 28311552 | bytes 786432 | tf_op jit(solution)/shard_map/pallas_call | solution.py:238
  59.6 2.3 %collective-permute-start.16 = (bf16[6,64,128]{2,1,0:T(8,128)(2,1)S(1)}, bf16[6,64,128]{2,1,0:T(8,128)(2,1)S(1)}, u32[]{:S(2)}, u32[]{:S(2)}) collective-permute-start(bf16[6,64,128]{2,1,0:T(8,128)(2,1)S(1)} %get-tuple-element.63), channel_id=1, source_target_pairs={{8,0},{10,2},{12,4},{14,6},{0,8},{2,10},{4,12},{6,14},{9,1},{11,3}... | collective-permute-start | bytes 294920 | tf_op jit(solution)/shard_map/ppermute | solution.py:525
  63.0 1.4 %collective-permute-start.22 = (bf16[4,2,16,1536]{3,2,1,0:T(8,128)(2,1)S(1)}, bf16[4,2,16,1536]{3,2,1,0:T(8,128)(2,1)S(1)}, u32[]{:S(2)}, u32[]{:S(2)}) collective-permute-start(bf16[4,2,16,1536]{3,2,1,0:T(8,128)(2,1)S(1)} %get-tuple-element.61.refs_1_), channel_id=1, source_target_pairs={{2,0},{0,2},{6,4},{4,6},{10,8},{8,10},{14,12},{12,14},{3,1},{1,3},... | collective-permute-start | bytes 1179656 | tf_op jit(solution)/shard_map/ppermute | solution.py:525
  64.8 2.2 %collective-permute-done.16.refs_2_ = bf16[6,64,128]{2,1,0:T(8,128)(2,1)S(1)} collective-permute-done((bf16[6,64,128]{2,1,0:T(8,128)(2,1)S(1)}, bf16[6,64,128]{2,1,0:T(8,128)(2,1)S(1)}, u32[]{:S(2)}, u32[]{:S(2)}) %collective-permute-start.16) | collective-permute-done | bytes 98336 | tf_op jit(solution)/shard_map/ppermute | solution.py:525
  69.2 1.6 %collective-permute-start.23 = (bf16[4,2,16,1536]{3,2,1,0:T(8,128)(2,1)S(1)}, bf16[4,2,16,1536]{3,2,1,0:T(8,128)(2,1)S(1)}, u32[]{:S(2)}, u32[]{:S(2)}) collective-permute-start(bf16[4,2,16,1536]{3,2,1,0:T(8,128)(2,1)S(1)} %get-tuple-element.66.refs_2_), channel_id=1, source_target_pairs={{2,0},{0,2},{6,4},{4,6},{10,8},{8,10},{14,12},{12,14},{3,1},{1,3},... | collective-permute-start | bytes 1179656 | tf_op jit(solution)/shard_map/ppermute | solution.py:525
  70.7 2.8 %elementals_early.1 = (f32[64,768]{1,0:T(8,128)S(1)}, bf16[64,768]{1,0:T(8,128)(2,1)S(1)}, bf16[64,768]{1,0:T(8,128)(2,1)S(1)}, bf16[64,768]{1,0:T(8,128)(2,1)S(1)}, bf16[2,384,3072]{2,1,0:T(8,128)(2,1)S(1)}) custom-call(s32[2]{0:T(128)S(1)} %pad_add_fusion.place_ref, s32[2]{0:T(128)S(1)} %copy-done.4, ...), custom_call_target="tpu_custom_call" | custom-call | flops 1207959552 | bytes 2359296 | tf_op jit(solution)/shard_map/elementals_early/pallas_call | solution.py:372
  74.9 2.6 %collective-permute-start.21 = (bf16[64,768]{1,0:T(8,128)(2,1)S(1)}, bf16[64,768]{1,0:T(8,128)(2,1)S(1)}, u32[]{:S(2)}, u32[]{:S(2)}) collective-permute-start(bf16[64,768]{1,0:T(8,128)(2,1)S(1)} %get-tuple-element.71), channel_id=1, source_target_pairs={{4,0},{6,2},{8,4},{10,6},{12,8},{14,10},{0,12},{2,14},{5,1},{7,3},... | collective-permute-start | bytes 294920 | tf_op jit(solution)/shard_map/ppermute | solution.py:525
  77.5 1.9 %collective-permute-done.23.refs_1_ = bf16[4,2,16,1536]{3,2,1,0:T(8,128)(2,1)S(1)} collective-permute-done((bf16[4,2,16,1536]{3,2,1,0:T(8,128)(2,1)S(1)}, bf16[4,2,16,1536]{3,2,1,0:T(8,128)(2,1)S(1)}, u32[]{:S(2)}, u32[]{:S(2)}) %collective-permute-start.23) | collective-permute-done | bytes 393248 | tf_op jit(solution)/shard_map/ppermute | solution.py:525
  79.3 2.1 %elementals_late.1 = (f32[32,768]{1,0:T(8,128)S(1)}, bf16[32,768]{1,0:T(8,128)(2,1)S(1)}, bf16[32,768]{1,0:T(8,128)(2,1)S(1)}, bf16[32,768]{1,0:T(8,128)(2,1)S(1)}) custom-call(s32[2]{0:T(128)S(1)} %pad_add_fusion.place_ref, bf16[4,2,16,1536]{3,2,1,0:T(8,128)(2,1)S(1)} %collective-permute-done.22.refs_0_, ...), custom_call_target="tpu_custom_call" | custom-call | flops 603979776 | bytes 2359296 | tf_op jit(solution)/shard_map/elementals_late/pallas_call | solution.py:372
  81.7 3.3 %collective-permute-start.25 = (bf16[32,768]{1,0:T(8,128)(2,1)S(1)}, bf16[32,768]{1,0:T(8,128)(2,1)S(1)}, u32[]{:S(2)}, u32[]{:S(2)}) collective-permute-start(bf16[32,768]{1,0:T(8,128)(2,1)S(1)} %get-tuple-element.75), channel_id=1, source_target_pairs={{8,0},{10,2},{12,4},{14,6},{0,8},{2,10},{4,12},{6,14},{9,1},{11,3}... | collective-permute-start | bytes 147464 | tf_op jit(solution)/shard_map/ppermute | solution.py:525
  85.4 2.2 %collective-permute-done.24.refs_5_ = bf16[32,768]{1,0:T(8,128)(2,1)S(1)} collective-permute-done((bf16[32,768]{1,0:T(8,128)(2,1)S(1)}, bf16[32,768]{1,0:T(8,128)(2,1)S(1)}, u32[]{:S(2)}, u32[]{:S(2)}) %collective-permute-start.24) | collective-permute-done | bytes 49184 | tf_op jit(solution)/shard_map/ppermute | solution.py:525
  89.7 2.1 %collective-permute-start.27 = (bf16[96,768]{1,0:T(8,128)(2,1)S(1)}, bf16[96,768]{1,0:T(8,128)(2,1)S(1)}, u32[]{:S(2)}, u32[]{:S(2)}) collective-permute-start(bf16[96,768]{1,0:T(8,128)(2,1)S(1)} %add_parts.1.refs_0_), channel_id=1, source_target_pairs={{4,0},{6,2},{8,4},{10,6},{12,8},{14,10},{0,12},{2,14},{5,1},{7,3},... | collective-permute-start | bytes 442376 | tf_op jit(solution)/shard_map/ppermute | solution.py:525
  93.5 2.7 %collective-permute-done.27.refs_1_ = bf16[96,768]{1,0:T(8,128)(2,1)S(1)} collective-permute-done((bf16[96,768]{1,0:T(8,128)(2,1)S(1)}, bf16[96,768]{1,0:T(8,128)(2,1)S(1)}, u32[]{:S(2)}, u32[]{:S(2)}) %collective-permute-start.27) | collective-permute-done | bytes 147488 | tf_op jit(solution)/shard_map/ppermute | solution.py:525
  96.2 1.4 %collective-permute-start.31 = (bf16[96,768]{1,0:T(8,128)(2,1)S(1)}, bf16[96,768]{1,0:T(8,128)(2,1)S(1)}, u32[]{:S(2)}, u32[]{:S(2)}) collective-permute-start(bf16[96,768]{1,0:T(8,128)(2,1)S(1)} %collective-permute-done.27.refs_1_), channel_id=1, source_target_pairs={{2,0},{0,2},{6,4},{4,6},{10,8},{8,10},{14,12},{12,14},{3,1},{1,3},... | collective-permute-start | bytes 442376 | tf_op jit(solution)/shard_map/ppermute | solution.py:525
  97.6 3.7 %collective-permute-done.28.refs_2_ = bf16[96,768]{1,0:T(8,128)(2,1)S(1)} collective-permute-done((bf16[96,768]{1,0:T(8,128)(2,1)S(1)}, bf16[96,768]{1,0:T(8,128)(2,1)S(1)}, u32[]{:S(2)}, u32[]{:S(2)}) %collective-permute-start.28) | collective-permute-done | bytes 147488 | tf_op jit(solution)/shard_map/ppermute | solution.py:525
  103.3 3.3 %project_first.1.first_ref = bf16[8,192,768]{2,1,0:T(8,128)(2,1)S(1)} custom-call(s32[2]{0:T(128)S(1)} %pad_add_fusion.place_ref, s32[2]{0:T(128)S(1)} %copy-done.4, bf16[8,2,192,384]{3,2,1,0:T(8,128)(2,1)S(1)} %bitcast.15, bf16[96,768]{1,0:T(8,128)(2,1)S(1)} %add_parts.1.refs_0_, bf16[96,768]{1,0:T(8,128)(2,1)S(1)} %collective-permute-done.27.refs_1_, ...), custom_call_target="tpu_custom_call" | custom-call | flops 1811939328 | bytes 4718592 | tf_op jit(solution)/shard_map/project_first/pallas_call | solution.py:487
  106.6 1.5 %collective-permute-done.33.refs_3_ = bf16[96,768]{1,0:T(8,128)(2,1)S(1)} collective-permute-done((bf16[96,768]{1,0:T(8,128)(2,1)S(1)}, bf16[96,768]{1,0:T(8,128)(2,1)S(1)}, u32[]{:S(2)}, u32[]{:S(2)}) %collective-permute-start.33) | collective-permute-done | bytes 147488 | tf_op jit(solution)/shard_map/ppermute | solution.py:525
  108.2 5.1 %project_second.1 = bf16[8,2,2,192,384]{4,3,2,1,0:T(8,128)(2,1)} custom-call(s32[2]{0:T(128)S(1)} %pad_add_fusion.place_ref, s32[2]{0:T(128)S(1)} %copy-done.4, bf16[8,2,192,384]{3,2,1,0:T(8,128)(2,1)S(1)} %bitcast.16, bf16[8,192,768]{2,1,0:T(8,128)(2,1)S(1)} %project_first.1.first_ref, bf16[96,768]{1,0:T(8,128)(2,1)S(1)} %collective-permute-done.30.refs_0_, ...), custom_call_target="tpu_custom_call" | custom-call | flops 1811939328 | bytes 7077888 | tf_op jit(solution)/shard_map/project_second/pallas_call | solution.py:503
  (69 shorter events, 20.1 us)
Async XLA Ops:
  1.3 10.7 %collective-permute-start = (bf16[600,128]{1,0:T(8,128)(2,1)S(1)}, bf16[600,128]{1,0:T(8,128)(2,1)S(1)}, u32[]{:S(2)}, u32[]{:S(2)}) collective-permute-start(bf16[600,128]{1,0:T(8,128)(2,1)S(1)} %get-tuple-element.41.refs_0_), channel_id=1, source_target_pairs={{12,0},{14,2},{0,4},{2,6},{4,8},{6,10},{8,12},{10,14},{13,1},{15,3... | collective-permute-start | bytes 460808 | tf_op jit(solution)/shard_map/ppermute | solution.py:525
  4.4 16.2 %collective-permute-start.1 = (bf16[600,128]{1,0:T(8,128)(2,1)S(1)}, bf16[600,128]{1,0:T(8,128)(2,1)S(1)}, u32[]{:S(2)}, u32[]{:S(2)}) collective-permute-start(bf16[600,128]{1,0:T(8,128)(2,1)S(1)} %get-tuple-element.42), channel_id=1, source_target_pairs={{8,0},{10,2},{12,4},{14,6},{0,8},{2,10},{4,12},{6,14},{9,1},{11,3}... | collective-permute-start | bytes 460808 | tf_op jit(solution)/shard_map/ppermute | solution.py:525
  7.0 13.6 %collective-permute-start.2 = (bf16[600,128]{1,0:T(8,128)(2,1)S(1)}, bf16[600,128]{1,0:T(8,128)(2,1)S(1)}, u32[]{:S(2)}, u32[]{:S(2)}) collective-permute-start(bf16[600,128]{1,0:T(8,128)(2,1)S(1)} %get-tuple-element.43), channel_id=1, source_target_pairs={{4,0},{6,2},{8,4},{10,6},{12,8},{14,10},{0,12},{2,14},{5,1},{7,3},... | collective-permute-start | bytes 460808 | tf_op jit(solution)/shard_map/ppermute | solution.py:525
  10.6 22.1 %collective-permute-start.6 = (bf16[384,128]{1,0:T(8,128)(2,1)S(1)}, bf16[384,128]{1,0:T(8,128)(2,1)S(1)}, u32[]{:S(2)}, u32[]{:S(2)}) collective-permute-start(bf16[384,128]{1,0:T(8,128)(2,1)S(1)} %get-tuple-element.48.refs_1_), channel_id=1, source_target_pairs={{12,0},{14,2},{0,4},{2,6},{4,8},{6,10},{8,12},{10,14},{13,1},{15,3... | collective-permute-start | bytes 294920 | tf_op jit(solution)/shard_map/ppermute | solution.py:525
  11.4 22.8 %collective-permute-start.7 = (bf16[384,128]{1,0:T(8,128)(2,1)S(1)}, bf16[384,128]{1,0:T(8,128)(2,1)S(1)}, u32[]{:S(2)}, u32[]{:S(2)}) collective-permute-start(bf16[384,128]{1,0:T(8,128)(2,1)S(1)} %get-tuple-element.49), channel_id=1, source_target_pairs={{8,0},{10,2},{12,4},{14,6},{0,8},{2,10},{4,12},{6,14},{9,1},{11,3}... | collective-permute-start | bytes 294920 | tf_op jit(solution)/shard_map/ppermute | solution.py:525
  12.0 25.1 %collective-permute-start.8 = (bf16[384,128]{1,0:T(8,128)(2,1)S(1)}, bf16[384,128]{1,0:T(8,128)(2,1)S(1)}, u32[]{:S(2)}, u32[]{:S(2)}) collective-permute-start(bf16[384,128]{1,0:T(8,128)(2,1)S(1)} %get-tuple-element.50), channel_id=1, source_target_pairs={{4,0},{6,2},{8,4},{10,6},{12,8},{14,10},{0,12},{2,14},{5,1},{7,3},... | collective-permute-start | bytes 294920 | tf_op jit(solution)/shard_map/ppermute | solution.py:525
  26.0 17.1 %collective-permute-start.3 = (bf16[6,64,128]{2,1,0:T(8,128)(2,1)S(1)}, bf16[6,64,128]{2,1,0:T(8,128)(2,1)S(1)}, u32[]{:S(2)}, u32[]{:S(2)}) collective-permute-start(bf16[6,64,128]{2,1,0:T(8,128)(2,1)S(1)} %get-tuple-element.45), channel_id=1, source_target_pairs={{4,0},{6,2},{8,4},{10,6},{12,8},{14,10},{0,12},{2,14},{5,1},{7,3},... | collective-permute-start | bytes 294920 | tf_op jit(solution)/shard_map/ppermute | solution.py:525
  32.7 14.7 %collective-permute-start.4 = (bf16[6,64,128]{2,1,0:T(8,128)(2,1)S(1)}, bf16[6,64,128]{2,1,0:T(8,128)(2,1)S(1)}, u32[]{:S(2)}, u32[]{:S(2)}) collective-permute-start(bf16[6,64,128]{2,1,0:T(8,128)(2,1)S(1)} %get-tuple-element.46), channel_id=1, source_target_pairs={{8,0},{10,2},{12,4},{14,6},{0,8},{2,10},{4,12},{6,14},{9,1},{11,3}... | collective-permute-start | bytes 294920 | tf_op jit(solution)/shard_map/ppermute | solution.py:525
  32.7 14.7 %collective-permute-start.5 = (bf16[6,64,128]{2,1,0:T(8,128)(2,1)S(1)}, bf16[6,64,128]{2,1,0:T(8,128)(2,1)S(1)}, u32[]{:S(2)}, u32[]{:S(2)}) collective-permute-start(bf16[6,64,128]{2,1,0:T(8,128)(2,1)S(1)} %get-tuple-element.47), channel_id=1, source_target_pairs={{12,0},{14,2},{0,4},{2,6},{4,8},{6,10},{8,12},{10,14},{13,1},{15,3... | collective-permute-start | bytes 294920 | tf_op jit(solution)/shard_map/ppermute | solution.py:525
  34.2 14.3 %collective-permute-start.12 = (bf16[384,128]{1,0:T(8,128)(2,1)S(1)}, bf16[384,128]{1,0:T(8,128)(2,1)S(1)}, u32[]{:S(2)}, u32[]{:S(2)}) collective-permute-start(bf16[384,128]{1,0:T(8,128)(2,1)S(1)} %get-tuple-element.56), channel_id=1, source_target_pairs={{12,0},{14,2},{0,4},{2,6},{4,8},{6,10},{8,12},{10,14},{13,1},{15,3... | collective-permute-start | bytes 294920 | tf_op jit(solution)/shard_map/ppermute | solution.py:525
  37.1 14.5 %collective-permute-start.13 = (bf16[384,128]{1,0:T(8,128)(2,1)S(1)}, bf16[384,128]{1,0:T(8,128)(2,1)S(1)}, u32[]{:S(2)}, u32[]{:S(2)}) collective-permute-start(bf16[384,128]{1,0:T(8,128)(2,1)S(1)} %get-tuple-element.57), channel_id=1, source_target_pairs={{8,0},{10,2},{12,4},{14,6},{0,8},{2,10},{4,12},{6,14},{9,1},{11,3}... | collective-permute-start | bytes 294920 | tf_op jit(solution)/shard_map/ppermute | solution.py:525
  43.0 11.2 %collective-permute-start.14 = (bf16[384,128]{1,0:T(8,128)(2,1)S(1)}, bf16[384,128]{1,0:T(8,128)(2,1)S(1)}, u32[]{:S(2)}, u32[]{:S(2)}) collective-permute-start(bf16[384,128]{1,0:T(8,128)(2,1)S(1)} %get-tuple-element.58), channel_id=1, source_target_pairs={{4,0},{6,2},{8,4},{10,6},{12,8},{14,10},{0,12},{2,14},{5,1},{7,3},... | collective-permute-start | bytes 294920 | tf_op jit(solution)/shard_map/ppermute | solution.py:525
  47.4 12.1 %collective-permute-start.10 = (bf16[6,64,128]{2,1,0:T(8,128)(2,1)S(1)}, bf16[6,64,128]{2,1,0:T(8,128)(2,1)S(1)}, u32[]{:S(2)}, u32[]{:S(2)}) collective-permute-start(bf16[6,64,128]{2,1,0:T(8,128)(2,1)S(1)} %get-tuple-element.54), channel_id=1, source_target_pairs={{8,0},{10,2},{12,4},{14,6},{0,8},{2,10},{4,12},{6,14},{9,1},{11,3}... | collective-permute-start | bytes 294920 | tf_op jit(solution)/shard_map/ppermute | solution.py:525
  47.5 14.4 %collective-permute-start.11 = (bf16[6,64,128]{2,1,0:T(8,128)(2,1)S(1)}, bf16[6,64,128]{2,1,0:T(8,128)(2,1)S(1)}, u32[]{:S(2)}, u32[]{:S(2)}) collective-permute-start(bf16[6,64,128]{2,1,0:T(8,128)(2,1)S(1)} %get-tuple-element.55), channel_id=1, source_target_pairs={{12,0},{14,2},{0,4},{2,6},{4,8},{6,10},{8,12},{10,14},{13,1},{15,3... | collective-permute-start | bytes 294920 | tf_op jit(solution)/shard_map/ppermute | solution.py:525
  48.5 22.2 %collective-permute-start.18 = (bf16[4,2,16,1536]{3,2,1,0:T(8,128)(2,1)S(1)}, bf16[4,2,16,1536]{3,2,1,0:T(8,128)(2,1)S(1)}, u32[]{:S(2)}, u32[]{:S(2)}) collective-permute-start(bf16[4,2,16,1536]{3,2,1,0:T(8,128)(2,1)S(1)} %get-tuple-element.52.refs_0_), channel_id=1, source_target_pairs={{2,0},{0,2},{6,4},{4,6},{10,8},{8,10},{14,12},{12,14},{3,1},{1,3},... | collective-permute-start | bytes 1179656 | tf_op jit(solution)/shard_map/ppermute | solution.py:525
  51.6 10.6 %collective-permute-start.9 = (bf16[6,64,128]{2,1,0:T(8,128)(2,1)S(1)}, bf16[6,64,128]{2,1,0:T(8,128)(2,1)S(1)}, u32[]{:S(2)}, u32[]{:S(2)}) collective-permute-start(bf16[6,64,128]{2,1,0:T(8,128)(2,1)S(1)} %get-tuple-element.53), channel_id=1, source_target_pairs={{4,0},{6,2},{8,4},{10,6},{12,8},{14,10},{0,12},{2,14},{5,1},{7,3},... | collective-permute-start | bytes 294920 | tf_op jit(solution)/shard_map/ppermute | solution.py:525
  59.3 5.5 %collective-permute-start.15 = (bf16[6,64,128]{2,1,0:T(8,128)(2,1)S(1)}, bf16[6,64,128]{2,1,0:T(8,128)(2,1)S(1)}, u32[]{:S(2)}, u32[]{:S(2)}) collective-permute-start(bf16[6,64,128]{2,1,0:T(8,128)(2,1)S(1)} %get-tuple-element.62), channel_id=1, source_target_pairs={{4,0},{6,2},{8,4},{10,6},{12,8},{14,10},{0,12},{2,14},{5,1},{7,3},... | collective-permute-start | bytes 294920 | tf_op jit(solution)/shard_map/ppermute | solution.py:525
  59.6 7.5 %collective-permute-start.16 = (bf16[6,64,128]{2,1,0:T(8,128)(2,1)S(1)}, bf16[6,64,128]{2,1,0:T(8,128)(2,1)S(1)}, u32[]{:S(2)}, u32[]{:S(2)}) collective-permute-start(bf16[6,64,128]{2,1,0:T(8,128)(2,1)S(1)} %get-tuple-element.63), channel_id=1, source_target_pairs={{8,0},{10,2},{12,4},{14,6},{0,8},{2,10},{4,12},{6,14},{9,1},{11,3}... | collective-permute-start | bytes 294920 | tf_op jit(solution)/shard_map/ppermute | solution.py:525
  61.9 6.4 %collective-permute-start.17 = (bf16[6,64,128]{2,1,0:T(8,128)(2,1)S(1)}, bf16[6,64,128]{2,1,0:T(8,128)(2,1)S(1)}, u32[]{:S(2)}, u32[]{:S(2)}) collective-permute-start(bf16[6,64,128]{2,1,0:T(8,128)(2,1)S(1)} %get-tuple-element.64), channel_id=1, source_target_pairs={{12,0},{14,2},{0,4},{2,6},{4,8},{6,10},{8,12},{10,14},{13,1},{15,3... | collective-permute-start | bytes 294920 | tf_op jit(solution)/shard_map/ppermute | solution.py:525
  63.0 14.4 %collective-permute-start.22 = (bf16[4,2,16,1536]{3,2,1,0:T(8,128)(2,1)S(1)}, bf16[4,2,16,1536]{3,2,1,0:T(8,128)(2,1)S(1)}, u32[]{:S(2)}, u32[]{:S(2)}) collective-permute-start(bf16[4,2,16,1536]{3,2,1,0:T(8,128)(2,1)S(1)} %get-tuple-element.61.refs_1_), channel_id=1, source_target_pairs={{2,0},{0,2},{6,4},{4,6},{10,8},{8,10},{14,12},{12,14},{3,1},{1,3},... | collective-permute-start | bytes 1179656 | tf_op jit(solution)/shard_map/ppermute | solution.py:525
  69.2 10.1 %collective-permute-start.23 = (bf16[4,2,16,1536]{3,2,1,0:T(8,128)(2,1)S(1)}, bf16[4,2,16,1536]{3,2,1,0:T(8,128)(2,1)S(1)}, u32[]{:S(2)}, u32[]{:S(2)}) collective-permute-start(bf16[4,2,16,1536]{3,2,1,0:T(8,128)(2,1)S(1)} %get-tuple-element.66.refs_2_), channel_id=1, source_target_pairs={{2,0},{0,2},{6,4},{4,6},{10,8},{8,10},{14,12},{12,14},{3,1},{1,3},... | collective-permute-start | bytes 1179656 | tf_op jit(solution)/shard_map/ppermute | solution.py:525
  73.6 11.4 %collective-permute-start.19 = (bf16[64,768]{1,0:T(8,128)(2,1)S(1)}, bf16[64,768]{1,0:T(8,128)(2,1)S(1)}, u32[]{:S(2)}, u32[]{:S(2)}) collective-permute-start(bf16[64,768]{1,0:T(8,128)(2,1)S(1)} %get-tuple-element.69), channel_id=1, source_target_pairs={{12,0},{14,2},{0,4},{2,6},{4,8},{6,10},{8,12},{10,14},{13,1},{15,3... | collective-permute-start | bytes 294920 | tf_op jit(solution)/shard_map/ppermute | solution.py:525
  73.6 11.7 %collective-permute-start.20 = (bf16[64,768]{1,0:T(8,128)(2,1)S(1)}, bf16[64,768]{1,0:T(8,128)(2,1)S(1)}, u32[]{:S(2)}, u32[]{:S(2)}) collective-permute-start(bf16[64,768]{1,0:T(8,128)(2,1)S(1)} %get-tuple-element.70), channel_id=1, source_target_pairs={{8,0},{10,2},{12,4},{14,6},{0,8},{2,10},{4,12},{6,14},{9,1},{11,3}... | collective-permute-start | bytes 294920 | tf_op jit(solution)/shard_map/ppermute | solution.py:525
  74.9 10.5 %collective-permute-start.21 = (bf16[64,768]{1,0:T(8,128)(2,1)S(1)}, bf16[64,768]{1,0:T(8,128)(2,1)S(1)}, u32[]{:S(2)}, u32[]{:S(2)}) collective-permute-start(bf16[64,768]{1,0:T(8,128)(2,1)S(1)} %get-tuple-element.71), channel_id=1, source_target_pairs={{4,0},{6,2},{8,4},{10,6},{12,8},{14,10},{0,12},{2,14},{5,1},{7,3},... | collective-permute-start | bytes 294920 | tf_op jit(solution)/shard_map/ppermute | solution.py:525
  81.4 6.1 %collective-permute-start.24 = (bf16[32,768]{1,0:T(8,128)(2,1)S(1)}, bf16[32,768]{1,0:T(8,128)(2,1)S(1)}, u32[]{:S(2)}, u32[]{:S(2)}) collective-permute-start(bf16[32,768]{1,0:T(8,128)(2,1)S(1)} %get-tuple-element.74), channel_id=1, source_target_pairs={{12,0},{14,2},{0,4},{2,6},{4,8},{6,10},{8,12},{10,14},{13,1},{15,3... | collective-permute-start | bytes 147464 | tf_op jit(solution)/shard_map/ppermute | solution.py:525
  81.7 6.5 %collective-permute-start.25 = (bf16[32,768]{1,0:T(8,128)(2,1)S(1)}, bf16[32,768]{1,0:T(8,128)(2,1)S(1)}, u32[]{:S(2)}, u32[]{:S(2)}) collective-permute-start(bf16[32,768]{1,0:T(8,128)(2,1)S(1)} %get-tuple-element.75), channel_id=1, source_target_pairs={{8,0},{10,2},{12,4},{14,6},{0,8},{2,10},{4,12},{6,14},{9,1},{11,3}... | collective-permute-start | bytes 147464 | tf_op jit(solution)/shard_map/ppermute | solution.py:525
  89.7 6.5 %collective-permute-start.27 = (bf16[96,768]{1,0:T(8,128)(2,1)S(1)}, bf16[96,768]{1,0:T(8,128)(2,1)S(1)}, u32[]{:S(2)}, u32[]{:S(2)}) collective-permute-start(bf16[96,768]{1,0:T(8,128)(2,1)S(1)} %add_parts.1.refs_0_), channel_id=1, source_target_pairs={{4,0},{6,2},{8,4},{10,6},{12,8},{14,10},{0,12},{2,14},{5,1},{7,3},... | collective-permute-start | bytes 442376 | tf_op jit(solution)/shard_map/ppermute | solution.py:525
  91.7 9.5 %collective-permute-start.28 = (bf16[96,768]{1,0:T(8,128)(2,1)S(1)}, bf16[96,768]{1,0:T(8,128)(2,1)S(1)}, u32[]{:S(2)}, u32[]{:S(2)}) collective-permute-start(bf16[96,768]{1,0:T(8,128)(2,1)S(1)} %add_parts.1.refs_0_), channel_id=1, source_target_pairs={{8,0},{10,2},{12,4},{14,6},{0,8},{2,10},{4,12},{6,14},{9,1},{11,3}... | collective-permute-start | bytes 442376 | tf_op jit(solution)/shard_map/ppermute | solution.py:525
  92.1 10.5 %collective-permute-start.29 = (bf16[96,768]{1,0:T(8,128)(2,1)S(1)}, bf16[96,768]{1,0:T(8,128)(2,1)S(1)}, u32[]{:S(2)}, u32[]{:S(2)}) collective-permute-start(bf16[96,768]{1,0:T(8,128)(2,1)S(1)} %add_parts.1.refs_0_), channel_id=1, source_target_pairs={{12,0},{14,2},{0,4},{2,6},{4,8},{6,10},{8,12},{10,14},{13,1},{15,3... | collective-permute-start | bytes 442376 | tf_op jit(solution)/shard_map/ppermute | solution.py:525
  92.4 14.2 %collective-permute-start.30 = (bf16[96,768]{1,0:T(8,128)(2,1)S(1)}, bf16[96,768]{1,0:T(8,128)(2,1)S(1)}, u32[]{:S(2)}, u32[]{:S(2)}) collective-permute-start(bf16[96,768]{1,0:T(8,128)(2,1)S(1)} %add_parts.1.refs_0_), channel_id=1, source_target_pairs={{2,0},{0,2},{6,4},{4,6},{10,8},{8,10},{14,12},{12,14},{3,1},{1,3},... | collective-permute-start | bytes 442376 | tf_op jit(solution)/shard_map/ppermute | solution.py:525
  96.2 10.4 %collective-permute-start.31 = (bf16[96,768]{1,0:T(8,128)(2,1)S(1)}, bf16[96,768]{1,0:T(8,128)(2,1)S(1)}, u32[]{:S(2)}, u32[]{:S(2)}) collective-permute-start(bf16[96,768]{1,0:T(8,128)(2,1)S(1)} %collective-permute-done.27.refs_1_), channel_id=1, source_target_pairs={{2,0},{0,2},{6,4},{4,6},{10,8},{8,10},{14,12},{12,14},{3,1},{1,3},... | collective-permute-start | bytes 442376 | tf_op jit(solution)/shard_map/ppermute | solution.py:525
  102.6 5.6 %collective-permute-start.33 = (bf16[96,768]{1,0:T(8,128)(2,1)S(1)}, bf16[96,768]{1,0:T(8,128)(2,1)S(1)}, u32[]{:S(2)}, u32[]{:S(2)}) collective-permute-start(bf16[96,768]{1,0:T(8,128)(2,1)S(1)} %collective-permute-done.29.refs_3_), channel_id=1, source_target_pairs={{2,0},{0,2},{6,4},{4,6},{10,8},{8,10},{14,12},{12,14},{3,1},{1,3},... | collective-permute-start | bytes 442376 | tf_op jit(solution)/shard_map/ppermute | solution.py:525
  (8 other events, 87.4 us)
